TPU v7x, 32 devices: a whole 2x2x4 slice. The times are simulated.
32 devices in a mesh: dp: 16 (over z, y, core), mp: 2 (over x).
Axes of the slice: x: 2, y: 2, z: 4, core: 2. Of those that a mesh axis runs over, the one named last changes fastest.
Arguments:
- tokens: bfloat16 [8976, 1024], P('dp'), may hold values from -6 to 6
- query_weight: bfloat16 [1024, 1024], P(None, 'mp'), may hold values from -0.1875 to 0.1875
- key_weight: bfloat16 [1024, 1024], P(None, 'mp'), may hold values from -0.1875 to 0.1875
- value_weight: bfloat16 [1024, 1024], P(None, 'mp'), may hold values from -0.1875 to 0.1875
- output_weight: bfloat16 [1024, 1024], P('mp'), may hold values from -1.5 to 1.5
- query_position: bfloat16 [1024, 1024], P(None, 'mp'), may hold values from -0.1875 to 0.1875
- key_position: bfloat16 [1024, 1024], P(None, 'mp'), may hold values from -0.1875 to 0.1875
- position_tables: bfloat16 [3, 128, 1024], replicated, may hold values from -6 to 6
- gain_one: float32 [1024], replicated, may hold values from 0.5 to 1.5
- shift_one: float32 [1024], replicated, may hold values from -2 to 2
- up_weight: bfloat16 [1024, 4096], P(None, 'mp'), may hold values from -0.1875 to 0.1875
- down_weight: bfloat16 [4096, 1024], P('mp'), may hold values from -0.09375 to 0.09375
- gain_two: float32 [1024], replicated, may hold values from 0.5 to 1.5
- shift_two: float32 [1024], replicated, may hold values from -2 to 2
- buckets: int32 [16, 3, 561, 561], P('dp'), may hold values from 0 to 127
- text_length: int32 [16], P('dp'), may hold values from 1 to 512, as said below
- cotangent: bfloat16 [8976, 1024], P('dp'), may hold values from -6 to 6
Outputs:
- layer_output: bfloat16 [8976, 1024], P('dp')
- input_gradient: bfloat16 [8976, 1024], P('dp')
- query_gradient: float32 [1024, 1024], P('dp', 'mp')
- key_gradient: float32 [1024, 1024], P('dp', 'mp')
- value_gradient: float32 [1024, 1024], P('dp', 'mp')
- output_gradient: float32 [1024, 1024], P('mp', 'dp')
- query_position_gradient: float32 [1024, 1024], P('dp', 'mp')
- key_position_gradient: float32 [1024, 1024], P('dp', 'mp')
- table_gradient: float32 [3, 128, 1024], P(None, None, ('dp', 'mp'))
- gain_one_gradient: float32 [1024], P('dp')
- shift_one_gradient: float32 [1024], P('dp')
- up_gradient: float32 [1024, 4096], P('dp', 'mp')
- down_gradient: float32 [4096, 1024], P('mp', 'dp')
- gain_two_gradient: float32 [1024], P('dp')
- shift_two_gradient: float32 [1024], P('dp')
Inputs may be any that keep to these rules, and one draw needn't show every extreme that they name: `text_length`: some page uses all 512 text tokens and some page uses exactly one.
All inputs are finite; a program needn't handle non-finite values.
Results may differ from a plain program's by a relative error of at most 0.015.
Values sent between devices are 32-bit elements; how exact they have to be, the bound alone decides.
No kernel may reach another device: no remote copies, remote signals or barrier semaphores. Data moves between devices by JAX's collectives and lax.ppermute only.
A program may use at most 384 MiB of HBM per device.

v0:
```python
import jax
import jax.numpy as jnp
from jax import lax
from jax.sharding import PartitionSpec as P

D = 1024
HEAD = 64
REL = 128
TEXT = 512


epsilon = 1e-05
highest = lax.Precision.HIGHEST


def product(left, right):
    return jnp.dot(left, right, preferred_element_type=jnp.float32)


def product_left(left, right):
    return lax.dot_general(
        left, right, (((0,), (0,)), ((), ())), preferred_element_type=jnp.float32
    )


def product_right(left, right):
    return lax.dot_general(
        left, right, (((1,), (1,)), ((), ())), preferred_element_type=jnp.float32
    )


def exact_left(left, right):
    return lax.dot_general(
        left, right, (((0,), (0,)), ((), ())), precision=highest, preferred_element_type=jnp.float32
    )


def exact_right(left, right):
    return lax.dot_general(
        left, right, (((1,), (1,)), ((), ())), precision=highest, preferred_element_type=jnp.float32
    )


def split_heads(flat, page_count, page_span):
    return flat.reshape(page_count, page_span, -1, HEAD).transpose(0, 2, 1, 3)


def merge_heads(split):
    return split.transpose(0, 2, 1, 3).reshape(-1, split.shape[1] * split.shape[3])


def norm_forward(summed, gain, shift):
    centred = summed - jnp.mean(summed, axis=1, keepdims=True)
    inverse = lax.rsqrt(jnp.mean(centred * centred, axis=1, keepdims=True) + epsilon)
    normal = centred * inverse
    return (normal * gain + shift, normal, inverse)


def norm_backward(upstream, normal, inverse, gain):
    scaled = upstream * gain
    inner = jnp.mean(scaled, axis=1, keepdims=True)
    aligned = jnp.mean(scaled * normal, axis=1, keepdims=True)
    return (
        inverse * (scaled - inner - normal * aligned),
        jnp.sum(upstream * normal, axis=0),
        jnp.sum(upstream, axis=0),
    )


def one_hot_of(bucket_plane):
    return (bucket_plane[:, :, None] == jnp.arange(REL, dtype=jnp.int32)[None, None, :]).astype(
        jnp.bfloat16
    )


def relative_scores(queries, keys_page, bucket, pos_key, pos_query):
    raw = jnp.einsum("hse,hte->hst", queries, keys_page, preferred_element_type=jnp.float32)
    for relation in range(3):
        selector = one_hot_of(bucket[relation])
        near_table = jnp.einsum(
            "hse,hbe->hsb", queries, pos_key[relation], preferred_element_type=jnp.float32
        ).astype(jnp.bfloat16)
        raw = raw + jnp.einsum(
            "hsb,stb->hst", near_table, selector, preferred_element_type=jnp.float32
        )
        far_table = jnp.einsum(
            "hte,hbe->hbt", keys_page, pos_query[relation], preferred_element_type=jnp.float32
        ).astype(jnp.bfloat16)
        raw = raw + jnp.einsum(
            "hbt,stb->hst", far_table, selector, preferred_element_type=jnp.float32
        )
    return raw


def shards(
    tokens,
    query_weight,
    key_weight,
    value_weight,
    output_weight,
    query_position,
    key_position,
    position_tables,
    gain_one,
    shift_one,
    up_weight,
    down_weight,
    gain_two,
    shift_two,
    buckets,
    text_length,
    cotangent,
):
    page_count = buckets.shape[0]
    page_span = buckets.shape[2]
    heads_local = query_weight.shape[1] // HEAD
    score_scale = (7.0 * HEAD) ** (-0.5)
    query_rows = split_heads(
        product(tokens, query_weight).astype(jnp.bfloat16), page_count, page_span
    )
    key_rows = split_heads(product(tokens, key_weight).astype(jnp.bfloat16), page_count, page_span)
    value_rows = split_heads(
        product(tokens, value_weight).astype(jnp.bfloat16), page_count, page_span
    )
    tables_flat = position_tables.reshape(3 * REL, D)
    pos_key = (
        product(tables_flat, key_position)
        .astype(jnp.bfloat16)
        .reshape(3, REL, heads_local, HEAD)
        .transpose(0, 2, 1, 3)
    )
    pos_query = (
        product(tables_flat, query_position)
        .astype(jnp.bfloat16)
        .reshape(3, REL, heads_local, HEAD)
        .transpose(0, 2, 1, 3)
    )

    def scores_of(queries, keys_page, bucket, used):
        raw = relative_scores(queries, keys_page, bucket, pos_key, pos_query)
        position = jnp.arange(page_span)
        key_valid = (position >= TEXT) | (position < used)
        return jnp.where(key_valid[None, None, :], raw * score_scale, -1e30)

    def page_forward(items):
        queries, keys_page, values_page, bucket, used = items
        scores = scores_of(queries, keys_page, bucket, used)
        row_max = jnp.max(scores, axis=2, keepdims=True)
        unscaled = jnp.exp(scores - row_max)
        row_total = jnp.sum(unscaled, axis=2, keepdims=True)
        probability = (unscaled / row_total).astype(jnp.bfloat16)
        context = jnp.einsum(
            "hst,hte->hse", probability, values_page, preferred_element_type=jnp.float32
        )
        return (context.astype(jnp.bfloat16), row_max + jnp.log(row_total))

    context, log_total = lax.map(
        page_forward, (query_rows, key_rows, value_rows, buckets, text_length)
    )
    context_flat = merge_heads(context)
    attended = lax.psum(product(context_flat, output_weight), "mp")
    first, normal_one, inverse_one = norm_forward(
        tokens.astype(jnp.float32) + attended, gain_one, shift_one
    )
    first_low = first.astype(jnp.bfloat16)
    upward = product(first_low, up_weight)
    hidden = jax.nn.gelu(upward, approximate=False).astype(jnp.bfloat16)
    feed = lax.psum(product(hidden, down_weight), "mp")
    final, normal_two, inverse_two = norm_forward(first + feed, gain_two, shift_two)
    layer_output = final.astype(jnp.bfloat16)
    second_back, gain_two_grad, shift_two_grad = norm_backward(
        cotangent.astype(jnp.float32), normal_two, inverse_two, gain_two
    )
    second_low = second_back.astype(jnp.bfloat16)
    down_grad = product_left(hidden, second_low)
    hidden_back = product_right(second_low, down_weight)
    gelu_back = jax.vjp(lambda inner_value: jax.nn.gelu(inner_value, approximate=False), upward)[1]
    upward_back = gelu_back(hidden_back)[0].astype(jnp.bfloat16)
    up_grad = product_left(first_low, upward_back)
    first_back = second_back + lax.psum(product_right(upward_back, up_weight), "mp")
    residual_back, gain_one_grad, shift_one_grad = norm_backward(
        first_back, normal_one, inverse_one, gain_one
    )
    residual_low = residual_back.astype(jnp.bfloat16)
    output_grad = product_left(context_flat, residual_low)
    context_back = split_heads(
        product_right(residual_low, output_weight).astype(jnp.bfloat16), page_count, page_span
    )

    def page_backward(items):
        queries, keys_page, values_page, bucket, used, log_page, upstream = items
        probability = jnp.exp(scores_of(queries, keys_page, bucket, used) - log_page)
        values_back = jnp.einsum(
            "hst,hse->hte",
            probability.astype(jnp.bfloat16),
            upstream,
            preferred_element_type=jnp.float32,
        )
        prob_back = jnp.einsum(
            "hse,hte->hst", upstream, values_page, preferred_element_type=jnp.float32
        )
        inner = jnp.sum(prob_back * probability, axis=2, keepdims=True)
        raw_back = (probability * (prob_back - inner) * score_scale).astype(jnp.bfloat16)
        query_back = jnp.einsum(
            "hst,hte->hse", raw_back, keys_page, preferred_element_type=jnp.float32
        )
        key_back = jnp.einsum("hst,hse->hte", raw_back, queries, preferred_element_type=jnp.float32)
        key_table_back = []
        query_table_back = []
        for relation in range(3):
            selector = one_hot_of(bucket[relation])
            near_back = jnp.einsum(
                "hst,stb->hsb", raw_back, selector, preferred_element_type=jnp.float32
            ).astype(jnp.bfloat16)
            far_back = jnp.einsum(
                "hst,stb->hbt", raw_back, selector, preferred_element_type=jnp.float32
            ).astype(jnp.bfloat16)
            query_back = query_back + jnp.einsum(
                "hsb,hbe->hse", near_back, pos_key[relation], preferred_element_type=jnp.float32
            )
            key_back = key_back + jnp.einsum(
                "hbt,hbe->hte", far_back, pos_query[relation], preferred_element_type=jnp.float32
            )
            key_table_back.append(
                jnp.einsum("hsb,hse->hbe", near_back, queries, preferred_element_type=jnp.float32)
            )
            query_table_back.append(
                jnp.einsum("hbt,hte->hbe", far_back, keys_page, preferred_element_type=jnp.float32)
            )
        return (
            query_back.astype(jnp.bfloat16),
            key_back.astype(jnp.bfloat16),
            values_back.astype(jnp.bfloat16),
            jnp.stack(key_table_back),
            jnp.stack(query_table_back),
        )

    query_back, key_back, values_back, key_table_back, query_table_back = lax.map(
        page_backward,
        (query_rows, key_rows, value_rows, buckets, text_length, log_total, context_back),
    )
    query_flat = merge_heads(query_back)
    key_flat = merge_heads(key_back)
    value_flat = merge_heads(values_back)
    query_grad = product_left(tokens, query_flat)
    key_grad = product_left(tokens, key_flat)
    value_grad = product_left(tokens, value_flat)
    input_part = (
        product_right(query_flat, query_weight)
        + product_right(key_flat, key_weight)
        + product_right(value_flat, value_weight)
    )
    input_gradient = (residual_back + lax.psum(input_part, "mp")).astype(jnp.bfloat16)
    key_table_sum = (
        jnp.sum(key_table_back, axis=0).transpose(0, 2, 1, 3).reshape(3 * REL, heads_local * HEAD)
    )
    query_table_sum = (
        jnp.sum(query_table_back, axis=0).transpose(0, 2, 1, 3).reshape(3 * REL, heads_local * HEAD)
    )
    tables_wide = tables_flat.astype(jnp.float32)
    key_position_grad = exact_left(tables_wide, key_table_sum)
    query_position_grad = exact_left(tables_wide, query_table_sum)
    table_part = exact_right(key_table_sum, key_position.astype(jnp.float32)) + exact_right(
        query_table_sum, query_position.astype(jnp.float32)
    )
    table_gradient = lax.psum_scatter(
        table_part.reshape(3, REL, D), ("dp", "mp"), scatter_dimension=2, tiled=True
    )
    summed = (
        lax.psum_scatter(query_grad, "dp", scatter_dimension=0, tiled=True),
        lax.psum_scatter(key_grad, "dp", scatter_dimension=0, tiled=True),
        lax.psum_scatter(value_grad, "dp", scatter_dimension=0, tiled=True),
        lax.psum_scatter(output_grad, "dp", scatter_dimension=1, tiled=True),
        lax.psum_scatter(query_position_grad, "dp", scatter_dimension=0, tiled=True),
        lax.psum_scatter(key_position_grad, "dp", scatter_dimension=0, tiled=True),
        lax.psum_scatter(up_grad, "dp", scatter_dimension=0, tiled=True),
        lax.psum_scatter(down_grad, "dp", scatter_dimension=1, tiled=True),
        lax.psum_scatter(gain_one_grad, "dp", scatter_dimension=0, tiled=True),
        lax.psum_scatter(shift_one_grad, "dp", scatter_dimension=0, tiled=True),
        lax.psum_scatter(gain_two_grad, "dp", scatter_dimension=0, tiled=True),
        lax.psum_scatter(shift_two_grad, "dp", scatter_dimension=0, tiled=True),
    )
    return (
        layer_output,
        input_gradient,
        summed[0],
        summed[1],
        summed[2],
        summed[3],
        summed[4],
        summed[5],
        table_gradient,
        summed[8],
        summed[9],
        summed[6],
        summed[7],
        summed[10],
        summed[11],
    )


def solution(mesh):
    return jax.shard_map(
        shards,
        mesh=mesh,
        in_specs=(
            P("dp", None),
            P(None, "mp"),
            P(None, "mp"),
            P(None, "mp"),
            P("mp", None),
            P(None, "mp"),
            P(None, "mp"),
            P(),
            P(),
            P(),
            P(None, "mp"),
            P("mp", None),
            P(),
            P(),
            P("dp", None, None, None),
            P("dp"),
            P("dp", None),
        ),
        out_specs=(
            P("dp", None),
            P("dp", None),
            P("dp", "mp"),
            P("dp", "mp"),
            P("dp", "mp"),
            P("mp", "dp"),
            P("dp", "mp"),
            P("dp", "mp"),
            P(None, None, ("dp", "mp")),
            P("dp"),
            P("dp"),
            P("dp", "mp"),
            P("mp", "dp"),
            P("dp"),
            P("dp"),
        ),
        check_vma=False,
    )
```

profile of v0, /device:TPU:0, one launch (start us, length us, event | category | flops | bytes accessed | tf_op | source)
XLA Modules:
  0.0 2157.7 jit_solution(1756214792686297062)
XLA Ops:
  32.2 6.2 fusion.141
  38.4 4.2 fusion.139
  46.2 49.1 %iota_compare_fusion = pred[561,561,128]{2,0,1:T(8,128)(4,1)} fusion(s32[561,561]{0,1:T(8,128)S(1)} %bitcast.250), kind=kLoop, calls=%fused_computation.1 | loop fusion | flops 40284288 | bytes 41543172 | tf_op jit(solution)/shard_map/while/body/eval_jaxpr/eq | solution.py:71
  95.3 4.3 copy.254
  99.6 51.1 %iota_compare_fusion.1 = pred[561,561,128]{2,0,1:T(8,128)(4,1)} fusion(s32[561,561]{0,1:T(8,128)} %bitcast.253), kind=kLoop, calls=%fused_computation.2 | loop fusion | flops 40284288 | bytes 41543172 | tf_op jit(solution)/shard_map/while/body/eval_jaxpr/eq | solution.py:71
  150.7 4.3 copy.249
  155.0 51.2 %iota_compare_fusion.2 = pred[561,561,128]{2,0,1:T(8,128)(4,1)} fusion(s32[561,561]{0,1:T(8,128)} %bitcast.256), kind=kLoop, calls=%fused_computation.3 | loop fusion | flops 40284288 | bytes 41543172 | tf_op jit(solution)/shard_map/while/body/eval_jaxpr/eq | solution.py:71
  206.3 78.3 %fusion.14 = f32[561,561,8]{1,2,0:T(8,128)} fusion(s32[561,561]{0,1:T(8,128)S(1)} %bitcast.257, bf16[8,128,561]{1,2,0:T(8,128)(2,1)S(1)} %copy-done.54), kind=kOutput, calls=%fused_computation.17 | convolution fusion | flops 684832896 | bytes 12478884 | tf_op jit(solution)/shard_map/while/body/eval_jaxpr/hbt,stb->hst/dot_general | solution.py:89
  284.6 14.6 copy.204
  299.2 53.4 %fusion.16 = f32[561,561,8]{1,2,0:T(8,128)} fusion(s32[561,561]{0,1:T(8,128)} %bitcast.254, bf16[8,128,561]{1,2,0:T(8,128)(2,1)} %convolution_convert_fusion.2), kind=kOutput, calls=%fused_computation.19 | convolution fusion | flops 684832896 | bytes 12478884 | tf_op jit(solution)/shard_map/while/body/eval_jaxpr/hbt,stb->hst/dot_general | solution.py:89
  352.6 14.6 copy.209
  367.2 53.2 %fusion.18 = f32[561,561,8]{1,2,0:T(8,128)} fusion(s32[561,561]{0,1:T(8,128)S(1)} %bitcast.251, bf16[8,128,561]{1,2,0:T(8,128)(2,1)} %convolution_convert_fusion), kind=kOutput, calls=%fused_computation.21 | convolution fusion | flops 684832896 | bytes 12478884 | tf_op jit(solution)/shard_map/while/body/eval_jaxpr/hbt,stb->hst/dot_general | solution.py:89
  420.4 14.7 copy.214
  435.1 15.0 copy.200
  450.8 50.4 %fusion.3 = f32[561,561,8]{1,2,0:T(8,128)} fusion(pred[561,561,128]{2,0,1:T(8,128)(4,1)} %iota_compare_fusion, bf16[8,561,128]{2,1,0:T(8,128)(2,1)S(1)} %copy-done.52), kind=kOutput, calls=%fused_computation.6 | convolution fusion | flops 644548608 | bytes 51504288 | tf_op jit(solution)/shard_map/while/body/eval_jaxpr/hsb,stb->hst/dot_general | solution.py:83
  501.1 50.4 %fusion.7 = f32[561,561,8]{1,2,0:T(8,128)} fusion(pred[561,561,128]{2,0,1:T(8,128)(4,1)} %iota_compare_fusion.1, bf16[8,561,128]{2,1,0:T(8,128)(2,1)S(1)} %copy-done.51), kind=kOutput, calls=%fused_computation.10 | convolution fusion | flops 644548608 | bytes 51504288 | tf_op jit(solution)/shard_map/while/body/eval_jaxpr/hsb,stb->hst/dot_general | solution.py:83
  551.6 55.4 %fusion.140 = (f32[8,561]{0,1:T(8,128)S(1)}, f32[8,561,561]{2,0,1:T(8,128)}) fusion(f32[561,561,8]{0,2,1:T(8,128)} %copy.214, f32[561,561,8]{1,2,0:T(8,128)} %fusion.3, f32[561,561,8]{0,2,1:T(8,128)} %copy.209, f32[561,561,8]{1,2,0:T(8,128)} %fusion.7, f32[561,561,8]{0,2,1:T(8,128)} %copy.204, f32[8,561,561]{2,0,1:T(8,128)} %copy.200, ...), kind=kOutput, calls=%fused_computation.201 | convolution fusion | flops 667203968 | bytes 111949232 | tf_op jit(solution)/shard_map/while/body/eval_jaxpr/hsb,stb->hst/dot_general | solution.py:83
  607.0 7.5 fusion.28
  614.7 6.8 fusion.29
  622.6 4.7 fusion.84
  630.5 70.8 %all-reduce.10.cloned.1.call-done = f32[561,1024]{1,0:T(8,128)} async-done(((f32[561,1024]{1,0:T(8,128)}), f32[561,1024]{1,0:T(8,128)}) %all-reduce.10.cloned.1.call-update) | async-done | bytes 2297872 | tf_op jit(solution)/shard_map/psum | solution.py:161
  704.7 16.1 multiply_convert_fusion.1
  726.3 68.1 %all-reduce.12.cloned.1.call-done = f32[561,1024]{1,0:T(8,128)} async-done(((f32[561,1024]{1,0:T(8,128)}), f32[561,1024]{1,0:T(8,128)}) %all-reduce.12.cloned.1.call-update) | async-done | bytes 2297872 | tf_op jit(solution)/shard_map/psum | solution.py:168
  800.6 7.4 add_convert_fusion
  813.5 68.1 %all-reduce.14.cloned.1.call-done = f32[561,1024]{1,0:T(8,128)} async-done(((f32[561,1024]{1,0:T(8,128)}), f32[561,1024]{1,0:T(8,128)}) %all-reduce.14.cloned.1.call-update) | async-done | bytes 2297872 | tf_op jit(solution)/shard_map/psum | solution.py:180
  881.6 6.4 multiply_reduce_fusion.1
  891.2 6.2 fusion.145
  897.4 15.1 copy.219
  912.5 42.0 %multiply_convert_fusion = bf16[8,561,561]{2,0,1:T(8,128)(2,1)} fusion(f32[8,561,561]{2,0,1:T(8,128)} %copy.219, f32[8,561,561]{2,0,1:T(8,128)} %get-tuple-element.176, f32[8,561]{0,1:T(8,128)S(1)} %copy-done.41), kind=kOutput, calls=%fused_computation.36 | output fusion | flops 17629424 | bytes 25195632 | tf_op jit(solution)/shard_map/while/body/eval_jaxpr/sub | solution.py:203
  954.5 50.0 %fusion.73 = bf16[8,561,128]{2,0,1:T(8,128)(2,1)} fusion(bf16[8,561,561]{2,0,1:T(8,128)(2,1)} %multiply_convert_fusion, pred[561,561,128]{2,0,1:T(8,128)(4,1)} %iota_compare_fusion), kind=kOutput, calls=%fused_computation.122 | convolution fusion | flops 645123072 | bytes 46468752 | tf_op jit(solution)/shard_map/while/body/eval_jaxpr/hst,stb->hsb/dot_general | solution.py:212
  1004.5 47.8 %fusion.76 = bf16[8,561,128]{2,0,1:T(8,128)(2,1)} fusion(bf16[8,561,561]{2,0,1:T(8,128)(2,1)S(1)} %copy-done.10, pred[561,561,128]{2,0,1:T(8,128)(4,1)} %iota_compare_fusion.1), kind=kOutput, calls=%fused_computation.123 | convolution fusion | flops 645123072 | bytes 46468752 | tf_op jit(solution)/shard_map/while/body/eval_jaxpr/hst,stb->hsb/dot_general | solution.py:212
  1052.3 48.2 %fusion.79 = bf16[8,561,128]{2,0,1:T(8,128)(2,1)} fusion(bf16[8,561,561]{2,0,1:T(8,128)(2,1)S(1)} %copy-done.10, pred[561,561,128]{2,0,1:T(8,128)(4,1)} %iota_compare_fusion.2), kind=kOutput, calls=%fused_computation.124 | convolution fusion | flops 645123072 | bytes 46468752 | tf_op jit(solution)/shard_map/while/body/eval_jaxpr/hst,stb->hsb/dot_general | solution.py:212
  1100.5 11.5 copy.228
  1112.0 53.8 %fusion.70 = bf16[8,128,561]{1,0,2:T(8,128)(2,1)S(1)} fusion(bf16[8,561,561]{1,0,2:T(8,128)(2,1)} %copy.228, s32[561,561]{0,1:T(8,128)S(1)} %bitcast.258), kind=kOutput, calls=%fused_computation.119 | convolution fusion | flops 685407360 | bytes 7443348 | tf_op jit(solution)/shard_map/while/body/eval_jaxpr/hst,stb->hbt/dot_general | solution.py:215
  1165.8 78.6 %fusion.72 = bf16[8,128,561]{1,0,2:T(8,128)(2,1)S(1)} fusion(bf16[8,561,561]{1,0,2:T(8,128)(2,1)S(1)} %copy-done.21, s32[561,561]{0,1:T(8,128)S(1)} %bitcast.252), kind=kOutput, calls=%fused_computation.121 | convolution fusion | flops 685407360 | bytes 7443348 | tf_op jit(solution)/shard_map/while/body/eval_jaxpr/hst,stb->hbt/dot_general | solution.py:215
  1244.5 78.8 %fusion.71 = bf16[8,128,561]{1,0,2:T(8,128)(2,1)S(1)} fusion(bf16[8,561,561]{1,0,2:T(8,128)(2,1)S(1)} %copy-done.21, s32[561,561]{0,1:T(8,128)S(1)} %bitcast.255), kind=kOutput, calls=%fused_computation.120 | convolution fusion | flops 685407360 | bytes 7443348 | tf_op jit(solution)/shard_map/while/body/eval_jaxpr/hst,stb->hbt/dot_general | solution.py:215
  1385.9 9.0 fusion.120
  1396.6 7.6 fusion.127
  1406.2 61.2 %all-reduce.4 = (f32[1024]{0:T(1024)S(1)}, f32[1024]{0:T(1024)S(1)}, f32[1024]{0:T(1024)S(1)}, f32[1024]{0:T(1024)S(1)}) all-reduce(f32[1024]{0:T(1024)S(1)} %copy-done.77, f32[1024]{0:T(1024)S(1)} %copy-done.78, f32[1024]{0:T(1024)S(1)} %copy-done.75, f32[1024]{0:T(1024)S(1)} %copy-done.76), channel_id=9, replica_groups=mesh['dp'=16,'mp'=2] {'dp'}, use_global_device_ids=true, to_apply=%region_23.24.clone | all-reduce | flops 4096 | bytes 32768
  1472.7 76.4 %reduce-scatter.22.cloned.1.call-done = f32[3,128,32]{1,2,0:T(8,128)} async-done(((f32[3,128,1024]{1,2,0:T(8,128)}), f32[3,128,32]{1,2,0:T(8,128)}) %reduce-scatter.22.cloned.1.call-update) | async-done | bytes 49168 | tf_op jit(solution)/shard_map/reduce_scatter | solution.py:266
  1549.1 61.9 %reduce-scatter.36.cloned.1.call-done = f32[64,512]{1,0:T(8,128)} async-done(((f32[1024,512]{1,0:T(8,128)}), f32[64,512]{1,0:T(8,128)}) %reduce-scatter.36.cloned.1.call-update) | async-done | bytes 131088
  1611.0 65.0 %reduce-scatter.34.cloned.1.call-done = f32[64,512]{1,0:T(8,128)} async-done(((f32[1024,512]{1,0:T(8,128)}), f32[64,512]{1,0:T(8,128)}) %reduce-scatter.34.cloned.1.call-update) | async-done | bytes 131088
  1676.0 65.0 %reduce-scatter.20.cloned.1.call-done = f32[512,64]{0,1:T(8,128)} async-done(((f32[512,1024]{0,1:T(8,128)}), f32[512,64]{0,1:T(8,128)}) %reduce-scatter.20.cloned.1.call-update) | async-done | bytes 131088 | tf_op jit(solution)/shard_map/reduce_scatter | solution.py:273
  1741.0 65.1 %reduce-scatter.32.cloned.1.call-done = f32[64,512]{1,0:T(8,128)} async-done(((f32[1024,512]{1,0:T(8,128)}), f32[64,512]{1,0:T(8,128)}) %reduce-scatter.32.cloned.1.call-update) | async-done | bytes 131088
  1806.1 64.9 %reduce-scatter.30.cloned.1.call-done = f32[64,512]{1,0:T(8,128)} async-done(((f32[1024,512]{1,0:T(8,128)}), f32[64,512]{1,0:T(8,128)}) %reduce-scatter.30.cloned.1.call-update) | async-done | bytes 131088
  1871.0 65.1 %reduce-scatter.28.cloned.1.call-done = f32[64,512]{1,0:T(8,128)} async-done(((f32[1024,512]{1,0:T(8,128)}), f32[64,512]{1,0:T(8,128)}) %reduce-scatter.28.cloned.1.call-update) | async-done | bytes 131088
  1936.0 106.9 %reduce-scatter.26.cloned.1.call-done = f32[2048,64]{0,1:T(8,128)} async-done(((f32[2048,1024]{0,1:T(8,128)}), f32[2048,64]{0,1:T(8,128)}) %reduce-scatter.26.cloned.1.call-update) | async-done | bytes 524304 | tf_op jit(solution)/shard_map/reduce_scatter | solution.py:277
  2042.9 107.8 %reduce-scatter.24.cloned.1.call-done = f32[64,2048]{1,0:T(8,128)} async-done(((f32[1024,2048]{1,0:T(8,128)}), f32[64,2048]{1,0:T(8,128)}) %reduce-scatter.24.cloned.1.call-update) | async-done | bytes 524304 | tf_op jit(solution)/shard_map/reduce_scatter | solution.py:276
  (306 shorter events, 126.8 us)
Async XLA Ops:
  7.2 621.1 %copy-start = (bf16[512,1024]{1,0:T(8,128)(2,1)S(1)}, bf16[512,1024]{1,0:T(8,128)(2,1)}, u32[]{:S(2)}) copy-start(bf16[512,1024]{1,0:T(8,128)(2,1)} %param.21) | copy-start | bytes 3145732
  7.2 694.1 %all-reduce.10.cloned.1.call-start = ((), (), s32[]{:S(2)}) async-start(), calls=%async_computation.9 | async-start | bytes 4653056 | tf_op jit(solution)/shard_map/psum | solution.py:161
  10.2 20.1 copy-start.30
  13.0 19.2 copy-start.13
  20.2 8.4 copy-start.32
  24.8 7.4 copy-start.11
  46.2 321.0 %copy-start.16 = (s32[1,1,561,561]{2,3,1,0:T(8,128)}, s32[1,1,561,561]{2,3,1,0:T(8,128)S(1)}, u32[]{:S(2)}) copy-start(s32[1,1,561,561]{2,3,1,0:T(8,128)S(1)} %copy.255) | copy-start | bytes 3776656
  155.0 51.3 %copy-start.19 = (s32[1,1,561,561]{2,3,1,0:T(8,128)S(1)}, s32[1,1,561,561]{2,3,1,0:T(8,128)}, u32[]{:S(2)}) copy-start(s32[1,1,561,561]{2,3,1,0:T(8,128)} %copy.249) | copy-start | bytes 3776656
  155.0 51.3 %copy-start.54 = (bf16[8,128,561]{1,2,0:T(8,128)(2,1)S(1)}, bf16[8,128,561]{1,2,0:T(8,128)(2,1)}, u32[]{:S(2)}) copy-start(bf16[8,128,561]{1,2,0:T(8,128)(2,1)} %convolution_convert_fusion.4) | copy-start | bytes 3446788
  435.1 15.7 copy-start.52
  450.8 50.4 %copy-start.51 = (bf16[8,561,128]{2,1,0:T(8,128)(2,1)S(1)}, bf16[8,561,128]{2,1,0:T(8,128)(2,1)}, u32[]{:S(2)}) copy-start(bf16[8,561,128]{2,1,0:T(8,128)(2,1)} %convolution_convert_fusion.3) | copy-start | bytes 3446788
  501.1 50.4 %copy-start.53 = (bf16[8,561,128]{2,1,0:T(8,128)(2,1)S(1)}, bf16[8,561,128]{2,1,0:T(8,128)(2,1)}, u32[]{:S(2)}) copy-start(bf16[8,561,128]{2,1,0:T(8,128)(2,1)} %convolution_convert_fusion.5) | copy-start | bytes 3446788
  607.0 7.7 copy-start.2
  630.5 163.9 %all-reduce.12.cloned.1.call-start = ((), (), s32[]{:S(2)}) async-start(), calls=%async_computation.10 | async-start | bytes 4653056 | tf_op jit(solution)/shard_map/psum | solution.py:168
  703.8 184.2 %copy-start.3 = (f32[561,1024]{1,0:T(8,128)}, f32[561,1024]{1,0:T(8,128)S(1)}, u32[]{:S(2)}) copy-start(f32[561,1024]{1,0:T(8,128)S(1)} %get-tuple-element.168) | copy-start | bytes 6893572
  703.8 184.2 %copy-start.63 = (f32[561]{0:T(1024)}, f32[561]{0:T(1024)S(1)}, u32[]{:S(2)}) copy-start(f32[561]{0:T(1024)S(1)} %broadcast_multiply_fusion.5) | copy-start | bytes 6736
  704.7 183.3 %copy-start.65 = (f32[561]{0:T(1024)}, f32[561]{0:T(1024)S(1)}, u32[]{:S(2)}) copy-start(f32[561]{0:T(1024)S(1)} %add_rsqrt_fusion.1) | copy-start | bytes 6736
  704.7 17.4 copy-start.86
  726.2 155.4 %all-reduce.14.cloned.1.call-start = ((), (), s32[]{:S(2)}) async-start(), calls=%async_computation.11 | async-start | bytes 4653056 | tf_op jit(solution)/shard_map/psum | solution.py:180
  796.9 84.7 %copy-start.67 = (f32[561]{0:T(1024)}, f32[561]{0:T(1024)S(1)}, u32[]{:S(2)}) copy-start(f32[561]{0:T(1024)S(1)} %broadcast_multiply_fusion.4) | copy-start | bytes 6736
  799.0 82.6 %copy-start.71 = (f32[561]{0:T(1024)}, f32[561]{0:T(1024)S(1)}, u32[]{:S(2)}) copy-start(f32[561]{0:T(1024)S(1)} %add_rsqrt_fusion) | copy-start | bytes 6736
  800.6 81.0 %copy-start.79 = (f32[561]{0:T(1024)}, f32[561]{0:T(1024)S(1)}, u32[]{:S(2)}) copy-start(f32[561]{0:T(1024)S(1)} %get-tuple-element.178) | copy-start | bytes 6736
  800.6 81.0 %copy-start.81 = (f32[561]{0:T(1024)}, f32[561]{0:T(1024)S(1)}, u32[]{:S(2)}) copy-start(f32[561]{0:T(1024)S(1)} %get-tuple-element.179) | copy-start | bytes 6736
  800.6 8.8 copy-start.89
  813.4 68.2 %copy-start.83 = (f32[1024]{0:T(1024)S(1)}, f32[1024]{0:T(1024)}, u32[]{:S(2)}) copy-start(f32[1024]{0:T(1024)} %param.30) | copy-start | bytes 12292
  813.5 656.3 %all-reduce.16.cloned.1.call-start = ((), (), s32[]{:S(2)}) async-start(), calls=%async_computation.12 | async-start | bytes 4653056 | tf_op jit(solution)/shard_map/psum | solution.py:253
  897.4 15.1 copy-start.41
  954.5 50.0 %copy-start.10 = (bf16[8,561,561]{2,0,1:T(8,128)(2,1)S(1)}, bf16[8,561,561]{2,0,1:T(8,128)(2,1)}, u32[]{:S(2)}) copy-start(bf16[8,561,561]{2,0,1:T(8,128)(2,1)} %multiply_convert_fusion) | copy-start | bytes 15106612
  1100.5 11.5 copy-start.20
  1112.0 53.8 %copy-start.17 = (s32[1,1,561,561]{2,3,1,0:T(8,128)S(1)}, s32[1,1,561,561]{2,3,1,0:T(8,128)}, u32[]{:S(2)}) copy-start(s32[1,1,561,561]{2,3,1,0:T(8,128)} %copy-done.16) | copy-start | bytes 3776656
  1112.0 53.8 %copy-start.21 = (bf16[8,561,561]{1,0,2:T(8,128)(2,1)S(1)}, bf16[8,561,561]{1,0,2:T(8,128)(2,1)}, u32[]{:S(2)}) copy-start(bf16[8,561,561]{1,0,2:T(8,128)(2,1)} %copy.228) | copy-start | bytes 15106612
  1165.8 163.2 %copy-start.45 = (bf16[8,128,561]{1,0,2:T(8,128)(2,1)}, bf16[8,128,561]{1,0,2:T(8,128)(2,1)S(1)}, u32[]{:S(2)}) copy-start(bf16[8,128,561]{1,0,2:T(8,128)(2,1)S(1)} %fusion.70) | copy-start | bytes 3446788
  1165.8 78.6 %copy-start.18 = (s32[1,1,561,561]{2,3,1,0:T(8,128)S(1)}, s32[1,1,561,561]{2,3,1,0:T(8,128)}, u32[]{:S(2)}) copy-start(s32[1,1,561,561]{2,3,1,0:T(8,128)} %copy.254) | copy-start | bytes 3776656
  1165.8 157.4 %slice-start = ((s8[5744640]{0:T(1024)(128)(4,1)}), s8[4194304]{0:T(1024)(128)(4,1)S(1)}, s32[]{:S(2)}) async-start(s8[5744640]{0:T(1024)(128)(4,1)} %bitcast.227), calls=%async_computation.22 | async-start | bytes 8388608
  1244.5 78.8 %slice-start.1 = ((s8[5744640]{0:T(1024)(128)(4,1)}), s8[1550336]{0:T(1024)(128)(4,1)S(1)}, s32[]{:S(2)}) async-start(s8[5744640]{0:T(1024)(128)(4,1)} %bitcast.227), calls=%async_computation.23 | async-start | bytes 3100672
  1244.5 78.8 %copy-start.14 = (bf16[561,512]{0,1:T(8,128)(2,1)S(1)}, bf16[561,512]{0,1:T(8,128)(2,1)}, u32[]{:S(2)}) copy-start(bf16[561,512]{0,1:T(8,128)(2,1)} %copy-done.13) | copy-start | bytes 1723396
  1329.0 8.5 copy-start.62
  1340.2 209.0 %reduce-scatter.22.cloned.1.call-start = ((), (), s32[]{:S(2)}) async-start(), calls=%async_computation.14 | async-start | bytes 1622016 | tf_op jit(solution)/shard_map/reduce_scatter | solution.py:266
  1355.2 255.8 %reduce-scatter.36.cloned.1.call-start = ((), (), s32[]{:S(2)}) async-start(), calls=%async_computation.21 | async-start | bytes 2228224
  1360.5 315.5 %reduce-scatter.34.cloned.1.call-start = ((), (), s32[]{:S(2)}) async-start(), calls=%async_computation.20 | async-start | bytes 2228224
  1367.8 373.2 %reduce-scatter.20.cloned.1.call-start = ((), (), s32[]{:S(2)}) async-start(), calls=%async_computation.13 | async-start | bytes 2228224 | tf_op jit(solution)/shard_map/reduce_scatter | solution.py:273
  1370.3 435.8 %reduce-scatter.32.cloned.1.call-start = ((), (), s32[]{:S(2)}) async-start(), calls=%async_computation.19 | async-start | bytes 2228224
  1374.7 496.2 %reduce-scatter.30.cloned.1.call-start = ((), (), s32[]{:S(2)}) async-start(), calls=%async_computation.18 | async-start | bytes 2228224
  1378.9 557.1 %reduce-scatter.28.cloned.1.call-start = ((), (), s32[]{:S(2)}) async-start(), calls=%async_computation.17 | async-start | bytes 2228224
  1385.8 657.1 %reduce-scatter.26.cloned.1.call-start = ((), (), s32[]{:S(2)}) async-start(), calls=%async_computation.16 | async-start | bytes 8912896 | tf_op jit(solution)/shard_map/reduce_scatter | solution.py:277
  1395.0 755.7 %reduce-scatter.24.cloned.1.call-start = ((), (), s32[]{:S(2)}) async-start(), calls=%async_computation.15 | async-start | bytes 8912896 | tf_op jit(solution)/shard_map/reduce_scatter | solution.py:276
  1404.3 65.5 %copy-start.7 = (f32[561,1024]{1,0:T(8,128)S(1)}, f32[561,1024]{1,0:T(8,128)}, u32[]{:S(2)}) copy-start(f32[561,1024]{1,0:T(8,128)} %copy-done.5) | copy-start | bytes 6893572
  1469.2 681.5 %copy-start.1 = (bf16[512,1024]{1,0:T(8,128)(2,1)S(1)}, bf16[512,1024]{1,0:T(8,128)(2,1)}, u32[]{:S(2)}) copy-start(bf16[512,1024]{1,0:T(8,128)(2,1)} %param.21) | copy-start | bytes 3145732
  (63 other events, 165.3 us)
Sparse Core Ops, SparseCore 0:
  630.6 70.6 all-reduce.9
  726.3 67.9 all-reduce.11
  813.6 67.9 all-reduce.13
  1340.3 67.9 all-reduce.15
  1411.0 138.1 reduce-scatter.21
  1553.3 57.6 reduce-scatter.35
  1615.3 60.6 reduce-scatter.33
  1680.3 60.6 reduce-scatter.19
  1745.3 60.7 reduce-scatter.31
  1810.3 60.6 reduce-scatter.29
  1875.3 60.6 reduce-scatter.27
  1940.5 102.3 reduce-scatter.25
  2047.6 103.0 reduce-scatter.23
where the time goes:
time: 2170 us; the launch traced here: 2160 us
  waiting for transfers between devices  885 us (41%)
  matrix products  828 us (38%)
  other arithmetic  225 us (10%)
  local copies, waits for them, and re-layouts  141 us (6%)
  blocking collectives  61.2 us (3%)
    unnamed x18, waiting for transfers between devices  322 us
    dot_general x3, matrix products, page_backward(): jnp.einsum('hst,stb->hbt', raw_back, selector, preferred_element_type=jnp...  211 us
    dot_general x3, matrix products, relative_scores(): jnp.einsum('hbt,stb->hst', far_table, selector, preferred_element_type=jn...  185 us
    dot_general x3, matrix products, relative_scores(): jnp.einsum('hsb,stb->hst', near_table, selector, preferred_element_type=j...  156 us
    eq x3, other arithmetic, one_hot_of(): bucket_plane[:, :, None] == jnp.arange(REL, dtype=jnp.int32)[None, None, :]  151 us
    dot_general x3, matrix products, page_backward(): jnp.einsum('hst,stb->hsb', raw_back, selector, preferred_element_type=jnp...  146 us
    reduce_scatter x1, waiting for transfers between devices, shards(): lax.psum_scatter(up_grad, 'dp', scatter_dimension=0, tiled=True)  108 us
    reduce_scatter x1, waiting for transfers between devices, shards(): lax.psum_scatter(down_grad, 'dp', scatter_dimension=1, tiled=True)  107 us
  transfers between devices with their start and end apart: 13, of which 12 were waited for; matrix products, arithmetic and copies ran while one was open for 3% of the time, Pallas kernels for 0%

commit v1 on v0

v1 whole, which is shorter than its diff:
```python
import functools

import jax
import jax.numpy as jnp
from jax import lax
from jax.experimental import pallas as pl
from jax.experimental.pallas import tpu as pltpu
from jax.sharding import PartitionSpec as P

D = 1024
epsilon = 1e-05
highest = lax.Precision.HIGHEST
HEAD = 64
REL = 128
TEXT = 512
bf16 = jnp.bfloat16
f32 = jnp.float32
LIMIT = 10900.0
VMEM_CAP = 62 * 2**20


def lane_gather(table, index):
    numbers = lax.GatherDimensionNumbers(
        offset_dims=(),
        collapsed_slice_dims=(1,),
        start_index_map=(1,),
        operand_batching_dims=(0,),
        start_indices_batching_dims=(0,),
    )
    return lax.gather(
        table, index[..., None], numbers, (1, 1), mode=lax.GatherScatterMode.PROMISE_IN_BOUNDS
    )


def nt(left, right):
    return lax.dot_general(left, right, (((1,), (1,)), ((), ())), preferred_element_type=f32)


def nn(left, right):
    return jnp.dot(left, right, preferred_element_type=f32)


def tn(left, right):
    return lax.dot_general(left, right, (((0,), (0,)), ((), ())), preferred_element_type=f32)


def lane_half(shape):
    return lax.broadcasted_iota(jnp.int32, shape, len(shape) - 1) < HEAD


def unpack_pair(packed):
    low = (packed << 16) >> 16
    high = (packed - low) >> 16
    return high.astype(f32), low.astype(f32)


def forward_kernel(
    used_ref, q_ref, k_ref, v_ref, pk_ref, pq_ref, b_ref,
    p_ref, ctx_ref, bp_ref, bt_ref,
    near_tab, far_tab, near_inv, far_inv, far_sum, near_sum, score, *, span, rows, cols, pairs, scale,
):
    for r in range(3):
        bp_ref[r, span - span % 8:rows, :] = jnp.zeros((rows - span + span % 8, cols), jnp.int32)
        bp_ref[r, :, span - span % 128:cols] = jnp.zeros((rows, cols - span + span % 128), jnp.int32)
        bp_ref[r, 0:span, 0:span] = b_ref[0, r]
    for r in range(3):
        for jb in range(cols // 128):
            high = min(128, rows - jb * 128)
            for ib in range(cols // 128):
                tall = min(128, rows - ib * 128)
                block = bp_ref[r, ib * 128:ib * 128 + tall, jb * 128:(jb + 1) * 128]
                if tall < 128:
                    block = jnp.concatenate([block, jnp.zeros((128 - tall, 128), jnp.int32)], axis=0)
                bt_ref[r, jb * 128:jb * 128 + high, ib * 128:(ib + 1) * 128] = block.T[:high]

    half = lane_half((64, 128))

    def make_tables(src_ref, pos_ref, tab, inv, p):
        cut = slice(p * 128, (p + 1) * 128)

        def body(step, carry):
            at = pl.ds(pl.multiple_of(step * 64, 64), 64)
            block = src_ref[at, cut]
            zero = jnp.zeros_like(block)
            first = nt(jnp.where(half, block, zero), pos_ref[:, cut]).astype(bf16).astype(f32)
            second = nt(jnp.where(half, zero, block), pos_ref[:, cut]).astype(bf16).astype(f32)
            top0 = jnp.maximum(jnp.max(jnp.abs(first), axis=1, keepdims=True), 1e-30)
            top1 = jnp.maximum(jnp.max(jnp.abs(second), axis=1, keepdims=True), 1e-30)
            whole0 = jnp.round(first * (LIMIT / top0)).astype(jnp.int32)
            whole1 = jnp.round(second * (LIMIT / top1)).astype(jnp.int32)
            tab[p, at, :] = whole0 * 65536 + whole1
            inv[2 * p, at, :] = jnp.broadcast_to(top0 * (1.0 / LIMIT), (64, 128))
            inv[2 * p + 1, at, :] = jnp.broadcast_to(top1 * (1.0 / LIMIT), (64, 128))
            return carry

        lax.fori_loop(0, rows // 64, body, 0)

    for p in range(pairs):
        make_tables(q_ref, pk_ref, near_tab, near_inv, p)
        make_tables(k_ref, pq_ref, far_tab, far_inv, p)

    def look_up(tab, index_ref, at, out, out_at):
        for c in range(cols // 128):
            total = [None] * pairs
            for r in range(3):
                index = index_ref[r, at, c * 128:(c + 1) * 128]
                for p in range(pairs):
                    got = lane_gather(tab[p, at, r * 128:(r + 1) * 128], index)
                    total[p] = got if total[p] is None else total[p] + got
            for p in range(pairs):
                out[p, out_at, c * 128:(c + 1) * 128] = total[p]

    def far_body(step, carry):
        at = pl.ds(pl.multiple_of(step * 8, 8), 8)
        look_up(far_tab, bt_ref, at, far_sum, at)
        return carry

    lax.fori_loop(0, rows // 8, far_body, 0)
    for p in range(pairs):
        far_sum[p, rows:, :] = jnp.zeros((cols - rows, cols), jnp.int32)

    used = used_ref[0]
    place = lax.broadcasted_iota(jnp.int32, (1, cols), 1)
    valid = ((place >= TEXT) & (place < span)) | (place < used)
    inv_rows = []
    for h in range(2 * pairs):
        inv_rows.append(jnp.concatenate(
            [far_inv[h, j * 128:min(rows, (j + 1) * 128), :].T[0:1] for j in range(cols // 128 - 1)]
            + [jnp.concatenate([far_inv[h, cols - 128:rows, :],
                                jnp.zeros((cols - rows, 128), f32)], axis=0).T[0:1]], axis=1))

    def block_body(start, tall):
        def near_body(step, carry):
            at = pl.ds(pl.multiple_of(start + step * 8, 8), 8)
            look_up(near_tab, bp_ref, at, near_sum, pl.ds(pl.multiple_of(step * 8, 8), 8))
            return carry

        lax.fori_loop(0, tall // 8, near_body, 0)
        at = pl.ds(start, tall)
        for p in range(pairs):
            cut = slice(p * 128, (p + 1) * 128)
            block = q_ref[at, cut]
            zero = jnp.zeros_like(block)
            mask = lane_half((tall, 128))
            score[0, 0:tall, :] = nt(jnp.where(mask, block, zero), k_ref[:, cut])
            score[1, 0:tall, :] = nt(jnp.where(mask, zero, block), k_ref[:, cut])
            for c in range(cols // 128):
                turned = far_sum[p, c * 128:(c + 1) * 128, pl.ds(start, 128)].T[0:tall]
                here = slice(c * 128, (c + 1) * 128)
                f0, f1 = unpack_pair(turned)
                n0, n1 = unpack_pair(near_sum[p, 0:tall, here])
                score[0, 0:tall, here] += (
                    f0 * inv_rows[2 * p][:, here] + n0 * near_inv[2 * p, at, :]
                )
                score[1, 0:tall, here] += (
                    f1 * inv_rows[2 * p + 1][:, here] + n1 * near_inv[2 * p + 1, at, :]
                )
            for h in range(2):
                for s in range(tall // 16):
                    raw = score[h, s * 16:(s + 1) * 16, :]
                    logits = jnp.where(valid, raw * scale, -1e30)
                    top = jnp.max(logits, axis=1, keepdims=True)
                    grown = jnp.exp(logits - top)
                    share = grown * (1.0 / jnp.sum(grown, axis=1, keepdims=True))
                    p_ref[2 * p + h, pl.ds(pl.multiple_of(start + s * 16, 16), 16), :] = share.astype(bf16)
            c0 = nn(p_ref[2 * p, at, :], v_ref[:, cut])
            c1 = nn(p_ref[2 * p + 1, at, :], v_ref[:, cut])
            ctx_ref[at, cut] = jnp.where(mask, c0, c1).astype(bf16)

    def outer(step, carry):
        block_body(pl.multiple_of(step * 128, 128), 128)
        return carry

    lax.fori_loop(0, rows // 128, outer, 0)
    if rows % 128:
        block_body(rows - rows % 128, rows % 128)


def project_kernel(x_ref, wq_ref, wk_ref, wv_ref, t_ref, kp_ref, qp_ref, qkv_ref, pk_ref, pq_ref, *, span, cols, width):
    tail = span - span % 128
    qkv_ref[span - span % 16:cols, :] = jnp.zeros((cols - span + span % 16, 3 * width), bf16)
    for n, w_ref in enumerate((wq_ref, wk_ref, wv_ref)):
        cut = slice(n * width, (n + 1) * width)

        def body(step, carry, cut=cut, w_ref=w_ref):
            at = pl.ds(pl.multiple_of(step * 128, 128), 128)
            qkv_ref[at, cut] = nn(x_ref[at, :], w_ref[...]).astype(bf16)
            return carry

        lax.fori_loop(0, span // 128, body, 0)
        if tail < span:
            qkv_ref[tail:span, cut] = nn(x_ref[tail:span, :], w_ref[...]).astype(bf16)
    for r in range(3):
        at = slice(r * REL, (r + 1) * REL)
        pk_ref[at, :] = nn(t_ref[r], kp_ref[...]).astype(bf16)
        pq_ref[at, :] = nn(t_ref[r], qp_ref[...]).astype(bf16)


def project(tokens, query_weight, key_weight, value_weight, tables, key_position, query_position, span):
    width = query_weight.shape[1]
    rows, cols = sizes(span)
    whole = pl.BlockSpec(memory_space=pltpu.VMEM)
    return pl.pallas_call(
        functools.partial(project_kernel, span=span, cols=cols, width=width),
        out_shape=(
            jax.ShapeDtypeStruct((cols, 3 * width), bf16),
            jax.ShapeDtypeStruct((3 * REL, width), bf16),
            jax.ShapeDtypeStruct((3 * REL, width), bf16),
        ),
        in_specs=[whole] * 7,
        out_specs=(whole,) * 3,
        compiler_params=pltpu.CompilerParams(vmem_limit_bytes=VMEM_CAP),
        cost_estimate=pl.CostEstimate(flops=4 * 10**9, bytes_accessed=9 * 10**6, transcendentals=0),
        name="project",
    )(tokens, query_weight, key_weight, value_weight, tables, key_position, query_position)


def pick(half, block, h):
    zero = jnp.zeros_like(block)
    return jnp.where(half, block, zero) if h == 0 else jnp.where(half, zero, block)


def draw_kernel(
    p_ref, up_ref, q_ref, k_ref, v_ref,
    d_ref, dt_ref, dq_ref, dk_ref, dv_ref, wide, flat, turned, *, rows, cols, scale,
):
    half = lane_half((64, 128))
    rows_half = lane_half((rows, 128))
    cols_half = lane_half((cols, 128))

    def body(step, carry):
        at = pl.ds(pl.multiple_of(step * 64, 64), 64)
        pair = []
        for h in range(2):
            reach = nt(pick(half, up_ref[at, :], h), v_ref[...])
            share = p_ref[h, at, :].astype(f32)
            inner = jnp.sum(reach * share, axis=1, keepdims=True)
            back = share * (reach - inner) * scale
            wide[h, at, :] = back
            flat[h, at, :] = back.astype(bf16)
            pair.append(back.reshape(8, 8, cols))
        d_ref[pl.ds(pl.multiple_of(step * 8, 8), 8), :, :] = jnp.concatenate(pair, axis=1).astype(bf16)
        return carry

    lax.fori_loop(0, rows // 64, body, 0)
    for jb in range(cols // 128):
        tall = min(128, rows - jb * 128)
        for ib in range(cols // 128):
            wide_rows = min(128, rows - ib * 128)
            pair = []
            for h in range(2):
                block = wide[h, ib * 128:ib * 128 + wide_rows, jb * 128:(jb + 1) * 128]
                if wide_rows < 128:
                    block = jnp.concatenate([block, jnp.zeros((128 - wide_rows, 128), f32)], axis=0)
                other = block.T[:tall]
                turned[h, jb * 128:jb * 128 + tall, ib * 128:(ib + 1) * 128] = other.astype(bf16)
                pair.append(other.reshape(tall // 8, 8, 128))
            dt_ref[jb * 16:jb * 16 + tall // 8, :, ib * 128:(ib + 1) * 128] = jnp.concatenate(
                pair, axis=1
            ).astype(bf16)
    dq_ref[...] = nn(flat[0], pick(cols_half, k_ref[...], 0)) + nn(flat[1], pick(cols_half, k_ref[...], 1))
    dk_ref[...] = nn(turned[0], pick(cols_half, q_ref[...], 0)) + nn(turned[1], pick(cols_half, q_ref[...], 1))
    dv = tn(p_ref[0], pick(rows_half, up_ref[...], 0)) + tn(p_ref[1], pick(rows_half, up_ref[...], 1))
    dv_ref[...] = dv[:rows].astype(bf16)


def scatter_kernel(d_ref, b_ref, merge_ref, out_ref, *, groups, cols):
    base = jnp.where(lax.broadcasted_iota(jnp.int32, (16, cols), 0) >= 8, 1.0, 0.0).astype(bf16)
    own = (lax.broadcasted_iota(jnp.int32, (256, 256), 0) % 8) == (
        lax.broadcasted_iota(jnp.int32, (256, 256), 1) % 8
    )
    zero = jnp.asarray(0.0, bf16)
    one = jnp.asarray(1.0, bf16)

    def body(g, carry):
        back = d_ref[g]
        for r in range(3):
            bucket = b_ref[r, pl.ds(pl.multiple_of(g * 8, 8), 8), :]
            low = (bucket & 31).astype(f32)
            high = (bucket >> 5).astype(f32)
            low = jnp.concatenate([low, low], axis=0).astype(bf16) - base
            high = jnp.concatenate([high, high], axis=0).astype(bf16)
            hot = jnp.concatenate(
                [jnp.where(low == jnp.asarray(2.0 * k, bf16), one, zero) for k in range(16)], axis=0
            )
            sieved = []
            for l in range(4):
                mask = high == jnp.asarray(float(l), bf16)
                for p in range(4):
                    sieved.append(jnp.where(mask, back[p * 16:(p + 1) * 16], zero))
            sums = nt(jnp.concatenate(sieved, axis=0), hot)
            sums = jnp.where(own, sums, 0.0).astype(bf16)
            total = None
            for l in range(4):
                term = nn(sums[l * 64:(l + 1) * 64], merge_ref[l])
                total = term if total is None else total + term
            out_ref[g, :, r * 128:(r + 1) * 128] = total.astype(bf16)
        return carry

    lax.fori_loop(0, groups, body, 0)


def close_kernel(s_ref, base_ref, pos_ref, side_ref, out_ref, table_ref, *, rows):
    rows2 = 2 * rows
    half3 = lane_half((rows // 8, 8, 128))
    flat = s_ref[...].reshape(rows2, 3 * REL)
    both = nn(flat, pos_ref[...]).reshape(rows // 8, 16, 128)
    mine = jnp.where(half3, both[:, 0:8, :], both[:, 8:16, :]).reshape(rows, 128)
    out_ref[...] = (base_ref[...] + mine).astype(bf16)
    side = side_ref[0:rows, :].astype(f32).reshape(rows // 8, 8, 128)
    zero = jnp.zeros_like(side)
    spread = jnp.concatenate([jnp.where(half3, side, zero), jnp.where(half3, zero, side)], axis=1)
    table_ref[...] = tn(flat, spread.reshape(rows2, 128).astype(bf16))


def merge_table():
    l = lax.broadcasted_iota(jnp.int32, (4, 256, 128), 0)
    a = lax.broadcasted_iota(jnp.int32, (4, 256, 128), 1) // 8
    c = lax.broadcasted_iota(jnp.int32, (4, 256, 128), 2)
    return (c == l * 32 + a).astype(bf16)


def sizes(span):
    return -(-span // 64) * 64, -(-span // 128) * 128


def attention_forward(qkv, pos_key, pos_query, buckets, used, scale):
    span = buckets.shape[2]
    rows, cols = sizes(span)
    width = pos_key.shape[1]
    pairs = width // 128
    whole = pl.BlockSpec(memory_space=pltpu.VMEM)
    i32 = jnp.int32

    def kernel(used_ref, qkv_ref, *rest):
        forward_kernel(
            used_ref, qkv_ref.at[:, 0:width], qkv_ref.at[:, width:2 * width],
            qkv_ref.at[:, 2 * width:3 * width], *rest,
            span=span, rows=rows, cols=cols, pairs=pairs, scale=scale,
        )

    return pl.pallas_call(
        kernel,
        out_shape=(
            jax.ShapeDtypeStruct((2 * pairs, rows, cols), bf16),
            jax.ShapeDtypeStruct((rows, width), bf16),
            jax.ShapeDtypeStruct((3, rows, cols), i32),
            jax.ShapeDtypeStruct((3, rows, cols), i32),
        ),
        in_specs=[pl.BlockSpec(memory_space=pltpu.SMEM)] + [whole] * 4,
        out_specs=(whole,) * 4,
        scratch_shapes=[
            pltpu.VMEM((pairs, rows, 3 * REL), i32),
            pltpu.VMEM((pairs, rows, 3 * REL), i32),
            pltpu.VMEM((2 * pairs, rows, 128), f32),
            pltpu.VMEM((2 * pairs, rows, 128), f32),
            pltpu.VMEM((pairs, cols, cols), i32),
            pltpu.VMEM((pairs, 128, cols), i32),
            pltpu.VMEM((2, 128, cols), f32),
        ],
        compiler_params=pltpu.CompilerParams(vmem_limit_bytes=VMEM_CAP),
        cost_estimate=pl.CostEstimate(flops=60000000000, bytes_accessed=25000000, transcendentals=0),
        name="attention_forward",
    )(used, qkv, pos_key, pos_query, buckets)


def attention_draw(share, upstream, qkv, scale):
    heads, rows, cols = share.shape
    width = upstream.shape[1]
    pairs = heads // 2
    groups = rows // 8
    return pl.pallas_call(
        functools.partial(draw_kernel, rows=rows, cols=cols, scale=scale),
        grid=(pairs,),
        in_specs=[
            pl.BlockSpec((2, rows, cols), lambda p: (p, 0, 0)),
            pl.BlockSpec((rows, 128), lambda p: (0, p)),
            pl.BlockSpec((cols, 128), lambda p: (0, p)),
            pl.BlockSpec((cols, 128), lambda p: (0, p + pairs)),
            pl.BlockSpec((cols, 128), lambda p: (0, p + 2 * pairs)),
        ],
        out_specs=(
            pl.BlockSpec((groups, 16, cols), lambda p: (0, p, 0)),
            pl.BlockSpec((groups, 16, cols), lambda p: (0, p, 0)),
            pl.BlockSpec((rows, 128), lambda p: (0, p)),
            pl.BlockSpec((rows, 128), lambda p: (0, p)),
            pl.BlockSpec((rows, 128), lambda p: (0, p)),
        ),
        out_shape=(
            jax.ShapeDtypeStruct((groups, 8 * heads, cols), bf16),
            jax.ShapeDtypeStruct((groups, 8 * heads, cols), bf16),
            jax.ShapeDtypeStruct((rows, width), f32),
            jax.ShapeDtypeStruct((rows, width), f32),
            jax.ShapeDtypeStruct((rows, width), bf16),
        ),
        scratch_shapes=[
            pltpu.VMEM((2, rows, cols), f32),
            pltpu.VMEM((2, rows, cols), bf16),
            pltpu.VMEM((2, rows, cols), bf16),
        ],
        compiler_params=pltpu.CompilerParams(vmem_limit_bytes=VMEM_CAP),
        cost_estimate=pl.CostEstimate(flops=20000000000, bytes_accessed=25000000, transcendentals=0),
        name="attention_draw",
    )(share, upstream, qkv, qkv, qkv)


def attention_scatter(back, buckets, merge):
    groups, _, cols = back.shape
    whole = pl.BlockSpec(memory_space=pltpu.VMEM)
    return pl.pallas_call(
        functools.partial(scatter_kernel, groups=groups, cols=cols),
        out_shape=jax.ShapeDtypeStruct((groups, back.shape[1], 3 * REL), bf16),
        in_specs=[whole] * 3,
        out_specs=whole,
        compiler_params=pltpu.CompilerParams(vmem_limit_bytes=VMEM_CAP),
        cost_estimate=pl.CostEstimate(flops=70000000000, bytes_accessed=12000000, transcendentals=0),
        name="attention_scatter",
    )(back, buckets, merge)


def attention_close(sums, base, pos, qkv, side):
    rows, width = base.shape
    pairs = width // 128
    groups = rows // 8
    return pl.pallas_call(
        functools.partial(close_kernel, rows=rows),
        grid=(pairs,),
        in_specs=[
            pl.BlockSpec((groups, 16, 3 * REL), lambda p: (0, p, 0)),
            pl.BlockSpec((rows, 128), lambda p: (0, p)),
            pl.BlockSpec((3 * REL, 128), lambda p: (0, p)),
            pl.BlockSpec((qkv.shape[0], 128), lambda p: (0, p + side * pairs)),
        ],
        out_specs=(
            pl.BlockSpec((rows, 128), lambda p: (0, p)),
            pl.BlockSpec((3 * REL, 128), lambda p: (0, p)),
        ),
        out_shape=(
            jax.ShapeDtypeStruct((rows, width), bf16),
            jax.ShapeDtypeStruct((3 * REL, width), f32),
        ),
        compiler_params=pltpu.CompilerParams(vmem_limit_bytes=VMEM_CAP),
        cost_estimate=pl.CostEstimate(flops=5000000000, bytes_accessed=10000000, transcendentals=0),
        name="attention_close",
    )(sums, base, pos, qkv)

def exact_left(left, right):
    return lax.dot_general(
        left, right, (((0,), (0,)), ((), ())), precision=highest, preferred_element_type=jnp.float32
    )


def exact_right(left, right):
    return lax.dot_general(
        left, right, (((1,), (1,)), ((), ())), precision=highest, preferred_element_type=jnp.float32
    )


def norm_forward(summed, gain, shift):
    centred = summed - jnp.mean(summed, axis=1, keepdims=True)
    inverse = lax.rsqrt(jnp.mean(centred * centred, axis=1, keepdims=True) + epsilon)
    normal = centred * inverse
    return (normal * gain + shift, normal, inverse)


def norm_backward(upstream, normal, inverse, gain):
    scaled = upstream * gain
    inner = jnp.mean(scaled, axis=1, keepdims=True)
    aligned = jnp.mean(scaled * normal, axis=1, keepdims=True)
    return (
        inverse * (scaled - inner - normal * aligned),
        jnp.sum(upstream * normal, axis=0),
        jnp.sum(upstream, axis=0),
    )


def shards(
    tokens,
    query_weight,
    key_weight,
    value_weight,
    output_weight,
    query_position,
    key_position,
    position_tables,
    gain_one,
    shift_one,
    up_weight,
    down_weight,
    gain_two,
    shift_two,
    buckets,
    text_length,
    cotangent,
):
    span = buckets.shape[2]
    rows, cols = sizes(span)
    score_scale = (7.0 * HEAD) ** (-0.5)
    tables_flat = position_tables.reshape(3 * REL, D)
    qkv, pos_key, pos_query = project(
        tokens, query_weight, key_weight, value_weight, position_tables, key_position, query_position, span
    )
    share, context, bucket_rows, bucket_cols = attention_forward(
        qkv, pos_key, pos_query, buckets, text_length, score_scale
    )
    context = context[:span]
    attended = lax.psum(nn(context, output_weight), "mp")
    first, normal_one, inverse_one = norm_forward(
        tokens.astype(f32) + attended, gain_one, shift_one
    )
    first_low = first.astype(bf16)
    upward = nn(first_low, up_weight)
    hidden = jax.nn.gelu(upward, approximate=False).astype(bf16)
    feed = lax.psum(nn(hidden, down_weight), "mp")
    final, normal_two, inverse_two = norm_forward(first + feed, gain_two, shift_two)
    layer_output = final.astype(bf16)
    second_back, gain_two_grad, shift_two_grad = norm_backward(
        cotangent.astype(f32), normal_two, inverse_two, gain_two
    )
    second_low = second_back.astype(bf16)
    down_grad = tn(hidden, second_low)
    hidden_back = nt(second_low, down_weight)
    gelu_back = jax.vjp(lambda inner_value: jax.nn.gelu(inner_value, approximate=False), upward)[1]
    upward_back = gelu_back(hidden_back)[0].astype(bf16)
    up_grad = tn(first_low, upward_back)
    first_back = second_back + lax.psum(nt(upward_back, up_weight), "mp")
    residual_back, gain_one_grad, shift_one_grad = norm_backward(
        first_back, normal_one, inverse_one, gain_one
    )
    residual_low = residual_back.astype(bf16)
    output_grad = tn(context, residual_low)
    context_back = jnp.pad(nt(residual_low, output_weight).astype(bf16), ((0, rows - span), (0, 0)))

    merge = merge_table()
    back, back_turned, query_base, key_base, value_back = attention_draw(
        share, context_back, qkv, score_scale
    )
    near_sums = attention_scatter(back, bucket_rows, merge)
    query_back, key_table_sum = attention_close(near_sums, query_base, pos_key, qkv, 0)
    far_sums = attention_scatter(back_turned, bucket_cols, merge)
    key_back, query_table_sum = attention_close(far_sums, key_base, pos_query, qkv, 1)
    query_flat, key_flat, value_flat = query_back[:span], key_back[:span], value_back[:span]
    query_grad = tn(tokens, query_flat)
    key_grad = tn(tokens, key_flat)
    value_grad = tn(tokens, value_flat)
    input_part = (
        nt(query_flat, query_weight) + nt(key_flat, key_weight) + nt(value_flat, value_weight)
    )
    input_gradient = (residual_back + lax.psum(input_part, "mp")).astype(bf16)
    tables_wide = tables_flat.astype(f32)
    key_position_grad = exact_left(tables_wide, key_table_sum)
    query_position_grad = exact_left(tables_wide, query_table_sum)
    table_part = exact_right(key_table_sum, key_position.astype(f32)) + exact_right(
        query_table_sum, query_position.astype(f32)
    )
    table_gradient = lax.psum_scatter(
        table_part.reshape(3, REL, D), ("dp", "mp"), scatter_dimension=2, tiled=True
    )
    summed = (
        lax.psum_scatter(query_grad, "dp", scatter_dimension=0, tiled=True),
        lax.psum_scatter(key_grad, "dp", scatter_dimension=0, tiled=True),
        lax.psum_scatter(value_grad, "dp", scatter_dimension=0, tiled=True),
        lax.psum_scatter(output_grad, "dp", scatter_dimension=1, tiled=True),
        lax.psum_scatter(query_position_grad, "dp", scatter_dimension=0, tiled=True),
        lax.psum_scatter(key_position_grad, "dp", scatter_dimension=0, tiled=True),
        lax.psum_scatter(up_grad, "dp", scatter_dimension=0, tiled=True),
        lax.psum_scatter(down_grad, "dp", scatter_dimension=1, tiled=True),
        lax.psum_scatter(gain_one_grad, "dp", scatter_dimension=0, tiled=True),
        lax.psum_scatter(shift_one_grad, "dp", scatter_dimension=0, tiled=True),
        lax.psum_scatter(gain_two_grad, "dp", scatter_dimension=0, tiled=True),
        lax.psum_scatter(shift_two_grad, "dp", scatter_dimension=0, tiled=True),
    )
    return (
        layer_output,
        input_gradient,
        summed[0],
        summed[1],
        summed[2],
        summed[3],
        summed[4],
        summed[5],
        table_gradient,
        summed[8],
        summed[9],
        summed[6],
        summed[7],
        summed[10],
        summed[11],
    )


def solution(mesh):
    return jax.shard_map(
        shards,
        mesh=mesh,
        in_specs=(
            P("dp", None),
            P(None, "mp"),
            P(None, "mp"),
            P(None, "mp"),
            P("mp", None),
            P(None, "mp"),
            P(None, "mp"),
            P(),
            P(),
            P(),
            P(None, "mp"),
            P("mp", None),
            P(),
            P(),
            P("dp", None, None, None),
            P("dp"),
            P("dp", None),
        ),
        out_specs=(
            P("dp", None),
            P("dp", None),
            P("dp", "mp"),
            P("dp", "mp"),
            P("dp", "mp"),
            P("mp", "dp"),
            P("dp", "mp"),
            P("dp", "mp"),
            P(None, None, ("dp", "mp")),
            P("dp"),
            P("dp"),
            P("dp", "mp"),
            P("mp", "dp"),
            P("dp"),
            P("dp"),
        ),
        check_vma=False,
    )
```

time: 2170 us -> 1390 us (0.64)
  matrix products: 828 us -> 81.5 us
  Pallas kernels: 0 us -> 280 us
  other arithmetic: 225 us -> 18.3 us
  local copies, waits for them, and re-layouts: 141 us -> 30.4 us
    dot_general x56 -> x15, matrix products: 816 us -> 70.1 us  [the longest x6 27.3 us: tn(): lax.dot_general(left, right, (((0,), (0,)), ((), ())), preferred_element_...]
    pallas_call x0 -> x7, Pallas kernels: none -> 280 us  [the longest x2 169 us: attention_scatter(): pl.pallas_call(functools.partial(scatter_kernel, groups=groups, cols=cols...]
    eq x3 -> x0, other arithmetic: 151 us -> none  [one_hot_of(): bucket_plane[:, :, None] == jnp.arange(REL, dtype=jnp.int32)[None, None, :]]
    dot_general x5 -> x0, local copies, waits for them, and re-layouts: 74 us -> none  [the longest x3 43.9 us: relative_scores(): jnp.einsum('hbt,stb->hst', far_table, selector, preferred_element_type=jn...]
    reduce_scatter x1, waiting for transfers between devices: 76.4 us -> 140 us  [shards(): lax.psum_scatter(table_part.reshape(3, REL, D), ('dp', 'mp'), scatter_dim...]
    reduce_scatter x1, waiting for transfers between devices: 65 us -> 9.95 us  [shards(): lax.psum_scatter(output_grad, 'dp', scatter_dimension=1, tiled=True)]
    sub x1 -> x0, other arithmetic: 42 us -> none  [page_backward(): prob_back - inner]
  transfers between devices with their start and end apart: 13 -> 13, of which waited for: 12 -> 12; matrix products, arithmetic and copies ran while one was open for 3% -> 4% of each run, Pallas kernels for 0% -> 0%
where the time goes in v1:
time: 1390 us; the launch traced here: 1380 us
  waiting for transfers between devices  892 us (64%)
  Pallas kernels  280 us (20%)
  matrix products  81.5 us (6%)
  blocking collectives  60.9 us (4%)
  local copies, waits for them, and re-layouts  30.4 us (2%)
  other arithmetic  18.3 us (1%)
  between operations  16.3 us (1%)
    unnamed x18, waiting for transfers between devices  322 us
    pallas_call x2, Pallas kernels, attention_scatter(): pl.pallas_call(functools.partial(scatter_kernel, groups=groups, cols=cols...  169 us
    reduce_scatter x1, waiting for transfers between devices, shards(): lax.psum_scatter(table_part.reshape(3, REL, D), ('dp', 'mp'), scatter_dim...  140 us
    reduce_scatter x1, waiting for transfers between devices, shards(): lax.psum_scatter(up_grad, 'dp', scatter_dimension=0, tiled=True)  108 us
    reduce_scatter x1, waiting for transfers between devices, shards(): lax.psum_scatter(down_grad, 'dp', scatter_dimension=1, tiled=True)  107 us
    psum x1, waiting for transfers between devices, shards(): attended = lax.psum(nn(context, output_weight), 'mp')  70.3 us
    pallas_call x1, Pallas kernels, attention_forward(): pl.pallas_call(kernel, out_shape=(jax.ShapeDtypeStruct((2 * pairs, rows,...  68.8 us
    psum x1, waiting for transfers between devices, shards(): feed = lax.psum(nn(hidden, down_weight), 'mp')  68.1 us
  transfers between devices with their start and end apart: 13, of which 12 were waited for; matrix products, arithmetic and copies ran while one was open for 4% of the time, Pallas kernels for 0%

profile of v1, /device:TPU:0, one launch (start us, length us, event | category | flops | bytes accessed | tf_op | source)
XLA Modules:
  0.0 1380.6 jit_solution(2664719384427963991)
XLA Ops:
  8.0 4.6 copy.39.rest_2_
  12.5 9.3 project.1
  21.8 68.8 %attention_forward.1 = (bf16[8,576,640]{2,1,0:T(8,128)(2,1)}, bf16[576,512]{1,0:T(8,128)(2,1)}, s32[3,576,640]{2,1,0:T(8,128)}, s32[3,576,640]{2,1,0:T(8,128)}) custom-call(s32[1]{0:T(128)S(6)} %copy.60.used_ref, bf16[640,1536]{1,0:T(8,128)(2,1)} %get-tuple-element.31.qkv_ref.q_ref.k_ref.v_ref.side_ref, bf16[384,512]{1,0:T(8,128)(2,1)} %get-tuple-element.32.rest_0_.pos_ref, ...), custom_call_target="tpu_custom_call" | custom-call | flops 60000002048 | bytes 25000000 | tf_op jit(solution)/shard_map/attention_forward/pallas_call | solution.py:342
  90.7 3.3 fusion.34
  94.5 70.3 %all-reduce.11.cloned.1.call-done = f32[561,1024]{1,0:T(8,128)} async-done(((f32[561,1024]{1,0:T(8,128)}), f32[561,1024]{1,0:T(8,128)}) %all-reduce.11.cloned.1.call-update) | async-done | bytes 2297872 | tf_op jit(solution)/shard_map/psum | solution.py:507
  164.8 2.4 fusion.47
  168.2 16.1 %multiply_convert_fusion = (bf16[561,2048]{1,0:T(8,128)(2,1)S(1)}, f32[561,2048]{1,0:T(8,128)}, f32[561,2048]{1,0:T(8,128)}) fusion(bf16[1024,2048]{1,0:T(8,128)(2,1)S(1)} %copy-done.47, f32[561,1024]{1,0:T(8,128)S(1)} %get-tuple-element.95, f32[1024]{0:T(1024)S(1)} %copy-done.43, f32[1024]{0:T(1024)S(1)} %copy-done.28, f32[561]{0:T(1024)S(1)} %add_rsqrt_fusion.1, ...), kind=kOutput, calls=%fused_computation.3 | convolution fusion | flops 2430557184 | bytes 17994120 | tf_op jit(solution)/shard_map/dot_general | solution.py:40
  185.8 4.0 fusion.48
  189.8 68.1 %all-reduce.13.cloned.1.call-done = f32[561,1024]{1,0:T(8,128)} async-done(((f32[561,1024]{1,0:T(8,128)}), f32[561,1024]{1,0:T(8,128)}) %all-reduce.13.cloned.1.call-update) | async-done | bytes 2297872 | tf_op jit(solution)/shard_map/psum | solution.py:514
  257.9 2.5 fusion.44
  264.2 6.9 add_convert_fusion
  272.5 4.1 fusion.49
  277.7 67.0 %all-reduce.15.cloned.1.call-done = f32[561,1024]{1,0:T(8,128)} async-done(((f32[561,1024]{1,0:T(8,128)}), f32[561,1024]{1,0:T(8,128)}) %all-reduce.15.cloned.1.call-update) | async-done | bytes 2297872 | tf_op jit(solution)/shard_map/psum | solution.py:526
  344.7 6.4 multiply_reduce_fusion
  353.5 21.5 %attention_draw.1 = (bf16[72,64,640]{2,1,0:T(8,128)(2,1)}, bf16[72,64,640]{2,1,0:T(8,128)(2,1)}, f32[576,512]{1,0:T(8,128)}, f32[576,512]{1,0:T(8,128)}, bf16[576,512]{1,0:T(8,128)(2,1)}) custom-call(bf16[8,576,640]{2,1,0:T(8,128)(2,1)} %get-tuple-element.35.p_ref, bf16[576,512]{1,0:T(8,128)(2,1)} %pad.4.up_ref, ...), custom_call_target="tpu_custom_call" | custom-call | flops 20000000000 | bytes 25000000 | tf_op jit(solution)/shard_map/attention_draw/pallas_call | solution.py:372
  375.1 84.5 %attention_scatter.2.s_ref = bf16[72,64,384]{2,1,0:T(8,128)(2,1)} custom-call(bf16[72,64,640]{2,1,0:T(8,128)(2,1)} %get-tuple-element.36.d_ref, s32[3,576,640]{2,1,0:T(8,128)} %get-tuple-element.37.b_ref, bf16[4,256,128]{2,1,0:T(8,128)(2,1)} %fusion.24.merge_ref), custom_call_target="tpu_custom_call" | custom-call | flops 70000001024 | bytes 12000000 | tf_op jit(solution)/shard_map/attention_scatter/pallas_call | solution.py:410
  459.6 5.5 attention_close.2
  465.1 3.3 fusion.31
  468.3 84.5 %attention_scatter.3.s_ref = bf16[72,64,384]{2,1,0:T(8,128)(2,1)} custom-call(bf16[72,64,640]{2,1,0:T(8,128)(2,1)} %get-tuple-element.40.d_ref, s32[3,576,640]{2,1,0:T(8,128)} %get-tuple-element.41.b_ref, bf16[4,256,128]{2,1,0:T(8,128)(2,1)} %fusion.24.merge_ref), custom_call_target="tpu_custom_call" | custom-call | flops 70000001024 | bytes 12000000 | tf_op jit(solution)/shard_map/attention_scatter/pallas_call | solution.py:410
  552.9 5.5 attention_close.3
  558.4 2.0 fusion.28
  560.5 2.3 add_add_fusion
  564.4 2.4 fusion.15
  568.0 2.8 fusion.50
  570.8 2.7 convolution_add_fusion
  575.3 3.0 convolution_bitcast_fusion.1
  578.2 1.9 copy.52
  580.2 3.0 convolution_bitcast_fusion
  583.2 1.9 copy.54
  585.1 2.3 convolution_bitcast_fusion.4
  587.4 1.9 copy.46
  589.4 2.3 convolution_bitcast_fusion.3
  591.6 1.8 copy.48
  593.6 3.6 convolution_bitcast_fusion.2
  597.2 3.1 copy.50
  600.7 9.1 fusion.18
  611.5 7.7 fusion.36
  621.0 60.9 %all-reduce.5 = (f32[1024]{0:T(1024)S(1)}, f32[1024]{0:T(1024)S(1)}, f32[1024]{0:T(1024)S(1)}, f32[1024]{0:T(1024)S(1)}) all-reduce(f32[1024]{0:T(1024)S(1)} %copy-done.36, f32[1024]{0:T(1024)S(1)} %copy-done.37, f32[1024]{0:T(1024)S(1)} %copy-done.34, f32[1024]{0:T(1024)S(1)} %copy-done.35), channel_id=9, replica_groups=mesh['dp'=16,'mp'=2] {'dp'}, use_global_device_ids=true, to_apply=%region_20.21.clone | all-reduce | flops 4096 | bytes 32768
  684.3 3.0 add_convert_fusion.1
  687.3 9.9 reduce-scatter.20.cloned.1.call-done
  697.3 139.7 %reduce-scatter.22.cloned.1.call-done = f32[3,128,32]{1,2,0:T(8,128)} async-done(((f32[3,128,1024]{1,2,0:T(8,128)}), f32[3,128,32]{1,2,0:T(8,128)}) %reduce-scatter.22.cloned.1.call-update) | async-done | bytes 49168 | tf_op jit(solution)/shard_map/reduce_scatter | solution.py:556
  836.9 62.0 %reduce-scatter.34.cloned.1.call-done = f32[64,512]{1,0:T(8,128)} async-done(((f32[1024,512]{1,0:T(8,128)}), f32[64,512]{1,0:T(8,128)}) %reduce-scatter.34.cloned.1.call-update) | async-done | bytes 131088
  898.9 65.1 %reduce-scatter.36.cloned.1.call-done = f32[64,512]{1,0:T(8,128)} async-done(((f32[1024,512]{1,0:T(8,128)}), f32[64,512]{1,0:T(8,128)}) %reduce-scatter.36.cloned.1.call-update) | async-done | bytes 131088
  964.0 65.0 %reduce-scatter.28.cloned.1.call-done = f32[64,512]{1,0:T(8,128)} async-done(((f32[1024,512]{1,0:T(8,128)}), f32[64,512]{1,0:T(8,128)}) %reduce-scatter.28.cloned.1.call-update) | async-done | bytes 131088
  1029.0 64.9 %reduce-scatter.30.cloned.1.call-done = f32[64,512]{1,0:T(8,128)} async-done(((f32[1024,512]{1,0:T(8,128)}), f32[64,512]{1,0:T(8,128)}) %reduce-scatter.30.cloned.1.call-update) | async-done | bytes 131088
  1093.9 65.1 %reduce-scatter.32.cloned.1.call-done = f32[64,512]{1,0:T(8,128)} async-done(((f32[1024,512]{1,0:T(8,128)}), f32[64,512]{1,0:T(8,128)}) %reduce-scatter.32.cloned.1.call-update) | async-done | bytes 131088
  1158.9 106.9 %reduce-scatter.26.cloned.1.call-done = f32[2048,64]{0,1:T(8,128)} async-done(((f32[2048,1024]{0,1:T(8,128)}), f32[2048,64]{0,1:T(8,128)}) %reduce-scatter.26.cloned.1.call-update) | async-done | bytes 524304 | tf_op jit(solution)/shard_map/reduce_scatter | solution.py:567
  1265.8 107.8 %reduce-scatter.24.cloned.1.call-done = f32[64,2048]{1,0:T(8,128)} async-done(((f32[1024,2048]{1,0:T(8,128)}), f32[64,2048]{1,0:T(8,128)}) %reduce-scatter.24.cloned.1.call-update) | async-done | bytes 524304 | tf_op jit(solution)/shard_map/reduce_scatter | solution.py:566
  (156 shorter events, 21.9 us)
Async XLA Ops:
  7.2 83.5 %copy-start = (bf16[512,1024]{1,0:T(8,128)(2,1)S(1)}, bf16[512,1024]{1,0:T(8,128)(2,1)}, u32[]{:S(2)}) copy-start(bf16[512,1024]{1,0:T(8,128)(2,1)} %param.21) | copy-start | bytes 3145732
  7.2 157.6 %all-reduce.11.cloned.1.call-start = ((), (), s32[]{:S(2)}) async-start(), calls=%async_computation.9 | async-start | bytes 4653056 | tf_op jit(solution)/shard_map/psum | solution.py:507
  94.0 163.9 %all-reduce.13.cloned.1.call-start = ((), (), s32[]{:S(2)}) async-start(), calls=%async_computation.10 | async-start | bytes 4653056 | tf_op jit(solution)/shard_map/psum | solution.py:514
  164.8 3.2 copy-start.47
  167.3 183.9 %copy-start.2 = (f32[561,1024]{1,0:T(8,128)}, f32[561,1024]{1,0:T(8,128)S(1)}, u32[]{:S(2)}) copy-start(f32[561,1024]{1,0:T(8,128)S(1)} %get-tuple-element.95) | copy-start | bytes 6893572
  167.3 183.8 %copy-start.22 = (f32[561]{0:T(1024)}, f32[561]{0:T(1024)S(1)}, u32[]{:S(2)}) copy-start(f32[561]{0:T(1024)S(1)} %broadcast_multiply_fusion.5) | copy-start | bytes 6736
  168.2 182.9 %copy-start.24 = (f32[561]{0:T(1024)}, f32[561]{0:T(1024)S(1)}, u32[]{:S(2)}) copy-start(f32[561]{0:T(1024)S(1)} %add_rsqrt_fusion.1) | copy-start | bytes 6736
  168.2 17.5 %copy-start.45 = (bf16[2048,1024]{1,0:T(8,128)(2,1)S(1)}, bf16[2048,1024]{1,0:T(8,128)(2,1)}, u32[]{:S(2)}) copy-start(bf16[2048,1024]{1,0:T(8,128)(2,1)} %param.28) | copy-start | bytes 12582916
  189.8 154.9 %all-reduce.15.cloned.1.call-start = ((), (), s32[]{:S(2)}) async-start(), calls=%async_computation.11 | async-start | bytes 4653056 | tf_op jit(solution)/shard_map/psum | solution.py:526
  257.9 6.3 copy-start.52
  260.4 3.7 copy-start.7
  260.4 2.1 copy-start.10
  260.4 2.1 copy-start.32
  260.5 84.2 %copy-start.26 = (f32[561]{0:T(1024)}, f32[561]{0:T(1024)S(1)}, u32[]{:S(2)}) copy-start(f32[561]{0:T(1024)S(1)} %broadcast_multiply_fusion.4) | copy-start | bytes 6736
  260.5 3.7 copy-start.46
  262.5 82.2 %copy-start.30 = (f32[561]{0:T(1024)}, f32[561]{0:T(1024)S(1)}, u32[]{:S(2)}) copy-start(f32[561]{0:T(1024)S(1)} %add_rsqrt_fusion) | copy-start | bytes 6736
  264.1 80.6 %copy-start.38 = (f32[561]{0:T(1024)}, f32[561]{0:T(1024)S(1)}, u32[]{:S(2)}) copy-start(f32[561]{0:T(1024)S(1)} %get-tuple-element.98) | copy-start | bytes 6736
  264.1 80.6 %copy-start.40 = (f32[561]{0:T(1024)}, f32[561]{0:T(1024)S(1)}, u32[]{:S(2)}) copy-start(f32[561]{0:T(1024)S(1)} %get-tuple-element.99) | copy-start | bytes 6736
  264.2 8.3 copy-start.48
  276.6 68.2 %copy-start.42 = (f32[1024]{0:T(1024)S(1)}, f32[1024]{0:T(1024)}, u32[]{:S(2)}) copy-start(f32[1024]{0:T(1024)} %param.30) | copy-start | bytes 12292
  276.6 407.7 %all-reduce.17.cloned.1.call-start = ((), (), s32[]{:S(2)}) async-start(), calls=%async_computation.12 | async-start | bytes 4653056 | tf_op jit(solution)/shard_map/psum | solution.py:549
  459.6 5.5 copy-start.16
  552.9 5.6 copy-start.17
  552.9 7.6 copy-start.18
  558.4 2.1 copy-start.9
  558.4 2.1 copy-start.14
  560.5 2.3 copy-start.13
  562.8 134.5 %reduce-scatter.20.cloned.1.call-start = ((), (), s32[]{:S(2)}) async-start(), calls=%async_computation.13 | async-start | bytes 2228224 | tf_op jit(solution)/shard_map/reduce_scatter | solution.py:563
  566.8 4.0 copy-start.12
  566.8 270.1 %reduce-scatter.22.cloned.1.call-start = ((), (), s32[]{:S(2)}) async-start(), calls=%async_computation.14 | async-start | bytes 1622016 | tf_op jit(solution)/shard_map/reduce_scatter | solution.py:556
  575.2 323.7 %reduce-scatter.34.cloned.1.call-start = ((), (), s32[]{:S(2)}) async-start(), calls=%async_computation.20 | async-start | bytes 2228224
  580.1 383.8 %reduce-scatter.36.cloned.1.call-start = ((), (), s32[]{:S(2)}) async-start(), calls=%async_computation.21 | async-start | bytes 2228224
  583.2 1.9 copy-start.21
  585.1 443.9 %reduce-scatter.28.cloned.1.call-start = ((), (), s32[]{:S(2)}) async-start(), calls=%async_computation.17 | async-start | bytes 2228224
  587.4 2.0 copy-start.20
  589.3 504.6 %reduce-scatter.30.cloned.1.call-start = ((), (), s32[]{:S(2)}) async-start(), calls=%async_computation.18 | async-start | bytes 2228224
  591.6 1.9 copy-start.19
  593.5 565.4 %reduce-scatter.32.cloned.1.call-start = ((), (), s32[]{:S(2)}) async-start(), calls=%async_computation.19 | async-start | bytes 2228224
  597.2 3.4 copy-start.8
  597.2 3.5 copy-start.27
  597.2 3.5 copy-start.31
  597.2 3.5 copy-start.33
  597.2 3.5 copy-start.39
  597.2 3.5 copy-start.41
  600.3 665.5 %reduce-scatter.26.cloned.1.call-start = ((), (), s32[]{:S(2)}) async-start(), calls=%async_computation.16 | async-start | bytes 8912896 | tf_op jit(solution)/shard_map/reduce_scatter | solution.py:567
  609.8 763.8 %reduce-scatter.24.cloned.1.call-start = ((), (), s32[]{:S(2)}) async-start(), calls=%async_computation.15 | async-start | bytes 8912896 | tf_op jit(solution)/shard_map/reduce_scatter | solution.py:566
  619.1 65.2 %copy-start.6 = (f32[561,1024]{1,0:T(8,128)S(1)}, f32[561,1024]{1,0:T(8,128)}, u32[]{:S(2)}) copy-start(f32[561,1024]{1,0:T(8,128)} %copy-done.4) | copy-start | bytes 6893572
  683.7 689.9 %copy-start.1 = (bf16[512,1024]{1,0:T(8,128)(2,1)S(1)}, bf16[512,1024]{1,0:T(8,128)(2,1)}, u32[]{:S(2)}) copy-start(bf16[512,1024]{1,0:T(8,128)(2,1)} %param.21) | copy-start | bytes 3145732
  (18 other events, 27.5 us)
Sparse Core Ops, SparseCore 0:
  94.1 70.6 all-reduce.10
  189.9 67.9 all-reduce.12
  276.7 67.9 all-reduce.14
  562.9 67.9 all-reduce.16
  635.1 62.1 reduce-scatter.19
  699.9 136.9 reduce-scatter.21
  841.2 57.6 reduce-scatter.33
  903.2 60.6 reduce-scatter.35
  968.3 60.6 reduce-scatter.27
  1033.1 60.6 reduce-scatter.29
  1098.2 60.7 reduce-scatter.31
  1163.4 102.3 reduce-scatter.25
  1270.5 103.1 reduce-scatter.23

commit v2 on v1

--- a/solution.py
+++ b/solution.py
@@ -9,7 +9,6 @@
 
 D = 1024
 epsilon = 1e-05
-highest = lax.Precision.HIGHEST
 HEAD = 64
 REL = 128
 TEXT = 512
@@ -300,17 +299,18 @@
     lax.fori_loop(0, groups, body, 0)
 
 
-def close_kernel(s_ref, base_ref, pos_ref, side_ref, out_ref, table_ref, *, rows):
+def close_kernel(*refs, rows, count):
+    base_ref, pos_ref, side_ref, out_ref, table_ref = refs[count:]
     rows2 = 2 * rows
     half3 = lane_half((rows // 8, 8, 128))
-    flat = s_ref[...].reshape(rows2, 3 * REL)
+    flat = jnp.concatenate([ref[...] for ref in refs[:count]], axis=0).reshape(rows2, 3 * REL)
     both = nn(flat, pos_ref[...]).reshape(rows // 8, 16, 128)
     mine = jnp.where(half3, both[:, 0:8, :], both[:, 8:16, :]).reshape(rows, 128)
-    out_ref[...] = (base_ref[...] + mine).astype(bf16)
+    out_ref[...] = base_ref[...] + mine
     side = side_ref[0:rows, :].astype(f32).reshape(rows // 8, 8, 128)
     zero = jnp.zeros_like(side)
     spread = jnp.concatenate([jnp.where(half3, side, zero), jnp.where(half3, zero, side)], axis=1)
-    table_ref[...] = tn(flat, spread.reshape(rows2, 128).astype(bf16))
+    table_ref[...] = tn(flat, spread.reshape(rows2, 128).astype(bf16)).astype(bf16)
 
 
 def merge_table():
@@ -404,16 +404,22 @@
     )(share, upstream, qkv, qkv, qkv)
 
 
-def attention_scatter(back, buckets, merge):
-    groups, _, cols = back.shape
+def attention_scatter(back, buckets, merge, part, count):
+    groups, high, cols = back.shape
+    groups = groups // count
     whole = pl.BlockSpec(memory_space=pltpu.VMEM)
     return pl.pallas_call(
         functools.partial(scatter_kernel, groups=groups, cols=cols),
-        out_shape=jax.ShapeDtypeStruct((groups, back.shape[1], 3 * REL), bf16),
-        in_specs=[whole] * 3,
-        out_specs=whole,
+        grid=(1,),
+        out_shape=jax.ShapeDtypeStruct((groups, high, 3 * REL), bf16),
+        in_specs=[
+            pl.BlockSpec((groups, high, cols), lambda g: (part, 0, 0)),
+            pl.BlockSpec((3, groups * 8, cols), lambda g: (0, part, 0)),
+            whole,
+        ],
+        out_specs=pl.BlockSpec((groups, high, 3 * REL), lambda g: (0, 0, 0)),
         compiler_params=pltpu.CompilerParams(vmem_limit_bytes=VMEM_CAP),
-        cost_estimate=pl.CostEstimate(flops=70000000000, bytes_accessed=12000000, transcendentals=0),
+        cost_estimate=pl.CostEstimate(flops=7 * 10**10 // count, bytes_accessed=12 * 10**6 // count, transcendentals=0),
         name="attention_scatter",
     )(back, buckets, merge)
 
@@ -423,10 +429,11 @@
     pairs = width // 128
     groups = rows // 8
     return pl.pallas_call(
-        functools.partial(close_kernel, rows=rows),
+        functools.partial(close_kernel, rows=rows, count=len(sums)),
         grid=(pairs,),
         in_specs=[
-            pl.BlockSpec((groups, 16, 3 * REL), lambda p: (0, p, 0)),
+            pl.BlockSpec((groups // len(sums), 16, 3 * REL), lambda p: (0, p, 0))
+        ] * len(sums) + [
             pl.BlockSpec((rows, 128), lambda p: (0, p)),
             pl.BlockSpec((3 * REL, 128), lambda p: (0, p)),
             pl.BlockSpec((qkv.shape[0], 128), lambda p: (0, p + side * pairs)),
@@ -436,24 +443,265 @@
             pl.BlockSpec((3 * REL, 128), lambda p: (0, p)),
         ),
         out_shape=(
-            jax.ShapeDtypeStruct((rows, width), bf16),
-            jax.ShapeDtypeStruct((3 * REL, width), f32),
+            jax.ShapeDtypeStruct((rows, width), f32),
+            jax.ShapeDtypeStruct((3 * REL, width), bf16),
         ),
         compiler_params=pltpu.CompilerParams(vmem_limit_bytes=VMEM_CAP),
         cost_estimate=pl.CostEstimate(flops=5000000000, bytes_accessed=10000000, transcendentals=0),
         name="attention_close",
-    )(sums, base, pos, qkv)
-
-def exact_left(left, right):
-    return lax.dot_general(
-        left, right, (((0,), (0,)), ((), ())), precision=highest, preferred_element_type=jnp.float32
-    )
-
-
-def exact_right(left, right):
-    return lax.dot_general(
-        left, right, (((1,), (1,)), ((), ())), precision=highest, preferred_element_type=jnp.float32
-    )
+    )(*sums, base, pos, qkv)
+
+
+def fill_turned(x_ref, turned, rows):
+    depth = x_ref.shape[1]
+    for a in range(0, rows, 128):
+        tall = min(128, rows - a)
+        for b in range(0, depth, 128):
+            block = x_ref[a:a + tall, b:b + 128]
+            if tall < 128:
+                block = jnp.concatenate([block, jnp.zeros((128 - tall, 128), block.dtype)], axis=0)
+            turned[b:b + 128, a:a + tall] = block.T[:, :tall]
+
+
+def each_block(pick_ref, blocks, keeps, bit, slot):
+    if not keeps:
+        return [(0, d, d) for d in range(blocks)]
+    shift = bit - 1
+    listed = []
+    for out in range(2):
+        value = pick_ref[slot] if out == 1 else 1 - pick_ref[slot]
+        for e in range(blocks // 2):
+            low = e & ((1 << shift) - 1)
+            listed.append((out, e, ((e >> shift) << (shift + 1)) + low + value * (1 << shift)))
+    return listed
+
+
+def weight_kernel(pick_ref, x_ref, y_ref, *rest, rows, blocks, deep, keeps, bit):
+    add_ref = rest[0] if keeps else None
+    outs = rest[1:3] if keeps else rest[0:1]
+    turned = rest[-1]
+
+    @pl.when(pl.program_id(0) == 0)
+    def _():
+        fill_turned(x_ref, turned, rows)
+
+    for out, place, d in each_block(pick_ref, blocks, keeps, bit, 1):
+        at = pl.ds(pl.multiple_of((2 * d + pick_ref[0]) * deep, deep), deep)
+        part = nn(turned[at, :], y_ref[...])
+        outs[out][place] = part + add_ref[d] if keeps else part
+
+
+def weight_half(pick, x, y, add=None, *, parts, bits, tile=512):
+    rows, depth = x.shape
+    wide = y.shape[1]
+    deep = depth // parts
+    blocks = parts // 2
+    keeps = add is not None
+
+    def tiled(n):
+        return pl.BlockSpec((n, deep, tile), lambda c: (0, 0, c))
+
+    ins = [
+        pl.BlockSpec(memory_space=pltpu.SMEM),
+        pl.BlockSpec((rows, depth), lambda c: (0, 0)),
+        pl.BlockSpec((rows, tile), lambda c: (0, c)),
+    ]
+    args = [pick, x, y]
+    shape = (jax.ShapeDtypeStruct((blocks, deep, wide), f32),)
+    specs = (tiled(blocks),)
+    if keeps:
+        ins.append(tiled(blocks))
+        args += add
+        shape = (jax.ShapeDtypeStruct((blocks // 2, deep, wide), f32),) * 2
+        specs = (tiled(blocks // 2),) * 2
+    return pl.pallas_call(
+        functools.partial(weight_kernel, rows=rows, blocks=blocks, deep=deep, keeps=keeps, bit=bits[0]),
+        grid=(wide // tile,),
+        in_specs=ins,
+        out_specs=specs,
+        out_shape=shape,
+        scratch_shapes=[pltpu.VMEM((depth, rows), bf16)],
+        compiler_params=pltpu.CompilerParams(vmem_limit_bytes=VMEM_CAP),
+        cost_estimate=pl.CostEstimate(
+            flops=rows * depth * wide, bytes_accessed=4 * depth * wide, transcendentals=0
+        ),
+        name="weight_half",
+    )(*args)
+
+
+def many_kernel(pick_ref, *refs, plan, widths, turns, blocks, deep, keeps, bits):
+    n_in = 2 * len(plan)
+    ins = refs[:n_in]
+    n_out = len(widths)
+    adds = refs[n_in:n_in + n_out] if keeps else None
+    outs = refs[n_in + n_out:n_in + 3 * n_out] if keeps else refs[n_in:n_in + n_out]
+    scratch = refs[len(refs) - sum(turns):]
+    left = []
+    used = 0
+    for n, turn in enumerate(turns):
+        if turn:
+            fill_turned(ins[2 * n], scratch[used], ins[2 * n].shape[0])
+            left.append(scratch[used])
+            used += 1
+        else:
+            left.append(ins[2 * n])
+    right = [ins[2 * n + 1][...] for n in range(len(plan))]
+    for group in range(n_out):
+        for out, place, d in each_block(pick_ref, blocks, keeps, bits[group], 1 + group):
+            at = pl.ds(pl.multiple_of((2 * d + pick_ref[0]) * deep, deep), deep)
+            target = outs[2 * group + out] if keeps else outs[group]
+            for n, (kind, own, start, wide) in enumerate(plan):
+                if own != group:
+                    continue
+                rows = left[n][at, :]
+                if kind == "copy":
+                    part = rows
+                elif kind == "nt":
+                    part = nt(rows, right[n])
+                else:
+                    part = nn(rows, right[n])
+                cut = slice(start, start + wide)
+                if keeps:
+                    part = part + adds[group][d, :, cut]
+                target[place, :, cut] = part
+
+
+def many_half(pick, pairs, plan, widths, add=None, *, parts, bits):
+    whole = pl.BlockSpec(memory_space=pltpu.VMEM)
+    turns = [kind != "nt" for kind, *_ in plan]
+    depth = max(left.shape[1] for (left, _), turn in zip(pairs, turns) if turn)
+    deep = depth // parts
+    blocks = parts // 2
+    keeps = add is not None
+    args = [pick] + [operand for pair in pairs for operand in pair] + (list(add) if keeps else [])
+    if keeps:
+        shape = [jax.ShapeDtypeStruct((blocks // 2, deep, w), f32) for w in widths for _ in range(2)]
+    else:
+        shape = [jax.ShapeDtypeStruct((blocks, deep, w), f32) for w in widths]
+    return pl.pallas_call(
+        functools.partial(
+            many_kernel, plan=plan, widths=widths, turns=turns, blocks=blocks, deep=deep,
+            keeps=keeps, bits=[b[0] for b in bits],
+        ),
+        in_specs=[pl.BlockSpec(memory_space=pltpu.SMEM)] + [whole] * (len(args) - 1),
+        out_specs=[whole] * len(shape),
+        out_shape=shape,
+        scratch_shapes=[
+            pltpu.VMEM((left.shape[1], left.shape[0]), left.dtype)
+            for (left, _), turn in zip(pairs, turns) if turn
+        ],
+        compiler_params=pltpu.CompilerParams(vmem_limit_bytes=VMEM_CAP),
+        cost_estimate=pl.CostEstimate(
+            flops=600 * depth * sum(widths), bytes_accessed=6 * depth * sum(widths), transcendentals=0
+        ),
+        name="many_half",
+    )(*args)
+
+
+def flipped(value, bit, size):
+    return lax.ppermute(value, "dp", [(i, i ^ (1 << bit)) for i in range(size)])
+
+
+def bit_of(index, bit):
+    return (index >> bit) & 1
+
+
+class Halving:
+    def __init__(self, make, index, size, orders):
+        self.make, self.index, self.size, self.orders = make, index, size, orders
+        mine = bit_of(index, 0).astype(jnp.int32)
+        self.pick = jnp.stack([mine] + [bit_of(index, bits[0]).astype(jnp.int32) for bits in orders])
+        self.other = self.pick.at[0].set(1 - mine)
+        self.stage = 0
+
+    def work(self):
+        if self.stage == 0:
+            self.pending = [(sent, None) for sent in self.make(self.other, None)]
+        elif self.stage == 1:
+            outs = self.make(self.pick, self.extra)
+            self.pending = [(outs[2 * g], outs[2 * g + 1]) for g in range(len(self.orders))]
+            self.axes = [
+                [b for b in range(self.size.bit_length() - 1, 0, -1) if b != bits[0] and b < self.size.bit_length() - 1]
+                for bits in self.orders
+            ]
+        else:
+            self.pending = [
+                self.split(g, held, extra) for g, (held, extra) in enumerate(zip(self.held, self.extra))
+            ]
+        return [part for pair in self.pending for part in pair if part is not None]
+
+    def split(self, g, held, extra):
+        bits = self.orders[g]
+        if self.stage > len(bits):
+            return held + extra, None
+        bit = bits[self.stage - 1]
+        axis = self.axes[g].index(bit)
+        shape = (2,) * len(self.axes[g]) + held.shape[-2:]
+        self.axes[g].remove(bit)
+        own = bit_of(self.index, bit)
+        held, extra = held.reshape(shape), extra.reshape(shape)
+
+        def half(value, at):
+            return lax.dynamic_index_in_dim(value, at, axis, keepdims=False)
+
+        return half(held, 1 - own) + half(extra, 1 - own), half(held, own) + half(extra, own)
+
+    def go(self, parts):
+        parts = list(parts)
+        pairs = [
+            tuple(None if part is None else parts.pop(0) for part in pair) for pair in self.pending
+        ]
+        self.held = [home for _, home in pairs]
+        last = self.stage > len(self.orders[0])
+        if last:
+            self.result = [away for away, _ in pairs]
+        else:
+            bit = lambda g: 0 if self.stage == 0 else self.orders[g][self.stage - 1]
+            self.extra = [flipped(away, bit(g), self.size) for g, (away, _) in enumerate(pairs)]
+        self.stage += 1
+
+    def step(self):
+        self.go(self.work())
+
+    def finish(self):
+        while self.stage <= len(self.orders[0]) + 1:
+            self.step()
+        return self.result
+
+
+def tie(values, *chains):
+    works = [chain.work() for chain in chains]
+    values, works = lax.optimization_barrier((values, works))
+    for chain, parts in zip(chains, works):
+        chain.go(parts)
+    return values
+
+
+def across(value):
+    return value + lax.ppermute(value, "mp", [(0, 1), (1, 0)])
+
+
+def join_kernel(base_ref, early_ref, mine_ref, w_ref, other_ref, ow_ref, out_ref, *, span):
+    weight = ow_ref[...].astype(bf16)
+    for start in range(0, span, 64):
+        tall = min(64, span - start)
+        at = slice(start, start + 64)
+        total = base_ref[at, :] + early_ref[at, :] + nt(mine_ref[at, :], w_ref[...])
+        total = total + nt(other_ref[at, :].astype(bf16), weight)
+        out_ref[start:start + tall, :] = total.astype(bf16)[:tall]
+
+
+def join(base, early, mine, weight, other, other_weight, span):
+    whole = pl.BlockSpec(memory_space=pltpu.VMEM)
+    return pl.pallas_call(
+        functools.partial(join_kernel, span=span),
+        in_specs=[whole] * 6,
+        out_specs=whole,
+        out_shape=jax.ShapeDtypeStruct((span, base.shape[1]), bf16),
+        compiler_params=pltpu.CompilerParams(vmem_limit_bytes=VMEM_CAP),
+        cost_estimate=pl.CostEstimate(flops=3 * 10**9, bytes_accessed=12 * 10**6, transcendentals=0),
+        name="join",
+    )(base, early, mine, weight, other, other_weight)
 
 
 def norm_forward(summed, gain, shift):
@@ -495,97 +743,153 @@
 ):
     span = buckets.shape[2]
     rows, cols = sizes(span)
+    size = lax.axis_size("dp")
+    index = lax.axis_index("dp")
+    bits = list(range(1, size.bit_length() - 1))
+    low_first, high_first = bits, bits[1:] + bits[:1]
     score_scale = (7.0 * HEAD) ** (-0.5)
     tables_flat = position_tables.reshape(3 * REL, D)
+    width = query_weight.shape[1]
+    spare = ((0, rows - span), (0, 0))
+
+    def chain(make, *orders):
+        return Halving(make, index, size, list(orders))
+
+    other_key_weight = lax.ppermute(key_weight.astype(f32), "mp", [(0, 1), (1, 0)])
     qkv, pos_key, pos_query = project(
         tokens, query_weight, key_weight, value_weight, position_tables, key_position, query_position, span
     )
+    tokens = jnp.pad(tokens, spare)
+    cotangent = jnp.pad(cotangent, spare)
     share, context, bucket_rows, bucket_cols = attention_forward(
         qkv, pos_key, pos_query, buckets, text_length, score_scale
     )
-    context = context[:span]
-    attended = lax.psum(nn(context, output_weight), "mp")
+    attended = across(nn(context, output_weight))
     first, normal_one, inverse_one = norm_forward(
         tokens.astype(f32) + attended, gain_one, shift_one
     )
     first_low = first.astype(bf16)
     upward = nn(first_low, up_weight)
     hidden = jax.nn.gelu(upward, approximate=False).astype(bf16)
-    feed = lax.psum(nn(hidden, down_weight), "mp")
+    feed = across(nn(hidden, down_weight))
     final, normal_two, inverse_two = norm_forward(first + feed, gain_two, shift_two)
-    layer_output = final.astype(bf16)
+    layer_output = final[:span].astype(bf16)
     second_back, gain_two_grad, shift_two_grad = norm_backward(
         cotangent.astype(f32), normal_two, inverse_two, gain_two
     )
     second_low = second_back.astype(bf16)
-    down_grad = tn(hidden, second_low)
     hidden_back = nt(second_low, down_weight)
     gelu_back = jax.vjp(lambda inner_value: jax.nn.gelu(inner_value, approximate=False), upward)[1]
     upward_back = gelu_back(hidden_back)[0].astype(bf16)
-    up_grad = tn(first_low, upward_back)
-    first_back = second_back + lax.psum(nt(upward_back, up_weight), "mp")
+
+    back_part = nt(upward_back, up_weight)
+    back_other = lax.ppermute(back_part, "mp", [(0, 1), (1, 0)])
+    down_chain = chain(
+        lambda pick, add: weight_half(pick, second_low, hidden, add, parts=size, bits=high_first), high_first
+    )
+    up_chain = chain(
+        lambda pick, add: weight_half(pick, first_low, upward_back, add, parts=size, bits=low_first), low_first
+    )
+    down_chain.step()
+    up_chain.step()
+    down_chain.step()
+    back_other = tie(back_other, up_chain)
+    first_back = second_back + back_part + back_other
     residual_back, gain_one_grad, shift_one_grad = norm_backward(
         first_back, normal_one, inverse_one, gain_one
     )
     residual_low = residual_back.astype(bf16)
-    output_grad = tn(context, residual_low)
-    context_back = jnp.pad(nt(residual_low, output_weight).astype(bf16), ((0, rows - span), (0, 0)))
+    context_back = nt(residual_low, output_weight).astype(bf16)
 
     merge = merge_table()
     back, back_turned, query_base, key_base, value_back = attention_draw(
         share, context_back, qkv, score_scale
     )
-    near_sums = attention_scatter(back, bucket_rows, merge)
-    query_back, key_table_sum = attention_close(near_sums, query_base, pos_key, qkv, 0)
-    far_sums = attention_scatter(back_turned, bucket_cols, merge)
-    key_back, query_table_sum = attention_close(far_sums, key_base, pos_query, qkv, 1)
-    query_flat, key_flat, value_flat = query_back[:span], key_back[:span], value_back[:span]
-    query_grad = tn(tokens, query_flat)
-    key_grad = tn(tokens, key_flat)
-    value_grad = tn(tokens, value_flat)
-    input_part = (
-        nt(query_flat, query_weight) + nt(key_flat, key_weight) + nt(value_flat, value_weight)
-    )
-    input_gradient = (residual_back + lax.psum(input_part, "mp")).astype(bf16)
-    tables_wide = tables_flat.astype(f32)
-    key_position_grad = exact_left(tables_wide, key_table_sum)
-    query_position_grad = exact_left(tables_wide, query_table_sum)
-    table_part = exact_right(key_table_sum, key_position.astype(f32)) + exact_right(
-        query_table_sum, query_position.astype(f32)
-    )
-    table_gradient = lax.psum_scatter(
-        table_part.reshape(3, REL, D), ("dp", "mp"), scatter_dimension=2, tiled=True
-    )
-    summed = (
-        lax.psum_scatter(query_grad, "dp", scatter_dimension=0, tiled=True),
-        lax.psum_scatter(key_grad, "dp", scatter_dimension=0, tiled=True),
-        lax.psum_scatter(value_grad, "dp", scatter_dimension=0, tiled=True),
-        lax.psum_scatter(output_grad, "dp", scatter_dimension=1, tiled=True),
-        lax.psum_scatter(query_position_grad, "dp", scatter_dimension=0, tiled=True),
-        lax.psum_scatter(key_position_grad, "dp", scatter_dimension=0, tiled=True),
-        lax.psum_scatter(up_grad, "dp", scatter_dimension=0, tiled=True),
-        lax.psum_scatter(down_grad, "dp", scatter_dimension=1, tiled=True),
-        lax.psum_scatter(gain_one_grad, "dp", scatter_dimension=0, tiled=True),
-        lax.psum_scatter(shift_one_grad, "dp", scatter_dimension=0, tiled=True),
-        lax.psum_scatter(gain_two_grad, "dp", scatter_dimension=0, tiled=True),
-        lax.psum_scatter(shift_two_grad, "dp", scatter_dimension=0, tiled=True),
-    )
+    nothing = jnp.zeros_like(gain_one)
+    gains = jnp.stack(
+        [gain_one_grad, shift_one_grad, gain_two_grad, shift_two_grad] + [nothing] * 4
+    )
+    gains = jnp.concatenate([gains, jnp.zeros((120, gains.shape[1]), f32)], axis=0)
+    dummy = jnp.zeros((8, 128), bf16)
+    outer_chain = chain(
+        lambda pick, add: many_half(
+            pick,
+            [(residual_low, context), (tokens, value_back), (gains, dummy)],
+            [("nn", 0, 0, width), ("nn", 0, width, width), ("copy", 0, 2 * width, 128)],
+            [2 * width + 128],
+            add, parts=size, bits=[low_first],
+        ),
+        low_first,
+    )
+    outer_chain.step()
+
+    def tail(rows_back, sums, position, orders):
+        return chain(
+            lambda pick, add: many_half(
+                pick,
+                [(tokens, rows_back), (tables_flat, sums), (position, sums)],
+                [("nn", 0, 0, width), ("nn", 1, 0, width), ("nt", 0, width, 3 * REL)],
+                [width + 3 * REL, width],
+                add, parts=size, bits=orders,
+            ),
+            *orders,
+        )
+
+    near = []
+    near.append(attention_scatter(back, bucket_rows, merge, 0, 2))
+    back, near = tie((back, near), outer_chain, down_chain)
+    near.append(attention_scatter(back, bucket_rows, merge, 1, 2))
+    near, back_turned = tie((near, back_turned), up_chain)
+    query_back, key_table_sum = attention_close(near, query_base, pos_key, qkv, 0)
+    query_low = query_back.astype(bf16)
+    early_part = nt(query_low, query_weight) + nt(value_back, value_weight)
+    early = across(early_part)
+    near_chain = tail(query_low, key_table_sum, key_position, [high_first, low_first])
+    back_turned = tie(back_turned, near_chain, down_chain)
+    far = []
+    far.append(attention_scatter(back_turned, bucket_cols, merge, 0, 2))
+    back_turned, far = tie((back_turned, far), near_chain, up_chain, outer_chain)
+    far.append(attention_scatter(back_turned, bucket_cols, merge, 1, 2))
+    far = tie(far, near_chain, outer_chain, up_chain, down_chain)
+    key_back, query_table_sum = attention_close(far, key_base, pos_query, qkv, 1)
+    key_other = lax.ppermute(key_back, "mp", [(0, 1), (1, 0)])
+    key_low = key_back.astype(bf16)
+    far_chain = tail(key_low, query_table_sum, query_position, [low_first, high_first])
+    far_chain.step()
+    far_chain.step()
+    input_gradient = join(
+        residual_back, early, key_low, key_weight, key_other, other_key_weight, span
+    )
+    (down_share,) = down_chain.finish()
+    (up_share,) = up_chain.finish()
+    (outer_share,) = outer_chain.finish()
+    near_main, key_position_grad = near_chain.finish()
+    far_main, query_position_grad = far_chain.finish()
+
+    table_rows = near_main[:, width:] + far_main[:, width:]
+    table_rows = table_rows.reshape(2, table_rows.shape[0] // 2, 3 * REL)
+    side = lax.axis_index("mp")
+    table_mine = lax.dynamic_index_in_dim(table_rows, side, 0, keepdims=False) + lax.ppermute(
+        lax.dynamic_index_in_dim(table_rows, 1 - side, 0, keepdims=False), "mp", [(0, 1), (1, 0)]
+    )
+    table_gradient = table_mine.T.reshape(3, REL, table_mine.shape[0])
+    gains_mine = outer_share[:, 2 * width:]
     return (
         layer_output,
         input_gradient,
-        summed[0],
-        summed[1],
-        summed[2],
-        summed[3],
-        summed[4],
-        summed[5],
+        near_main[:, 0:width],
+        far_main[:, 0:width],
+        outer_share[:, width:2 * width],
+        outer_share[:, 0:width].T,
+        query_position_grad,
+        key_position_grad,
         table_gradient,
-        summed[8],
-        summed[9],
-        summed[6],
-        summed[7],
-        summed[10],
-        summed[11],
+        gains_mine[:, 0],
+        gains_mine[:, 1],
+        up_share,
+        down_share.T,
+        gains_mine[:, 2],
+        gains_mine[:, 3],
     )
 
 

time: 1390 us -> 724 us (0.52)
  waiting for transfers between devices: 892 us -> 191 us
  Pallas kernels: 280 us -> 364 us
  blocking collectives: 60.9 us -> 0 us
  other arithmetic: 18.3 us -> 60.4 us
  matrix products: 81.5 us -> 42.4 us
  starting transfers between devices: 1.64 us -> 35.4 us
  between operations: 16.3 us -> 2.11 us
    reduce_scatter x4 -> x0, waiting for transfers between devices: 364 us -> none  [the longest x1 140 us: shards(): lax.psum_scatter(table_part.reshape(3, REL, D), ('dp', 'mp'), scatter_dim...]
    unnamed x18 -> x0, waiting for transfers between devices: 322 us -> none
    psum x4 -> x0, waiting for transfers between devices: 205 us -> none  [the longest x1 70.3 us: shards(): attended = lax.psum(nn(context, output_weight), 'mp')]
    ppermute x0 -> x35, waiting for transfers between devices: none -> 191 us  [the longest x3 102 us: across(): return value + lax.ppermute(value, 'mp', [(0, 1), (1, 0)])]
    pallas_call x2 -> x13, Pallas kernels: 11 us -> 92.1 us  [the longest x6 39.4 us: many_half(): pl.pallas_call(functools.partial(many_kernel, plan=plan, widths=widths, t...]
    unnamed x1 -> x0, blocking collectives: 60.9 us -> none
    dot_general x10 -> x0, matrix products: 38.7 us -> none  [the longest x6 27.3 us: tn(): lax.dot_general(left, right, (((0,), (0,)), ((), ())), preferred_element_...]
    ppermute x0 -> x35, starting transfers between devices: none -> 35.4 us  [the longest x28 25 us: flipped(): return lax.ppermute(value, 'dp', [(i, i ^ 1 << bit) for i in range(size)])]
  transfers between devices with their start and end apart: 13 -> 35, of which waited for: 12 -> 11; matrix products, arithmetic and copies ran while one was open for 4% -> 11% of each run, Pallas kernels for 0% -> 38%
where the time goes in v2:
time: 724 us; the launch traced here: 715 us
  Pallas kernels  364 us (50%)
  waiting for transfers between devices  191 us (26%)
  other arithmetic  60.4 us (8%)
  matrix products  42.4 us (6%)
  starting transfers between devices  35.4 us (5%)
  local copies, waits for them, and re-layouts  19.4 us (3%)
    pallas_call x4, Pallas kernels, attention_scatter(): pl.pallas_call(functools.partial(scatter_kernel, groups=groups, cols=cols...  173 us
    ppermute x3, waiting for transfers between devices, across(): return value + lax.ppermute(value, 'mp', [(0, 1), (1, 0)])  102 us
    pallas_call x1, Pallas kernels, attention_forward(): pl.pallas_call(kernel, out_shape=(jax.ShapeDtypeStruct((2 * pairs, rows,...  68.7 us
    ppermute x28, waiting for transfers between devices, flipped(): return lax.ppermute(value, 'dp', [(i, i ^ 1 << bit) for i in range(size)])  57.6 us
    pallas_call x6, Pallas kernels, many_half(): pl.pallas_call(functools.partial(many_kernel, plan=plan, widths=widths, t...  39.4 us
    ppermute x1, waiting for transfers between devices, shards(): back_other = lax.ppermute(back_part, 'mp', [(0, 1), (1, 0)])  31.4 us
    pallas_call x4, Pallas kernels, weight_half(): pl.pallas_call(functools.partial(weight_kernel, rows=rows, blocks=blocks,...  31.1 us
    ppermute x28, starting transfers between devices, flipped(): return lax.ppermute(value, 'dp', [(i, i ^ 1 << bit) for i in range(size)])  25 us
  transfers between devices with their start and end apart: 35, of which 11 were waited for; matrix products, arithmetic and copies ran while one was open for 11% of the time, Pallas kernels for 38%

profile of v2, /device:TPU:0, one launch (start us, length us, event | category | flops | bytes accessed | tf_op | source)
XLA Modules:
  0.0 715.1 jit_solution(14147573752352618032)
XLA Ops:
  0.7 4.6 copy.47.rest_2_
  5.9 9.3 %project.1 = (bf16[640,1536]{1,0:T(8,128)(2,1)}, bf16[384,512]{1,0:T(8,128)(2,1)}, bf16[384,512]{1,0:T(8,128)(2,1)}) custom-call(bf16[561,1024]{1,0:T(8,128)(2,1)} %x_ref.1, bf16[1024,512]{1,0:T(8,128)(2,1)} %wq_ref.1, bf16[1024,512]{1,0:T(8,128)(2,1)} %w_ref.1, bf16[1024,512]{1,0:T(8,128)(2,1)} %wv_ref.1, bf16[3,128,1024]{2,1,0:T(8,128)(2,1)} %t_ref.1, ...), custom_call_target="tpu_custom_call" | custom-call | flops 4000000000 | bytes 9000000 | tf_op jit(solution)/shard_map/project/pallas_call | solution.py:202
  15.3 68.7 %attention_forward.1 = (bf16[8,576,640]{2,1,0:T(8,128)(2,1)}, bf16[576,512]{1,0:T(8,128)(2,1)}, s32[3,576,640]{2,1,0:T(8,128)}, s32[3,576,640]{2,1,0:T(8,128)}) custom-call(s32[1]{0:T(128)S(6)} %copy.83.used_ref, bf16[640,1536]{1,0:T(8,128)(2,1)} %get-tuple-element.144.qkv_ref.q_ref.k_ref.v_ref.refs_4_, bf16[384,512]{1,0:T(8,128)(2,1)} %get-tuple-element.145.rest_0_.refs_3_, ...), custom_call_target="tpu_custom_call" | custom-call | flops 60000002048 | bytes 25000000 | tf_op jit(solution)/shard_map/attention_forward/pallas_call | solution.py:342
  86.0 3.0 collective-permute-start
  89.0 51.2 %collective-permute-done = f32[576,1024]{1,0:T(8,128)S(1)} collective-permute-done((f32[576,1024]{1,0:T(8,128)S(1)}, f32[576,1024]{1,0:T(8,128)S(1)}, u32[]{:S(2)}, u32[]{:S(2)}) %collective-permute-start) | collective-permute-done | bytes 2359328 | tf_op jit(solution)/shard_map/ppermute | solution.py:681
  143.7 14.2 %multiply_convert_fusion = (bf16[576,2048]{1,0:T(8,128)(2,1)S(1)}, f32[576,2048]{1,0:T(8,128)}, f32[576,2048]{1,0:T(8,128)}) fusion(bf16[576,1024]{1,0:T(8,128)(2,1)S(1)} %fusion.15.x_ref, bf16[1024,2048]{1,0:T(8,128)(2,1)S(1)} %copy-done.38), kind=kOutput, calls=%fused_computation.3 | convolution fusion | flops 2492596224 | bytes 17170432 | tf_op jit(solution)/shard_map/dot_general | solution.py:39
  158.0 4.0 fusion.33
  164.0 50.8 %collective-permute-done.1 = f32[576,1024]{1,0:T(8,128)} collective-permute-done((f32[576,1024]{1,0:T(8,128)}, f32[576,1024]{1,0:T(8,128)}, u32[]{:S(2)}, u32[]{:S(2)}) %collective-permute-start.1) | collective-permute-done | bytes 2359328 | tf_op jit(solution)/shard_map/ppermute | solution.py:681
  214.7 3.2 fusion.29
  223.4 7.4 %weight_half.6 = f32[8,64,2048]{2,1,0:T(8,128)} custom-call(s32[2]{0:T(128)} %copy-done.34, bf16[576,1024]{1,0:T(8,128)(2,1)} %fusion.27.x_ref, bf16[576,2048]{1,0:T(8,128)(2,1)} %copy-done.9), custom_call_target="tpu_custom_call" | custom-call | flops 1207959552 | bytes 8388608 | tf_op jit(solution)/shard_map/weight_half/pallas_call | solution.py:517
  230.8 10.6 %add_convert_fusion.y_ref = bf16[576,2048]{1,0:T(8,128)(2,1)} fusion(f32[576,2048]{1,0:T(8,128)} %get-tuple-element.251, f32[576,2048]{1,0:T(8,128)} %get-tuple-element.274, bf16[576,1024]{1,0:T(8,128)(2,1)} %fusion.27.x_ref, bf16[2048,1024]{1,0:T(8,128)(2,1)} %param.38), kind=kOutput, calls=%fused_computation.2 | convolution fusion | flops 2432434176 | bytes 17170432 | tf_op jit(solution)/shard_map/dot_general | solution.py:35
  241.4 7.8 %weight_half.4 = f32[8,64,2048]{2,1,0:T(8,128)} custom-call(s32[2]{0:T(128)} %copy-done.30, bf16[576,1024]{1,0:T(8,128)(2,1)} %copy-done.6, bf16[576,2048]{1,0:T(8,128)(2,1)} %add_convert_fusion.y_ref), custom_call_target="tpu_custom_call" | custom-call | flops 1207959552 | bytes 8388608 | tf_op jit(solution)/shard_map/weight_half/pallas_call | solution.py:517
  249.7 7.0 fusion.34
  261.5 7.9 %weight_half.7 = (f32[4,64,2048]{2,1,0:T(8,128)}, f32[4,64,2048]{2,1,0:T(8,128)}) custom-call(s32[2]{0:T(128)} %copy-done.33, bf16[576,1024]{1,0:T(8,128)(2,1)} %fusion.27.x_ref, bf16[576,2048]{1,0:T(8,128)(2,1)} %copy-done.9, f32[8,64,2048]{2,1,0:T(8,128)} %collective-permute-done.5.rest_0_), custom_call_target="tpu_custom_call" | custom-call | flops 1207959552 | bytes 8388608 | tf_op jit(solution)/shard_map/weight_half/pallas_call | solution.py:517
  271.0 7.9 %weight_half.5 = (f32[4,64,2048]{2,1,0:T(8,128)}, f32[4,64,2048]{2,1,0:T(8,128)}) custom-call(s32[2]{0:T(128)} %copy-done.29, bf16[576,1024]{1,0:T(8,128)(2,1)} %copy-done.6, bf16[576,2048]{1,0:T(8,128)(2,1)} %add_convert_fusion.y_ref, f32[8,64,2048]{2,1,0:T(8,128)} %collective-permute-done.3.rest_0_), custom_call_target="tpu_custom_call" | custom-call | flops 1207959552 | bytes 8388608 | tf_op jit(solution)/shard_map/weight_half/pallas_call | solution.py:517
  278.9 31.4 %collective-permute-done.2 = f32[576,1024]{1,0:T(8,128)} collective-permute-done((f32[576,1024]{1,0:T(8,128)}, f32[576,1024]{1,0:T(8,128)}, u32[]{:S(2)}, u32[]{:S(2)}) %collective-permute-start.2) | collective-permute-done | bytes 2359328 | tf_op jit(solution)/shard_map/ppermute | solution.py:786
  310.3 6.1 multiply_reduce_fusion
  316.4 2.1 fusion.28
  321.2 21.5 %attention_draw.1 = (bf16[72,64,640]{2,1,0:T(8,128)(2,1)}, bf16[72,64,640]{2,1,0:T(8,128)(2,1)}, f32[576,512]{1,0:T(8,128)}, f32[576,512]{1,0:T(8,128)}, bf16[576,512]{1,0:T(8,128)(2,1)}) custom-call(bf16[8,576,640]{2,1,0:T(8,128)(2,1)} %get-tuple-element.151.p_ref, bf16[576,512]{1,0:T(8,128)(2,1)} %convolution_convert_fusion.up_ref, ...), custom_call_target="tpu_custom_call" | custom-call | flops 20000000000 | bytes 25000000 | tf_op jit(solution)/shard_map/attention_draw/pallas_call | solution.py:372
  345.0 6.0 many_half.6
  352.5 43.1 %attention_scatter.4.refs_0_ = bf16[36,64,384]{2,1,0:T(8,128)(2,1)} custom-call(bf16[72,64,640]{2,1,0:T(8,128)(2,1)} %get-tuple-element.160.d_ref, s32[3,576,640]{2,1,0:T(8,128)} %get-tuple-element.153.b_ref, bf16[4,256,128]{2,1,0:T(8,128)(2,1)} %fusion.20.merge_ref), custom_call_target="tpu_custom_call" | custom-call | flops 35000000512 | bytes 6000000 | tf_op jit(solution)/shard_map/attention_scatter/pallas_call | solution.py:411
  395.7 4.0 add_bitcast_fusion
  399.6 3.2 fusion.16
  402.8 6.8 many_half.7
  409.6 2.6 collective-permute-start.9
  412.2 43.1 %attention_scatter.5.refs_1_ = bf16[36,64,384]{2,1,0:T(8,128)(2,1)} custom-call(bf16[72,64,640]{2,1,0:T(8,128)(2,1)} %get-tuple-element.160.d_ref, s32[3,576,640]{2,1,0:T(8,128)} %get-tuple-element.153.b_ref, bf16[4,256,128]{2,1,0:T(8,128)(2,1)} %fusion.20.merge_ref), custom_call_target="tpu_custom_call" | custom-call | flops 35000000512 | bytes 6000000 | tf_op jit(solution)/shard_map/attention_scatter/pallas_call | solution.py:411
  455.3 5.5 attention_close.2
  466.0 2.2 convolution_add_fusion
  469.6 6.2 many_half.8
  475.9 2.3 add_bitcast_fusion.4
  478.7 43.4 %attention_scatter.6.refs_0_ = bf16[36,64,384]{2,1,0:T(8,128)(2,1)} custom-call(bf16[72,64,640]{2,1,0:T(8,128)(2,1)} %get-tuple-element.187.d_ref, s32[3,576,640]{2,1,0:T(8,128)} %get-tuple-element.175.b_ref, bf16[4,256,128]{2,1,0:T(8,128)(2,1)} %fusion.20.merge_ref), custom_call_target="tpu_custom_call" | custom-call | flops 35000000512 | bytes 6000000 | tf_op jit(solution)/shard_map/attention_scatter/pallas_call | solution.py:411
  525.0 2.3 fusion.18
  527.3 8.8 %collective-permute-done.18 = f32[64,2048]{1,0:T(8,128)S(1)} collective-permute-done((f32[64,2048]{1,0:T(8,128)}, f32[64,2048]{1,0:T(8,128)S(1)}, u32[]{:S(2)}, u32[]{:S(2)}) %collective-permute-start.18) | collective-permute-done | bytes 524320 | tf_op jit(solution)/shard_map/ppermute | solution.py:602
  537.0 7.1 many_half.9
  547.3 43.1 %attention_scatter.7.refs_1_ = bf16[36,64,384]{2,1,0:T(8,128)(2,1)} custom-call(bf16[72,64,640]{2,1,0:T(8,128)(2,1)} %get-tuple-element.187.d_ref, s32[3,576,640]{2,1,0:T(8,128)} %get-tuple-element.175.b_ref, bf16[4,256,128]{2,1,0:T(8,128)(2,1)} %fusion.20.merge_ref), custom_call_target="tpu_custom_call" | custom-call | flops 35000000512 | bytes 6000000 | tf_op jit(solution)/shard_map/attention_scatter/pallas_call | solution.py:411
  597.5 5.5 attention_close.3
  602.9 2.2 convert_element_type.56.mine_ref.refs_1_
  605.1 6.1 many_half.10
  611.7 2.9 convert_element_type.57
  616.8 2.6 collective-permute-start.28
  619.4 7.1 many_half.11
  627.8 3.0 fusion.14
  630.8 4.5 add.387.early_ref
  637.0 2.6 collective-permute-start.33
  642.1 19.2 %collective-permute-done.21 = f32[2,64,896]{2,1,0:T(8,128)S(1)} collective-permute-done((f32[2,64,896]{2,1,0:T(8,128)S(1)}, f32[2,64,896]{2,1,0:T(8,128)S(1)}, u32[]{:S(2)}, u32[]{:S(2)}) %collective-permute-start.21) | collective-permute-done | bytes 458784 | tf_op jit(solution)/shard_map/ppermute | solution.py:602
  669.5 9.3 %collective-permute-done.29 = f32[4,64,512]{2,1,0:T(8,128)S(1)} collective-permute-done((f32[4,64,512]{2,1,0:T(8,128)S(1)}, f32[4,64,512]{2,1,0:T(8,128)S(1)}, u32[]{:S(2)}, u32[]{:S(2)}) %collective-permute-start.29) | collective-permute-done | bytes 524320 | tf_op jit(solution)/shard_map/ppermute | solution.py:602
  679.6 13.6 %collective-permute-done.26 = f32[2,64,896]{2,1,0:T(8,128)S(1)} collective-permute-done((f32[2,64,896]{2,1,0:T(8,128)S(1)}, f32[2,64,896]{2,1,0:T(8,128)S(1)}, u32[]{:S(2)}, u32[]{:S(2)}) %collective-permute-start.26) | collective-permute-done | bytes 458784 | tf_op jit(solution)/shard_map/ppermute | solution.py:602
  695.2 10.7 %join.1 = bf16[561,1024]{1,0:T(8,128)(2,1)} custom-call(f32[576,1024]{1,0:T(8,128)} %get-tuple-element.245.base_ref, f32[576,1024]{1,0:T(8,128)} %add.387.early_ref, bf16[576,512]{1,0:T(8,128)(2,1)} %convert_element_type.56.mine_ref.refs_1_, bf16[1024,512]{1,0:T(8,128)(2,1)} %w_ref.1, f32[576,512]{1,0:T(8,128)} %copy-done.39, ...), custom_call_target="tpu_custom_call" | custom-call | flops 3000000000 | bytes 12000000 | tf_op jit(solution)/shard_map/join/pallas_call | solution.py:696
  (204 shorter events, 75.0 us)
Async XLA Ops:
  0.6 83.4 %copy-start = (bf16[512,1024]{1,0:T(8,128)(2,1)S(1)}, bf16[512,1024]{1,0:T(8,128)(2,1)}, u32[]{:S(2)}) copy-start(bf16[512,1024]{1,0:T(8,128)(2,1)} %param.31) | copy-start | bytes 3145732
  84.0 56.2 %copy-start.11 = (bf16[561,1024]{1,0:T(8,128)(2,1)S(1)}, bf16[561,1024]{1,0:T(8,128)(2,1)}, u32[]{:S(2)}) copy-start(bf16[561,1024]{1,0:T(8,128)(2,1)} %x_ref.1) | copy-start | bytes 3446788
  86.0 54.3 %collective-permute-start = (f32[576,1024]{1,0:T(8,128)S(1)}, f32[576,1024]{1,0:T(8,128)S(1)}, u32[]{:S(2)}, u32[]{:S(2)}) collective-permute-start(f32[576,1024]{1,0:T(8,128)S(1)} %fusion.32), channel_id=1, source_target_pairs={{0,1},{1,0},{2,3},{3,2},{4,5},{5,4},{6,7},{7,6},{8,9},{9,8},{10,11... | collective-permute-start | bytes 7077896 | tf_op jit(solution)/shard_map/ppermute | solution.py:681
  140.6 74.1 %copy-start.2 = (f32[576,1024]{1,0:T(8,128)}, f32[576,1024]{1,0:T(8,128)S(1)}, u32[]{:S(2)}) copy-start(f32[576,1024]{1,0:T(8,128)S(1)} %get-tuple-element.253) | copy-start | bytes 7077892
  143.7 14.3 %copy-start.37 = (bf16[2048,1024]{1,0:T(8,128)(2,1)S(1)}, bf16[2048,1024]{1,0:T(8,128)(2,1)}, u32[]{:S(2)}) copy-start(bf16[2048,1024]{1,0:T(8,128)(2,1)} %param.38) | copy-start | bytes 12582916
  162.0 52.7 %collective-permute-start.1 = (f32[576,1024]{1,0:T(8,128)}, f32[576,1024]{1,0:T(8,128)}, u32[]{:S(2)}, u32[]{:S(2)}) collective-permute-start(f32[576,1024]{1,0:T(8,128)} %fusion.33), channel_id=1, source_target_pairs={{0,1},{1,0},{2,3},{3,2},{4,5},{5,4},{6,7},{7,6},{8,9},{9,8},{10,11... | collective-permute-start | bytes 7077896 | tf_op jit(solution)/shard_map/ppermute | solution.py:681
  163.8 54.1 %copy-start.33 = (s32[2]{0:T(128)}, s32[2]{0:T(128)S(1)}, u32[]{:S(2)}) copy-start(s32[2]{0:T(128)S(1)} %pad_add_fusion.1.pick_ref) | copy-start | bytes 28
  163.9 54.0 %copy-start.29 = (s32[2]{0:T(128)}, s32[2]{0:T(128)S(1)}, u32[]{:S(2)}) copy-start(s32[2]{0:T(128)S(1)} %pad_add_fusion.pick_ref) | copy-start | bytes 28
  163.9 54.0 %copy-start.34 = (s32[2]{0:T(128)}, s32[2]{0:T(128)S(1)}, u32[]{:S(2)}) copy-start(s32[2]{0:T(128)S(1)} %constant_dynamic-update-slice_fusion.2.pick_ref) | copy-start | bytes 28
  163.9 54.0 %copy-start.30 = (s32[2]{0:T(128)}, s32[2]{0:T(128)S(1)}, u32[]{:S(2)}) copy-start(s32[2]{0:T(128)S(1)} %constant_dynamic-update-slice_fusion.3.pick_ref) | copy-start | bytes 28
  230.8 30.6 %collective-permute-start.5 = (f32[8,64,2048]{2,1,0:T(8,128)}, f32[8,64,2048]{2,1,0:T(8,128)}, u32[]{:S(2)}, u32[]{:S(2)}) collective-permute-start(f32[8,64,2048]{2,1,0:T(8,128)} %weight_half.6), channel_id=1, source_target_pairs={{0,2},{2,0},{4,6},{6,4},{8,10},{10,8},{12,14},{14,12},{16,18},{18,... | collective-permute-start | bytes 12582920 | tf_op jit(solution)/shard_map/ppermute | solution.py:602
  249.2 21.8 %collective-permute-start.3 = (f32[8,64,2048]{2,1,0:T(8,128)}, f32[8,64,2048]{2,1,0:T(8,128)}, u32[]{:S(2)}, u32[]{:S(2)}) collective-permute-start(f32[8,64,2048]{2,1,0:T(8,128)} %weight_half.4), channel_id=1, source_target_pairs={{0,2},{2,0},{4,6},{6,4},{8,10},{10,8},{12,14},{14,12},{16,18},{18,... | collective-permute-start | bytes 12582920 | tf_op jit(solution)/shard_map/ppermute | solution.py:602
  256.7 53.6 %collective-permute-start.2 = (f32[576,1024]{1,0:T(8,128)}, f32[576,1024]{1,0:T(8,128)}, u32[]{:S(2)}, u32[]{:S(2)}) collective-permute-start(f32[576,1024]{1,0:T(8,128)} %fusion.34), channel_id=1, source_target_pairs={{0,1},{1,0},{2,3},{3,2},{4,5},{5,4},{6,7},{7,6},{8,9},{9,8},{10,11... | collective-permute-start | bytes 7077896 | tf_op jit(solution)/shard_map/ppermute | solution.py:786
  269.4 126.3 %collective-permute-start.6 = (f32[4,64,2048]{2,1,0:T(8,128)}, f32[4,64,2048]{2,1,0:T(8,128)}, u32[]{:S(2)}, u32[]{:S(2)}) collective-permute-start(f32[4,64,2048]{2,1,0:T(8,128)} %get-tuple-element.158), channel_id=1, source_target_pairs={{0,8},{2,10},{4,12},{6,14},{8,0},{10,2},{12,4},{14,6},{16,24},{18,... | collective-permute-start | bytes 6291464 | tf_op jit(solution)/shard_map/ppermute | solution.py:602
  351.0 51.8 %collective-permute-start.4 = (f32[8,64,1152]{2,1,0:T(8,128)}, f32[8,64,1152]{2,1,0:T(8,128)}, u32[]{:S(2)}, u32[]{:S(2)}) collective-permute-start(f32[8,64,1152]{2,1,0:T(8,128)} %many_half.6), channel_id=1, source_target_pairs={{0,2},{2,0},{4,6},{6,4},{8,10},{10,8},{12,14},{14,12},{16,18},{18,... | collective-permute-start | bytes 7077896 | tf_op jit(solution)/shard_map/ppermute | solution.py:602
  351.0 48.6 %collective-permute-start.7 = (f32[4,64,2048]{2,1,0:T(8,128)}, f32[4,64,2048]{2,1,0:T(8,128)}, u32[]{:S(2)}, u32[]{:S(2)}) collective-permute-start(f32[4,64,2048]{2,1,0:T(8,128)} %get-tuple-element.163), channel_id=1, source_target_pairs={{0,4},{2,6},{4,0},{6,2},{8,12},{10,14},{12,8},{14,10},{16,20},{18,... | collective-permute-start | bytes 6291464 | tf_op jit(solution)/shard_map/ppermute | solution.py:602
  409.6 66.2 %collective-permute-start.9 = (f32[2,64,2048]{2,1,0:T(8,128)}, f32[2,64,2048]{2,1,0:T(8,128)}, u32[]{:S(2)}, u32[]{:S(2)}) collective-permute-start(f32[2,64,2048]{2,1,0:T(8,128)} %get-tuple-element.173), channel_id=1, source_target_pairs={{0,16},{2,18},{4,20},{6,22},{8,24},{10,26},{12,28},{14,30},{16,0},... | collective-permute-start | bytes 3145736 | tf_op jit(solution)/shard_map/ppermute | solution.py:602
  462.2 62.8 %collective-permute-start.13 = (f32[4,64,1152]{2,1,0:T(8,128)}, f32[4,64,1152]{2,1,0:T(8,128)}, u32[]{:S(2)}, u32[]{:S(2)}) collective-permute-start(f32[4,64,1152]{2,1,0:T(8,128)} %get-tuple-element.185), channel_id=1, source_target_pairs={{0,4},{2,6},{4,0},{6,2},{8,12},{10,14},{12,8},{14,10},{16,20},{18,... | collective-permute-start | bytes 3538952 | tf_op jit(solution)/shard_map/ppermute | solution.py:602
  463.6 58.6 %collective-permute-start.12 = (f32[2,64,2048]{2,1,0:T(8,128)}, f32[2,64,2048]{2,1,0:T(8,128)}, u32[]{:S(2)}, u32[]{:S(2)}) collective-permute-start(f32[2,64,2048]{2,1,0:T(8,128)} %get-tuple-element.183), channel_id=1, source_target_pairs={{0,8},{2,10},{4,12},{6,14},{8,0},{10,2},{12,4},{14,6},{16,24},{18,... | collective-permute-start | bytes 3145736 | tf_op jit(solution)/shard_map/ppermute | solution.py:602
  468.2 162.7 %collective-permute-start.8 = (f32[576,1024]{1,0:T(8,128)}, f32[576,1024]{1,0:T(8,128)}, u32[]{:S(2)}, u32[]{:S(2)}) collective-permute-start(f32[576,1024]{1,0:T(8,128)} %convolution_add_fusion), channel_id=1, source_target_pairs={{0,1},{1,0},{2,3},{3,2},{4,5},{5,4},{6,7},{7,6},{8,9},{9,8},{10,11... | collective-permute-start | bytes 7077896 | tf_op jit(solution)/shard_map/ppermute | solution.py:681
  478.2 58.9 %collective-permute-start.10 = (f32[8,64,896]{2,1,0:T(8,128)}, f32[8,64,896]{2,1,0:T(8,128)}, u32[]{:S(2)}, u32[]{:S(2)}) collective-permute-start(f32[8,64,896]{2,1,0:T(8,128)} %get-tuple-element.176), channel_id=1, source_target_pairs={{0,2},{2,0},{4,6},{6,4},{8,10},{10,8},{12,14},{14,12},{16,18},{18,... | collective-permute-start | bytes 5505032 | tf_op jit(solution)/shard_map/ppermute | solution.py:602
  478.2 58.9 %collective-permute-start.11 = (f32[8,64,512]{2,1,0:T(8,128)}, f32[8,64,512]{2,1,0:T(8,128)}, u32[]{:S(2)}, u32[]{:S(2)}) collective-permute-start(f32[8,64,512]{2,1,0:T(8,128)} %get-tuple-element.177), channel_id=1, source_target_pairs={{0,2},{2,0},{4,6},{6,4},{8,10},{10,8},{12,14},{14,12},{16,18},{18,... | collective-permute-start | bytes 3145736 | tf_op jit(solution)/shard_map/ppermute | solution.py:602
  478.7 44.2 %copy-start.13 = (f32[2,64,2048]{2,1,0:T(8,128)S(1)}, f32[2,64,2048]{2,1,0:T(8,128)}, u32[]{:S(2)}) copy-start(f32[2,64,2048]{2,1,0:T(8,128)} %get-tuple-element.182) | copy-start | bytes 3145732
  522.1 14.0 %collective-permute-start.18 = (f32[64,2048]{1,0:T(8,128)}, f32[64,2048]{1,0:T(8,128)S(1)}, u32[]{:S(2)}, u32[]{:S(2)}) collective-permute-start(f32[64,2048]{1,0:T(8,128)} %get-tuple-element.197), channel_id=1, source_target_pairs={{0,4},{2,6},{4,0},{6,2},{8,12},{10,14},{12,8},{14,10},{16,20},{18,... | collective-permute-start | bytes 1572872 | tf_op jit(solution)/shard_map/ppermute | solution.py:602
  544.2 46.3 %collective-permute-start.17 = (f32[64,2048]{1,0:T(8,128)}, f32[64,2048]{1,0:T(8,128)}, u32[]{:S(2)}, u32[]{:S(2)}) collective-permute-start(f32[64,2048]{1,0:T(8,128)} %get-tuple-element.195), channel_id=1, source_target_pairs={{0,16},{2,18},{4,20},{6,22},{8,24},{10,26},{12,28},{14,30},{16,0},... | collective-permute-start | bytes 1572872 | tf_op jit(solution)/shard_map/ppermute | solution.py:602
  544.5 49.9 %collective-permute-start.16 = (f32[2,64,1152]{2,1,0:T(8,128)}, f32[2,64,1152]{2,1,0:T(8,128)}, u32[]{:S(2)}, u32[]{:S(2)}) collective-permute-start(f32[2,64,1152]{2,1,0:T(8,128)} %get-tuple-element.193), channel_id=1, source_target_pairs={{0,8},{2,10},{4,12},{6,14},{8,0},{10,2},{12,4},{14,6},{16,24},{18,... | collective-permute-start | bytes 1769480 | tf_op jit(solution)/shard_map/ppermute | solution.py:602
  544.9 47.5 %collective-permute-start.15 = (f32[4,64,512]{2,1,0:T(8,128)}, f32[4,64,512]{2,1,0:T(8,128)}, u32[]{:S(2)}, u32[]{:S(2)}) collective-permute-start(f32[4,64,512]{2,1,0:T(8,128)} %get-tuple-element.191), channel_id=1, source_target_pairs={{0,4},{2,6},{4,0},{6,2},{8,12},{10,14},{12,8},{14,10},{16,20},{18,... | collective-permute-start | bytes 1572872 | tf_op jit(solution)/shard_map/ppermute | solution.py:602
  545.7 50.5 %collective-permute-start.14 = (f32[4,64,896]{2,1,0:T(8,128)}, f32[4,64,896]{2,1,0:T(8,128)}, u32[]{:S(2)}, u32[]{:S(2)}) collective-permute-start(f32[4,64,896]{2,1,0:T(8,128)} %get-tuple-element.189), channel_id=1, source_target_pairs={{0,8},{2,10},{4,12},{6,14},{8,0},{10,2},{12,4},{14,6},{16,24},{18,... | collective-permute-start | bytes 2752520 | tf_op jit(solution)/shard_map/ppermute | solution.py:602
  611.2 8.2 %collective-permute-start.23 = (f32[8,64,896]{2,1,0:T(8,128)}, f32[8,64,896]{2,1,0:T(8,128)}, u32[]{:S(2)}, u32[]{:S(2)}) collective-permute-start(f32[8,64,896]{2,1,0:T(8,128)} %get-tuple-element.205), channel_id=1, source_target_pairs={{0,2},{2,0},{4,6},{6,4},{8,10},{10,8},{12,14},{14,12},{16,18},{18,... | collective-permute-start | bytes 5505032 | tf_op jit(solution)/shard_map/ppermute | solution.py:602
  611.2 5.6 collective-permute-start.24
  614.6 79.5 %collective-permute-start.20 = (f32[1024,512]{1,0:T(8,128)}, f32[1024,512]{1,0:T(8,128)}, u32[]{:S(2)}, u32[]{:S(2)}) collective-permute-start(f32[1024,512]{1,0:T(8,128)} %convert_element_type.57), channel_id=1, source_target_pairs={{0,1},{1,0},{2,3},{3,2},{4,5},{5,4},{6,7},{7,6},{8,9},{9,8},{10,11... | collective-permute-start | bytes 6291464 | tf_op jit(solution)/shard_map/ppermute | solution.py:758
  615.1 20.8 %collective-permute-start.32 = (f32[2,64,512]{2,1,0:T(8,128)}, f32[2,64,512]{2,1,0:T(8,128)S(1)}, u32[]{:S(2)}, u32[]{:S(2)}) collective-permute-start(f32[2,64,512]{2,1,0:T(8,128)} %get-tuple-element.214), channel_id=1, source_target_pairs={{0,8},{2,10},{4,12},{6,14},{8,0},{10,2},{12,4},{14,6},{16,24},{18,... | collective-permute-start | bytes 786440 | tf_op jit(solution)/shard_map/ppermute | solution.py:602
  616.8 19.5 %collective-permute-start.28 = (f32[64,1152]{1,0:T(8,128)}, f32[64,1152]{1,0:T(8,128)S(1)}, u32[]{:S(2)}, u32[]{:S(2)}) collective-permute-start(f32[64,1152]{1,0:T(8,128)} %get-tuple-element.210), channel_id=1, source_target_pairs={{0,16},{2,18},{4,20},{6,22},{8,24},{10,26},{12,28},{14,30},{16,0},... | collective-permute-start | bytes 884744 | tf_op jit(solution)/shard_map/ppermute | solution.py:602
  626.6 38.1 %collective-permute-start.25 = (f32[4,64,896]{2,1,0:T(8,128)}, f32[4,64,896]{2,1,0:T(8,128)S(1)}, u32[]{:S(2)}, u32[]{:S(2)}) collective-permute-start(f32[4,64,896]{2,1,0:T(8,128)} %get-tuple-element.208), channel_id=1, source_target_pairs={{0,4},{2,6},{4,0},{6,2},{8,12},{10,14},{12,8},{14,10},{16,20},{18,... | collective-permute-start | bytes 2752520 | tf_op jit(solution)/shard_map/ppermute | solution.py:602
  635.3 28.7 %copy-start.40 = (f32[4,64,512]{2,1,0:T(8,128)S(1)}, f32[4,64,512]{2,1,0:T(8,128)}, u32[]{:S(2)}) copy-start(f32[4,64,512]{2,1,0:T(8,128)} %get-tuple-element.212) | copy-start | bytes 1572868
  635.3 29.4 %copy-start.21 = (f32[4,64,896]{2,1,0:T(8,128)S(1)}, f32[4,64,896]{2,1,0:T(8,128)}, u32[]{:S(2)}) copy-start(f32[4,64,896]{2,1,0:T(8,128)} %get-tuple-element.207) | copy-start | bytes 2752516
  635.3 58.7 %collective-permute-start.19 = (f32[576,512]{1,0:T(8,128)S(1)}, f32[576,512]{1,0:T(8,128)S(1)}, u32[]{:S(2)}, u32[]{:S(2)}) collective-permute-start(f32[576,512]{1,0:T(8,128)S(1)} %copy-done.17), channel_id=1, source_target_pairs={{0,1},{1,0},{2,3},{3,2},{4,5},{5,4},{6,7},{7,6},{8,9},{9,8},{10,11... | collective-permute-start | bytes 3538952 | tf_op jit(solution)/shard_map/ppermute | solution.py:855
  635.9 25.4 %collective-permute-start.21 = (f32[2,64,896]{2,1,0:T(8,128)S(1)}, f32[2,64,896]{2,1,0:T(8,128)S(1)}, u32[]{:S(2)}, u32[]{:S(2)}) collective-permute-start(f32[2,64,896]{2,1,0:T(8,128)S(1)} %get-tuple-element.203), channel_id=1, source_target_pairs={{0,16},{2,18},{4,20},{6,22},{8,24},{10,26},{12,28},{14,30},{16,0},... | collective-permute-start | bytes 1376264 | tf_op jit(solution)/shard_map/ppermute | solution.py:602
  637.0 27.0 %collective-permute-start.33 = (f32[64,512]{1,0:T(8,128)S(1)}, f32[64,512]{1,0:T(8,128)S(1)}, u32[]{:S(2)}, u32[]{:S(2)}) collective-permute-start(f32[64,512]{1,0:T(8,128)S(1)} %add_bitcast_fusion.12), channel_id=1, source_target_pairs={{0,16},{2,18},{4,20},{6,22},{8,24},{10,26},{12,28},{14,30},{16,0},... | collective-permute-start | bytes 393224 | tf_op jit(solution)/shard_map/ppermute | solution.py:602
  640.6 38.2 %copy-start.23 = (f32[4,64,512]{2,1,0:T(8,128)S(1)}, f32[4,64,512]{2,1,0:T(8,128)}, u32[]{:S(2)}) copy-start(f32[4,64,512]{2,1,0:T(8,128)} %get-tuple-element.211) | copy-start | bytes 1572868
  661.3 7.5 %collective-permute-start.22 = (f32[64,896]{1,0:T(8,128)S(1)}, f32[64,896]{1,0:T(8,128)S(1)}, u32[]{:S(2)}, u32[]{:S(2)}) collective-permute-start(f32[64,896]{1,0:T(8,128)S(1)} %add_bitcast_fusion.11), channel_id=1, source_target_pairs={{0,4},{2,6},{4,0},{6,2},{8,12},{10,14},{12,8},{14,10},{16,20},{18,... | collective-permute-start | bytes 688136 | tf_op jit(solution)/shard_map/ppermute | solution.py:602
  664.0 14.8 %collective-permute-start.29 = (f32[4,64,512]{2,1,0:T(8,128)S(1)}, f32[4,64,512]{2,1,0:T(8,128)S(1)}, u32[]{:S(2)}, u32[]{:S(2)}) collective-permute-start(f32[4,64,512]{2,1,0:T(8,128)S(1)} %copy-done.40), channel_id=1, source_target_pairs={{0,8},{2,10},{4,12},{6,14},{8,0},{10,2},{12,4},{14,6},{16,24},{18,... | collective-permute-start | bytes 1572872 | tf_op jit(solution)/shard_map/ppermute | solution.py:602
  664.8 28.5 %collective-permute-start.26 = (f32[2,64,896]{2,1,0:T(8,128)S(1)}, f32[2,64,896]{2,1,0:T(8,128)S(1)}, u32[]{:S(2)}, u32[]{:S(2)}) collective-permute-start(f32[2,64,896]{2,1,0:T(8,128)S(1)} %fusion.21), channel_id=1, source_target_pairs={{0,8},{2,10},{4,12},{6,14},{8,0},{10,2},{12,4},{14,6},{16,24},{18,... | collective-permute-start | bytes 1376264 | tf_op jit(solution)/shard_map/ppermute | solution.py:602
  679.6 26.3 %collective-permute-start.30 = (f32[2,64,512]{2,1,0:T(8,128)}, f32[2,64,512]{2,1,0:T(8,128)}, u32[]{:S(2)}, u32[]{:S(2)}) collective-permute-start(f32[2,64,512]{2,1,0:T(8,128)} %get-tuple-element.269), channel_id=1, source_target_pairs={{0,16},{2,18},{4,20},{6,22},{8,24},{10,26},{12,28},{14,30},{16,0},... | collective-permute-start | bytes 786440 | tf_op jit(solution)/shard_map/ppermute | solution.py:602
  694.1 13.6 %collective-permute-start.27 = (f32[64,896]{1,0:T(8,128)}, f32[64,896]{1,0:T(8,128)}, u32[]{:S(2)}, u32[]{:S(2)}) collective-permute-start(f32[64,896]{1,0:T(8,128)} %fusion.24), channel_id=1, source_target_pairs={{0,16},{2,18},{4,20},{6,22},{8,24},{10,26},{12,28},{14,30},{16,0},... | collective-permute-start | bytes 688136 | tf_op jit(solution)/shard_map/ppermute | solution.py:602
  695.2 19.5 %copy-start.1 = (bf16[512,1024]{1,0:T(8,128)(2,1)S(1)}, bf16[512,1024]{1,0:T(8,128)(2,1)}, u32[]{:S(2)}) copy-start(bf16[512,1024]{1,0:T(8,128)(2,1)} %param.31) | copy-start | bytes 3145732
  706.8 5.0 collective-permute-start.31
  708.8 5.3 collective-permute-start.34
  (28 other events, 108.8 us)

commit v3 on v2

--- a/solution.py
+++ b/solution.py
@@ -53,92 +53,116 @@
     return high.astype(f32), low.astype(f32)
 
 
-def forward_kernel(
-    used_ref, q_ref, k_ref, v_ref, pk_ref, pq_ref, b_ref,
-    p_ref, ctx_ref, bp_ref, bt_ref,
-    near_tab, far_tab, near_inv, far_inv, far_sum, near_sum, score, *, span, rows, cols, pairs, scale,
+def fill_tables(src_ref, first, tall, pos_ref, tab, inv, p):
+    half = lane_half((64, 128))
+    cut = slice(p * 128, (p + 1) * 128)
+
+    def body(step, carry):
+        at = pl.ds(pl.multiple_of(step * 64, 64), 64)
+        block = src_ref[pl.ds(pl.multiple_of(first + step * 64, 64), 64), cut]
+        zero = jnp.zeros_like(block)
+        first_head = nt(jnp.where(half, block, zero), pos_ref[:, cut]).astype(bf16).astype(f32)
+        second_head = nt(jnp.where(half, zero, block), pos_ref[:, cut]).astype(bf16).astype(f32)
+        top0 = jnp.maximum(jnp.max(jnp.abs(first_head), axis=1, keepdims=True), 1e-30)
+        top1 = jnp.maximum(jnp.max(jnp.abs(second_head), axis=1, keepdims=True), 1e-30)
+        whole0 = jnp.round(first_head * (LIMIT / top0)).astype(jnp.int32)
+        whole1 = jnp.round(second_head * (LIMIT / top1)).astype(jnp.int32)
+        tab[p, at, :] = whole0 * 65536 + whole1
+        inv[2 * p, at, :] = jnp.broadcast_to(top0 * (1.0 / LIMIT), (64, 128))
+        inv[2 * p + 1, at, :] = jnp.broadcast_to(top1 * (1.0 / LIMIT), (64, 128))
+        return carry
+
+    lax.fori_loop(0, tall // 64, body, 0)
+
+
+def look_up(tab, index_ref, at, store, *, pairs, cols):
+    for c in range(cols // 128):
+        total = [None] * pairs
+        for r in range(3):
+            index = index_ref[r, at, c * 128:(c + 1) * 128]
+            for p in range(pairs):
+                got = lane_gather(tab[p, at, r * 128:(r + 1) * 128], index)
+                total[p] = got if total[p] is None else total[p] + got
+        for p in range(pairs):
+            store(p, c, total[p])
+
+
+def prepare_rows(
+    k_ref, pq_ref, b_ref, head_ref, rest_ref, bt_ref, far_head, far_rest, inv_ref,
+    far_tab, far_inv, *, span, rows, cols, pairs, split,
 ):
+    edge = span - span % 8 - split
     for r in range(3):
-        bp_ref[r, span - span % 8:rows, :] = jnp.zeros((rows - span + span % 8, cols), jnp.int32)
-        bp_ref[r, :, span - span % 128:cols] = jnp.zeros((rows, cols - span + span % 128), jnp.int32)
-        bp_ref[r, 0:span, 0:span] = b_ref[0, r]
+        head_ref[r, :, span - span % 128:cols] = jnp.zeros((split, cols - span + span % 128), jnp.int32)
+        rest_ref[r, edge:rows - split, :] = jnp.zeros((rows - split - edge, cols), jnp.int32)
+        rest_ref[r, :, span - span % 128:cols] = jnp.zeros((rows - split, cols - span + span % 128), jnp.int32)
+        head_ref[r, :, 0:span] = b_ref[0, r, 0:split]
+        rest_ref[r, 0:span - split, 0:span] = b_ref[0, r, split:span]
     for r in range(3):
         for jb in range(cols // 128):
             high = min(128, rows - jb * 128)
             for ib in range(cols // 128):
                 tall = min(128, rows - ib * 128)
-                block = bp_ref[r, ib * 128:ib * 128 + tall, jb * 128:(jb + 1) * 128]
+                here = slice(jb * 128, (jb + 1) * 128)
+                if ib * 128 < split:
+                    block = head_ref[r, ib * 128:ib * 128 + tall, here]
+                else:
+                    block = rest_ref[r, ib * 128 - split:ib * 128 - split + tall, here]
                 if tall < 128:
                     block = jnp.concatenate([block, jnp.zeros((128 - tall, 128), jnp.int32)], axis=0)
                 bt_ref[r, jb * 128:jb * 128 + high, ib * 128:(ib + 1) * 128] = block.T[:high]
-
-    half = lane_half((64, 128))
-
-    def make_tables(src_ref, pos_ref, tab, inv, p):
-        cut = slice(p * 128, (p + 1) * 128)
-
-        def body(step, carry):
-            at = pl.ds(pl.multiple_of(step * 64, 64), 64)
-            block = src_ref[at, cut]
-            zero = jnp.zeros_like(block)
-            first = nt(jnp.where(half, block, zero), pos_ref[:, cut]).astype(bf16).astype(f32)
-            second = nt(jnp.where(half, zero, block), pos_ref[:, cut]).astype(bf16).astype(f32)
-            top0 = jnp.maximum(jnp.max(jnp.abs(first), axis=1, keepdims=True), 1e-30)
-            top1 = jnp.maximum(jnp.max(jnp.abs(second), axis=1, keepdims=True), 1e-30)
-            whole0 = jnp.round(first * (LIMIT / top0)).astype(jnp.int32)
-            whole1 = jnp.round(second * (LIMIT / top1)).astype(jnp.int32)
-            tab[p, at, :] = whole0 * 65536 + whole1
-            inv[2 * p, at, :] = jnp.broadcast_to(top0 * (1.0 / LIMIT), (64, 128))
-            inv[2 * p + 1, at, :] = jnp.broadcast_to(top1 * (1.0 / LIMIT), (64, 128))
-            return carry
-
-        lax.fori_loop(0, rows // 64, body, 0)
-
     for p in range(pairs):
-        make_tables(q_ref, pk_ref, near_tab, near_inv, p)
-        make_tables(k_ref, pq_ref, far_tab, far_inv, p)
-
-    def look_up(tab, index_ref, at, out, out_at):
-        for c in range(cols // 128):
-            total = [None] * pairs
-            for r in range(3):
-                index = index_ref[r, at, c * 128:(c + 1) * 128]
-                for p in range(pairs):
-                    got = lane_gather(tab[p, at, r * 128:(r + 1) * 128], index)
-                    total[p] = got if total[p] is None else total[p] + got
-            for p in range(pairs):
-                out[p, out_at, c * 128:(c + 1) * 128] = total[p]
+        fill_tables(k_ref, 0, rows, pq_ref, far_tab, far_inv, p)
 
     def far_body(step, carry):
         at = pl.ds(pl.multiple_of(step * 8, 8), 8)
-        look_up(far_tab, bt_ref, at, far_sum, at)
+
+        def store(p, c, total):
+            if c * 128 < split:
+                far_head[p, at, c * 128:(c + 1) * 128] = total
+            else:
+                far_rest[p, at, c * 128 - split:(c + 1) * 128 - split] = total
+
+        look_up(far_tab, bt_ref, at, store, pairs=pairs, cols=cols)
         return carry
 
     lax.fori_loop(0, rows // 8, far_body, 0)
     for p in range(pairs):
-        far_sum[p, rows:, :] = jnp.zeros((cols - rows, cols), jnp.int32)
-
+        far_head[p, rows:, :] = jnp.zeros((cols - rows, split), jnp.int32)
+        far_rest[p, rows:, :] = jnp.zeros((cols - rows, cols - split), jnp.int32)
+    for h in range(2 * pairs):
+        inv_ref[h:h + 1, :] = jnp.concatenate(
+            [far_inv[h, j * 128:min(rows, (j + 1) * 128), :].T[0:1] for j in range(cols // 128 - 1)]
+            + [jnp.concatenate([far_inv[h, cols - 128:rows, :],
+                                jnp.zeros((cols - rows, 128), f32)], axis=0).T[0:1]], axis=1)
+
+
+def forward_rows(
+    used_ref, q_ref, k_ref, v_ref, pk_ref, b_ref, far_sum, inv_ref, p_ref, ctx_ref,
+    near_tab, near_inv, near_sum, score, *, first, rows, span, cols, pairs, scale,
+):
+    for p in range(pairs):
+        fill_tables(q_ref, first, rows, pk_ref, near_tab, near_inv, p)
     used = used_ref[0]
     place = lax.broadcasted_iota(jnp.int32, (1, cols), 1)
     valid = ((place >= TEXT) & (place < span)) | (place < used)
-    inv_rows = []
-    for h in range(2 * pairs):
-        inv_rows.append(jnp.concatenate(
-            [far_inv[h, j * 128:min(rows, (j + 1) * 128), :].T[0:1] for j in range(cols // 128 - 1)]
-            + [jnp.concatenate([far_inv[h, cols - 128:rows, :],
-                                jnp.zeros((cols - rows, 128), f32)], axis=0).T[0:1]], axis=1))
 
     def block_body(start, tall):
         def near_body(step, carry):
             at = pl.ds(pl.multiple_of(start + step * 8, 8), 8)
-            look_up(near_tab, bp_ref, at, near_sum, pl.ds(pl.multiple_of(step * 8, 8), 8))
+            out_at = pl.ds(pl.multiple_of(step * 8, 8), 8)
+
+            def store(p, c, total):
+                near_sum[p, out_at, c * 128:(c + 1) * 128] = total
+
+            look_up(near_tab, b_ref, at, store, pairs=pairs, cols=cols)
             return carry
 
         lax.fori_loop(0, tall // 8, near_body, 0)
         at = pl.ds(start, tall)
         for p in range(pairs):
             cut = slice(p * 128, (p + 1) * 128)
-            block = q_ref[at, cut]
+            block = q_ref[pl.ds(pl.multiple_of(first + start, 64), tall), cut]
             zero = jnp.zeros_like(block)
             mask = lane_half((tall, 128))
             score[0, 0:tall, :] = nt(jnp.where(mask, block, zero), k_ref[:, cut])
@@ -149,10 +173,10 @@
                 f0, f1 = unpack_pair(turned)
                 n0, n1 = unpack_pair(near_sum[p, 0:tall, here])
                 score[0, 0:tall, here] += (
-                    f0 * inv_rows[2 * p][:, here] + n0 * near_inv[2 * p, at, :]
+                    f0 * inv_ref[2 * p:2 * p + 1, here] + n0 * near_inv[2 * p, at, :]
                 )
                 score[1, 0:tall, here] += (
-                    f1 * inv_rows[2 * p + 1][:, here] + n1 * near_inv[2 * p + 1, at, :]
+                    f1 * inv_ref[2 * p + 1:2 * p + 2, here] + n1 * near_inv[2 * p + 1, at, :]
                 )
             for h in range(2):
                 for s in range(tall // 16):
@@ -220,12 +244,12 @@
 
 
 def draw_kernel(
-    p_ref, up_ref, q_ref, k_ref, v_ref,
-    d_ref, dt_ref, dq_ref, dk_ref, dv_ref, wide, flat, turned, *, rows, cols, scale,
+    p_ref, up_ref, q_ref, k_ref, v_ref, *refs, first, tall, rows, cols, scale, adds,
 ):
+    extra = refs[:adds]
+    d_ref, dt_ref, dq_ref, dk_ref, dv_ref, wide, flat, turned = refs[adds:]
+    lanes = turned.shape[2]
     half = lane_half((64, 128))
-    rows_half = lane_half((rows, 128))
-    cols_half = lane_half((cols, 128))
 
     def body(step, carry):
         at = pl.ds(pl.multiple_of(step * 64, 64), 64)
@@ -241,29 +265,36 @@
         d_ref[pl.ds(pl.multiple_of(step * 8, 8), 8), :, :] = jnp.concatenate(pair, axis=1).astype(bf16)
         return carry
 
-    lax.fori_loop(0, rows // 64, body, 0)
+    lax.fori_loop(0, tall // 64, body, 0)
     for jb in range(cols // 128):
-        tall = min(128, rows - jb * 128)
-        for ib in range(cols // 128):
-            wide_rows = min(128, rows - ib * 128)
+        high = min(128, rows - jb * 128)
+        for ib in range(lanes // 128):
+            wide_rows = min(128, tall - ib * 128)
             pair = []
             for h in range(2):
                 block = wide[h, ib * 128:ib * 128 + wide_rows, jb * 128:(jb + 1) * 128]
                 if wide_rows < 128:
                     block = jnp.concatenate([block, jnp.zeros((128 - wide_rows, 128), f32)], axis=0)
-                other = block.T[:tall]
-                turned[h, jb * 128:jb * 128 + tall, ib * 128:(ib + 1) * 128] = other.astype(bf16)
-                pair.append(other.reshape(tall // 8, 8, 128))
-            dt_ref[jb * 16:jb * 16 + tall // 8, :, ib * 128:(ib + 1) * 128] = jnp.concatenate(
+                other = block.T[:high]
+                turned[h, jb * 128:jb * 128 + high, ib * 128:(ib + 1) * 128] = other.astype(bf16)
+                pair.append(other.reshape(high // 8, 8, 128))
+            dt_ref[jb * 16:jb * 16 + high // 8, :, ib * 128:(ib + 1) * 128] = jnp.concatenate(
                 pair, axis=1
             ).astype(bf16)
-    dq_ref[...] = nn(flat[0], pick(cols_half, k_ref[...], 0)) + nn(flat[1], pick(cols_half, k_ref[...], 1))
-    dk_ref[...] = nn(turned[0], pick(cols_half, q_ref[...], 0)) + nn(turned[1], pick(cols_half, q_ref[...], 1))
-    dv = tn(p_ref[0], pick(rows_half, up_ref[...], 0)) + tn(p_ref[1], pick(rows_half, up_ref[...], 1))
-    dv_ref[...] = dv[:rows].astype(bf16)
-
-
-def scatter_kernel(d_ref, b_ref, merge_ref, out_ref, *, groups, cols):
+    keys, queries, ups = k_ref[...], q_ref[first:first + lanes, :], up_ref[...]
+    cols_half, lanes_half, tall_half = (lane_half((n, 128)) for n in (cols, lanes, tall))
+    dq_ref[...] = nn(flat[0], pick(cols_half, keys, 0)) + nn(flat[1], pick(cols_half, keys, 1))
+    dk = nn(turned[0], pick(lanes_half, queries, 0)) + nn(turned[1], pick(lanes_half, queries, 1))
+    dv = tn(p_ref[0], pick(tall_half, ups, 0)) + tn(p_ref[1], pick(tall_half, ups, 1))
+    dv = dv[:rows]
+    if adds:
+        dk, dv = dk + extra[0][...], dv + extra[1][...]
+    dk_ref[...] = dk
+    dv_ref[...] = dv.astype(dv_ref.dtype)
+
+
+def scatter_kernel(*refs, groups, cols):
+    *d_refs, b_ref, merge_ref, out_ref = refs
     base = jnp.where(lax.broadcasted_iota(jnp.int32, (16, cols), 0) >= 8, 1.0, 0.0).astype(bf16)
     own = (lax.broadcasted_iota(jnp.int32, (256, 256), 0) % 8) == (
         lax.broadcasted_iota(jnp.int32, (256, 256), 1) % 8
@@ -272,7 +303,7 @@
     one = jnp.asarray(1.0, bf16)
 
     def body(g, carry):
-        back = d_ref[g]
+        back = jnp.concatenate([d_ref[g] for d_ref in d_refs], axis=1) if len(d_refs) > 1 else d_refs[0][g]
         for r in range(3):
             bucket = b_ref[r, pl.ds(pl.multiple_of(g * 8, 8), 8), :]
             low = (bucket & 31).astype(f32)
@@ -324,7 +355,16 @@
     return -(-span // 64) * 64, -(-span // 128) * 128
 
 
-def attention_forward(qkv, pos_key, pos_query, buckets, used, scale):
+def forward_scratch(pairs, tall, cols):
+    return [
+        pltpu.VMEM((pairs, tall, 3 * REL), jnp.int32),
+        pltpu.VMEM((2 * pairs, tall, 128), f32),
+        pltpu.VMEM((pairs, 128, cols), jnp.int32),
+        pltpu.VMEM((2, 128, cols), f32),
+    ]
+
+
+def attention_head(qkv, pos_key, pos_query, buckets, used, scale, split):
     span = buckets.shape[2]
     rows, cols = sizes(span)
     width = pos_key.shape[1]
@@ -332,108 +372,142 @@
     whole = pl.BlockSpec(memory_space=pltpu.VMEM)
     i32 = jnp.int32
 
-    def kernel(used_ref, qkv_ref, *rest):
-        forward_kernel(
-            used_ref, qkv_ref.at[:, 0:width], qkv_ref.at[:, width:2 * width],
-            qkv_ref.at[:, 2 * width:3 * width], *rest,
-            span=span, rows=rows, cols=cols, pairs=pairs, scale=scale,
+    def kernel(
+        used_ref, qkv_ref, pk_ref, pq_ref, b_ref, p_ref, ctx_ref, head_ref, rest_ref, bt_ref, far_rest, inv_ref,
+        far_tab, far_inv, far_head, *scratch,
+    ):
+        k_ref = qkv_ref.at[:, width:2 * width]
+        prepare_rows(
+            k_ref, pq_ref, b_ref, head_ref, rest_ref, bt_ref, far_head, far_rest, inv_ref, far_tab, far_inv,
+            span=span, rows=rows, cols=cols, pairs=pairs, split=split,
+        )
+        forward_rows(
+            used_ref, qkv_ref.at[:, 0:width], k_ref, qkv_ref.at[:, 2 * width:3 * width], pk_ref, head_ref,
+            far_head, inv_ref, p_ref, ctx_ref, *scratch,
+            first=0, rows=split, span=span, cols=cols, pairs=pairs, scale=scale,
         )
 
     return pl.pallas_call(
         kernel,
         out_shape=(
-            jax.ShapeDtypeStruct((2 * pairs, rows, cols), bf16),
-            jax.ShapeDtypeStruct((rows, width), bf16),
+            jax.ShapeDtypeStruct((2 * pairs, split, cols), bf16),
+            jax.ShapeDtypeStruct((split, width), bf16),
+            jax.ShapeDtypeStruct((3, split, cols), i32),
+            jax.ShapeDtypeStruct((3, rows - split, cols), i32),
             jax.ShapeDtypeStruct((3, rows, cols), i32),
-            jax.ShapeDtypeStruct((3, rows, cols), i32),
+            jax.ShapeDtypeStruct((pairs, cols, cols - split), i32),
+            jax.ShapeDtypeStruct((2 * pairs, cols), f32),
         ),
         in_specs=[pl.BlockSpec(memory_space=pltpu.SMEM)] + [whole] * 4,
-        out_specs=(whole,) * 4,
+        out_specs=(whole,) * 7,
         scratch_shapes=[
             pltpu.VMEM((pairs, rows, 3 * REL), i32),
-            pltpu.VMEM((pairs, rows, 3 * REL), i32),
             pltpu.VMEM((2 * pairs, rows, 128), f32),
-            pltpu.VMEM((2 * pairs, rows, 128), f32),
-            pltpu.VMEM((pairs, cols, cols), i32),
-            pltpu.VMEM((pairs, 128, cols), i32),
-            pltpu.VMEM((2, 128, cols), f32),
-        ],
+            pltpu.VMEM((pairs, cols, split), i32),
+        ] + forward_scratch(pairs, split, cols),
         compiler_params=pltpu.CompilerParams(vmem_limit_bytes=VMEM_CAP),
-        cost_estimate=pl.CostEstimate(flops=60000000000, bytes_accessed=25000000, transcendentals=0),
-        name="attention_forward",
+        cost_estimate=pl.CostEstimate(flops=4 * 10**10, bytes_accessed=25000000, transcendentals=0),
+        name="attention_head",
     )(used, qkv, pos_key, pos_query, buckets)
 
 
-def attention_draw(share, upstream, qkv, scale):
-    heads, rows, cols = share.shape
+def attention_rest(qkv, pos_key, bucket_rest, far_rest, inverse, used, scale, split, span):
+    rows, cols = sizes(span)
+    width = pos_key.shape[1]
+    pairs = width // 128
+    whole = pl.BlockSpec(memory_space=pltpu.VMEM)
+
+    def kernel(used_ref, qkv_ref, pk_ref, b_ref, far_ref, inv_ref, p_ref, ctx_ref, *scratch):
+        forward_rows(
+            used_ref, qkv_ref.at[:, 0:width], qkv_ref.at[:, width:2 * width], qkv_ref.at[:, 2 * width:3 * width],
+            pk_ref, b_ref, far_ref, inv_ref, p_ref, ctx_ref, *scratch,
+            first=split, rows=rows - split, span=span, cols=cols, pairs=pairs, scale=scale,
+        )
+
+    return pl.pallas_call(
+        kernel,
+        out_shape=(
+            jax.ShapeDtypeStruct((2 * pairs, rows - split, cols), bf16),
+            jax.ShapeDtypeStruct((rows - split, width), bf16),
+        ),
+        in_specs=[pl.BlockSpec(memory_space=pltpu.SMEM)] + [whole] * 5,
+        out_specs=(whole,) * 2,
+        scratch_shapes=forward_scratch(pairs, rows - split, cols),
+        compiler_params=pltpu.CompilerParams(vmem_limit_bytes=VMEM_CAP),
+        cost_estimate=pl.CostEstimate(flops=2 * 10**10, bytes_accessed=12000000, transcendentals=0),
+        name="attention_rest",
+    )(used, qkv, pos_key, bucket_rest, far_rest, inverse)
+
+
+def attention_draw(share, upstream, qkv, scale, first, rows, adds=()):
+    heads, tall, cols = share.shape
     width = upstream.shape[1]
     pairs = heads // 2
-    groups = rows // 8
+    lanes = -(-tall // 128) * 128
+
+    def column(n):
+        return pl.BlockSpec((n, 128), lambda p: (0, p))
+
     return pl.pallas_call(
-        functools.partial(draw_kernel, rows=rows, cols=cols, scale=scale),
+        functools.partial(draw_kernel, first=first, tall=tall, rows=rows, cols=cols, scale=scale, adds=len(adds)),
         grid=(pairs,),
         in_specs=[
-            pl.BlockSpec((2, rows, cols), lambda p: (p, 0, 0)),
-            pl.BlockSpec((rows, 128), lambda p: (0, p)),
+            pl.BlockSpec((2, tall, cols), lambda p: (p, 0, 0)),
+            column(tall),
             pl.BlockSpec((cols, 128), lambda p: (0, p)),
             pl.BlockSpec((cols, 128), lambda p: (0, p + pairs)),
             pl.BlockSpec((cols, 128), lambda p: (0, p + 2 * pairs)),
-        ],
+        ] + [column(rows)] * len(adds),
         out_specs=(
-            pl.BlockSpec((groups, 16, cols), lambda p: (0, p, 0)),
-            pl.BlockSpec((groups, 16, cols), lambda p: (0, p, 0)),
-            pl.BlockSpec((rows, 128), lambda p: (0, p)),
-            pl.BlockSpec((rows, 128), lambda p: (0, p)),
-            pl.BlockSpec((rows, 128), lambda p: (0, p)),
+            pl.BlockSpec((tall // 8, 16, cols), lambda p: (0, p, 0)),
+            pl.BlockSpec((rows // 8, 16, lanes), lambda p: (0, p, 0)),
+            column(tall), column(rows), column(rows),
         ),
         out_shape=(
-            jax.ShapeDtypeStruct((groups, 8 * heads, cols), bf16),
-            jax.ShapeDtypeStruct((groups, 8 * heads, cols), bf16),
+            jax.ShapeDtypeStruct((tall // 8, 8 * heads, cols), bf16),
+            jax.ShapeDtypeStruct((rows // 8, 8 * heads, lanes), bf16),
+            jax.ShapeDtypeStruct((tall, width), f32),
             jax.ShapeDtypeStruct((rows, width), f32),
-            jax.ShapeDtypeStruct((rows, width), f32),
-            jax.ShapeDtypeStruct((rows, width), bf16),
+            jax.ShapeDtypeStruct((rows, width), bf16 if adds else f32),
         ),
         scratch_shapes=[
-            pltpu.VMEM((2, rows, cols), f32),
-            pltpu.VMEM((2, rows, cols), bf16),
-            pltpu.VMEM((2, rows, cols), bf16),
+            pltpu.VMEM((2, tall, cols), f32),
+            pltpu.VMEM((2, tall, cols), bf16),
+            pltpu.VMEM((2, rows, lanes), bf16),
         ],
         compiler_params=pltpu.CompilerParams(vmem_limit_bytes=VMEM_CAP),
-        cost_estimate=pl.CostEstimate(flops=20000000000, bytes_accessed=25000000, transcendentals=0),
+        cost_estimate=pl.CostEstimate(flops=10**10, bytes_accessed=12000000, transcendentals=0),
         name="attention_draw",
-    )(share, upstream, qkv, qkv, qkv)
-
-
-def attention_scatter(back, buckets, merge, part, count):
-    groups, high, cols = back.shape
+    )(share, upstream, qkv, qkv, qkv, *adds)
+
+
+def attention_scatter(backs, buckets, merge, part, count):
+    groups, high, _ = backs[0].shape
+    cols = buckets.shape[2]
     groups = groups // count
     whole = pl.BlockSpec(memory_space=pltpu.VMEM)
     return pl.pallas_call(
         functools.partial(scatter_kernel, groups=groups, cols=cols),
         grid=(1,),
         out_shape=jax.ShapeDtypeStruct((groups, high, 3 * REL), bf16),
-        in_specs=[
-            pl.BlockSpec((groups, high, cols), lambda g: (part, 0, 0)),
+        in_specs=[pl.BlockSpec((groups, high, b.shape[2]), lambda g: (part, 0, 0)) for b in backs] + [
             pl.BlockSpec((3, groups * 8, cols), lambda g: (0, part, 0)),
             whole,
         ],
         out_specs=pl.BlockSpec((groups, high, 3 * REL), lambda g: (0, 0, 0)),
         compiler_params=pltpu.CompilerParams(vmem_limit_bytes=VMEM_CAP),
-        cost_estimate=pl.CostEstimate(flops=7 * 10**10 // count, bytes_accessed=12 * 10**6 // count, transcendentals=0),
+        cost_estimate=pl.CostEstimate(flops=10**9 * groups, bytes_accessed=2 * 10**5 * groups, transcendentals=0),
         name="attention_scatter",
-    )(back, buckets, merge)
+    )(*backs, buckets, merge)
 
 
 def attention_close(sums, base, pos, qkv, side):
     rows, width = base.shape
     pairs = width // 128
-    groups = rows // 8
     return pl.pallas_call(
         functools.partial(close_kernel, rows=rows, count=len(sums)),
         grid=(pairs,),
-        in_specs=[
-            pl.BlockSpec((groups // len(sums), 16, 3 * REL), lambda p: (0, p, 0))
-        ] * len(sums) + [
+        in_specs=[pl.BlockSpec((part.shape[0], 16, 3 * REL), lambda p: (0, p, 0)) for part in sums] + [
             pl.BlockSpec((rows, 128), lambda p: (0, p)),
             pl.BlockSpec((3 * REL, 128), lambda p: (0, p)),
             pl.BlockSpec((qkv.shape[0], 128), lambda p: (0, p + side * pairs)),
@@ -476,24 +550,29 @@
     return listed
 
 
-def weight_kernel(pick_ref, x_ref, y_ref, *rest, rows, blocks, deep, keeps, bit):
+def weight_kernel(pick_ref, *refs, count, blocks, deep, keeps, bit):
+    xs, ys, rest = refs[:count], refs[count:2 * count], refs[2 * count:]
     add_ref = rest[0] if keeps else None
     outs = rest[1:3] if keeps else rest[0:1]
-    turned = rest[-1]
+    turned = rest[-count:]
 
     @pl.when(pl.program_id(0) == 0)
     def _():
-        fill_turned(x_ref, turned, rows)
+        for x_ref, wide in zip(xs, turned):
+            fill_turned(x_ref, wide, x_ref.shape[0])
 
     for out, place, d in each_block(pick_ref, blocks, keeps, bit, 1):
         at = pl.ds(pl.multiple_of((2 * d + pick_ref[0]) * deep, deep), deep)
-        part = nn(turned[at, :], y_ref[...])
-        outs[out][place] = part + add_ref[d] if keeps else part
-
-
-def weight_half(pick, x, y, add=None, *, parts, bits, tile=512):
-    rows, depth = x.shape
-    wide = y.shape[1]
+        part = add_ref[d] if keeps else None
+        for wide, y_ref in zip(turned, ys):
+            term = nn(wide[at, :], y_ref[...])
+            part = term if part is None else part + term
+        outs[out][place] = part
+
+
+def weight_half(pick, xs, ys, add=None, *, parts, bits, tile=512):
+    depth = xs[0].shape[1]
+    wide = ys[0].shape[1]
     deep = depth // parts
     blocks = parts // 2
     keeps = add is not None
@@ -501,12 +580,10 @@
     def tiled(n):
         return pl.BlockSpec((n, deep, tile), lambda c: (0, 0, c))
 
-    ins = [
-        pl.BlockSpec(memory_space=pltpu.SMEM),
-        pl.BlockSpec((rows, depth), lambda c: (0, 0)),
-        pl.BlockSpec((rows, tile), lambda c: (0, c)),
-    ]
-    args = [pick, x, y]
+    ins = [pl.BlockSpec(memory_space=pltpu.SMEM)]
+    ins += [pl.BlockSpec(x.shape, lambda c: (0, 0)) for x in xs]
+    ins += [pl.BlockSpec((y.shape[0], tile), lambda c: (0, c)) for y in ys]
+    args = [pick, *xs, *ys]
     shape = (jax.ShapeDtypeStruct((blocks, deep, wide), f32),)
     specs = (tiled(blocks),)
     if keeps:
@@ -514,13 +591,14 @@
         args += add
         shape = (jax.ShapeDtypeStruct((blocks // 2, deep, wide), f32),) * 2
         specs = (tiled(blocks // 2),) * 2
+    rows = sum(x.shape[0] for x in xs)
     return pl.pallas_call(
-        functools.partial(weight_kernel, rows=rows, blocks=blocks, deep=deep, keeps=keeps, bit=bits[0]),
+        functools.partial(weight_kernel, count=len(xs), blocks=blocks, deep=deep, keeps=keeps, bit=bits[0]),
         grid=(wide // tile,),
         in_specs=ins,
         out_specs=specs,
         out_shape=shape,
-        scratch_shapes=[pltpu.VMEM((depth, rows), bf16)],
+        scratch_shapes=[pltpu.VMEM((depth, x.shape[0]), bf16) for x in xs],
         compiler_params=pltpu.CompilerParams(vmem_limit_bytes=VMEM_CAP),
         cost_estimate=pl.CostEstimate(
             flops=rows * depth * wide, bytes_accessed=4 * depth * wide, transcendentals=0
@@ -677,31 +755,71 @@
     return values
 
 
-def across(value):
-    return value + lax.ppermute(value, "mp", [(0, 1), (1, 0)])
-
-
-def join_kernel(base_ref, early_ref, mine_ref, w_ref, other_ref, ow_ref, out_ref, *, span):
+def swap(value):
+    return lax.ppermute(value.astype(f32), "mp", [(0, 1), (1, 0)])
+
+
+def join_kernel(head_ref, rest_ref, early_ref, early_other_ref, mine_ref, w_ref, other_ref, ow_ref, out_ref, *, span):
     weight = ow_ref[...].astype(bf16)
+    split = head_ref.shape[0]
     for start in range(0, span, 64):
         tall = min(64, span - start)
         at = slice(start, start + 64)
-        total = base_ref[at, :] + early_ref[at, :] + nt(mine_ref[at, :], w_ref[...])
+        base = head_ref[at, :] if start < split else rest_ref[start - split:start - split + 64, :]
+        total = base + early_ref[at, :] + early_other_ref[at, :] + nt(mine_ref[at, :], w_ref[...])
         total = total + nt(other_ref[at, :].astype(bf16), weight)
         out_ref[start:start + tall, :] = total.astype(bf16)[:tall]
 
 
-def join(base, early, mine, weight, other, other_weight, span):
+def join(bases, early, early_other, mine, weight, other, other_weight, span):
     whole = pl.BlockSpec(memory_space=pltpu.VMEM)
     return pl.pallas_call(
         functools.partial(join_kernel, span=span),
-        in_specs=[whole] * 6,
+        in_specs=[whole] * 8,
         out_specs=whole,
-        out_shape=jax.ShapeDtypeStruct((span, base.shape[1]), bf16),
+        out_shape=jax.ShapeDtypeStruct((span, early.shape[1]), bf16),
         compiler_params=pltpu.CompilerParams(vmem_limit_bytes=VMEM_CAP),
         cost_estimate=pl.CostEstimate(flops=3 * 10**9, bytes_accessed=12 * 10**6, transcendentals=0),
         name="join",
-    )(base, early, mine, weight, other, other_weight)
+    )(*bases, early, early_other, mine, weight, other, other_weight)
+
+
+def attend_kernel(
+    t_ref, c_ref, o_ref, w_ref, ow_ref, gain_ref, shift_ref, first_ref, low_ref, normal_ref, inverse_ref,
+):
+    weight = ow_ref[...].astype(bf16)
+
+    def body(step, carry):
+        at = pl.ds(pl.multiple_of(step * 64, 64), 64)
+        summed = t_ref[at, :].astype(f32) + nn(c_ref[at, :], w_ref[...])
+        summed = summed + nn(o_ref[at, :].astype(bf16), weight)
+        first, normal, inverse = norm_forward(summed, gain_ref[...], shift_ref[...])
+        first_ref[at, :] = first
+        low_ref[at, :] = first.astype(bf16)
+        normal_ref[at, :] = normal
+        inverse_ref[at, :] = inverse
+        return carry
+
+    lax.fori_loop(0, t_ref.shape[0] // 64, body, 0)
+
+
+def attend(tokens, context, other, weight, other_weight, gain, shift):
+    tall, depth = tokens.shape
+    whole = pl.BlockSpec(memory_space=pltpu.VMEM)
+    return pl.pallas_call(
+        attend_kernel,
+        in_specs=[whole] * 7,
+        out_specs=(whole,) * 4,
+        out_shape=(
+            jax.ShapeDtypeStruct((tall, depth), f32),
+            jax.ShapeDtypeStruct((tall, depth), bf16),
+            jax.ShapeDtypeStruct((tall, depth), f32),
+            jax.ShapeDtypeStruct((tall, 1), f32),
+        ),
+        compiler_params=pltpu.CompilerParams(vmem_limit_bytes=VMEM_CAP),
+        cost_estimate=pl.CostEstimate(flops=2 * 10**9, bytes_accessed=8 * 10**6, transcendentals=0),
+        name="attend",
+    )(tokens, context, other, weight, other_weight, gain[None], shift[None])
 
 
 def norm_forward(summed, gain, shift):
@@ -755,56 +873,98 @@
     def chain(make, *orders):
         return Halving(make, index, size, list(orders))
 
-    other_key_weight = lax.ppermute(key_weight.astype(f32), "mp", [(0, 1), (1, 0)])
+    split = rows // 2 // 128 * 128
+    other_output = swap(output_weight)
     qkv, pos_key, pos_query = project(
         tokens, query_weight, key_weight, value_weight, position_tables, key_position, query_position, span
     )
     tokens = jnp.pad(tokens, spare)
     cotangent = jnp.pad(cotangent, spare)
-    share, context, bucket_rows, bucket_cols = attention_forward(
-        qkv, pos_key, pos_query, buckets, text_length, score_scale
-    )
-    attended = across(nn(context, output_weight))
-    first, normal_one, inverse_one = norm_forward(
-        tokens.astype(f32) + attended, gain_one, shift_one
-    )
-    first_low = first.astype(bf16)
-    upward = nn(first_low, up_weight)
-    hidden = jax.nn.gelu(upward, approximate=False).astype(bf16)
-    feed = across(nn(hidden, down_weight))
-    final, normal_two, inverse_two = norm_forward(first + feed, gain_two, shift_two)
-    layer_output = final[:span].astype(bf16)
-    second_back, gain_two_grad, shift_two_grad = norm_backward(
-        cotangent.astype(f32), normal_two, inverse_two, gain_two
-    )
-    second_low = second_back.astype(bf16)
-    hidden_back = nt(second_low, down_weight)
-    gelu_back = jax.vjp(lambda inner_value: jax.nn.gelu(inner_value, approximate=False), upward)[1]
-    upward_back = gelu_back(hidden_back)[0].astype(bf16)
-
-    back_part = nt(upward_back, up_weight)
-    back_other = lax.ppermute(back_part, "mp", [(0, 1), (1, 0)])
+    edges = [(0, split), (split, rows)]
+
+    share_head, context_head, bucket_head, bucket_rest, bucket_cols, far_rest, far_inverse = attention_head(
+        qkv, pos_key, pos_query, buckets, text_length, score_scale, split
+    )
+    other_head = swap(context_head)
+    far_rest, other_output = lax.optimization_barrier((far_rest, other_output))
+    share_rest, context_rest = attention_rest(
+        qkv, pos_key, bucket_rest, far_rest, far_inverse, text_length, score_scale, split, span
+    )
+    other_rest = swap(context_rest)
+    shares = [share_head, share_rest]
+    contexts = [context_head, context_rest]
+    contexts_other = [other_head, other_rest]
+
+    def gelu(value):
+        return jax.nn.gelu(value, approximate=False)
+
+    firsts, firsts_low, normals_one, inverses_one, upwards, hiddens, feeds, feeds_other = ([] for _ in range(8))
+    for (low, high), context, other in zip(edges, contexts, contexts_other):
+        first, first_low, normal_one, inverse_one = attend(
+            tokens[low:high], context, other, output_weight, other_output, gain_one, shift_one
+        )
+        firsts.append(first)
+        normals_one.append(normal_one)
+        inverses_one.append(inverse_one)
+        firsts_low.append(first_low)
+        upwards.append(nn(firsts_low[-1], up_weight))
+        hiddens.append(gelu(upwards[-1]).astype(bf16))
+        feeds.append(nn(hiddens[-1], down_weight))
+        feeds_other.append(swap(feeds[-1]))
+
+    finals, seconds_back, seconds_low, upwards_back, backs_part, backs_other, two_sums = ([] for _ in range(7))
+    for n, (low, high) in enumerate(edges):
+        final, normal_two, inverse_two = norm_forward(
+            firsts[n] + feeds[n] + feeds_other[n], gain_two, shift_two
+        )
+        finals.append(final.astype(bf16))
+        second_back, *sums = norm_backward(
+            cotangent[low:high].astype(f32), normal_two, inverse_two, gain_two
+        )
+        two_sums.append(sums)
+        seconds_back.append(second_back)
+        seconds_low.append(second_back.astype(bf16))
+        hidden_back = nt(seconds_low[n], down_weight)
+        upwards_back.append(jax.vjp(gelu, upwards[n])[1](hidden_back)[0].astype(bf16))
+        backs_part.append(nt(upwards_back[n], up_weight))
+        backs_other.append(swap(backs_part[n]))
+    layer_output = jnp.concatenate(finals, axis=0)[:span]
+    gain_two_grad, shift_two_grad = (two_sums[0][n] + two_sums[1][n] for n in range(2))
+
+    backs_part, down_pair, up_pair = lax.optimization_barrier(
+        (backs_part, (seconds_low, hiddens), (firsts_low, upwards_back))
+    )
     down_chain = chain(
-        lambda pick, add: weight_half(pick, second_low, hidden, add, parts=size, bits=high_first), high_first
+        lambda pick, add: weight_half(pick, *down_pair, add, parts=size, bits=high_first), high_first
     )
     up_chain = chain(
-        lambda pick, add: weight_half(pick, first_low, upward_back, add, parts=size, bits=low_first), low_first
+        lambda pick, add: weight_half(pick, *up_pair, add, parts=size, bits=low_first), low_first
     )
     down_chain.step()
     up_chain.step()
     down_chain.step()
-    back_other = tie(back_other, up_chain)
-    first_back = second_back + back_part + back_other
-    residual_back, gain_one_grad, shift_one_grad = norm_backward(
-        first_back, normal_one, inverse_one, gain_one
-    )
-    residual_low = residual_back.astype(bf16)
-    context_back = nt(residual_low, output_weight).astype(bf16)
+    backs_other[1] = tie(backs_other[1], up_chain)
+    residuals_back, residuals_low, contexts_back, one_sums = ([] for _ in range(4))
+    for n in range(2):
+        residual_back, *sums = norm_backward(
+            seconds_back[n] + backs_part[n] + backs_other[n], normals_one[n], inverses_one[n], gain_one
+        )
+        one_sums.append(sums)
+        residuals_back.append(residual_back)
+        residuals_low.append(residual_back.astype(bf16))
+        contexts_back.append(nt(residuals_low[n], output_weight).astype(bf16))
+    gain_one_grad, shift_one_grad = (one_sums[0][n] + one_sums[1][n] for n in range(2))
 
     merge = merge_table()
-    back, back_turned, query_base, key_base, value_back = attention_draw(
-        share, context_back, qkv, score_scale
-    )
+    back_head, turned_head, query_head, key_head, value_head = attention_draw(
+        shares[0], contexts_back[0], qkv, score_scale, 0, rows
+    )
+    back_rest, turned_rest, query_rest, key_base, value_back = attention_draw(
+        shares[1], contexts_back[1], qkv, score_scale, split, rows, (key_head, value_head)
+    )
+    query_base = jnp.concatenate([query_head, query_rest], axis=0)
+    residual_low = jnp.concatenate(residuals_low, axis=0)
+    context = jnp.concatenate(contexts, axis=0)
     nothing = jnp.zeros_like(gain_one)
     gains = jnp.stack(
         [gain_one_grad, shift_one_grad, gain_two_grad, shift_two_grad] + [nothing] * 4
@@ -836,29 +996,30 @@
         )
 
     near = []
-    near.append(attention_scatter(back, bucket_rows, merge, 0, 2))
-    back, near = tie((back, near), outer_chain, down_chain)
-    near.append(attention_scatter(back, bucket_rows, merge, 1, 2))
-    near, back_turned = tie((near, back_turned), up_chain)
+    near.append(attention_scatter([back_head], bucket_head, merge, 0, 1))
+    back_rest, near, key_wide = tie((back_rest, near, key_weight.astype(f32)), outer_chain, down_chain)
+    other_key_weight = swap(key_wide)
+    near.append(attention_scatter([back_rest], bucket_rest, merge, 0, 1))
+    near, backs, other_key_weight = tie((near, [turned_head, turned_rest], other_key_weight), up_chain)
     query_back, key_table_sum = attention_close(near, query_base, pos_key, qkv, 0)
     query_low = query_back.astype(bf16)
-    early_part = nt(query_low, query_weight) + nt(value_back, value_weight)
-    early = across(early_part)
+    early = nt(query_low, query_weight) + nt(value_back, value_weight)
+    early_other = swap(early)
     near_chain = tail(query_low, key_table_sum, key_position, [high_first, low_first])
-    back_turned = tie(back_turned, near_chain, down_chain)
+    backs = tie(backs, near_chain, down_chain)
     far = []
-    far.append(attention_scatter(back_turned, bucket_cols, merge, 0, 2))
-    back_turned, far = tie((back_turned, far), near_chain, up_chain, outer_chain)
-    far.append(attention_scatter(back_turned, bucket_cols, merge, 1, 2))
+    far.append(attention_scatter(backs, bucket_cols, merge, 0, 2))
+    backs, far, early_other = tie((backs, far, early_other), near_chain, up_chain, outer_chain)
+    far.append(attention_scatter(backs, bucket_cols, merge, 1, 2))
     far = tie(far, near_chain, outer_chain, up_chain, down_chain)
     key_back, query_table_sum = attention_close(far, key_base, pos_query, qkv, 1)
-    key_other = lax.ppermute(key_back, "mp", [(0, 1), (1, 0)])
+    key_other = swap(key_back)
     key_low = key_back.astype(bf16)
     far_chain = tail(key_low, query_table_sum, query_position, [low_first, high_first])
     far_chain.step()
     far_chain.step()
     input_gradient = join(
-        residual_back, early, key_low, key_weight, key_other, other_key_weight, span
+        residuals_back, early, early_other, key_low, key_weight, key_other, other_key_weight, span
     )
     (down_share,) = down_chain.finish()
     (up_share,) = up_chain.finish()

time: 724 us -> 645 us (0.89)
  waiting for transfers between devices: 191 us -> 82.8 us
  Pallas kernels: 364 us -> 389 us
    ppermute x6 -> x10, waiting for transfers between devices: 133 us -> 35 us  [swap(): return lax.ppermute(value.astype(f32), 'mp', [(0, 1), (1, 0)])]
    pallas_call x6 -> x10, Pallas kernels: 121 us -> 145 us  [the longest x1 49.8 us: attention_head(): pl.pallas_call(kernel, out_shape=(jax.ShapeDtypeStruct((2 * pairs, split,...]
    ppermute x28, waiting for transfers between devices: 57.6 us -> 47.8 us  [flipped(): return lax.ppermute(value, 'dp', [(i, i ^ 1 << bit) for i in range(size)])]
    dot_general x5 -> x8, matrix products: 22.2 us -> 18.5 us  [nt(): lax.dot_general(left, right, (((1,), (1,)), ((), ())), preferred_element_...]
    dot_general x3 -> x4, matrix products: 20.2 us -> 21 us  [nn(): return jnp.dot(left, right, preferred_element_type=f32)]
  transfers between devices with their start and end apart: 35 -> 39, of which waited for: 11 -> 12; matrix products, arithmetic and copies ran while one was open for 11% -> 15% of each run, Pallas kernels for 38% -> 54%
where the time goes in v3:
time: 645 us; the launch traced here: 635 us
  Pallas kernels  389 us (60%)
  waiting for transfers between devices  82.8 us (13%)
  other arithmetic  61 us (9%)
  starting transfers between devices  42.1 us (7%)
  matrix products  39.4 us (6%)
  local copies, waits for them, and re-layouts  18.1 us (3%)
    pallas_call x4, Pallas kernels, attention_scatter(): pl.pallas_call(functools.partial(scatter_kernel, groups=groups, cols=cols...  173 us
    pallas_call x1, Pallas kernels, attention_head(): pl.pallas_call(kernel, out_shape=(jax.ShapeDtypeStruct((2 * pairs, split,...  49.8 us
    ppermute x28, waiting for transfers between devices, flipped(): return lax.ppermute(value, 'dp', [(i, i ^ 1 << bit) for i in range(size)])  47.8 us
    pallas_call x6, Pallas kernels, many_half(): pl.pallas_call(functools.partial(many_kernel, plan=plan, widths=widths, t...  39.4 us
    ppermute x10, waiting for transfers between devices, swap(): return lax.ppermute(value.astype(f32), 'mp', [(0, 1), (1, 0)])  35 us
    pallas_call x4, Pallas kernels, weight_half(): pl.pallas_call(functools.partial(weight_kernel, count=len(xs), blocks=blo...  30.8 us
    ppermute x28, starting transfers between devices, flipped(): return lax.ppermute(value, 'dp', [(i, i ^ 1 << bit) for i in range(size)])  28.7 us
    pallas_call x1, Pallas kernels, attention_rest(): pl.pallas_call(kernel, out_shape=(jax.ShapeDtypeStruct((2 * pairs, rows -...  25.8 us
  transfers between devices with their start and end apart: 39, of which 12 were waited for; matrix products, arithmetic and copies ran while one was open for 15% of the time, Pallas kernels for 54%

profile of v3, /device:TPU:0, one launch (start us, length us, event | category | flops | bytes accessed | tf_op | source)
XLA Modules:
  0.0 635.1 jit_solution(2010363082133242443)
XLA Ops:
  0.6 2.8 convert_element_type.73
  3.4 3.0 collective-permute-start.1
  7.1 4.6 copy.47.b_ref
  11.6 9.3 %project.1 = (bf16[640,1536]{1,0:T(8,128)(2,1)}, bf16[384,512]{1,0:T(8,128)(2,1)}, bf16[384,512]{1,0:T(8,128)(2,1)}) custom-call(bf16[561,1024]{1,0:T(8,128)(2,1)} %x_ref.1, bf16[1024,512]{1,0:T(8,128)(2,1)} %wq_ref.1, bf16[1024,512]{1,0:T(8,128)(2,1)} %w_ref.5, bf16[1024,512]{1,0:T(8,128)(2,1)} %wv_ref.1, bf16[3,128,1024]{2,1,0:T(8,128)(2,1)} %t_ref.1, ...), custom_call_target="tpu_custom_call" | custom-call | flops 4000000000 | bytes 9000000 | tf_op jit(solution)/shard_map/project/pallas_call | solution.py:226
  21.0 49.8 %attention_head.1 = (bf16[8,256,640]{2,1,0:T(8,128)(2,1)}, bf16[256,512]{1,0:T(8,128)(2,1)}, s32[3,256,640]{2,1,0:T(8,128)}, s32[3,320,640]{2,1,0:T(8,128)}, s32...) custom-call(s32[1]{0:T(128)S(6)} %copy.84.used_ref, ...), custom_call_target="tpu_custom_call" | custom-call | flops 40000000000 | bytes 25000000 | tf_op jit(solution)/shard_map/attention_head/pallas_call | solution.py:390
  74.4 25.8 %attention_rest.1 = (bf16[8,320,640]{2,1,0:T(8,128)(2,1)}, bf16[320,512]{1,0:T(8,128)(2,1)}) custom-call(s32[1]{0:T(128)S(6)} %copy.84.used_ref, bf16[640,1536]{1,0:T(8,128)(2,1)} %get-tuple-element.180.qkv_ref.q_ref.k_ref.v_ref.refs_4_, bf16[384,512]{1,0:T(8,128)(2,1)} %get-tuple-element.181.pk_ref.refs_3_, ...), custom_call_target="tpu_custom_call" | custom-call | flops 20000000000 | bytes 12000000 | tf_op jit(solution)/shard_map/attention_rest/pallas_call | solution.py:427
  104.2 6.7 %attend.2 = (f32[256,1024]{1,0:T(8,128)}, bf16[256,1024]{1,0:T(8,128)(2,1)}, f32[256,1024]{1,0:T(8,128)}, f32[256,1]{1,0:T(8,128)}) custom-call(bf16[256,1024]{1,0:T(8,128)(2,1)} %slice.97.t_ref, bf16[256,512]{1,0:T(8,128)(2,1)} %get-tuple-element.183.c_ref, f32[256,512]{1,0:T(8,128)} %collective-permute-done.o_ref, bf16[512,1024]{1,0:T(8,128)(2,1)} %w_ref.4, ...), custom_call_target="tpu_custom_call" | custom-call | flops 2000000000 | bytes 8000000 | tf_op jit(solution)/shard_map/attend/pallas_call | solution.py:809
  111.0 8.9 %multiply_convert_fusion.1 = (bf16[256,2048]{1,0:T(8,128)(2,1)S(1)}, f32[256,2048]{1,0:T(8,128)}, f32[256,2048]{1,0:T(8,128)}) fusion(bf16[256,1024]{1,0:T(8,128)(2,1)} %get-tuple-element.199.refs_0_, bf16[1024,2048]{1,0:T(8,128)(2,1)} %param.37), kind=kOutput, calls=%fused_computation.20 | convolution fusion | flops 1107820544 | bytes 9961472 | tf_op jit(solution)/shard_map/dot_general | solution.py:39
  121.4 7.8 %attend.3 = (f32[320,1024]{1,0:T(8,128)}, bf16[320,1024]{1,0:T(8,128)(2,1)}, f32[320,1024]{1,0:T(8,128)}, f32[320,1]{1,0:T(8,128)}) custom-call(bf16[320,1024]{1,0:T(8,128)(2,1)} %pad_slice_fusion.1.t_ref, bf16[320,512]{1,0:T(8,128)(2,1)} %get-tuple-element.191.c_ref, f32[320,512]{1,0:T(8,128)} %collective-permute-done.3.o_ref, bf16[512,1024]{1,0:T(8,128)(2,1)} %w_ref.4, ...), custom_call_target="tpu_custom_call" | custom-call | flops 2000000000 | bytes 8000000 | tf_op jit(solution)/shard_map/attend/pallas_call | solution.py:809
  129.2 9.3 %multiply_convert_fusion = (bf16[320,2048]{1,0:T(8,128)(2,1)S(1)}, f32[320,2048]{1,0:T(8,128)S(1)}, f32[320,2048]{1,0:T(8,128)S(1)}) fusion(bf16[320,1024]{1,0:T(8,128)(2,1)} %get-tuple-element.200.refs_1_, bf16[1024,2048]{1,0:T(8,128)(2,1)} %param.37), kind=kOutput, calls=%fused_computation.4 | convolution fusion | flops 1384775680 | bytes 11403264 | tf_op jit(solution)/shard_map/dot_general | solution.py:39
  142.0 5.4 collective-permute-done.2
  156.4 17.0 %collective-permute-done.4 = f32[320,1024]{1,0:T(8,128)S(1)} collective-permute-done((f32[320,1024]{1,0:T(8,128)S(1)}, f32[320,1024]{1,0:T(8,128)S(1)}, u32[]{:S(2)}, u32[]{:S(2)}) %collective-permute-start.4) | collective-permute-done | bytes 1310752 | tf_op jit(solution)/shard_map/ppermute | solution.py:759
  178.7 2.6 fusion.48
  181.3 7.5 %weight_half.4 = f32[8,64,2048]{2,1,0:T(8,128)} custom-call(s32[2]{0:T(128)} %copy-done.43, bf16[256,1024]{1,0:T(8,128)(2,1)} %get-tuple-element.199.refs_0_, bf16[320,1024]{1,0:T(8,128)(2,1)} %get-tuple-element.200.refs_1_, bf16[256,2048]{1,0:T(8,128)(2,1)} %copy-done.16, bf16[320,2048]{1,0:T(8,128)(2,1)} %copy-done.9), custom_call_target="tpu_custom_call" | custom-call | flops 1207959552 | bytes 8388608 | tf_op jit(solution)/shard_map/weight_half/pallas_call | solution.py:595
  189.4 2.9 convert_element_type.90
  194.9 7.4 %weight_half.6 = f32[8,64,2048]{2,1,0:T(8,128)} custom-call(s32[2]{0:T(128)} %copy-done.48, bf16[256,1024]{1,0:T(8,128)(2,1)} %copy-done.10, bf16[320,1024]{1,0:T(8,128)(2,1)} %copy-done.5, bf16[256,2048]{1,0:T(8,128)(2,1)} %copy-done.15, bf16[320,2048]{1,0:T(8,128)(2,1)} %copy-done.8), custom_call_target="tpu_custom_call" | custom-call | flops 1207959552 | bytes 8388608 | tf_op jit(solution)/shard_map/weight_half/pallas_call | solution.py:595
  204.5 10.8 %collective-permute-done.5 = f32[256,1024]{1,0:T(8,128)} collective-permute-done((f32[256,1024]{1,0:T(8,128)}, f32[256,1024]{1,0:T(8,128)}, u32[]{:S(2)}, u32[]{:S(2)}) %collective-permute-start.5) | collective-permute-done | bytes 1048608 | tf_op jit(solution)/shard_map/ppermute | solution.py:759
  215.3 4.1 multiply_reduce_fusion.4
  222.0 11.1 %attention_draw.2 = (bf16[32,64,640]{2,1,0:T(8,128)(2,1)}, bf16[72,64,256]{2,1,0:T(8,128)(2,1)}, f32[256,512]{1,0:T(8,128)}, f32[576,512]{1,0:T(8,128)}, f32[576,512]{1,0:T(8,128)}) custom-call(bf16[8,256,640]{2,1,0:T(8,128)(2,1)} %get-tuple-element.208.p_ref, bf16[256,512]{1,0:T(8,128)(2,1)} %convolution_convert_fusion.1.up_ref, ...), custom_call_target="tpu_custom_call" | custom-call | flops 10000000000 | bytes 12000000 | tf_op jit(solution)/shard_map/attention_draw/pallas_call | solution.py:451
  233.1 7.9 %weight_half.5 = (f32[4,64,2048]{2,1,0:T(8,128)}, f32[4,64,2048]{2,1,0:T(8,128)}) custom-call(s32[2]{0:T(128)} %copy-done.42, bf16[256,1024]{1,0:T(8,128)(2,1)} %get-tuple-element.199.refs_0_, bf16[320,1024]{1,0:T(8,128)(2,1)} %get-tuple-element.200.refs_1_, bf16[256,2048]{1,0:T(8,128)(2,1)} %copy-done.16, bf16[320,2048]{1,0:T(8,128)(2,1)} %copy-done.9, ...), custom_call_target="tpu_custom_call" | custom-call | flops 1207959552 | bytes 8388608 | tf_op jit(solution)/shard_map/weight_half/pallas_call | solution.py:595
  242.9 4.3 multiply_reduce_fusion
  251.5 7.9 %weight_half.7 = (f32[4,64,2048]{2,1,0:T(8,128)}, f32[4,64,2048]{2,1,0:T(8,128)}) custom-call(s32[2]{0:T(128)} %copy-done.44, bf16[256,1024]{1,0:T(8,128)(2,1)} %copy-done.10, bf16[320,1024]{1,0:T(8,128)(2,1)} %copy-done.5, bf16[256,2048]{1,0:T(8,128)(2,1)} %copy-done.15, bf16[320,2048]{1,0:T(8,128)(2,1)} %copy-done.8, ...), custom_call_target="tpu_custom_call" | custom-call | flops 1207959552 | bytes 8388608 | tf_op jit(solution)/shard_map/weight_half/pallas_call | solution.py:595
  261.0 13.5 %attention_draw.3 = (bf16[40,64,640]{2,1,0:T(8,128)(2,1)}, bf16[72,64,384]{2,1,0:T(8,128)(2,1)}, f32[320,512]{1,0:T(8,128)}, f32[576,512]{1,0:T(8,128)}, bf16[576,512]{1,0:T(8,128)(2,1)}) custom-call(bf16[8,320,640]{2,1,0:T(8,128)(2,1)} %get-tuple-element.207.p_ref, bf16[320,512]{1,0:T(8,128)(2,1)} %convolution_convert_fusion.up_ref, ...), custom_call_target="tpu_custom_call" | custom-call | flops 10000000000 | bytes 12000000 | tf_op jit(solution)/shard_map/attention_draw/pallas_call | solution.py:451
  276.8 6.0 many_half.6
  284.3 38.6 %attention_scatter.4.refs_0_ = bf16[32,64,384]{2,1,0:T(8,128)(2,1)} custom-call(bf16[32,64,640]{2,1,0:T(8,128)(2,1)} %get-tuple-element.212.refs_0_, s32[3,256,640]{2,1,0:T(8,128)} %get-tuple-element.213.refs_1_, bf16[4,256,128]{2,1,0:T(8,128)(2,1)} %fusion.30.refs_2_.refs_3_), custom_call_target="tpu_custom_call" | custom-call | flops 32000000000 | bytes 6400000 | tf_op jit(solution)/shard_map/attention_scatter/pallas_call | solution.py:489
  325.0 3.0 add_bitcast_fusion
  327.9 3.2 collective-permute-done.12
  331.2 3.2 fusion.26
  334.3 6.8 %many_half.7 = (f32[4,64,1152]{2,1,0:T(8,128)}, f32[4,64,1152]{2,1,0:T(8,128)}) custom-call(s32[2]{0:T(128)} %copy-done.42, bf16[576,1024]{1,0:T(8,128)(2,1)} %pad_maximum_fusion.refs_0_, bf16[576,512]{1,0:T(8,128)(2,1)} %copy-done.17, bf16[576,1024]{1,0:T(8,128)(2,1)} %pad.16.refs_2_.refs_0_, bf16[576,512]{1,0:T(8,128)(2,1)} %get-tuple-element.214.refs_3_, ...), custom_call_target="tpu_custom_call" | custom-call | flops 707788800 | bytes 7077888 | tf_op jit(solution)/shard_map/many_half/pallas_call | solution.py:659
  341.2 2.6 collective-permute-start.13
  345.8 47.7 %attention_scatter.5.refs_1_ = bf16[40,64,384]{2,1,0:T(8,128)(2,1)} custom-call(bf16[40,64,640]{2,1,0:T(8,128)(2,1)} %get-tuple-element.224.refs_0_, s32[3,320,640]{2,1,0:T(8,128)} %get-tuple-element.188.b_ref.refs_1_, bf16[4,256,128]{2,1,0:T(8,128)(2,1)} %fusion.30.refs_2_.refs_3_), custom_call_target="tpu_custom_call" | custom-call | flops 40000000000 | bytes 8000000 | tf_op jit(solution)/shard_map/attention_scatter/pallas_call | solution.py:489
  393.5 2.4 add_bitcast_fusion.4
  398.1 5.5 attention_close.2
  407.5 6.2 many_half.8
  415.2 4.3 convolution_add_fusion.early_ref
  421.0 43.4 %attention_scatter.6.refs_0_ = bf16[36,64,384]{2,1,0:T(8,128)(2,1)} custom-call(bf16[72,64,256]{2,1,0:T(8,128)(2,1)} %get-tuple-element.257.refs_0_, bf16[72,64,384]{2,1,0:T(8,128)(2,1)} %get-tuple-element.258.refs_1_, s32[3,576,640]{2,1,0:T(8,128)} %get-tuple-element.244.refs_2_, bf16[4,256,128]{2,1,0:T(8,128)(2,1)} %fusion.30.refs_2_.refs_3_), custom_call_target="tpu_custom_call" | custom-call | flops 35999997952 | bytes 7200000 | tf_op jit(solution)/shard_map/attention_scatter/pallas_call | solution.py:489
  468.0 7.1 %many_half.9 = (f32[4,64,896]{2,1,0:T(8,128)}, f32[4,64,896]{2,1,0:T(8,128)}, f32[4,64,512]{2,1,0:T(8,128)}, f32[4,64,512]{2,1,0:T(8,128)}) custom-call(s32[3]{0:T(128)} %copy-done.46, bf16[576,1024]{1,0:T(8,128)(2,1)} %pad.16.refs_2_.refs_0_, bf16[576,512]{1,0:T(8,128)(2,1)} %copy-done.2, bf16[384,1024]{1,0:T(8,128)(2,1)} %bitcast.177, ...), custom_call_target="tpu_custom_call" | custom-call | flops 865075200 | bytes 8650752 | tf_op jit(solution)/shard_map/many_half/pallas_call | solution.py:659
  479.0 43.1 %attention_scatter.7.refs_1_ = bf16[36,64,384]{2,1,0:T(8,128)(2,1)} custom-call(bf16[72,64,256]{2,1,0:T(8,128)(2,1)} %get-tuple-element.257.refs_0_, bf16[72,64,384]{2,1,0:T(8,128)(2,1)} %get-tuple-element.258.refs_1_, s32[3,576,640]{2,1,0:T(8,128)} %get-tuple-element.244.refs_2_, bf16[4,256,128]{2,1,0:T(8,128)(2,1)} %fusion.30.refs_2_.refs_3_), custom_call_target="tpu_custom_call" | custom-call | flops 35999997952 | bytes 7200000 | tf_op jit(solution)/shard_map/attention_scatter/pallas_call | solution.py:489
  529.0 5.5 attention_close.3
  536.6 6.1 many_half.10
  544.8 2.6 collective-permute-start.32
  548.4 7.2 %many_half.11 = (f32[4,64,896]{2,1,0:T(8,128)}, f32[4,64,896]{2,1,0:T(8,128)}, f32[4,64,512]{2,1,0:T(8,128)}, f32[4,64,512]{2,1,0:T(8,128)}) custom-call(s32[3]{0:T(128)} %copy-done.45, bf16[576,1024]{1,0:T(8,128)(2,1)} %pad.16.refs_2_.refs_0_, bf16[576,512]{1,0:T(8,128)(2,1)} %convert_element_type.92.mine_ref.refs_1_, bf16[384,1024]{1,0:T(8,128)(2,1)} %bitcast.179, ...), custom_call_target="tpu_custom_call" | custom-call | flops 865075200 | bytes 8650752 | tf_op jit(solution)/shard_map/many_half/pallas_call | solution.py:659
  557.7 2.6 collective-permute-start.25
  564.1 20.3 %collective-permute-done.25 = f32[2,64,896]{2,1,0:T(8,128)S(1)} collective-permute-done((f32[2,64,896]{2,1,0:T(8,128)S(1)}, f32[2,64,896]{2,1,0:T(8,128)S(1)}, u32[]{:S(2)}, u32[]{:S(2)}) %collective-permute-start.25) | collective-permute-done | bytes 458784 | tf_op jit(solution)/shard_map/ppermute | solution.py:680
  591.2 9.6 %collective-permute-done.33 = f32[4,64,512]{2,1,0:T(8,128)S(1)} collective-permute-done((f32[4,64,512]{2,1,0:T(8,128)S(1)}, f32[4,64,512]{2,1,0:T(8,128)S(1)}, u32[]{:S(2)}, u32[]{:S(2)}) %collective-permute-start.33) | collective-permute-done | bytes 524320 | tf_op jit(solution)/shard_map/ppermute | solution.py:680
  602.0 10.9 %collective-permute-done.30 = f32[2,64,896]{2,1,0:T(8,128)S(1)} collective-permute-done((f32[2,64,896]{2,1,0:T(8,128)S(1)}, f32[2,64,896]{2,1,0:T(8,128)S(1)}, u32[]{:S(2)}, u32[]{:S(2)}) %collective-permute-start.30) | collective-permute-done | bytes 458784 | tf_op jit(solution)/shard_map/ppermute | solution.py:680
  613.7 2.6 collective-permute-start.31
  616.3 11.3 %join.1 = bf16[561,1024]{1,0:T(8,128)(2,1)} custom-call(f32[256,1024]{1,0:T(8,128)} %get-tuple-element.325.head_ref, f32[320,1024]{1,0:T(8,128)} %get-tuple-element.327.rest_ref, f32[576,1024]{1,0:T(8,128)} %convolution_add_fusion.early_ref, f32[576,1024]{1,0:T(8,128)} %collective-permute-done.14.early_other_ref, ...), custom_call_target="tpu_custom_call" | custom-call | flops 3000000000 | bytes 12000000 | tf_op jit(solution)/shard_map/join/pallas_call | solution.py:776
  (267 shorter events, 100.8 us)
Async XLA Ops:
  3.4 71.0 %collective-permute-start.1 = (f32[512,1024]{1,0:T(8,128)}, f32[512,1024]{1,0:T(8,128)}, u32[]{:S(2)}, u32[]{:S(2)}) collective-permute-start(f32[512,1024]{1,0:T(8,128)} %convert_element_type.73), channel_id=1, source_target_pairs={{0,1},{1,0},{2,3},{3,2},{4,5},{5,4},{6,7},{7,6},{8,9},{9,8},{10,11... | collective-permute-start | bytes 6291464 | tf_op jit(solution)/shard_map/ppermute | solution.py:759
  21.0 51.6 %copy-start.3 = (bf16[561,1024]{1,0:T(8,128)(2,1)S(1)}, bf16[561,1024]{1,0:T(8,128)(2,1)}, u32[]{:S(2)}) copy-start(bf16[561,1024]{1,0:T(8,128)(2,1)} %x_ref.1) | copy-start | bytes 3446788
  72.6 31.6 %collective-permute-start = (f32[256,512]{1,0:T(8,128)}, f32[256,512]{1,0:T(8,128)}, u32[]{:S(2)}, u32[]{:S(2)}) collective-permute-start(f32[256,512]{1,0:T(8,128)} %get-tuple-element.363), channel_id=1, source_target_pairs={{0,1},{1,0},{2,3},{3,2},{4,5},{5,4},{6,7},{7,6},{8,9},{9,8},{10,11... | collective-permute-start | bytes 1572872 | tf_op jit(solution)/shard_map/ppermute | solution.py:759
  73.5 26.7 %copy-start.42 = (s32[2]{0:T(128)}, s32[2]{0:T(128)S(1)}, u32[]{:S(2)}) copy-start(s32[2]{0:T(128)S(1)} %get-tuple-element.368.pick_ref) | copy-start | bytes 28
  73.5 118.8 %copy-start.44 = (s32[2]{0:T(128)}, s32[2]{0:T(128)S(1)}, u32[]{:S(2)}) copy-start(s32[2]{0:T(128)S(1)} %get-tuple-element.369.pick_ref) | copy-start | bytes 28
  102.2 19.2 %collective-permute-start.3 = (f32[320,512]{1,0:T(8,128)}, f32[320,512]{1,0:T(8,128)}, u32[]{:S(2)}, u32[]{:S(2)}) collective-permute-start(f32[320,512]{1,0:T(8,128)} %get-tuple-element.359), channel_id=1, source_target_pairs={{0,1},{1,0},{2,3},{3,2},{4,5},{5,4},{6,7},{7,6},{8,9},{9,8},{10,11... | collective-permute-start | bytes 1966088 | tf_op jit(solution)/shard_map/ppermute | solution.py:759
  121.2 26.2 %collective-permute-start.2 = (f32[256,1024]{1,0:T(8,128)S(1)}, f32[256,1024]{1,0:T(8,128)}, u32[]{:S(2)}, u32[]{:S(2)}) collective-permute-start(f32[256,1024]{1,0:T(8,128)S(1)} %fusion.45), channel_id=1, source_target_pairs={{0,1},{1,0},{2,3},{3,2},{4,5},{5,4},{6,7},{7,6},{8,9},{9,8},{10,11... | collective-permute-start | bytes 3145736 | tf_op jit(solution)/shard_map/ppermute | solution.py:759
  140.1 33.3 %collective-permute-start.4 = (f32[320,1024]{1,0:T(8,128)S(1)}, f32[320,1024]{1,0:T(8,128)S(1)}, u32[]{:S(2)}, u32[]{:S(2)}) collective-permute-start(f32[320,1024]{1,0:T(8,128)S(1)} %fusion.46), channel_id=1, source_target_pairs={{0,1},{1,0},{2,3},{3,2},{4,5},{5,4},{6,7},{7,6},{8,9},{9,8},{10,11... | collective-permute-start | bytes 3932168 | tf_op jit(solution)/shard_map/ppermute | solution.py:759
  188.8 44.2 %collective-permute-start.7 = (f32[8,64,2048]{2,1,0:T(8,128)}, f32[8,64,2048]{2,1,0:T(8,128)}, u32[]{:S(2)}, u32[]{:S(2)}) collective-permute-start(f32[8,64,2048]{2,1,0:T(8,128)} %weight_half.4), channel_id=1, source_target_pairs={{0,2},{2,0},{4,6},{6,4},{8,10},{10,8},{12,14},{14,12},{16,18},{18,... | collective-permute-start | bytes 12582920 | tf_op jit(solution)/shard_map/ppermute | solution.py:680
  188.9 26.4 %collective-permute-start.5 = (f32[256,1024]{1,0:T(8,128)}, f32[256,1024]{1,0:T(8,128)}, u32[]{:S(2)}, u32[]{:S(2)}) collective-permute-start(f32[256,1024]{1,0:T(8,128)} %fusion.47), channel_id=1, source_target_pairs={{0,1},{1,0},{2,3},{3,2},{4,5},{5,4},{6,7},{7,6},{8,9},{9,8},{10,11... | collective-permute-start | bytes 3145736 | tf_op jit(solution)/shard_map/ppermute | solution.py:759
  202.4 49.1 %collective-permute-start.9 = (f32[8,64,2048]{2,1,0:T(8,128)}, f32[8,64,2048]{2,1,0:T(8,128)}, u32[]{:S(2)}, u32[]{:S(2)}) collective-permute-start(f32[8,64,2048]{2,1,0:T(8,128)} %weight_half.6), channel_id=1, source_target_pairs={{0,2},{2,0},{4,6},{6,4},{8,10},{10,8},{12,14},{14,12},{16,18},{18,... | collective-permute-start | bytes 12582920 | tf_op jit(solution)/shard_map/ppermute | solution.py:680
  202.9 40.0 %collective-permute-start.6 = (f32[320,1024]{1,0:T(8,128)}, f32[320,1024]{1,0:T(8,128)}, u32[]{:S(2)}, u32[]{:S(2)}) collective-permute-start(f32[320,1024]{1,0:T(8,128)} %fusion.48), channel_id=1, source_target_pairs={{0,1},{1,0},{2,3},{3,2},{4,5},{5,4},{6,7},{7,6},{8,9},{9,8},{10,11... | collective-permute-start | bytes 3932168 | tf_op jit(solution)/shard_map/ppermute | solution.py:759
  259.4 64.7 %collective-permute-start.10 = (f32[4,64,2048]{2,1,0:T(8,128)}, f32[4,64,2048]{2,1,0:T(8,128)}, u32[]{:S(2)}, u32[]{:S(2)}) collective-permute-start(f32[4,64,2048]{2,1,0:T(8,128)} %get-tuple-element.222), channel_id=1, source_target_pairs={{0,8},{2,10},{4,12},{6,14},{8,0},{10,2},{12,4},{14,6},{16,24},{18,... | collective-permute-start | bytes 6291464 | tf_op jit(solution)/shard_map/ppermute | solution.py:680
  282.8 51.5 %collective-permute-start.8 = (f32[8,64,1152]{2,1,0:T(8,128)}, f32[8,64,1152]{2,1,0:T(8,128)}, u32[]{:S(2)}, u32[]{:S(2)}) collective-permute-start(f32[8,64,1152]{2,1,0:T(8,128)} %many_half.6), channel_id=1, source_target_pairs={{0,2},{2,0},{4,6},{6,4},{8,10},{10,8},{12,14},{14,12},{16,18},{18,... | collective-permute-start | bytes 7077896 | tf_op jit(solution)/shard_map/ppermute | solution.py:680
  282.8 48.4 %collective-permute-start.12 = (f32[4,64,2048]{2,1,0:T(8,128)}, f32[4,64,2048]{2,1,0:T(8,128)}, u32[]{:S(2)}, u32[]{:S(2)}) collective-permute-start(f32[4,64,2048]{2,1,0:T(8,128)} %get-tuple-element.229), channel_id=1, source_target_pairs={{0,4},{2,6},{4,0},{6,2},{8,12},{10,14},{12,8},{14,10},{16,20},{18,... | collective-permute-start | bytes 6291464 | tf_op jit(solution)/shard_map/ppermute | solution.py:680
  284.3 38.6 %copy-start.31 = (f32[320,512]{1,0:T(8,128)S(1)}, f32[320,512]{1,0:T(8,128)}, u32[]{:S(2)}) copy-start(f32[320,512]{1,0:T(8,128)} %get-tuple-element.233) | copy-start | bytes 1966084
  284.3 38.6 %copy-start.32 = (f32[256,512]{1,0:T(8,128)S(1)}, f32[256,512]{1,0:T(8,128)}, u32[]{:S(2)}) copy-start(f32[256,512]{1,0:T(8,128)} %get-tuple-element.232) | copy-start | bytes 1572868
  341.2 52.3 %collective-permute-start.13 = (f32[2,64,2048]{2,1,0:T(8,128)}, f32[2,64,2048]{2,1,0:T(8,128)}, u32[]{:S(2)}, u32[]{:S(2)}) collective-permute-start(f32[2,64,2048]{2,1,0:T(8,128)} %get-tuple-element.241), channel_id=1, source_target_pairs={{0,16},{2,18},{4,20},{6,22},{8,24},{10,26},{12,28},{14,30},{16,0},... | collective-permute-start | bytes 3145736 | tf_op jit(solution)/shard_map/ppermute | solution.py:680
  343.7 54.4 %collective-permute-start.11 = (f32[1024,512]{1,0:T(8,128)}, f32[1024,512]{1,0:T(8,128)}, u32[]{:S(2)}, u32[]{:S(2)}) collective-permute-start(f32[1024,512]{1,0:T(8,128)} %convert_element_type.90), channel_id=1, source_target_pairs={{0,1},{1,0},{2,3},{3,2},{4,5},{5,4},{6,7},{7,6},{8,9},{9,8},{10,11... | collective-permute-start | bytes 6291464 | tf_op jit(solution)/shard_map/ppermute | solution.py:759
  344.3 51.6 %collective-permute-start.18 = (f32[4,64,1152]{2,1,0:T(8,128)}, f32[4,64,1152]{2,1,0:T(8,128)}, u32[]{:S(2)}, u32[]{:S(2)}) collective-permute-start(f32[4,64,1152]{2,1,0:T(8,128)} %get-tuple-element.254), channel_id=1, source_target_pairs={{0,4},{2,6},{4,0},{6,2},{8,12},{10,14},{12,8},{14,10},{16,20},{18,... | collective-permute-start | bytes 3538952 | tf_op jit(solution)/shard_map/ppermute | solution.py:680
  413.7 50.7 %collective-permute-start.23 = (f32[64,2048]{1,0:T(8,128)}, f32[64,2048]{1,0:T(8,128)S(1)}, u32[]{:S(2)}, u32[]{:S(2)}) collective-permute-start(f32[64,2048]{1,0:T(8,128)} %get-tuple-element.268), channel_id=1, source_target_pairs={{0,4},{2,6},{4,0},{6,2},{8,12},{10,14},{12,8},{14,10},{16,20},{18,... | collective-permute-start | bytes 1572872 | tf_op jit(solution)/shard_map/ppermute | solution.py:680
  414.2 51.1 %collective-permute-start.17 = (f32[2,64,2048]{2,1,0:T(8,128)}, f32[2,64,2048]{2,1,0:T(8,128)}, u32[]{:S(2)}, u32[]{:S(2)}) collective-permute-start(f32[2,64,2048]{2,1,0:T(8,128)} %get-tuple-element.252), channel_id=1, source_target_pairs={{0,8},{2,10},{4,12},{6,14},{8,0},{10,2},{12,4},{14,6},{16,24},{18,... | collective-permute-start | bytes 3145736 | tf_op jit(solution)/shard_map/ppermute | solution.py:680
  414.7 53.3 %collective-permute-start.15 = (f32[8,64,896]{2,1,0:T(8,128)}, f32[8,64,896]{2,1,0:T(8,128)}, u32[]{:S(2)}, u32[]{:S(2)}) collective-permute-start(f32[8,64,896]{2,1,0:T(8,128)} %get-tuple-element.245), channel_id=1, source_target_pairs={{0,2},{2,0},{4,6},{6,4},{8,10},{10,8},{12,14},{14,12},{16,18},{18,... | collective-permute-start | bytes 5505032 | tf_op jit(solution)/shard_map/ppermute | solution.py:680
  414.7 53.3 %collective-permute-start.16 = (f32[8,64,512]{2,1,0:T(8,128)}, f32[8,64,512]{2,1,0:T(8,128)}, u32[]{:S(2)}, u32[]{:S(2)}) collective-permute-start(f32[8,64,512]{2,1,0:T(8,128)} %get-tuple-element.246), channel_id=1, source_target_pairs={{0,2},{2,0},{4,6},{6,4},{8,10},{10,8},{12,14},{14,12},{16,18},{18,... | collective-permute-start | bytes 3145736 | tf_op jit(solution)/shard_map/ppermute | solution.py:680
  419.5 55.6 %collective-permute-start.14 = (f32[576,1024]{1,0:T(8,128)}, f32[576,1024]{1,0:T(8,128)}, u32[]{:S(2)}, u32[]{:S(2)}) collective-permute-start(f32[576,1024]{1,0:T(8,128)} %convolution_add_fusion.early_ref), channel_id=1, source_target_pairs={{0,1},{1,0},{2,3},{3,2},{4,5},{5,4},{6,7},{7,6},{8,9},{9,8},{10,11... | collective-permute-start | bytes 7077896 | tf_op jit(solution)/shard_map/ppermute | solution.py:759
  421.0 43.4 %copy-start.22 = (f32[64,2048]{1,0:T(8,128)S(1)}, f32[64,2048]{1,0:T(8,128)}, u32[]{:S(2)}) copy-start(f32[64,2048]{1,0:T(8,128)} %get-tuple-element.267) | copy-start | bytes 1572868
  475.1 47.0 %collective-permute-start.22 = (f32[64,2048]{1,0:T(8,128)}, f32[64,2048]{1,0:T(8,128)}, u32[]{:S(2)}, u32[]{:S(2)}) collective-permute-start(f32[64,2048]{1,0:T(8,128)} %get-tuple-element.266), channel_id=1, source_target_pairs={{0,16},{2,18},{4,20},{6,22},{8,24},{10,26},{12,28},{14,30},{16,0},... | collective-permute-start | bytes 1572872 | tf_op jit(solution)/shard_map/ppermute | solution.py:680
  475.5 50.6 %collective-permute-start.21 = (f32[2,64,1152]{2,1,0:T(8,128)}, f32[2,64,1152]{2,1,0:T(8,128)S(1)}, u32[]{:S(2)}, u32[]{:S(2)}) collective-permute-start(f32[2,64,1152]{2,1,0:T(8,128)} %get-tuple-element.264), channel_id=1, source_target_pairs={{0,8},{2,10},{4,12},{6,14},{8,0},{10,2},{12,4},{14,6},{16,24},{18,... | collective-permute-start | bytes 1769480 | tf_op jit(solution)/shard_map/ppermute | solution.py:680
  477.0 47.1 %collective-permute-start.20 = (f32[4,64,512]{2,1,0:T(8,128)}, f32[4,64,512]{2,1,0:T(8,128)}, u32[]{:S(2)}, u32[]{:S(2)}) collective-permute-start(f32[4,64,512]{2,1,0:T(8,128)} %get-tuple-element.262), channel_id=1, source_target_pairs={{0,4},{2,6},{4,0},{6,2},{8,12},{10,14},{12,8},{14,10},{16,20},{18,... | collective-permute-start | bytes 1572872 | tf_op jit(solution)/shard_map/ppermute | solution.py:680
  478.6 48.4 %collective-permute-start.19 = (f32[4,64,896]{2,1,0:T(8,128)}, f32[4,64,896]{2,1,0:T(8,128)}, u32[]{:S(2)}, u32[]{:S(2)}) collective-permute-start(f32[4,64,896]{2,1,0:T(8,128)} %get-tuple-element.260), channel_id=1, source_target_pairs={{0,8},{2,10},{4,12},{6,14},{8,0},{10,2},{12,4},{14,6},{16,24},{18,... | collective-permute-start | bytes 2752520 | tf_op jit(solution)/shard_map/ppermute | solution.py:680
  542.7 5.6 collective-permute-start.27
  542.8 5.6 collective-permute-start.28
  543.3 17.1 %collective-permute-start.36 = (f32[2,64,512]{2,1,0:T(8,128)}, f32[2,64,512]{2,1,0:T(8,128)}, u32[]{:S(2)}, u32[]{:S(2)}) collective-permute-start(f32[2,64,512]{2,1,0:T(8,128)} %get-tuple-element.286), channel_id=1, source_target_pairs={{0,8},{2,10},{4,12},{6,14},{8,0},{10,2},{12,4},{14,6},{16,24},{18,... | collective-permute-start | bytes 786440 | tf_op jit(solution)/shard_map/ppermute | solution.py:680
  544.8 16.8 %collective-permute-start.32 = (f32[64,1152]{1,0:T(8,128)}, f32[64,1152]{1,0:T(8,128)}, u32[]{:S(2)}, u32[]{:S(2)}) collective-permute-start(f32[64,1152]{1,0:T(8,128)} %get-tuple-element.282), channel_id=1, source_target_pairs={{0,16},{2,18},{4,20},{6,22},{8,24},{10,26},{12,28},{14,30},{16,0},... | collective-permute-start | bytes 884744 | tf_op jit(solution)/shard_map/ppermute | solution.py:680
  555.6 32.3 %collective-permute-start.29 = (f32[4,64,896]{2,1,0:T(8,128)}, f32[4,64,896]{2,1,0:T(8,128)S(1)}, u32[]{:S(2)}, u32[]{:S(2)}) collective-permute-start(f32[4,64,896]{2,1,0:T(8,128)} %get-tuple-element.280), channel_id=1, source_target_pairs={{0,4},{2,6},{4,0},{6,2},{8,12},{10,14},{12,8},{14,10},{16,20},{18,... | collective-permute-start | bytes 2752520 | tf_op jit(solution)/shard_map/ppermute | solution.py:680
  556.1 29.9 %copy-start.53 = (f32[4,64,512]{2,1,0:T(8,128)S(1)}, f32[4,64,512]{2,1,0:T(8,128)}, u32[]{:S(2)}) copy-start(f32[4,64,512]{2,1,0:T(8,128)} %get-tuple-element.284) | copy-start | bytes 1572868
  557.2 30.6 %copy-start.29 = (f32[4,64,896]{2,1,0:T(8,128)S(1)}, f32[4,64,896]{2,1,0:T(8,128)}, u32[]{:S(2)}) copy-start(f32[4,64,896]{2,1,0:T(8,128)} %get-tuple-element.279) | copy-start | bytes 2752516
  557.2 59.1 %collective-permute-start.24 = (f32[576,512]{1,0:T(8,128)S(1)}, f32[576,512]{1,0:T(8,128)}, u32[]{:S(2)}, u32[]{:S(2)}) collective-permute-start(f32[576,512]{1,0:T(8,128)S(1)} %copy-done.24), channel_id=1, source_target_pairs={{0,1},{1,0},{2,3},{3,2},{4,5},{5,4},{6,7},{7,6},{8,9},{9,8},{10,11... | collective-permute-start | bytes 3538952 | tf_op jit(solution)/shard_map/ppermute | solution.py:759
  557.7 26.7 %collective-permute-start.25 = (f32[2,64,896]{2,1,0:T(8,128)S(1)}, f32[2,64,896]{2,1,0:T(8,128)S(1)}, u32[]{:S(2)}, u32[]{:S(2)}) collective-permute-start(f32[2,64,896]{2,1,0:T(8,128)S(1)} %copy-done.34), channel_id=1, source_target_pairs={{0,16},{2,18},{4,20},{6,22},{8,24},{10,26},{12,28},{14,30},{16,0},... | collective-permute-start | bytes 1376264 | tf_op jit(solution)/shard_map/ppermute | solution.py:680
  561.3 25.0 %collective-permute-start.37 = (f32[64,512]{1,0:T(8,128)S(1)}, f32[64,512]{1,0:T(8,128)S(1)}, u32[]{:S(2)}, u32[]{:S(2)}) collective-permute-start(f32[64,512]{1,0:T(8,128)S(1)} %add_bitcast_fusion.12), channel_id=1, source_target_pairs={{0,16},{2,18},{4,20},{6,22},{8,24},{10,26},{12,28},{14,30},{16,0},... | collective-permute-start | bytes 393224 | tf_op jit(solution)/shard_map/ppermute | solution.py:680
  562.6 38.2 %copy-start.33 = (f32[4,64,512]{2,1,0:T(8,128)S(1)}, f32[4,64,512]{2,1,0:T(8,128)}, u32[]{:S(2)}) copy-start(f32[4,64,512]{2,1,0:T(8,128)} %get-tuple-element.283) | copy-start | bytes 1572868
  584.4 6.1 collective-permute-start.26
  586.0 14.8 %collective-permute-start.33 = (f32[4,64,512]{2,1,0:T(8,128)S(1)}, f32[4,64,512]{2,1,0:T(8,128)S(1)}, u32[]{:S(2)}, u32[]{:S(2)}) collective-permute-start(f32[4,64,512]{2,1,0:T(8,128)S(1)} %copy-done.53), channel_id=1, source_target_pairs={{0,8},{2,10},{4,12},{6,14},{8,0},{10,2},{12,4},{14,6},{16,24},{18,... | collective-permute-start | bytes 1572872 | tf_op jit(solution)/shard_map/ppermute | solution.py:680
  587.9 25.0 %collective-permute-start.30 = (f32[2,64,896]{2,1,0:T(8,128)S(1)}, f32[2,64,896]{2,1,0:T(8,128)S(1)}, u32[]{:S(2)}, u32[]{:S(2)}) collective-permute-start(f32[2,64,896]{2,1,0:T(8,128)S(1)} %fusion.31), channel_id=1, source_target_pairs={{0,8},{2,10},{4,12},{6,14},{8,0},{10,2},{12,4},{14,6},{16,24},{18,... | collective-permute-start | bytes 1376264 | tf_op jit(solution)/shard_map/ppermute | solution.py:680
  600.9 26.7 %collective-permute-start.34 = (f32[2,64,512]{2,1,0:T(8,128)S(1)}, f32[2,64,512]{2,1,0:T(8,128)S(1)}, u32[]{:S(2)}, u32[]{:S(2)}) collective-permute-start(f32[2,64,512]{2,1,0:T(8,128)S(1)} %get-tuple-element.355), channel_id=1, source_target_pairs={{0,16},{2,18},{4,20},{6,22},{8,24},{10,26},{12,28},{14,30},{16,0},... | collective-permute-start | bytes 786440 | tf_op jit(solution)/shard_map/ppermute | solution.py:680
  613.7 14.5 %collective-permute-start.31 = (f32[64,896]{1,0:T(8,128)}, f32[64,896]{1,0:T(8,128)}, u32[]{:S(2)}, u32[]{:S(2)}) collective-permute-start(f32[64,896]{1,0:T(8,128)} %fusion.34), channel_id=1, source_target_pairs={{0,16},{2,18},{4,20},{6,22},{8,24},{10,26},{12,28},{14,30},{16,0},... | collective-permute-start | bytes 688136 | tf_op jit(solution)/shard_map/ppermute | solution.py:680
  627.7 5.0 collective-permute-start.35
  629.3 4.8 collective-permute-start.38
  (47 other events, 280.0 us)

commit v4 on v3

--- a/solution.py
+++ b/solution.py
@@ -302,24 +302,30 @@
     zero = jnp.asarray(0.0, bf16)
     one = jnp.asarray(1.0, bf16)
 
-    def body(g, carry):
-        back = jnp.concatenate([d_ref[g] for d_ref in d_refs], axis=1) if len(d_refs) > 1 else d_refs[0][g]
-        for r in range(3):
-            bucket = b_ref[r, pl.ds(pl.multiple_of(g * 8, 8), 8), :]
-            low = (bucket & 31).astype(f32)
-            high = (bucket >> 5).astype(f32)
-            low = jnp.concatenate([low, low], axis=0).astype(bf16) - base
-            high = jnp.concatenate([high, high], axis=0).astype(bf16)
-            hot = jnp.concatenate(
-                [jnp.where(low == jnp.asarray(2.0 * k, bf16), one, zero) for k in range(16)], axis=0
-            )
-            sieved = []
-            for l in range(4):
-                mask = high == jnp.asarray(float(l), bf16)
-                for p in range(4):
-                    sieved.append(jnp.where(mask, back[p * 16:(p + 1) * 16], zero))
-            sums = nt(jnp.concatenate(sieved, axis=0), hot)
-            sums = jnp.where(own, sums, 0.0).astype(bf16)
+    def sieve(g, r, back):
+        bucket = b_ref[r, pl.ds(pl.multiple_of(g * 8, 8), 8), :]
+        low = (bucket & 31).astype(f32)
+        high = (bucket >> 5).astype(f32)
+        low = jnp.concatenate([low, low], axis=0).astype(bf16) - base
+        high = jnp.concatenate([high, high], axis=0).astype(bf16)
+        hot = jnp.concatenate(
+            [jnp.where(low == jnp.asarray(2.0 * k, bf16), one, zero) for k in range(16)], axis=0
+        )
+        sieved = []
+        for l in range(4):
+            mask = high == jnp.asarray(float(l), bf16)
+            for p in range(4):
+                sieved.append(jnp.where(mask, back[p * 16:(p + 1) * 16], zero))
+        sums = nt(jnp.concatenate(sieved, axis=0), hot)
+        return jnp.where(own, sums, 0.0).astype(bf16)
+
+    def body(step, carry):
+        got = []
+        for g in (2 * step, 2 * step + 1):
+            back = jnp.concatenate([d_ref[g] for d_ref in d_refs], axis=1) if len(d_refs) > 1 else d_refs[0][g]
+            for r in range(3):
+                got.append((g, r, sieve(g, r, back)))
+        for g, r, sums in got:
             total = None
             for l in range(4):
                 term = nn(sums[l * 64:(l + 1) * 64], merge_ref[l])
@@ -327,7 +333,7 @@
             out_ref[g, :, r * 128:(r + 1) * 128] = total.astype(bf16)
         return carry
 
-    lax.fori_loop(0, groups, body, 0)
+    lax.fori_loop(0, groups // 2, body, 0)
 
 
 def close_kernel(*refs, rows, count):
@@ -481,22 +487,20 @@
     )(share, upstream, qkv, qkv, qkv, *adds)
 
 
-def attention_scatter(backs, buckets, merge, part, count):
-    groups, high, _ = backs[0].shape
+def attention_scatter(backs, buckets, merge, first, count):
+    high = backs[0].shape[1]
     cols = buckets.shape[2]
-    groups = groups // count
-    whole = pl.BlockSpec(memory_space=pltpu.VMEM)
     return pl.pallas_call(
-        functools.partial(scatter_kernel, groups=groups, cols=cols),
-        grid=(1,),
-        out_shape=jax.ShapeDtypeStruct((groups, high, 3 * REL), bf16),
-        in_specs=[pl.BlockSpec((groups, high, b.shape[2]), lambda g: (part, 0, 0)) for b in backs] + [
-            pl.BlockSpec((3, groups * 8, cols), lambda g: (0, part, 0)),
-            whole,
+        functools.partial(scatter_kernel, groups=8, cols=cols),
+        grid=(count,),
+        out_shape=jax.ShapeDtypeStruct((8 * count, high, 3 * REL), bf16),
+        in_specs=[pl.BlockSpec((8, high, b.shape[2]), lambda g: (first + g, 0, 0)) for b in backs] + [
+            pl.BlockSpec((3, 64, cols), lambda g: (0, first + g, 0)),
+            pl.BlockSpec(merge.shape, lambda g: (0, 0, 0)),
         ],
-        out_specs=pl.BlockSpec((groups, high, 3 * REL), lambda g: (0, 0, 0)),
+        out_specs=pl.BlockSpec((8, high, 3 * REL), lambda g: (g, 0, 0)),
         compiler_params=pltpu.CompilerParams(vmem_limit_bytes=VMEM_CAP),
-        cost_estimate=pl.CostEstimate(flops=10**9 * groups, bytes_accessed=2 * 10**5 * groups, transcendentals=0),
+        cost_estimate=pl.CostEstimate(flops=5 * 10**9 * count, bytes_accessed=10**6 * count, transcendentals=0),
         name="attention_scatter",
     )(*backs, buckets, merge)
 
@@ -646,8 +650,8 @@
 
 def many_half(pick, pairs, plan, widths, add=None, *, parts, bits):
     whole = pl.BlockSpec(memory_space=pltpu.VMEM)
-    turns = [kind != "nt" for kind, *_ in plan]
-    depth = max(left.shape[1] for (left, _), turn in zip(pairs, turns) if turn)
+    turns = [kind in ("turn", "copy") for kind, *_ in plan]
+    depth = max(left.shape[1 if turn else 0] for (left, _), turn in zip(pairs, turns))
     deep = depth // parts
     blocks = parts // 2
     keeps = add is not None
@@ -741,8 +745,11 @@
     def step(self):
         self.go(self.work())
 
+    def over(self):
+        return self.stage > len(self.orders[0]) + 1
+
     def finish(self):
-        while self.stage <= len(self.orders[0]) + 1:
+        while not self.over():
             self.step()
         return self.result
 
@@ -864,7 +871,7 @@
     size = lax.axis_size("dp")
     index = lax.axis_index("dp")
     bits = list(range(1, size.bit_length() - 1))
-    low_first, high_first = bits, bits[1:] + bits[:1]
+    low_first, high_first = bits, bits[1:2] + bits[:1] + bits[2:]
     score_scale = (7.0 * HEAD) ** (-0.5)
     tables_flat = position_tables.reshape(3 * REL, D)
     width = query_weight.shape[1]
@@ -880,6 +887,7 @@
     )
     tokens = jnp.pad(tokens, spare)
     cotangent = jnp.pad(cotangent, spare)
+    tokens_turned, tables_turned = tokens.T, tables_flat.T
     edges = [(0, split), (split, rows)]
 
     share_head, context_head, bucket_head, bucket_rest, bucket_cols, far_rest, far_inverse = attention_head(
@@ -974,8 +982,8 @@
     outer_chain = chain(
         lambda pick, add: many_half(
             pick,
-            [(residual_low, context), (tokens, value_back), (gains, dummy)],
-            [("nn", 0, 0, width), ("nn", 0, width, width), ("copy", 0, 2 * width, 128)],
+            [(residual_low, context), (tokens_turned, value_back), (gains, dummy)],
+            [("turn", 0, 0, width), ("nn", 0, width, width), ("copy", 0, 2 * width, 128)],
             [2 * width + 128],
             add, parts=size, bits=[low_first],
         ),
@@ -987,7 +995,7 @@
         return chain(
             lambda pick, add: many_half(
                 pick,
-                [(tokens, rows_back), (tables_flat, sums), (position, sums)],
+                [(tokens_turned, rows_back), (tables_turned, sums), (position, sums)],
                 [("nn", 0, 0, width), ("nn", 1, 0, width), ("nt", 0, width, 3 * REL)],
                 [width + 3 * REL, width],
                 add, parts=size, bits=orders,
@@ -996,10 +1004,10 @@
         )
 
     near = []
-    near.append(attention_scatter([back_head], bucket_head, merge, 0, 1))
+    near.append(attention_scatter([back_head], bucket_head, merge, 0, split // 64))
     back_rest, near, key_wide = tie((back_rest, near, key_weight.astype(f32)), outer_chain, down_chain)
     other_key_weight = swap(key_wide)
-    near.append(attention_scatter([back_rest], bucket_rest, merge, 0, 1))
+    near.append(attention_scatter([back_rest], bucket_rest, merge, 0, (rows - split) // 64))
     near, backs, other_key_weight = tie((near, [turned_head, turned_rest], other_key_weight), up_chain)
     query_back, key_table_sum = attention_close(near, query_base, pos_key, qkv, 0)
     query_low = query_back.astype(bf16)
@@ -1008,10 +1016,13 @@
     near_chain = tail(query_low, key_table_sum, key_position, [high_first, low_first])
     backs = tie(backs, near_chain, down_chain)
     far = []
-    far.append(attention_scatter(backs, bucket_cols, merge, 0, 2))
-    backs, far, early_other = tie((backs, far, early_other), near_chain, up_chain, outer_chain)
-    far.append(attention_scatter(backs, bucket_cols, merge, 1, 2))
-    far = tie(far, near_chain, outer_chain, up_chain, down_chain)
+    blocks = rows // 64
+    cuts = [n * blocks // 3 for n in range(4)]
+    for part, chains in enumerate((
+        (near_chain, up_chain, outer_chain), (near_chain, down_chain), (near_chain, outer_chain, up_chain, down_chain),
+    )):
+        far.append(attention_scatter(backs, bucket_cols, merge, cuts[part], cuts[part + 1] - cuts[part]))
+        backs, far, early_other = tie((backs, far, early_other), *[c for c in chains if not c.over()])
     key_back, query_table_sum = attention_close(far, key_base, pos_query, qkv, 1)
     key_other = swap(key_back)
     key_low = key_back.astype(bf16)

time: 645 us -> 653 us (1.012)
  waiting for transfers between devices: 82.8 us -> 173 us
  Pallas kernels: 389 us -> 301 us
    pallas_call x4 -> x5, Pallas kernels: 173 us -> 86.1 us  [attention_scatter(): pl.pallas_call(functools.partial(scatter_kernel, groups=8, cols=cols), gr...]
    ppermute x28, waiting for transfers between devices: 47.8 us -> 108 us  [flipped(): return lax.ppermute(value, 'dp', [(i, i ^ 1 << bit) for i in range(size)])]
    ppermute x10, waiting for transfers between devices: 35 us -> 63.2 us  [swap(): return lax.ppermute(value.astype(f32), 'mp', [(0, 1), (1, 0)])]
    add x10 -> x12, other arithmetic: 17.9 us -> 22.8 us  [split(): half(held, own) + half(extra, own)]
  transfers between devices with their start and end apart: 39 -> 39, of which waited for: 12 -> 13; matrix products, arithmetic and copies ran while one was open for 15% -> 16% of each run, Pallas kernels for 54% -> 43%
where the time goes in v4:
time: 653 us; the launch traced here: 643 us
  Pallas kernels  301 us (46%)
  waiting for transfers between devices  173 us (26%)
  other arithmetic  65.1 us (10%)
  starting transfers between devices  45 us (7%)
  matrix products  35.7 us (5%)
  local copies, waits for them, and re-layouts  22 us (3%)
    ppermute x28, waiting for transfers between devices, flipped(): return lax.ppermute(value, 'dp', [(i, i ^ 1 << bit) for i in range(size)])  108 us
    pallas_call x5, Pallas kernels, attention_scatter(): pl.pallas_call(functools.partial(scatter_kernel, groups=8, cols=cols), gr...  86.1 us
    ppermute x10, waiting for transfers between devices, swap(): return lax.ppermute(value.astype(f32), 'mp', [(0, 1), (1, 0)])  63.2 us
    pallas_call x1, Pallas kernels, attention_head(): pl.pallas_call(kernel, out_shape=(jax.ShapeDtypeStruct((2 * pairs, split,...  49.8 us
    pallas_call x6, Pallas kernels, many_half(): pl.pallas_call(functools.partial(many_kernel, plan=plan, widths=widths, t...  37.1 us
    ppermute x28, starting transfers between devices, flipped(): return lax.ppermute(value, 'dp', [(i, i ^ 1 << bit) for i in range(size)])  31.4 us
    pallas_call x4, Pallas kernels, weight_half(): pl.pallas_call(functools.partial(weight_kernel, count=len(xs), blocks=blo...  30.9 us
    pallas_call x1, Pallas kernels, attention_rest(): pl.pallas_call(kernel, out_shape=(jax.ShapeDtypeStruct((2 * pairs, rows -...  25.8 us
  transfers between devices with their start and end apart: 39, of which 13 were waited for; matrix products, arithmetic and copies ran while one was open for 16% of the time, Pallas kernels for 43%

profile of v4, /device:TPU:0, one launch (start us, length us, event | category | flops | bytes accessed | tf_op | source)
XLA Modules:
  0.0 643.4 jit_solution(15874585813030505316)
XLA Ops:
  3.4 3.0 collective-permute-start.1
  7.0 4.6 copy.60.b_ref
  11.6 9.3 %project.1 = (bf16[640,1536]{1,0:T(8,128)(2,1)}, bf16[384,512]{1,0:T(8,128)(2,1)}, bf16[384,512]{1,0:T(8,128)(2,1)}) custom-call(bf16[561,1024]{1,0:T(8,128)(2,1)} %x_ref.1, bf16[1024,512]{1,0:T(8,128)(2,1)} %wq_ref.1, bf16[1024,512]{1,0:T(8,128)(2,1)} %w_ref.5, bf16[1024,512]{1,0:T(8,128)(2,1)} %wv_ref.1, bf16[3,128,1024]{2,1,0:T(8,128)(2,1)} %t_ref.1, ...), custom_call_target="tpu_custom_call" | custom-call | flops 4000000000 | bytes 9000000 | tf_op jit(solution)/shard_map/project/pallas_call | solution.py:226
  21.0 49.8 %attention_head.1 = (bf16[8,256,640]{2,1,0:T(8,128)(2,1)}, bf16[256,512]{1,0:T(8,128)(2,1)}, s32[3,256,640]{2,1,0:T(8,128)}, s32[3,320,640]{2,1,0:T(8,128)}, s32...) custom-call(s32[1]{0:T(128)S(6)} %copy.120.used_ref, ...), custom_call_target="tpu_custom_call" | custom-call | flops 40000000000 | bytes 25000000 | tf_op jit(solution)/shard_map/attention_head/pallas_call | solution.py:396
  76.6 25.8 %attention_rest.1 = (bf16[8,320,640]{2,1,0:T(8,128)(2,1)}, bf16[320,512]{1,0:T(8,128)(2,1)}) custom-call(s32[1]{0:T(128)S(6)} %copy.120.used_ref, bf16[640,1536]{1,0:T(8,128)(2,1)} %get-tuple-element.191.qkv_ref.q_ref.k_ref.v_ref.refs_4_.refs_5_, bf16[384,512]{1,0:T(8,128)(2,1)} %get-tuple-element.192.pk_ref.refs_3_, ...), custom_call_target="tpu_custom_call" | custom-call | flops 20000000000 | bytes 12000000 | tf_op jit(solution)/shard_map/attention_rest/pallas_call | solution.py:433
  105.7 6.7 %attend.2 = (f32[256,1024]{1,0:T(8,128)}, bf16[256,1024]{1,0:T(8,128)(2,1)}, f32[256,1024]{1,0:T(8,128)}, f32[256,1]{1,0:T(8,128)}) custom-call(bf16[256,1024]{1,0:T(8,128)(2,1)} %slice.97.t_ref, bf16[256,512]{1,0:T(8,128)(2,1)} %get-tuple-element.194.c_ref, f32[256,512]{1,0:T(8,128)} %collective-permute-done.o_ref, bf16[512,1024]{1,0:T(8,128)(2,1)} %w_ref.4, ...), custom_call_target="tpu_custom_call" | custom-call | flops 2000000000 | bytes 8000000 | tf_op jit(solution)/shard_map/attend/pallas_call | solution.py:816
  112.4 8.8 %multiply_convert_fusion.1 = (bf16[256,2048]{1,0:T(8,128)(2,1)S(1)}, f32[256,2048]{1,0:T(8,128)}, f32[256,2048]{1,0:T(8,128)}) fusion(bf16[256,1024]{1,0:T(8,128)(2,1)} %get-tuple-element.210.refs_0_, bf16[1024,2048]{1,0:T(8,128)(2,1)} %param.37), kind=kOutput, calls=%fused_computation.20 | convolution fusion | flops 1107820544 | bytes 9961472 | tf_op jit(solution)/shard_map/dot_general | solution.py:39
  122.8 7.8 %attend.3 = (f32[320,1024]{1,0:T(8,128)}, bf16[320,1024]{1,0:T(8,128)(2,1)}, f32[320,1024]{1,0:T(8,128)}, f32[320,1]{1,0:T(8,128)}) custom-call(bf16[320,1024]{1,0:T(8,128)(2,1)} %copy.62.t_ref, bf16[320,512]{1,0:T(8,128)(2,1)} %get-tuple-element.202.c_ref, f32[320,512]{1,0:T(8,128)} %collective-permute-done.3.o_ref, bf16[512,1024]{1,0:T(8,128)(2,1)} %w_ref.4, ...), custom_call_target="tpu_custom_call" | custom-call | flops 2000000000 | bytes 8000000 | tf_op jit(solution)/shard_map/attend/pallas_call | solution.py:816
  130.5 9.3 %multiply_convert_fusion = (bf16[320,2048]{1,0:T(8,128)(2,1)S(1)}, f32[320,2048]{1,0:T(8,128)S(1)}, f32[320,2048]{1,0:T(8,128)S(1)}) fusion(bf16[320,1024]{1,0:T(8,128)(2,1)} %get-tuple-element.211.refs_1_, bf16[1024,2048]{1,0:T(8,128)(2,1)} %param.37), kind=kOutput, calls=%fused_computation.4 | convolution fusion | flops 1384775680 | bytes 11403264 | tf_op jit(solution)/shard_map/dot_general | solution.py:39
  143.4 5.4 collective-permute-done.2
  157.7 17.1 %collective-permute-done.4 = f32[320,1024]{1,0:T(8,128)S(1)} collective-permute-done((f32[320,1024]{1,0:T(8,128)S(1)}, f32[320,1024]{1,0:T(8,128)S(1)}, u32[]{:S(2)}, u32[]{:S(2)}) %collective-permute-start.4) | collective-permute-done | bytes 1310752 | tf_op jit(solution)/shard_map/ppermute | solution.py:766
  182.7 7.4 %weight_half.6 = f32[8,64,2048]{2,1,0:T(8,128)} custom-call(s32[2]{0:T(128)} %copy-done.48, bf16[256,1024]{1,0:T(8,128)(2,1)} %copy-done.10, bf16[320,1024]{1,0:T(8,128)(2,1)} %copy-done.5, bf16[256,2048]{1,0:T(8,128)(2,1)} %copy-done.15, bf16[320,2048]{1,0:T(8,128)(2,1)} %copy-done.8), custom_call_target="tpu_custom_call" | custom-call | flops 1207959552 | bytes 8388608 | tf_op jit(solution)/shard_map/weight_half/pallas_call | solution.py:599
  190.1 7.6 %weight_half.4 = f32[8,64,2048]{2,1,0:T(8,128)} custom-call(s32[2]{0:T(128)} %copy-done.44, bf16[256,1024]{1,0:T(8,128)(2,1)} %get-tuple-element.210.refs_0_, bf16[320,1024]{1,0:T(8,128)(2,1)} %get-tuple-element.211.refs_1_, bf16[256,2048]{1,0:T(8,128)(2,1)} %copy-done.16, bf16[320,2048]{1,0:T(8,128)(2,1)} %copy-done.9), custom_call_target="tpu_custom_call" | custom-call | flops 1207959552 | bytes 8388608 | tf_op jit(solution)/shard_map/weight_half/pallas_call | solution.py:599
  198.6 2.9 convert_element_type.92
  207.1 17.5 %collective-permute-done.5 = f32[256,1024]{1,0:T(8,128)} collective-permute-done((f32[256,1024]{1,0:T(8,128)}, f32[256,1024]{1,0:T(8,128)}, u32[]{:S(2)}, u32[]{:S(2)}) %collective-permute-start.5) | collective-permute-done | bytes 1048608 | tf_op jit(solution)/shard_map/ppermute | solution.py:766
  224.6 3.8 multiply_reduce_fusion.4
  231.0 11.1 %attention_draw.2 = (bf16[32,64,640]{2,1,0:T(8,128)(2,1)}, bf16[72,64,256]{2,1,0:T(8,128)(2,1)}, f32[256,512]{1,0:T(8,128)}, f32[576,512]{1,0:T(8,128)}, f32[576,512]{1,0:T(8,128)}) custom-call(bf16[8,256,640]{2,1,0:T(8,128)(2,1)} %get-tuple-element.219.p_ref, bf16[256,512]{1,0:T(8,128)(2,1)} %convolution_convert_fusion.1.up_ref, ...), custom_call_target="tpu_custom_call" | custom-call | flops 10000000000 | bytes 12000000 | tf_op jit(solution)/shard_map/attention_draw/pallas_call | solution.py:457
  242.1 8.0 %weight_half.7 = (f32[4,64,2048]{2,1,0:T(8,128)}, f32[4,64,2048]{2,1,0:T(8,128)}) custom-call(s32[2]{0:T(128)} %copy-done.45, bf16[256,1024]{1,0:T(8,128)(2,1)} %copy-done.10, bf16[320,1024]{1,0:T(8,128)(2,1)} %copy-done.5, bf16[256,2048]{1,0:T(8,128)(2,1)} %copy-done.15, bf16[320,2048]{1,0:T(8,128)(2,1)} %copy-done.8, ...), custom_call_target="tpu_custom_call" | custom-call | flops 1207959552 | bytes 8388608 | tf_op jit(solution)/shard_map/weight_half/pallas_call | solution.py:599
  251.7 7.9 %weight_half.5 = (f32[4,64,2048]{2,1,0:T(8,128)}, f32[4,64,2048]{2,1,0:T(8,128)}) custom-call(s32[2]{0:T(128)} %copy-done.43, bf16[256,1024]{1,0:T(8,128)(2,1)} %get-tuple-element.210.refs_0_, bf16[320,1024]{1,0:T(8,128)(2,1)} %get-tuple-element.211.refs_1_, bf16[256,2048]{1,0:T(8,128)(2,1)} %copy-done.16, bf16[320,2048]{1,0:T(8,128)(2,1)} %copy-done.9, ...), custom_call_target="tpu_custom_call" | custom-call | flops 1207959552 | bytes 8388608 | tf_op jit(solution)/shard_map/weight_half/pallas_call | solution.py:599
  259.6 4.3 multiply_reduce_fusion
  266.6 13.5 %attention_draw.3 = (bf16[40,64,640]{2,1,0:T(8,128)(2,1)}, bf16[72,64,384]{2,1,0:T(8,128)(2,1)}, f32[320,512]{1,0:T(8,128)}, f32[576,512]{1,0:T(8,128)}, bf16[576,512]{1,0:T(8,128)(2,1)}) custom-call(bf16[8,320,640]{2,1,0:T(8,128)(2,1)} %get-tuple-element.218.p_ref, bf16[320,512]{1,0:T(8,128)(2,1)} %convolution_convert_fusion.up_ref, ...), custom_call_target="tpu_custom_call" | custom-call | flops 10000000000 | bytes 12000000 | tf_op jit(solution)/shard_map/attention_draw/pallas_call | solution.py:457
  283.3 5.8 many_half.6
  290.6 19.1 %attention_scatter.5.refs_0_ = bf16[32,64,384]{2,1,0:T(8,128)(2,1)} custom-call(bf16[32,64,640]{2,1,0:T(8,128)(2,1)} %get-tuple-element.223.refs_0_, s32[3,256,640]{2,1,0:T(8,128)} %get-tuple-element.224.refs_1_, bf16[4,256,128]{2,1,0:T(8,128)(2,1)} %fusion.32.refs_2_.refs_3_), custom_call_target="tpu_custom_call" | custom-call | flops 20000000000 | bytes 4000000 | tf_op jit(solution)/shard_map/attention_scatter/pallas_call | solution.py:493
  311.7 3.3 fusion.28
  315.1 22.4 %collective-permute-done.12 = f32[4,64,2048]{2,1,0:T(8,128)} collective-permute-done((f32[4,64,2048]{2,1,0:T(8,128)}, f32[4,64,2048]{2,1,0:T(8,128)}, u32[]{:S(2)}, u32[]{:S(2)}) %collective-permute-start.12) | collective-permute-done | bytes 2097184 | tf_op jit(solution)/shard_map/ppermute | solution.py:684
  340.3 6.6 %many_half.7 = (f32[4,64,1152]{2,1,0:T(8,128)}, f32[4,64,1152]{2,1,0:T(8,128)}) custom-call(s32[2]{0:T(128)} %copy-done.43, bf16[576,1024]{1,0:T(8,128)(2,1)} %pad_maximum_fusion.refs_0_, bf16[576,512]{1,0:T(8,128)(2,1)} %copy-done.17, bf16[1024,576]{1,0:T(8,128)(2,1)} %pad_bitcast_fusion.refs_2_.refs_0_, bf16[576,512]{1,0:T(8,128)(2,1)} %get-tuple-element.225.refs_3_, ...), custom_call_target="tpu_custom_call" | custom-call | flops 707788800 | bytes 7077888 | tf_op jit(solution)/shard_map/many_half/pallas_call | solution.py:663
  349.4 22.9 %attention_scatter.6.refs_1_ = bf16[40,64,384]{2,1,0:T(8,128)(2,1)} custom-call(bf16[40,64,640]{2,1,0:T(8,128)(2,1)} %get-tuple-element.235.refs_0_, s32[3,320,640]{2,1,0:T(8,128)} %get-tuple-element.199.b_ref.refs_1_, bf16[4,256,128]{2,1,0:T(8,128)(2,1)} %fusion.32.refs_2_.refs_3_), custom_call_target="tpu_custom_call" | custom-call | flops 24999999488 | bytes 5000000 | tf_op jit(solution)/shard_map/attention_scatter/pallas_call | solution.py:493
  372.3 23.2 %collective-permute-done.11.ow_ref = f32[1024,512]{1,0:T(8,128)} collective-permute-done((f32[1024,512]{1,0:T(8,128)}, f32[1024,512]{1,0:T(8,128)}, u32[]{:S(2)}, u32[]{:S(2)}) %collective-permute-start.11) | collective-permute-done | bytes 2097184 | tf_op jit(solution)/shard_map/ppermute | solution.py:766
  395.6 5.5 attention_close.2
  410.7 5.8 many_half.8
  422.2 14.6 %attention_scatter.7.refs_0_ = bf16[24,64,384]{2,1,0:T(8,128)(2,1)} custom-call(bf16[72,64,256]{2,1,0:T(8,128)(2,1)} %get-tuple-element.276.refs_0_, bf16[72,64,384]{2,1,0:T(8,128)(2,1)} %get-tuple-element.277.refs_1_, s32[3,576,640]{2,1,0:T(8,128)} %get-tuple-element.255.refs_2_, bf16[4,256,128]{2,1,0:T(8,128)(2,1)} %fusion.32.refs_2_.refs_3_), custom_call_target="tpu_custom_call" | custom-call | flops 15000000512 | bytes 3000000 | tf_op jit(solution)/shard_map/attention_scatter/pallas_call | solution.py:493
  436.8 17.2 %collective-permute-done.21 = f32[64,2048]{1,0:T(8,128)} collective-permute-done((f32[64,2048]{1,0:T(8,128)}, f32[64,2048]{1,0:T(8,128)}, u32[]{:S(2)}, u32[]{:S(2)}) %collective-permute-start.21) | collective-permute-done | bytes 524320 | tf_op jit(solution)/shard_map/ppermute | solution.py:684
  458.4 6.7 %many_half.9 = (f32[4,64,896]{2,1,0:T(8,128)}, f32[4,64,896]{2,1,0:T(8,128)}, f32[4,64,512]{2,1,0:T(8,128)}, f32[4,64,512]{2,1,0:T(8,128)}) custom-call(s32[3]{0:T(128)} %copy-done.47, bf16[1024,576]{1,0:T(8,128)(2,1)} %pad_bitcast_fusion.refs_2_.refs_0_, bf16[576,512]{1,0:T(8,128)(2,1)} %copy-done.4, bf16[1024,384]{1,0:T(8,128)(2,1)} %bitcast.210, ...), custom_call_target="tpu_custom_call" | custom-call | flops 865075200 | bytes 8650752 | tf_op jit(solution)/shard_map/many_half/pallas_call | solution.py:663
  465.1 3.4 collective-permute-start.25
  471.0 14.9 %attention_scatter.8.refs_1_ = bf16[24,64,384]{2,1,0:T(8,128)(2,1)} custom-call(bf16[72,64,256]{2,1,0:T(8,128)(2,1)} %get-tuple-element.276.refs_0_, bf16[72,64,384]{2,1,0:T(8,128)(2,1)} %get-tuple-element.277.refs_1_, s32[3,576,640]{2,1,0:T(8,128)} %get-tuple-element.255.refs_2_, bf16[4,256,128]{2,1,0:T(8,128)(2,1)} %fusion.32.refs_2_.refs_3_), custom_call_target="tpu_custom_call" | custom-call | flops 15000000512 | bytes 3000000 | tf_op jit(solution)/shard_map/attention_scatter/pallas_call | solution.py:493
  485.8 6.0 collective-permute-done.25
  496.5 16.4 %collective-permute-done.19 = f32[4,64,896]{2,1,0:T(8,128)} collective-permute-done((f32[4,64,896]{2,1,0:T(8,128)}, f32[4,64,896]{2,1,0:T(8,128)}, u32[]{:S(2)}, u32[]{:S(2)}) %collective-permute-start.19) | collective-permute-done | bytes 917536 | tf_op jit(solution)/shard_map/ppermute | solution.py:684
  516.4 14.6 %attention_scatter.9.refs_2_ = bf16[24,64,384]{2,1,0:T(8,128)(2,1)} custom-call(bf16[72,64,256]{2,1,0:T(8,128)(2,1)} %get-tuple-element.276.refs_0_, bf16[72,64,384]{2,1,0:T(8,128)(2,1)} %get-tuple-element.277.refs_1_, s32[3,576,640]{2,1,0:T(8,128)} %get-tuple-element.255.refs_2_, bf16[4,256,128]{2,1,0:T(8,128)(2,1)} %fusion.32.refs_2_.refs_3_), custom_call_target="tpu_custom_call" | custom-call | flops 15000000512 | bytes 3000000 | tf_op jit(solution)/shard_map/attention_scatter/pallas_call | solution.py:493
  534.4 5.5 attention_close.3
  542.1 5.7 many_half.10
  549.9 3.5 collective-permute-done.29.refs_7_
  553.4 6.6 %many_half.11 = (f32[4,64,896]{2,1,0:T(8,128)}, f32[4,64,896]{2,1,0:T(8,128)}, f32[4,64,512]{2,1,0:T(8,128)}, f32[4,64,512]{2,1,0:T(8,128)}) custom-call(s32[3]{0:T(128)} %copy-done.46, bf16[1024,576]{1,0:T(8,128)(2,1)} %pad_bitcast_fusion.refs_2_.refs_0_, bf16[576,512]{1,0:T(8,128)(2,1)} %convert_element_type.94.mine_ref.refs_1_, ...), custom_call_target="tpu_custom_call" | custom-call | flops 865075200 | bytes 8650752 | tf_op jit(solution)/shard_map/many_half/pallas_call | solution.py:663
  561.6 3.7 collective-permute-start.33
  565.4 2.9 collective-permute-start.37
  569.4 24.8 %collective-permute-done.37 = f32[64,512]{1,0:T(8,128)S(1)} collective-permute-done((f32[64,512]{1,0:T(8,128)}, f32[64,512]{1,0:T(8,128)S(1)}, u32[]{:S(2)}, u32[]{:S(2)}) %collective-permute-start.37) | collective-permute-done | bytes 131104 | tf_op jit(solution)/shard_map/ppermute | solution.py:684
  600.2 11.4 %join.1 = bf16[561,1024]{1,0:T(8,128)(2,1)} custom-call(f32[256,1024]{1,0:T(8,128)} %get-tuple-element.347.head_ref, f32[320,1024]{1,0:T(8,128)} %get-tuple-element.349.rest_ref, f32[576,1024]{1,0:T(8,128)} %convolution_add_fusion.early_ref, f32[576,1024]{1,0:T(8,128)} %collective-permute-done.14.early_other_ref, ...), custom_call_target="tpu_custom_call" | custom-call | flops 3000000000 | bytes 12000000 | tf_op jit(solution)/shard_map/join/pallas_call | solution.py:783
  613.4 6.4 collective-permute-done.31
  624.9 11.4 %collective-permute-done.32 = f32[64,896]{1,0:T(8,128)S(1)} collective-permute-done((f32[64,896]{1,0:T(8,128)S(1)}, f32[64,896]{1,0:T(8,128)S(1)}, u32[]{:S(2)}, u32[]{:S(2)}) %collective-permute-start.32) | collective-permute-done | bytes 229408 | tf_op jit(solution)/shard_map/ppermute | solution.py:684
  (271 shorter events, 119.1 us)
Async XLA Ops:
  3.4 73.2 %collective-permute-start.1 = (f32[512,1024]{1,0:T(8,128)}, f32[512,1024]{1,0:T(8,128)}, u32[]{:S(2)}, u32[]{:S(2)}) collective-permute-start(f32[512,1024]{1,0:T(8,128)} %convert_element_type.75), channel_id=1, source_target_pairs={{0,1},{1,0},{2,3},{3,2},{4,5},{5,4},{6,7},{7,6},{8,9},{9,8},{10,11... | collective-permute-start | bytes 6291464 | tf_op jit(solution)/shard_map/ppermute | solution.py:766
  21.0 51.7 %copy-start.19 = (bf16[561,1024]{1,0:T(8,128)(2,1)S(1)}, bf16[561,1024]{1,0:T(8,128)(2,1)}, u32[]{:S(2)}) copy-start(bf16[561,1024]{1,0:T(8,128)(2,1)} %x_ref.1) | copy-start | bytes 3446788
  72.6 33.1 %collective-permute-start = (f32[256,512]{1,0:T(8,128)}, f32[256,512]{1,0:T(8,128)}, u32[]{:S(2)}, u32[]{:S(2)}) collective-permute-start(f32[256,512]{1,0:T(8,128)} %get-tuple-element.387), channel_id=1, source_target_pairs={{0,1},{1,0},{2,3},{3,2},{4,5},{5,4},{6,7},{7,6},{8,9},{9,8},{10,11... | collective-permute-start | bytes 1572872 | tf_op jit(solution)/shard_map/ppermute | solution.py:766
  76.6 25.9 %copy-start.43 = (s32[2]{0:T(128)}, s32[2]{0:T(128)S(1)}, u32[]{:S(2)}) copy-start(s32[2]{0:T(128)S(1)} %get-tuple-element.394.pick_ref) | copy-start | bytes 28
  76.6 25.9 %copy-start.45 = (s32[2]{0:T(128)}, s32[2]{0:T(128)S(1)}, u32[]{:S(2)}) copy-start(s32[2]{0:T(128)S(1)} %get-tuple-element.395.pick_ref) | copy-start | bytes 28
  76.6 25.9 %copy-start.48 = (s32[2]{0:T(128)}, s32[2]{0:T(128)S(1)}, u32[]{:S(2)}) copy-start(s32[2]{0:T(128)S(1)} %constant_dynamic-update-slice_fusion.2.pick_ref) | copy-start | bytes 28
  76.6 25.8 %copy-start.44 = (s32[2]{0:T(128)}, s32[2]{0:T(128)S(1)}, u32[]{:S(2)}) copy-start(s32[2]{0:T(128)S(1)} %constant_dynamic-update-slice_fusion.3.pick_ref) | copy-start | bytes 28
  103.6 19.1 %collective-permute-start.3 = (f32[320,512]{1,0:T(8,128)S(1)}, f32[320,512]{1,0:T(8,128)}, u32[]{:S(2)}, u32[]{:S(2)}) collective-permute-start(f32[320,512]{1,0:T(8,128)S(1)} %get-tuple-element.383), channel_id=1, source_target_pairs={{0,1},{1,0},{2,3},{3,2},{4,5},{5,4},{6,7},{7,6},{8,9},{9,8},{10,11... | collective-permute-start | bytes 1966088 | tf_op jit(solution)/shard_map/ppermute | solution.py:766
  122.6 26.2 %collective-permute-start.2 = (f32[256,1024]{1,0:T(8,128)S(1)}, f32[256,1024]{1,0:T(8,128)}, u32[]{:S(2)}, u32[]{:S(2)}) collective-permute-start(f32[256,1024]{1,0:T(8,128)S(1)} %fusion.50), channel_id=1, source_target_pairs={{0,1},{1,0},{2,3},{3,2},{4,5},{5,4},{6,7},{7,6},{8,9},{9,8},{10,11... | collective-permute-start | bytes 3145736 | tf_op jit(solution)/shard_map/ppermute | solution.py:766
  141.4 33.4 %collective-permute-start.4 = (f32[320,1024]{1,0:T(8,128)S(1)}, f32[320,1024]{1,0:T(8,128)S(1)}, u32[]{:S(2)}, u32[]{:S(2)}) collective-permute-start(f32[320,1024]{1,0:T(8,128)S(1)} %fusion.51), channel_id=1, source_target_pairs={{0,1},{1,0},{2,3},{3,2},{4,5},{5,4},{6,7},{7,6},{8,9},{9,8},{10,11... | collective-permute-start | bytes 3932168 | tf_op jit(solution)/shard_map/ppermute | solution.py:766
  190.1 52.0 %collective-permute-start.9 = (f32[8,64,2048]{2,1,0:T(8,128)}, f32[8,64,2048]{2,1,0:T(8,128)}, u32[]{:S(2)}, u32[]{:S(2)}) collective-permute-start(f32[8,64,2048]{2,1,0:T(8,128)} %weight_half.6), channel_id=1, source_target_pairs={{0,2},{2,0},{4,6},{6,4},{8,10},{10,8},{12,14},{14,12},{16,18},{18,... | collective-permute-start | bytes 12582920 | tf_op jit(solution)/shard_map/ppermute | solution.py:684
  197.7 53.9 %collective-permute-start.7 = (f32[8,64,2048]{2,1,0:T(8,128)}, f32[8,64,2048]{2,1,0:T(8,128)}, u32[]{:S(2)}, u32[]{:S(2)}) collective-permute-start(f32[8,64,2048]{2,1,0:T(8,128)} %weight_half.4), channel_id=1, source_target_pairs={{0,2},{2,0},{4,6},{6,4},{8,10},{10,8},{12,14},{14,12},{16,18},{18,... | collective-permute-start | bytes 12582920 | tf_op jit(solution)/shard_map/ppermute | solution.py:684
  198.2 26.3 %collective-permute-start.5 = (f32[256,1024]{1,0:T(8,128)}, f32[256,1024]{1,0:T(8,128)}, u32[]{:S(2)}, u32[]{:S(2)}) collective-permute-start(f32[256,1024]{1,0:T(8,128)} %fusion.52), channel_id=1, source_target_pairs={{0,1},{1,0},{2,3},{3,2},{4,5},{5,4},{6,7},{7,6},{8,9},{9,8},{10,11... | collective-permute-start | bytes 3145736 | tf_op jit(solution)/shard_map/ppermute | solution.py:766
  205.4 54.3 %collective-permute-start.6 = (f32[320,1024]{1,0:T(8,128)}, f32[320,1024]{1,0:T(8,128)}, u32[]{:S(2)}, u32[]{:S(2)}) collective-permute-start(f32[320,1024]{1,0:T(8,128)} %fusion.53), channel_id=1, source_target_pairs={{0,1},{1,0},{2,3},{3,2},{4,5},{5,4},{6,7},{7,6},{8,9},{9,8},{10,11... | collective-permute-start | bytes 3932168 | tf_op jit(solution)/shard_map/ppermute | solution.py:766
  250.1 60.8 %collective-permute-start.10 = (f32[4,64,2048]{2,1,0:T(8,128)}, f32[4,64,2048]{2,1,0:T(8,128)}, u32[]{:S(2)}, u32[]{:S(2)}) collective-permute-start(f32[4,64,2048]{2,1,0:T(8,128)} %get-tuple-element.233), channel_id=1, source_target_pairs={{0,8},{2,10},{4,12},{6,14},{8,0},{10,2},{12,4},{14,6},{16,24},{18,... | collective-permute-start | bytes 6291464 | tf_op jit(solution)/shard_map/ppermute | solution.py:684
  289.1 51.2 %collective-permute-start.8 = (f32[8,64,1152]{2,1,0:T(8,128)}, f32[8,64,1152]{2,1,0:T(8,128)}, u32[]{:S(2)}, u32[]{:S(2)}) collective-permute-start(f32[8,64,1152]{2,1,0:T(8,128)} %many_half.6), channel_id=1, source_target_pairs={{0,2},{2,0},{4,6},{6,4},{8,10},{10,8},{12,14},{14,12},{16,18},{18,... | collective-permute-start | bytes 7077896 | tf_op jit(solution)/shard_map/ppermute | solution.py:684
  289.1 48.4 %collective-permute-start.12 = (f32[4,64,2048]{2,1,0:T(8,128)}, f32[4,64,2048]{2,1,0:T(8,128)}, u32[]{:S(2)}, u32[]{:S(2)}) collective-permute-start(f32[4,64,2048]{2,1,0:T(8,128)} %get-tuple-element.240), channel_id=1, source_target_pairs={{0,4},{2,6},{4,0},{6,2},{8,12},{10,14},{12,8},{14,10},{16,20},{18,... | collective-permute-start | bytes 6291464 | tf_op jit(solution)/shard_map/ppermute | solution.py:684
  311.7 25.7 %copy-start.21 = (f32[4,64,2048]{2,1,0:T(8,128)S(1)}, f32[4,64,2048]{2,1,0:T(8,128)}, u32[]{:S(2)}) copy-start(f32[4,64,2048]{2,1,0:T(8,128)} %get-tuple-element.239) | copy-start | bytes 6291460
  346.9 69.6 %collective-permute-start.18 = (f32[4,64,1152]{2,1,0:T(8,128)}, f32[4,64,1152]{2,1,0:T(8,128)}, u32[]{:S(2)}, u32[]{:S(2)}) collective-permute-start(f32[4,64,1152]{2,1,0:T(8,128)} %get-tuple-element.265), channel_id=1, source_target_pairs={{0,4},{2,6},{4,0},{6,2},{8,12},{10,14},{12,8},{14,10},{16,20},{18,... | collective-permute-start | bytes 3538952 | tf_op jit(solution)/shard_map/ppermute | solution.py:684
  348.4 47.2 %collective-permute-start.11 = (f32[1024,512]{1,0:T(8,128)}, f32[1024,512]{1,0:T(8,128)}, u32[]{:S(2)}, u32[]{:S(2)}) collective-permute-start(f32[1024,512]{1,0:T(8,128)} %convert_element_type.92), channel_id=1, source_target_pairs={{0,1},{1,0},{2,3},{3,2},{4,5},{5,4},{6,7},{7,6},{8,9},{9,8},{10,11... | collective-permute-start | bytes 6291464 | tf_op jit(solution)/shard_map/ppermute | solution.py:766
  348.9 59.4 %collective-permute-start.13 = (f32[2,64,2048]{2,1,0:T(8,128)}, f32[2,64,2048]{2,1,0:T(8,128)}, u32[]{:S(2)}, u32[]{:S(2)}) collective-permute-start(f32[2,64,2048]{2,1,0:T(8,128)} %get-tuple-element.252), channel_id=1, source_target_pairs={{0,4},{2,6},{4,0},{6,2},{8,12},{10,14},{12,8},{14,10},{16,20},{18,... | collective-permute-start | bytes 3145736 | tf_op jit(solution)/shard_map/ppermute | solution.py:684
  406.5 58.6 %collective-permute-start.14 = (f32[576,1024]{1,0:T(8,128)}, f32[576,1024]{1,0:T(8,128)}, u32[]{:S(2)}, u32[]{:S(2)}) collective-permute-start(f32[576,1024]{1,0:T(8,128)} %convolution_add_fusion.early_ref), channel_id=1, source_target_pairs={{0,1},{1,0},{2,3},{3,2},{4,5},{5,4},{6,7},{7,6},{8,9},{9,8},{10,11... | collective-permute-start | bytes 7077896 | tf_op jit(solution)/shard_map/ppermute | solution.py:766
  416.4 42.0 %collective-permute-start.15 = (f32[8,64,896]{2,1,0:T(8,128)}, f32[8,64,896]{2,1,0:T(8,128)}, u32[]{:S(2)}, u32[]{:S(2)}) collective-permute-start(f32[8,64,896]{2,1,0:T(8,128)} %get-tuple-element.256), channel_id=1, source_target_pairs={{0,2},{2,0},{4,6},{6,4},{8,10},{10,8},{12,14},{14,12},{16,18},{18,... | collective-permute-start | bytes 5505032 | tf_op jit(solution)/shard_map/ppermute | solution.py:684
  419.0 37.1 %collective-permute-start.17 = (f32[2,64,2048]{2,1,0:T(8,128)}, f32[2,64,2048]{2,1,0:T(8,128)}, u32[]{:S(2)}, u32[]{:S(2)}) collective-permute-start(f32[2,64,2048]{2,1,0:T(8,128)} %get-tuple-element.263), channel_id=1, source_target_pairs={{0,8},{2,10},{4,12},{6,14},{8,0},{10,2},{12,4},{14,6},{16,24},{18,... | collective-permute-start | bytes 3145736 | tf_op jit(solution)/shard_map/ppermute | solution.py:684
  419.4 39.0 %collective-permute-start.16 = (f32[8,64,512]{2,1,0:T(8,128)}, f32[8,64,512]{2,1,0:T(8,128)}, u32[]{:S(2)}, u32[]{:S(2)}) collective-permute-start(f32[8,64,512]{2,1,0:T(8,128)} %get-tuple-element.257), channel_id=1, source_target_pairs={{0,2},{2,0},{4,6},{6,4},{8,10},{10,8},{12,14},{14,12},{16,18},{18,... | collective-permute-start | bytes 3145736 | tf_op jit(solution)/shard_map/ppermute | solution.py:684
  419.6 34.4 %collective-permute-start.21 = (f32[64,2048]{1,0:T(8,128)}, f32[64,2048]{1,0:T(8,128)}, u32[]{:S(2)}, u32[]{:S(2)}) collective-permute-start(f32[64,2048]{1,0:T(8,128)} %get-tuple-element.275), channel_id=1, source_target_pairs={{0,16},{2,18},{4,20},{6,22},{8,24},{10,26},{12,28},{14,30},{16,0},... | collective-permute-start | bytes 1572872 | tf_op jit(solution)/shard_map/ppermute | solution.py:684
  465.1 26.8 %copy-start.23 = (f32[64,2048]{1,0:T(8,128)S(1)}, f32[64,2048]{1,0:T(8,128)}, u32[]{:S(2)}) copy-start(f32[64,2048]{1,0:T(8,128)} %get-tuple-element.287) | copy-start | bytes 1572868
  465.1 26.7 %collective-permute-start.25 = (f32[64,2048]{1,0:T(8,128)}, f32[64,2048]{1,0:T(8,128)S(1)}, u32[]{:S(2)}, u32[]{:S(2)}) collective-permute-start(f32[64,2048]{1,0:T(8,128)} %get-tuple-element.288), channel_id=1, source_target_pairs={{0,16},{2,18},{4,20},{6,22},{8,24},{10,26},{12,28},{14,30},{16,0},... | collective-permute-start | bytes 1572872 | tf_op jit(solution)/shard_map/ppermute | solution.py:684
  468.6 26.1 %collective-permute-start.24 = (f32[2,64,1152]{2,1,0:T(8,128)}, f32[2,64,1152]{2,1,0:T(8,128)}, u32[]{:S(2)}, u32[]{:S(2)}) collective-permute-start(f32[2,64,1152]{2,1,0:T(8,128)} %get-tuple-element.286), channel_id=1, source_target_pairs={{0,8},{2,10},{4,12},{6,14},{8,0},{10,2},{12,4},{14,6},{16,24},{18,... | collective-permute-start | bytes 1769480 | tf_op jit(solution)/shard_map/ppermute | solution.py:684
  469.9 22.8 %collective-permute-start.20 = (f32[4,64,512]{2,1,0:T(8,128)}, f32[4,64,512]{2,1,0:T(8,128)}, u32[]{:S(2)}, u32[]{:S(2)}) collective-permute-start(f32[4,64,512]{2,1,0:T(8,128)} %get-tuple-element.273), channel_id=1, source_target_pairs={{0,4},{2,6},{4,0},{6,2},{8,12},{10,14},{12,8},{14,10},{16,20},{18,... | collective-permute-start | bytes 1572872 | tf_op jit(solution)/shard_map/ppermute | solution.py:684
  470.4 42.5 %collective-permute-start.19 = (f32[4,64,896]{2,1,0:T(8,128)}, f32[4,64,896]{2,1,0:T(8,128)}, u32[]{:S(2)}, u32[]{:S(2)}) collective-permute-start(f32[4,64,896]{2,1,0:T(8,128)} %get-tuple-element.271), channel_id=1, source_target_pairs={{0,8},{2,10},{4,12},{6,14},{8,0},{10,2},{12,4},{14,6},{16,24},{18,... | collective-permute-start | bytes 2752520 | tf_op jit(solution)/shard_map/ppermute | solution.py:684
  485.8 27.1 %copy-start.32 = (f32[4,64,896]{2,1,0:T(8,128)S(1)}, f32[4,64,896]{2,1,0:T(8,128)}, u32[]{:S(2)}) copy-start(f32[4,64,896]{2,1,0:T(8,128)} %get-tuple-element.270) | copy-start | bytes 2752516
  514.2 16.8 %collective-permute-start.23 = (f32[2,64,512]{2,1,0:T(8,128)}, f32[2,64,512]{2,1,0:T(8,128)}, u32[]{:S(2)}, u32[]{:S(2)}) collective-permute-start(f32[2,64,512]{2,1,0:T(8,128)} %get-tuple-element.284), channel_id=1, source_target_pairs={{0,8},{2,10},{4,12},{6,14},{8,0},{10,2},{12,4},{14,6},{16,24},{18,... | collective-permute-start | bytes 786440 | tf_op jit(solution)/shard_map/ppermute | solution.py:684
  516.0 16.6 %collective-permute-start.22 = (f32[2,64,896]{2,1,0:T(8,128)S(1)}, f32[2,64,896]{2,1,0:T(8,128)}, u32[]{:S(2)}, u32[]{:S(2)}) collective-permute-start(f32[2,64,896]{2,1,0:T(8,128)S(1)} %get-tuple-element.282), channel_id=1, source_target_pairs={{0,4},{2,6},{4,0},{6,2},{8,12},{10,14},{12,8},{14,10},{16,20},{18,... | collective-permute-start | bytes 1376264 | tf_op jit(solution)/shard_map/ppermute | solution.py:684
  547.8 5.6 collective-permute-start.28
  547.8 5.6 collective-permute-start.29
  548.3 51.9 %collective-permute-start.26 = (f32[576,512]{1,0:T(8,128)}, f32[576,512]{1,0:T(8,128)}, u32[]{:S(2)}, u32[]{:S(2)}) collective-permute-start(f32[576,512]{1,0:T(8,128)} %get-tuple-element.294), channel_id=1, source_target_pairs={{0,1},{1,0},{2,3},{3,2},{4,5},{5,4},{6,7},{7,6},{8,9},{9,8},{10,11... | collective-permute-start | bytes 3538952 | tf_op jit(solution)/shard_map/ppermute | solution.py:766
  560.0 37.3 %collective-permute-start.30 = (f32[4,64,896]{2,1,0:T(8,128)}, f32[4,64,896]{2,1,0:T(8,128)S(1)}, u32[]{:S(2)}, u32[]{:S(2)}) collective-permute-start(f32[4,64,896]{2,1,0:T(8,128)} %get-tuple-element.302), channel_id=1, source_target_pairs={{0,4},{2,6},{4,0},{6,2},{8,12},{10,14},{12,8},{14,10},{16,20},{18,... | collective-permute-start | bytes 2752520 | tf_op jit(solution)/shard_map/ppermute | solution.py:684
  561.6 34.1 %collective-permute-start.33 = (f32[64,1152]{1,0:T(8,128)}, f32[64,1152]{1,0:T(8,128)S(1)}, u32[]{:S(2)}, u32[]{:S(2)}) collective-permute-start(f32[64,1152]{1,0:T(8,128)} %get-tuple-element.304), channel_id=1, source_target_pairs={{0,16},{2,18},{4,20},{6,22},{8,24},{10,26},{12,28},{14,30},{16,0},... | collective-permute-start | bytes 884744 | tf_op jit(solution)/shard_map/ppermute | solution.py:684
  565.4 29.5 %collective-permute-start.27 = (f32[64,896]{1,0:T(8,128)}, f32[64,896]{1,0:T(8,128)S(1)}, u32[]{:S(2)}, u32[]{:S(2)}) collective-permute-start(f32[64,896]{1,0:T(8,128)} %get-tuple-element.297), channel_id=1, source_target_pairs={{0,16},{2,18},{4,20},{6,22},{8,24},{10,26},{12,28},{14,30},{16,0},... | collective-permute-start | bytes 688136 | tf_op jit(solution)/shard_map/ppermute | solution.py:684
  565.4 28.8 %collective-permute-start.37 = (f32[64,512]{1,0:T(8,128)}, f32[64,512]{1,0:T(8,128)S(1)}, u32[]{:S(2)}, u32[]{:S(2)}) collective-permute-start(f32[64,512]{1,0:T(8,128)} %get-tuple-element.308), channel_id=1, source_target_pairs={{0,16},{2,18},{4,20},{6,22},{8,24},{10,26},{12,28},{14,30},{16,0},... | collective-permute-start | bytes 393224 | tf_op jit(solution)/shard_map/ppermute | solution.py:684
  568.3 29.0 %copy-start.28 = (f32[4,64,896]{2,1,0:T(8,128)S(1)}, f32[4,64,896]{2,1,0:T(8,128)}, u32[]{:S(2)}) copy-start(f32[4,64,896]{2,1,0:T(8,128)} %get-tuple-element.301) | copy-start | bytes 2752516
  595.7 15.9 %collective-permute-start.34 = (f32[4,64,512]{2,1,0:T(8,128)}, f32[4,64,512]{2,1,0:T(8,128)}, u32[]{:S(2)}, u32[]{:S(2)}) collective-permute-start(f32[4,64,512]{2,1,0:T(8,128)} %get-tuple-element.306), channel_id=1, source_target_pairs={{0,8},{2,10},{4,12},{6,14},{8,0},{10,2},{12,4},{14,6},{16,24},{18,... | collective-permute-start | bytes 1572872 | tf_op jit(solution)/shard_map/ppermute | solution.py:684
  598.2 21.6 %collective-permute-start.31 = (f32[2,64,896]{2,1,0:T(8,128)}, f32[2,64,896]{2,1,0:T(8,128)}, u32[]{:S(2)}, u32[]{:S(2)}) collective-permute-start(f32[2,64,896]{2,1,0:T(8,128)} %fusion.33), channel_id=1, source_target_pairs={{0,8},{2,10},{4,12},{6,14},{8,0},{10,2},{12,4},{14,6},{16,24},{18,... | collective-permute-start | bytes 1376264 | tf_op jit(solution)/shard_map/ppermute | solution.py:684
  612.8 9.5 %collective-permute-start.35 = (f32[2,64,512]{2,1,0:T(8,128)S(1)}, f32[2,64,512]{2,1,0:T(8,128)S(1)}, u32[]{:S(2)}, u32[]{:S(2)}) collective-permute-start(f32[2,64,512]{2,1,0:T(8,128)S(1)} %fusion.36), channel_id=1, source_target_pairs={{0,4},{2,6},{4,0},{6,2},{8,12},{10,14},{12,8},{14,10},{16,20},{18,... | collective-permute-start | bytes 786440 | tf_op jit(solution)/shard_map/ppermute | solution.py:684
  620.8 15.5 %collective-permute-start.32 = (f32[64,896]{1,0:T(8,128)S(1)}, f32[64,896]{1,0:T(8,128)S(1)}, u32[]{:S(2)}, u32[]{:S(2)}) collective-permute-start(f32[64,896]{1,0:T(8,128)S(1)} %fusion.39), channel_id=1, source_target_pairs={{0,16},{2,18},{4,20},{6,22},{8,24},{10,26},{12,28},{14,30},{16,0},... | collective-permute-start | bytes 688136 | tf_op jit(solution)/shard_map/ppermute | solution.py:684
  622.3 17.4 %collective-permute-start.36 = (f32[64,512]{1,0:T(8,128)S(1)}, f32[64,512]{1,0:T(8,128)S(1)}, u32[]{:S(2)}, u32[]{:S(2)}) collective-permute-start(f32[64,512]{1,0:T(8,128)S(1)} %fusion.40), channel_id=1, source_target_pairs={{0,16},{2,18},{4,20},{6,22},{8,24},{10,26},{12,28},{14,30},{16,0},... | collective-permute-start | bytes 393224 | tf_op jit(solution)/shard_map/ppermute | solution.py:684
  638.2 4.2 collective-permute-start.38
  (47 other events, 324.8 us)

commit v5 on v4

--- a/solution.py
+++ b/solution.py
@@ -482,7 +482,7 @@
             pltpu.VMEM((2, rows, lanes), bf16),
         ],
         compiler_params=pltpu.CompilerParams(vmem_limit_bytes=VMEM_CAP),
-        cost_estimate=pl.CostEstimate(flops=10**10, bytes_accessed=12000000, transcendentals=0),
+        cost_estimate=pl.CostEstimate(flops=10**6, bytes_accessed=10**4, transcendentals=0),
         name="attention_draw",
     )(share, upstream, qkv, qkv, qkv, *adds)
 
@@ -500,7 +500,7 @@
         ],
         out_specs=pl.BlockSpec((8, high, 3 * REL), lambda g: (g, 0, 0)),
         compiler_params=pltpu.CompilerParams(vmem_limit_bytes=VMEM_CAP),
-        cost_estimate=pl.CostEstimate(flops=5 * 10**9 * count, bytes_accessed=10**6 * count, transcendentals=0),
+        cost_estimate=pl.CostEstimate(flops=10**6, bytes_accessed=10**4, transcendentals=0),
         name="attention_scatter",
     )(*backs, buckets, merge)
 
@@ -695,6 +695,7 @@
         self.pick = jnp.stack([mine] + [bit_of(index, bits[0]).astype(jnp.int32) for bits in orders])
         self.other = self.pick.at[0].set(1 - mine)
         self.stage = 0
+        self.extra = None
 
     def work(self):
         if self.stage == 0:
@@ -755,6 +756,10 @@
 
 
 def tie(values, *chains):
+    chains = [chain for chain in chains if not chain.over()]
+    values, extras = lax.optimization_barrier((values, [chain.extra for chain in chains]))
+    for chain, extra in zip(chains, extras):
+        chain.extra = extra
     works = [chain.work() for chain in chains]
     values, works = lax.optimization_barrier((values, works))
     for chain, parts in zip(chains, works):
@@ -764,31 +769,6 @@
 
 def swap(value):
     return lax.ppermute(value.astype(f32), "mp", [(0, 1), (1, 0)])
-
-
-def join_kernel(head_ref, rest_ref, early_ref, early_other_ref, mine_ref, w_ref, other_ref, ow_ref, out_ref, *, span):
-    weight = ow_ref[...].astype(bf16)
-    split = head_ref.shape[0]
-    for start in range(0, span, 64):
-        tall = min(64, span - start)
-        at = slice(start, start + 64)
-        base = head_ref[at, :] if start < split else rest_ref[start - split:start - split + 64, :]
-        total = base + early_ref[at, :] + early_other_ref[at, :] + nt(mine_ref[at, :], w_ref[...])
-        total = total + nt(other_ref[at, :].astype(bf16), weight)
-        out_ref[start:start + tall, :] = total.astype(bf16)[:tall]
-
-
-def join(bases, early, early_other, mine, weight, other, other_weight, span):
-    whole = pl.BlockSpec(memory_space=pltpu.VMEM)
-    return pl.pallas_call(
-        functools.partial(join_kernel, span=span),
-        in_specs=[whole] * 8,
-        out_specs=whole,
-        out_shape=jax.ShapeDtypeStruct((span, early.shape[1]), bf16),
-        compiler_params=pltpu.CompilerParams(vmem_limit_bytes=VMEM_CAP),
-        cost_estimate=pl.CostEstimate(flops=3 * 10**9, bytes_accessed=12 * 10**6, transcendentals=0),
-        name="join",
-    )(*bases, early, early_other, mine, weight, other, other_weight)
 
 
 def attend_kernel(
@@ -942,6 +922,7 @@
     backs_part, down_pair, up_pair = lax.optimization_barrier(
         (backs_part, (seconds_low, hiddens), (firsts_low, upwards_back))
     )
+    up_pair, backs_other[0] = lax.optimization_barrier((up_pair, backs_other[0]))
     down_chain = chain(
         lambda pick, add: weight_half(pick, *down_pair, add, parts=size, bits=high_first), high_first
     )
@@ -950,26 +931,26 @@
     )
     down_chain.step()
     up_chain.step()
-    down_chain.step()
-    backs_other[1] = tie(backs_other[1], up_chain)
-    residuals_back, residuals_low, contexts_back, one_sums = ([] for _ in range(4))
-    for n in range(2):
+    backs_other[0] = tie(backs_other[0], down_chain)
+    backs_other[0] = tie(backs_other[0], up_chain)
+    merge = merge_table()
+    residuals_back, residuals_low, one_sums = [], [], []
+
+    def draw(n, adds=()):
         residual_back, *sums = norm_backward(
             seconds_back[n] + backs_part[n] + backs_other[n], normals_one[n], inverses_one[n], gain_one
         )
         one_sums.append(sums)
         residuals_back.append(residual_back)
         residuals_low.append(residual_back.astype(bf16))
-        contexts_back.append(nt(residuals_low[n], output_weight).astype(bf16))
+        context_back = nt(residuals_low[n], output_weight).astype(bf16)
+        return attention_draw(shares[n], context_back, qkv, score_scale, edges[n][0], rows, adds)
+
+    back_head, turned_head, query_head, key_head, value_head = draw(0)
+    back_head, key_head, backs_other[1] = lax.optimization_barrier((back_head, key_head, backs_other[1]))
+    back_rest, turned_rest, query_rest, key_base, value_back = draw(1, (key_head, value_head))
     gain_one_grad, shift_one_grad = (one_sums[0][n] + one_sums[1][n] for n in range(2))
-
-    merge = merge_table()
-    back_head, turned_head, query_head, key_head, value_head = attention_draw(
-        shares[0], contexts_back[0], qkv, score_scale, 0, rows
-    )
-    back_rest, turned_rest, query_rest, key_base, value_back = attention_draw(
-        shares[1], contexts_back[1], qkv, score_scale, split, rows, (key_head, value_head)
-    )
+    back_rest, value_back = tie((back_rest, value_back), down_chain)
     query_base = jnp.concatenate([query_head, query_rest], axis=0)
     residual_low = jnp.concatenate(residuals_low, axis=0)
     context = jnp.concatenate(contexts, axis=0)
@@ -1004,34 +985,31 @@
         )
 
     near = []
+    blocks = rows // 64
+    back_head, back_rest = tie((back_head, back_rest), up_chain)
     near.append(attention_scatter([back_head], bucket_head, merge, 0, split // 64))
-    back_rest, near, key_wide = tie((back_rest, near, key_weight.astype(f32)), outer_chain, down_chain)
-    other_key_weight = swap(key_wide)
-    near.append(attention_scatter([back_rest], bucket_rest, merge, 0, (rows - split) // 64))
-    near, backs, other_key_weight = tie((near, [turned_head, turned_rest], other_key_weight), up_chain)
+    back_rest, near = tie((back_rest, near), down_chain)
+    back_rest, near = tie((back_rest, near), outer_chain)
+    near.append(attention_scatter([back_rest], bucket_rest, merge, 0, blocks - split // 64))
+    near, backs = tie((near, [turned_head, turned_rest]), up_chain)
     query_back, key_table_sum = attention_close(near, query_base, pos_key, qkv, 0)
     query_low = query_back.astype(bf16)
     early = nt(query_low, query_weight) + nt(value_back, value_weight)
-    early_other = swap(early)
     near_chain = tail(query_low, key_table_sum, key_position, [high_first, low_first])
-    backs = tie(backs, near_chain, down_chain)
+    backs, key_table_sum = tie((backs, key_table_sum), near_chain, outer_chain, down_chain)
     far = []
-    blocks = rows // 64
     cuts = [n * blocks // 3 for n in range(4)]
-    for part, chains in enumerate((
-        (near_chain, up_chain, outer_chain), (near_chain, down_chain), (near_chain, outer_chain, up_chain, down_chain),
-    )):
+    for part, chains in enumerate(((near_chain,), (outer_chain, up_chain), (near_chain, outer_chain))):
         far.append(attention_scatter(backs, bucket_cols, merge, cuts[part], cuts[part + 1] - cuts[part]))
-        backs, far, early_other = tie((backs, far, early_other), *[c for c in chains if not c.over()])
+        backs, far = tie((backs, far), *chains)
     key_back, query_table_sum = attention_close(far, key_base, pos_query, qkv, 1)
-    key_other = swap(key_back)
     key_low = key_back.astype(bf16)
+    input_part = early + nt(key_low, key_weight)
+    input_other = swap(input_part)
     far_chain = tail(key_low, query_table_sum, query_position, [low_first, high_first])
     far_chain.step()
     far_chain.step()
-    input_gradient = join(
-        residuals_back, early, early_other, key_low, key_weight, key_other, other_key_weight, span
-    )
+    input_gradient = (jnp.concatenate(residuals_back, axis=0) + input_part + input_other)[:span].astype(bf16)
     (down_share,) = down_chain.finish()
     (up_share,) = up_chain.finish()
     (outer_share,) = outer_chain.finish()

time: 653 us -> 550 us (0.84)
  waiting for transfers between devices: 173 us -> 82.9 us
  Pallas kernels: 301 us -> 289 us
    ppermute x28, waiting for transfers between devices: 108 us -> 38.3 us  [flipped(): return lax.ppermute(value, 'dp', [(i, i ^ 1 << bit) for i in range(size)])]
    ppermute x10 -> x8, waiting for transfers between devices: 63.2 us -> 43.4 us  [swap(): return lax.ppermute(value.astype(f32), 'mp', [(0, 1), (1, 0)])]
    pallas_call x1 -> x0, Pallas kernels: 11.4 us -> none  [join(): pl.pallas_call(functools.partial(join_kernel, span=span), in_specs=[whole...]
    dot_general x8 -> x9, matrix products: 14.8 us -> 18.7 us  [nt(): lax.dot_general(left, right, (((1,), (1,)), ((), ())), preferred_element_...]
    add x12 -> x10, other arithmetic: 22.8 us -> 19.5 us  [split(): half(held, own) + half(extra, own)]
  transfers between devices with their start and end apart: 39 -> 37, of which waited for: 13 -> 12; matrix products, arithmetic and copies ran while one was open for 16% -> 20% of each run, Pallas kernels for 43% -> 51%
where the time goes in v5:
time: 550 us; the launch traced here: 540 us
  Pallas kernels  289 us (53%)
  waiting for transfers between devices  82.9 us (15%)
  other arithmetic  66.2 us (12%)
  starting transfers between devices  39.7 us (7%)
  matrix products  39.6 us (7%)
  local copies, waits for them, and re-layouts  20.1 us (4%)
    pallas_call x5, Pallas kernels, attention_scatter(): pl.pallas_call(functools.partial(scatter_kernel, groups=8, cols=cols), gr...  85.8 us
    pallas_call x1, Pallas kernels, attention_head(): pl.pallas_call(kernel, out_shape=(jax.ShapeDtypeStruct((2 * pairs, split,...  49.8 us
    ppermute x8, waiting for transfers between devices, swap(): return lax.ppermute(value.astype(f32), 'mp', [(0, 1), (1, 0)])  43.4 us
    ppermute x28, waiting for transfers between devices, flipped(): return lax.ppermute(value, 'dp', [(i, i ^ 1 << bit) for i in range(size)])  38.3 us
    pallas_call x6, Pallas kernels, many_half(): pl.pallas_call(functools.partial(many_kernel, plan=plan, widths=widths, t...  37.3 us
    pallas_call x4, Pallas kernels, weight_half(): pl.pallas_call(functools.partial(weight_kernel, count=len(xs), blocks=blo...  30.9 us
    ppermute x28, starting transfers between devices, flipped(): return lax.ppermute(value, 'dp', [(i, i ^ 1 << bit) for i in range(size)])  28.8 us
    pallas_call x1, Pallas kernels, attention_rest(): pl.pallas_call(kernel, out_shape=(jax.ShapeDtypeStruct((2 * pairs, rows -...  25.9 us
  transfers between devices with their start and end apart: 37, of which 12 were waited for; matrix products, arithmetic and copies ran while one was open for 20% of the time, Pallas kernels for 51%

profile of v5, /device:TPU:0, one launch (start us, length us, event | category | flops | bytes accessed | tf_op | source)
XLA Modules:
  0.0 540.3 jit_solution(11091847791512466298)
XLA Ops:
  0.6 2.9 convert_element_type.73
  3.5 3.0 collective-permute-start.1
  7.1 4.6 copy.60.b_ref
  11.7 9.3 %project.1 = (bf16[640,1536]{1,0:T(8,128)(2,1)}, bf16[384,512]{1,0:T(8,128)(2,1)}, bf16[384,512]{1,0:T(8,128)(2,1)}) custom-call(bf16[561,1024]{1,0:T(8,128)(2,1)} %x_ref.1, bf16[1024,512]{1,0:T(8,128)(2,1)} %wq_ref.1, bf16[1024,512]{1,0:T(8,128)(2,1)} %wk_ref.1, bf16[1024,512]{1,0:T(8,128)(2,1)} %wv_ref.1, bf16[3,128,1024]{2,1,0:T(8,128)(2,1)} %t_ref.1, ...), custom_call_target="tpu_custom_call" | custom-call | flops 4000000000 | bytes 9000000 | tf_op jit(solution)/shard_map/project/pallas_call | solution.py:226
  21.0 49.8 %attention_head.1 = (bf16[8,256,640]{2,1,0:T(8,128)(2,1)}, bf16[256,512]{1,0:T(8,128)(2,1)}, s32[3,256,640]{2,1,0:T(8,128)}, s32[3,320,640]{2,1,0:T(8,128)}, s32...) custom-call(s32[1]{0:T(128)S(6)} %copy.120.used_ref, ...), custom_call_target="tpu_custom_call" | custom-call | flops 40000000000 | bytes 25000000 | tf_op jit(solution)/shard_map/attention_head/pallas_call | solution.py:396
  75.8 25.9 %attention_rest.1 = (bf16[8,320,640]{2,1,0:T(8,128)(2,1)}, bf16[320,512]{1,0:T(8,128)(2,1)}) custom-call(s32[1]{0:T(128)S(6)} %copy.120.used_ref, bf16[640,1536]{1,0:T(8,128)(2,1)} %get-tuple-element.242.qkv_ref.q_ref.k_ref.v_ref.refs_4_.refs_5_, bf16[384,512]{1,0:T(8,128)(2,1)} %get-tuple-element.243.pk_ref.refs_3_, ...), custom_call_target="tpu_custom_call" | custom-call | flops 20000000000 | bytes 12000000 | tf_op jit(solution)/shard_map/attention_rest/pallas_call | solution.py:433
  104.9 6.7 %attend.2 = (f32[256,1024]{1,0:T(8,128)}, bf16[256,1024]{1,0:T(8,128)(2,1)}, f32[256,1024]{1,0:T(8,128)}, f32[256,1]{1,0:T(8,128)}) custom-call(bf16[256,1024]{1,0:T(8,128)(2,1)} %slice.101.t_ref, bf16[256,512]{1,0:T(8,128)(2,1)} %get-tuple-element.245.c_ref, f32[256,512]{1,0:T(8,128)} %collective-permute-done.o_ref, bf16[512,1024]{1,0:T(8,128)(2,1)} %w_ref.3, ...), custom_call_target="tpu_custom_call" | custom-call | flops 2000000000 | bytes 8000000 | tf_op jit(solution)/shard_map/attend/pallas_call | solution.py:796
  111.6 8.8 %multiply_convert_fusion.1 = (bf16[256,2048]{1,0:T(8,128)(2,1)S(1)}, f32[256,2048]{1,0:T(8,128)}, f32[256,2048]{1,0:T(8,128)}) fusion(bf16[256,1024]{1,0:T(8,128)(2,1)} %get-tuple-element.272.refs_0_, bf16[1024,2048]{1,0:T(8,128)(2,1)} %param.37), kind=kOutput, calls=%fused_computation.25 | convolution fusion | flops 1107820544 | bytes 9961472 | tf_op jit(solution)/shard_map/dot_general | solution.py:39
  121.9 7.8 %attend.3 = (f32[320,1024]{1,0:T(8,128)}, bf16[320,1024]{1,0:T(8,128)(2,1)}, f32[320,1024]{1,0:T(8,128)}, f32[320,1]{1,0:T(8,128)}) custom-call(bf16[320,1024]{1,0:T(8,128)(2,1)} %copy.62.t_ref, bf16[320,512]{1,0:T(8,128)(2,1)} %get-tuple-element.253.c_ref, f32[320,512]{1,0:T(8,128)} %collective-permute-done.3.o_ref, bf16[512,1024]{1,0:T(8,128)(2,1)} %w_ref.3, ...), custom_call_target="tpu_custom_call" | custom-call | flops 2000000000 | bytes 8000000 | tf_op jit(solution)/shard_map/attend/pallas_call | solution.py:796
  129.7 9.3 %multiply_convert_fusion = (bf16[320,2048]{1,0:T(8,128)(2,1)S(1)}, f32[320,2048]{1,0:T(8,128)S(1)}, f32[320,2048]{1,0:T(8,128)S(1)}) fusion(bf16[320,1024]{1,0:T(8,128)(2,1)} %get-tuple-element.273.refs_1_, bf16[1024,2048]{1,0:T(8,128)(2,1)} %param.37), kind=kOutput, calls=%fused_computation.4 | convolution fusion | flops 1384775680 | bytes 11403264 | tf_op jit(solution)/shard_map/dot_general | solution.py:39
  142.5 5.4 collective-permute-done.2
  157.1 18.8 %collective-permute-done.4 = f32[320,1024]{1,0:T(8,128)S(1)} collective-permute-done((f32[320,1024]{1,0:T(8,128)S(1)}, f32[320,1024]{1,0:T(8,128)S(1)}, u32[]{:S(2)}, u32[]{:S(2)}) %collective-permute-start.4) | collective-permute-done | bytes 1310752 | tf_op jit(solution)/shard_map/ppermute | solution.py:771
  181.2 2.6 fusion.54
  183.8 7.4 %weight_half.4 = f32[8,64,2048]{2,1,0:T(8,128)} custom-call(s32[2]{0:T(128)} %copy-done.47, bf16[256,1024]{1,0:T(8,128)(2,1)} %copy-done.12, bf16[320,1024]{1,0:T(8,128)(2,1)} %copy-done.6, bf16[256,2048]{1,0:T(8,128)(2,1)} %copy-done.17, bf16[320,2048]{1,0:T(8,128)(2,1)} %copy-done.10), custom_call_target="tpu_custom_call" | custom-call | flops 1207959552 | bytes 8388608 | tf_op jit(solution)/shard_map/weight_half/pallas_call | solution.py:599
  191.2 5.2 collective-permute-done.5
  196.5 7.6 %weight_half.6 = f32[8,64,2048]{2,1,0:T(8,128)} custom-call(s32[2]{0:T(128)} %copy-done.43, bf16[256,1024]{1,0:T(8,128)(2,1)} %get-tuple-element.272.refs_0_, bf16[320,1024]{1,0:T(8,128)(2,1)} %get-tuple-element.273.refs_1_, bf16[256,2048]{1,0:T(8,128)(2,1)} %copy-done.18, bf16[320,2048]{1,0:T(8,128)(2,1)} %copy-done.11), custom_call_target="tpu_custom_call" | custom-call | flops 1207959552 | bytes 8388608 | tf_op jit(solution)/shard_map/weight_half/pallas_call | solution.py:599
  204.1 2.6 pad_bitcast_fusion.refs_2_.refs_0_
  207.5 8.0 %weight_half.5 = (f32[4,64,2048]{2,1,0:T(8,128)}, f32[4,64,2048]{2,1,0:T(8,128)}) custom-call(s32[2]{0:T(128)} %copy-done.46, bf16[256,1024]{1,0:T(8,128)(2,1)} %copy-done.12, bf16[320,1024]{1,0:T(8,128)(2,1)} %copy-done.6, bf16[256,2048]{1,0:T(8,128)(2,1)} %copy-done.17, bf16[320,2048]{1,0:T(8,128)(2,1)} %copy-done.10, ...), custom_call_target="tpu_custom_call" | custom-call | flops 1207959552 | bytes 8388608 | tf_op jit(solution)/shard_map/weight_half/pallas_call | solution.py:599
  217.3 7.9 %weight_half.7 = (f32[4,64,2048]{2,1,0:T(8,128)}, f32[4,64,2048]{2,1,0:T(8,128)}) custom-call(s32[2]{0:T(128)} %copy-done.42, bf16[256,1024]{1,0:T(8,128)(2,1)} %get-tuple-element.272.refs_0_, bf16[320,1024]{1,0:T(8,128)(2,1)} %get-tuple-element.273.refs_1_, bf16[256,2048]{1,0:T(8,128)(2,1)} %copy-done.18, bf16[320,2048]{1,0:T(8,128)(2,1)} %copy-done.11, ...), custom_call_target="tpu_custom_call" | custom-call | flops 1207959552 | bytes 8388608 | tf_op jit(solution)/shard_map/weight_half/pallas_call | solution.py:599
  225.2 4.1 multiply_reduce_fusion.4
  231.9 11.1 %attention_draw.2 = (bf16[32,64,640]{2,1,0:T(8,128)(2,1)}, bf16[72,64,256]{2,1,0:T(8,128)(2,1)}, f32[256,512]{1,0:T(8,128)}, f32[576,512]{1,0:T(8,128)}, f32[576,512]{1,0:T(8,128)}) custom-call(bf16[8,256,640]{2,1,0:T(8,128)(2,1)} %get-tuple-element.284.p_ref, bf16[256,512]{1,0:T(8,128)(2,1)} %convolution_convert_fusion.1.up_ref, ...), custom_call_target="tpu_custom_call" | custom-call | flops 1000000 | bytes 10000 | tf_op jit(solution)/shard_map/attention_draw/pallas_call | solution.py:457
  244.6 4.6 multiply_reduce_fusion
  250.7 2.8 fusion.45
  254.8 13.8 %attention_draw.3 = (bf16[40,64,640]{2,1,0:T(8,128)(2,1)}, bf16[72,64,384]{2,1,0:T(8,128)(2,1)}, f32[320,512]{1,0:T(8,128)}, f32[576,512]{1,0:T(8,128)}, bf16[576,512]{1,0:T(8,128)(2,1)}) custom-call(bf16[8,320,640]{2,1,0:T(8,128)(2,1)} %get-tuple-element.290.p_ref, bf16[320,512]{1,0:T(8,128)(2,1)} %convolution_convert_fusion.up_ref, ...), custom_call_target="tpu_custom_call" | custom-call | flops 1000000 | bytes 10000 | tf_op jit(solution)/shard_map/attention_draw/pallas_call | solution.py:457
  270.7 3.2 fusion.29
  274.4 5.8 %many_half.6 = f32[8,64,1152]{2,1,0:T(8,128)} custom-call(s32[2]{0:T(128)} %copy-done.43, bf16[576,1024]{1,0:T(8,128)(2,1)} %pad_maximum_fusion.1.refs_0_, bf16[576,512]{1,0:T(8,128)(2,1)} %copy-done.19, bf16[1024,576]{1,0:T(8,128)(2,1)} %pad_bitcast_fusion.refs_2_.refs_0_, bf16[576,512]{1,0:T(8,128)(2,1)} %get-tuple-element.316.refs_3_, ...), custom_call_target="tpu_custom_call" | custom-call | flops 707788800 | bytes 7077888 | tf_op jit(solution)/shard_map/many_half/pallas_call | solution.py:663
  280.8 11.1 %collective-permute-done.10 = f32[4,64,2048]{2,1,0:T(8,128)} collective-permute-done((f32[4,64,2048]{2,1,0:T(8,128)}, f32[4,64,2048]{2,1,0:T(8,128)}, u32[]{:S(2)}, u32[]{:S(2)}) %collective-permute-start.10) | collective-permute-done | bytes 2097184 | tf_op jit(solution)/shard_map/ppermute | solution.py:684
  291.9 3.5 fusion.27
  296.6 18.7 %attention_scatter.5.refs_0_ = bf16[32,64,384]{2,1,0:T(8,128)(2,1)} custom-call(bf16[32,64,640]{2,1,0:T(8,128)(2,1)} %get-tuple-element.307.refs_0_, s32[3,256,640]{2,1,0:T(8,128)} %get-tuple-element.308.refs_1_, bf16[4,256,128]{2,1,0:T(8,128)(2,1)} %fusion.33.refs_2_.refs_3_), custom_call_target="tpu_custom_call" | custom-call | flops 1000000 | bytes 10000 | tf_op jit(solution)/shard_map/attention_scatter/pallas_call | solution.py:493
  315.3 2.7 add_bitcast_fusion.2
  318.1 6.6 %many_half.7 = (f32[4,64,1152]{2,1,0:T(8,128)}, f32[4,64,1152]{2,1,0:T(8,128)}) custom-call(s32[2]{0:T(128)} %copy-done.42, bf16[576,1024]{1,0:T(8,128)(2,1)} %pad_maximum_fusion.1.refs_0_, bf16[576,512]{1,0:T(8,128)(2,1)} %copy-done.19, bf16[1024,576]{1,0:T(8,128)(2,1)} %pad_bitcast_fusion.refs_2_.refs_0_, bf16[576,512]{1,0:T(8,128)(2,1)} %get-tuple-element.316.refs_3_, ...), custom_call_target="tpu_custom_call" | custom-call | flops 707788800 | bytes 7077888 | tf_op jit(solution)/shard_map/many_half/pallas_call | solution.py:663
  332.6 22.9 %attention_scatter.6.refs_1_ = bf16[40,64,384]{2,1,0:T(8,128)(2,1)} custom-call(bf16[40,64,640]{2,1,0:T(8,128)(2,1)} %get-tuple-element.323.refs_0_, s32[3,320,640]{2,1,0:T(8,128)} %get-tuple-element.250.b_ref.refs_1_, bf16[4,256,128]{2,1,0:T(8,128)(2,1)} %fusion.33.refs_2_.refs_3_), custom_call_target="tpu_custom_call" | custom-call | flops 1000000 | bytes 10000 | tf_op jit(solution)/shard_map/attention_scatter/pallas_call | solution.py:493
  357.7 5.4 %attention_close.2 = (f32[576,512]{1,0:T(8,128)}, bf16[384,512]{1,0:T(8,128)(2,1)}) custom-call(bf16[32,64,384]{2,1,0:T(8,128)(2,1)} %attention_scatter.5.refs_0_, bf16[40,64,384]{2,1,0:T(8,128)(2,1)} %attention_scatter.6.refs_1_, f32[576,512]{1,0:T(8,128)} %pad_maximum_fusion.2.refs_2_, bf16[384,512]{1,0:T(8,128)(2,1)} %get-tuple-element.243.pk_ref.refs_3_, ...), custom_call_target="tpu_custom_call" | custom-call | flops 5000000000 | bytes 10000000 | tf_op jit(solution)/shard_map/attention_close/pallas_call | solution.py:511
  365.3 5.8 %many_half.8 = (f32[8,64,896]{2,1,0:T(8,128)}, f32[8,64,512]{2,1,0:T(8,128)}) custom-call(s32[3]{0:T(128)} %copy-done.49, bf16[1024,576]{1,0:T(8,128)(2,1)} %pad_bitcast_fusion.refs_2_.refs_0_, bf16[576,512]{1,0:T(8,128)(2,1)} %convert_element_type.90.refs_1_, bf16[1024,384]{1,0:T(8,128)(2,1)} %bitcast.211, ...), custom_call_target="tpu_custom_call" | custom-call | flops 865075200 | bytes 8650752 | tf_op jit(solution)/shard_map/many_half/pallas_call | solution.py:663
  378.1 14.8 %attention_scatter.7.refs_0_ = bf16[24,64,384]{2,1,0:T(8,128)(2,1)} custom-call(bf16[72,64,256]{2,1,0:T(8,128)(2,1)} %get-tuple-element.378.refs_0_, bf16[72,64,384]{2,1,0:T(8,128)(2,1)} %get-tuple-element.379.refs_1_, s32[3,576,640]{2,1,0:T(8,128)} %get-tuple-element.353.refs_2_, bf16[4,256,128]{2,1,0:T(8,128)(2,1)} %fusion.33.refs_2_.refs_3_), custom_call_target="tpu_custom_call" | custom-call | flops 1000000 | bytes 10000 | tf_op jit(solution)/shard_map/attention_scatter/pallas_call | solution.py:493
  392.9 6.7 %many_half.9 = (f32[4,64,896]{2,1,0:T(8,128)}, f32[4,64,896]{2,1,0:T(8,128)}, f32[4,64,512]{2,1,0:T(8,128)}, f32[4,64,512]{2,1,0:T(8,128)}) custom-call(s32[3]{0:T(128)} %copy-done.45, bf16[1024,576]{1,0:T(8,128)(2,1)} %pad_bitcast_fusion.refs_2_.refs_0_, bf16[576,512]{1,0:T(8,128)(2,1)} %convert_element_type.90.refs_1_, bf16[1024,384]{1,0:T(8,128)(2,1)} %bitcast.212, ...), custom_call_target="tpu_custom_call" | custom-call | flops 865075200 | bytes 8650752 | tf_op jit(solution)/shard_map/many_half/pallas_call | solution.py:663
  400.1 14.7 %attention_scatter.8.refs_1_ = bf16[24,64,384]{2,1,0:T(8,128)(2,1)} custom-call(bf16[72,64,256]{2,1,0:T(8,128)(2,1)} %get-tuple-element.378.refs_0_, bf16[72,64,384]{2,1,0:T(8,128)(2,1)} %get-tuple-element.379.refs_1_, s32[3,576,640]{2,1,0:T(8,128)} %get-tuple-element.353.refs_2_, bf16[4,256,128]{2,1,0:T(8,128)(2,1)} %fusion.33.refs_2_.refs_3_), custom_call_target="tpu_custom_call" | custom-call | flops 1000000 | bytes 10000 | tf_op jit(solution)/shard_map/attention_scatter/pallas_call | solution.py:493
  418.3 2.8 collective-permute-start.22
  423.4 14.6 %attention_scatter.9.refs_2_ = bf16[24,64,384]{2,1,0:T(8,128)(2,1)} custom-call(bf16[72,64,256]{2,1,0:T(8,128)(2,1)} %get-tuple-element.378.refs_0_, bf16[72,64,384]{2,1,0:T(8,128)(2,1)} %get-tuple-element.379.refs_1_, s32[3,576,640]{2,1,0:T(8,128)} %get-tuple-element.353.refs_2_, bf16[4,256,128]{2,1,0:T(8,128)(2,1)} %fusion.33.refs_2_.refs_3_), custom_call_target="tpu_custom_call" | custom-call | flops 1000000 | bytes 10000 | tf_op jit(solution)/shard_map/attention_scatter/pallas_call | solution.py:493
  442.3 5.5 %attention_close.3 = (f32[576,512]{1,0:T(8,128)}, bf16[384,512]{1,0:T(8,128)(2,1)}) custom-call(bf16[24,64,384]{2,1,0:T(8,128)(2,1)} %attention_scatter.7.refs_0_, bf16[24,64,384]{2,1,0:T(8,128)(2,1)} %attention_scatter.8.refs_1_, bf16[24,64,384]{2,1,0:T(8,128)(2,1)} %attention_scatter.9.refs_2_, f32[576,512]{1,0:T(8,128)} %get-tuple-element.397.refs_3_, ...), custom_call_target="tpu_custom_call" | custom-call | flops 5000000000 | bytes 10000000 | tf_op jit(solution)/shard_map/attention_close/pallas_call | solution.py:511
  449.9 5.8 %many_half.10 = (f32[8,64,896]{2,1,0:T(8,128)}, f32[8,64,512]{2,1,0:T(8,128)}) custom-call(s32[3]{0:T(128)} %copy-done.48, bf16[1024,576]{1,0:T(8,128)(2,1)} %pad_bitcast_fusion.refs_2_.refs_0_, bf16[576,512]{1,0:T(8,128)(2,1)} %convert_element_type.91.refs_1_, bf16[1024,384]{1,0:T(8,128)(2,1)} %bitcast.213, ...), custom_call_target="tpu_custom_call" | custom-call | flops 865075200 | bytes 8650752 | tf_op jit(solution)/shard_map/many_half/pallas_call | solution.py:663
  466.9 6.6 %many_half.11 = (f32[4,64,896]{2,1,0:T(8,128)}, f32[4,64,896]{2,1,0:T(8,128)}, f32[4,64,512]{2,1,0:T(8,128)}, f32[4,64,512]{2,1,0:T(8,128)}) custom-call(s32[3]{0:T(128)} %copy-done.44, bf16[1024,576]{1,0:T(8,128)(2,1)} %pad_bitcast_fusion.refs_2_.refs_0_, bf16[576,512]{1,0:T(8,128)(2,1)} %convert_element_type.91.refs_1_, bf16[1024,384]{1,0:T(8,128)(2,1)} %bitcast.214, ...), custom_call_target="tpu_custom_call" | custom-call | flops 865075200 | bytes 8650752 | tf_op jit(solution)/shard_map/many_half/pallas_call | solution.py:663
  479.6 3.8 collective-permute-done.35
  485.0 8.2 %collective-permute-done.25 = f32[64,896]{1,0:T(8,128)S(1)} collective-permute-done((f32[64,896]{1,0:T(8,128)S(1)}, f32[64,896]{1,0:T(8,128)S(1)}, u32[]{:S(2)}, u32[]{:S(2)}) %collective-permute-start.25) | collective-permute-done | bytes 229408 | tf_op jit(solution)/shard_map/ppermute | solution.py:684
  500.1 14.0 %collective-permute-done.23 = f32[576,1024]{1,0:T(8,128)} collective-permute-done((f32[576,1024]{1,0:T(8,128)}, f32[576,1024]{1,0:T(8,128)}, u32[]{:S(2)}, u32[]{:S(2)}) %collective-permute-start.23) | collective-permute-done | bytes 2359328 | tf_op jit(solution)/shard_map/ppermute | solution.py:771
  514.2 4.0 fusion.6
  518.7 2.8 collective-permute-start.33
  521.5 13.5 %collective-permute-done.30 = f32[64,896]{1,0:T(8,128)S(1)} collective-permute-done((f32[64,896]{1,0:T(8,128)S(1)}, f32[64,896]{1,0:T(8,128)S(1)}, u32[]{:S(2)}, u32[]{:S(2)}) %collective-permute-start.30) | collective-permute-done | bytes 229408 | tf_op jit(solution)/shard_map/ppermute | solution.py:684
  (266 shorter events, 104.2 us)
Async XLA Ops:
  3.5 72.2 %collective-permute-start.1 = (f32[512,1024]{1,0:T(8,128)}, f32[512,1024]{1,0:T(8,128)}, u32[]{:S(2)}, u32[]{:S(2)}) collective-permute-start(f32[512,1024]{1,0:T(8,128)} %convert_element_type.73), channel_id=1, source_target_pairs={{0,1},{1,0},{2,3},{3,2},{4,5},{5,4},{6,7},{7,6},{8,9},{9,8},{10,11... | collective-permute-start | bytes 6291464 | tf_op jit(solution)/shard_map/ppermute | solution.py:771
  21.0 51.7 %copy-start.23 = (bf16[561,1024]{1,0:T(8,128)(2,1)S(1)}, bf16[561,1024]{1,0:T(8,128)(2,1)}, u32[]{:S(2)}) copy-start(bf16[561,1024]{1,0:T(8,128)(2,1)} %x_ref.1) | copy-start | bytes 3446788
  72.7 32.2 %collective-permute-start = (f32[256,512]{1,0:T(8,128)}, f32[256,512]{1,0:T(8,128)}, u32[]{:S(2)}, u32[]{:S(2)}) collective-permute-start(f32[256,512]{1,0:T(8,128)} %get-tuple-element.485), channel_id=1, source_target_pairs={{0,1},{1,0},{2,3},{3,2},{4,5},{5,4},{6,7},{7,6},{8,9},{9,8},{10,11... | collective-permute-start | bytes 1572872 | tf_op jit(solution)/shard_map/ppermute | solution.py:771
  75.6 26.0 %copy-start.46 = (s32[2]{0:T(128)}, s32[2]{0:T(128)S(1)}, u32[]{:S(2)}) copy-start(s32[2]{0:T(128)S(1)} %pad_add_fusion.pick_ref) | copy-start | bytes 28
  75.7 25.9 %copy-start.42 = (s32[2]{0:T(128)}, s32[2]{0:T(128)S(1)}, u32[]{:S(2)}) copy-start(s32[2]{0:T(128)S(1)} %pad_add_fusion.1.pick_ref) | copy-start | bytes 28
  75.7 25.9 %copy-start.47 = (s32[2]{0:T(128)}, s32[2]{0:T(128)S(1)}, u32[]{:S(2)}) copy-start(s32[2]{0:T(128)S(1)} %constant_dynamic-update-slice_fusion.3.pick_ref) | copy-start | bytes 28
  75.8 25.9 %copy-start.43 = (s32[2]{0:T(128)}, s32[2]{0:T(128)S(1)}, u32[]{:S(2)}) copy-start(s32[2]{0:T(128)S(1)} %constant_dynamic-update-slice_fusion.2.pick_ref) | copy-start | bytes 28
  102.8 19.1 %collective-permute-start.3 = (f32[320,512]{1,0:T(8,128)S(1)}, f32[320,512]{1,0:T(8,128)}, u32[]{:S(2)}, u32[]{:S(2)}) collective-permute-start(f32[320,512]{1,0:T(8,128)S(1)} %get-tuple-element.481), channel_id=1, source_target_pairs={{0,1},{1,0},{2,3},{3,2},{4,5},{5,4},{6,7},{7,6},{8,9},{9,8},{10,11... | collective-permute-start | bytes 1966088 | tf_op jit(solution)/shard_map/ppermute | solution.py:771
  121.7 26.2 %collective-permute-start.2 = (f32[256,1024]{1,0:T(8,128)S(1)}, f32[256,1024]{1,0:T(8,128)}, u32[]{:S(2)}, u32[]{:S(2)}) collective-permute-start(f32[256,1024]{1,0:T(8,128)S(1)} %fusion.51), channel_id=1, source_target_pairs={{0,1},{1,0},{2,3},{3,2},{4,5},{5,4},{6,7},{7,6},{8,9},{9,8},{10,11... | collective-permute-start | bytes 3145736 | tf_op jit(solution)/shard_map/ppermute | solution.py:771
  140.6 35.3 %collective-permute-start.4 = (f32[320,1024]{1,0:T(8,128)S(1)}, f32[320,1024]{1,0:T(8,128)S(1)}, u32[]{:S(2)}, u32[]{:S(2)}) collective-permute-start(f32[320,1024]{1,0:T(8,128)S(1)} %fusion.52), channel_id=1, source_target_pairs={{0,1},{1,0},{2,3},{3,2},{4,5},{5,4},{6,7},{7,6},{8,9},{9,8},{10,11... | collective-permute-start | bytes 3932168 | tf_op jit(solution)/shard_map/ppermute | solution.py:771
  157.0 39.5 %collective-permute-start.5 = (f32[256,1024]{1,0:T(8,128)}, f32[256,1024]{1,0:T(8,128)}, u32[]{:S(2)}, u32[]{:S(2)}) collective-permute-start(f32[256,1024]{1,0:T(8,128)} %fusion.53), channel_id=1, source_target_pairs={{0,1},{1,0},{2,3},{3,2},{4,5},{5,4},{6,7},{7,6},{8,9},{9,8},{10,11... | collective-permute-start | bytes 3145736 | tf_op jit(solution)/shard_map/ppermute | solution.py:771
  191.2 16.3 %collective-permute-start.6 = (f32[8,64,2048]{2,1,0:T(8,128)}, f32[8,64,2048]{2,1,0:T(8,128)}, u32[]{:S(2)}, u32[]{:S(2)}) collective-permute-start(f32[8,64,2048]{2,1,0:T(8,128)} %weight_half.4), channel_id=1, source_target_pairs={{0,2},{2,0},{4,6},{6,4},{8,10},{10,8},{12,14},{14,12},{16,18},{18,... | collective-permute-start | bytes 12582920 | tf_op jit(solution)/shard_map/ppermute | solution.py:684
  204.1 13.2 %collective-permute-start.7 = (f32[8,64,2048]{2,1,0:T(8,128)}, f32[8,64,2048]{2,1,0:T(8,128)}, u32[]{:S(2)}, u32[]{:S(2)}) collective-permute-start(f32[8,64,2048]{2,1,0:T(8,128)} %weight_half.6), channel_id=1, source_target_pairs={{0,2},{2,0},{4,6},{6,4},{8,10},{10,8},{12,14},{14,12},{16,18},{18,... | collective-permute-start | bytes 12582920 | tf_op jit(solution)/shard_map/ppermute | solution.py:684
  207.0 35.9 %collective-permute-start.8 = (f32[320,1024]{1,0:T(8,128)}, f32[320,1024]{1,0:T(8,128)}, u32[]{:S(2)}, u32[]{:S(2)}) collective-permute-start(f32[320,1024]{1,0:T(8,128)} %fusion.54), channel_id=1, source_target_pairs={{0,1},{1,0},{2,3},{3,2},{4,5},{5,4},{6,7},{7,6},{8,9},{9,8},{10,11... | collective-permute-start | bytes 3932168 | tf_op jit(solution)/shard_map/ppermute | solution.py:771
  215.5 54.3 %collective-permute-start.9 = (f32[4,64,2048]{2,1,0:T(8,128)}, f32[4,64,2048]{2,1,0:T(8,128)}, u32[]{:S(2)}, u32[]{:S(2)}) collective-permute-start(f32[4,64,2048]{2,1,0:T(8,128)} %get-tuple-element.295), channel_id=1, source_target_pairs={{0,8},{2,10},{4,12},{6,14},{8,0},{10,2},{12,4},{14,6},{16,24},{18,... | collective-permute-start | bytes 6291464 | tf_op jit(solution)/shard_map/ppermute | solution.py:684
  243.0 48.9 %collective-permute-start.10 = (f32[4,64,2048]{2,1,0:T(8,128)}, f32[4,64,2048]{2,1,0:T(8,128)}, u32[]{:S(2)}, u32[]{:S(2)}) collective-permute-start(f32[4,64,2048]{2,1,0:T(8,128)} %get-tuple-element.301), channel_id=1, source_target_pairs={{0,4},{2,6},{4,0},{6,2},{8,12},{10,14},{12,8},{14,10},{16,20},{18,... | collective-permute-start | bytes 6291464 | tf_op jit(solution)/shard_map/ppermute | solution.py:684
  280.2 37.8 %collective-permute-start.12 = (f32[8,64,1152]{2,1,0:T(8,128)}, f32[8,64,1152]{2,1,0:T(8,128)}, u32[]{:S(2)}, u32[]{:S(2)}) collective-permute-start(f32[8,64,1152]{2,1,0:T(8,128)} %many_half.6), channel_id=1, source_target_pairs={{0,2},{2,0},{4,6},{6,4},{8,10},{10,8},{12,14},{14,12},{16,18},{18,... | collective-permute-start | bytes 7077896 | tf_op jit(solution)/shard_map/ppermute | solution.py:684
  280.2 35.1 %collective-permute-start.11 = (f32[2,64,2048]{2,1,0:T(8,128)}, f32[2,64,2048]{2,1,0:T(8,128)}, u32[]{:S(2)}, u32[]{:S(2)}) collective-permute-start(f32[2,64,2048]{2,1,0:T(8,128)} %get-tuple-element.309), channel_id=1, source_target_pairs={{0,4},{2,6},{4,0},{6,2},{8,12},{10,14},{12,8},{14,10},{16,20},{18,... | collective-permute-start | bytes 3145736 | tf_op jit(solution)/shard_map/ppermute | solution.py:684
  295.3 60.2 %collective-permute-start.13 = (f32[2,64,2048]{2,1,0:T(8,128)}, f32[2,64,2048]{2,1,0:T(8,128)}, u32[]{:S(2)}, u32[]{:S(2)}) collective-permute-start(f32[2,64,2048]{2,1,0:T(8,128)} %get-tuple-element.326), channel_id=1, source_target_pairs={{0,8},{2,10},{4,12},{6,14},{8,0},{10,2},{12,4},{14,6},{16,24},{18,... | collective-permute-start | bytes 3145736 | tf_op jit(solution)/shard_map/ppermute | solution.py:684
  324.7 46.5 %collective-permute-start.14 = (f32[4,64,1152]{2,1,0:T(8,128)}, f32[4,64,1152]{2,1,0:T(8,128)}, u32[]{:S(2)}, u32[]{:S(2)}) collective-permute-start(f32[4,64,1152]{2,1,0:T(8,128)} %get-tuple-element.341), channel_id=1, source_target_pairs={{0,4},{2,6},{4,0},{6,2},{8,12},{10,14},{12,8},{14,10},{16,20},{18,... | collective-permute-start | bytes 3538952 | tf_op jit(solution)/shard_map/ppermute | solution.py:684
  326.4 29.1 %copy-start.45 = (s32[3]{0:T(128)}, s32[3]{0:T(128)S(1)}, u32[]{:S(2)}) copy-start(s32[3]{0:T(128)S(1)} %get-tuple-element.492.pick_ref) | copy-start | bytes 40
  326.4 73.7 %copy-start.44 = (s32[3]{0:T(128)}, s32[3]{0:T(128)S(1)}, u32[]{:S(2)}) copy-start(s32[3]{0:T(128)S(1)} %get-tuple-element.493.pick_ref) | copy-start | bytes 40
  326.4 29.1 %copy-start.49 = (s32[3]{0:T(128)}, s32[3]{0:T(128)S(1)}, u32[]{:S(2)}) copy-start(s32[3]{0:T(128)S(1)} %constant_dynamic-update-slice_fusion.1.pick_ref) | copy-start | bytes 40
  330.0 41.1 %collective-permute-start.15 = (f32[64,2048]{1,0:T(8,128)}, f32[64,2048]{1,0:T(8,128)}, u32[]{:S(2)}, u32[]{:S(2)}) collective-permute-start(f32[64,2048]{1,0:T(8,128)} %get-tuple-element.342), channel_id=1, source_target_pairs={{0,16},{2,18},{4,20},{6,22},{8,24},{10,26},{12,28},{14,30},{16,0},... | collective-permute-start | bytes 1572872 | tf_op jit(solution)/shard_map/ppermute | solution.py:684
  375.7 17.3 %collective-permute-start.16 = (f32[8,64,896]{2,1,0:T(8,128)}, f32[8,64,896]{2,1,0:T(8,128)}, u32[]{:S(2)}, u32[]{:S(2)}) collective-permute-start(f32[8,64,896]{2,1,0:T(8,128)} %get-tuple-element.354), channel_id=1, source_target_pairs={{0,2},{2,0},{4,6},{6,4},{8,10},{10,8},{12,14},{14,12},{16,18},{18,... | collective-permute-start | bytes 5505032 | tf_op jit(solution)/shard_map/ppermute | solution.py:684
  375.7 17.3 %collective-permute-start.17 = (f32[8,64,512]{2,1,0:T(8,128)}, f32[8,64,512]{2,1,0:T(8,128)}, u32[]{:S(2)}, u32[]{:S(2)}) collective-permute-start(f32[8,64,512]{2,1,0:T(8,128)} %get-tuple-element.355), channel_id=1, source_target_pairs={{0,2},{2,0},{4,6},{6,4},{8,10},{10,8},{12,14},{14,12},{16,18},{18,... | collective-permute-start | bytes 3145736 | tf_op jit(solution)/shard_map/ppermute | solution.py:684
  376.2 38.7 %collective-permute-start.18 = (f32[2,64,1152]{2,1,0:T(8,128)}, f32[2,64,1152]{2,1,0:T(8,128)}, u32[]{:S(2)}, u32[]{:S(2)}) collective-permute-start(f32[2,64,1152]{2,1,0:T(8,128)} %get-tuple-element.368), channel_id=1, source_target_pairs={{0,8},{2,10},{4,12},{6,14},{8,0},{10,2},{12,4},{14,6},{16,24},{18,... | collective-permute-start | bytes 1769480 | tf_op jit(solution)/shard_map/ppermute | solution.py:684
  377.7 37.1 %collective-permute-start.19 = (f32[64,2048]{1,0:T(8,128)}, f32[64,2048]{1,0:T(8,128)}, u32[]{:S(2)}, u32[]{:S(2)}) collective-permute-start(f32[64,2048]{1,0:T(8,128)} %get-tuple-element.369), channel_id=1, source_target_pairs={{0,16},{2,18},{4,20},{6,22},{8,24},{10,26},{12,28},{14,30},{16,0},... | collective-permute-start | bytes 1572872 | tf_op jit(solution)/shard_map/ppermute | solution.py:684
  399.7 38.4 %collective-permute-start.20 = (f32[4,64,896]{2,1,0:T(8,128)}, f32[4,64,896]{2,1,0:T(8,128)}, u32[]{:S(2)}, u32[]{:S(2)}) collective-permute-start(f32[4,64,896]{2,1,0:T(8,128)} %get-tuple-element.382), channel_id=1, source_target_pairs={{0,8},{2,10},{4,12},{6,14},{8,0},{10,2},{12,4},{14,6},{16,24},{18,... | collective-permute-start | bytes 2752520 | tf_op jit(solution)/shard_map/ppermute | solution.py:684
  414.9 23.2 %collective-permute-start.21 = (f32[4,64,512]{2,1,0:T(8,128)}, f32[4,64,512]{2,1,0:T(8,128)}, u32[]{:S(2)}, u32[]{:S(2)}) collective-permute-start(f32[4,64,512]{2,1,0:T(8,128)} %get-tuple-element.383), channel_id=1, source_target_pairs={{0,4},{2,6},{4,0},{6,2},{8,12},{10,14},{12,8},{14,10},{16,20},{18,... | collective-permute-start | bytes 1572872 | tf_op jit(solution)/shard_map/ppermute | solution.py:684
  418.3 19.7 %collective-permute-start.22 = (f32[64,1152]{1,0:T(8,128)S(1)}, f32[64,1152]{1,0:T(8,128)S(1)}, u32[]{:S(2)}, u32[]{:S(2)}) collective-permute-start(f32[64,1152]{1,0:T(8,128)S(1)} %get-tuple-element.384), channel_id=1, source_target_pairs={{0,16},{2,18},{4,20},{6,22},{8,24},{10,26},{12,28},{14,30},{16,0},... | collective-permute-start | bytes 884744 | tf_op jit(solution)/shard_map/ppermute | solution.py:684
  455.7 11.2 %collective-permute-start.26 = (f32[8,64,896]{2,1,0:T(8,128)}, f32[8,64,896]{2,1,0:T(8,128)}, u32[]{:S(2)}, u32[]{:S(2)}) collective-permute-start(f32[8,64,896]{2,1,0:T(8,128)} %get-tuple-element.402), channel_id=1, source_target_pairs={{0,2},{2,0},{4,6},{6,4},{8,10},{10,8},{12,14},{14,12},{16,18},{18,... | collective-permute-start | bytes 5505032 | tf_op jit(solution)/shard_map/ppermute | solution.py:684
  460.5 53.7 %collective-permute-start.23 = (f32[576,1024]{1,0:T(8,128)}, f32[576,1024]{1,0:T(8,128)}, u32[]{:S(2)}, u32[]{:S(2)}) collective-permute-start(f32[576,1024]{1,0:T(8,128)} %add_add_fusion), channel_id=1, source_target_pairs={{0,1},{1,0},{2,3},{3,2},{4,5},{5,4},{6,7},{7,6},{8,9},{9,8},{10,11... | collective-permute-start | bytes 7077896 | tf_op jit(solution)/shard_map/ppermute | solution.py:771
  462.0 4.9 collective-permute-start.27
  463.1 13.0 %collective-permute-start.24 = (f32[2,64,896]{2,1,0:T(8,128)S(1)}, f32[2,64,896]{2,1,0:T(8,128)}, u32[]{:S(2)}, u32[]{:S(2)}) collective-permute-start(f32[2,64,896]{2,1,0:T(8,128)S(1)} %copy-done.35), channel_id=1, source_target_pairs={{0,4},{2,6},{4,0},{6,2},{8,12},{10,14},{12,8},{14,10},{16,20},{18,... | collective-permute-start | bytes 1376264 | tf_op jit(solution)/shard_map/ppermute | solution.py:684
  464.6 9.5 %collective-permute-start.34 = (f32[2,64,512]{2,1,0:T(8,128)}, f32[2,64,512]{2,1,0:T(8,128)S(1)}, u32[]{:S(2)}, u32[]{:S(2)}) collective-permute-start(f32[2,64,512]{2,1,0:T(8,128)} %get-tuple-element.410), channel_id=1, source_target_pairs={{0,8},{2,10},{4,12},{6,14},{8,0},{10,2},{12,4},{14,6},{16,24},{18,... | collective-permute-start | bytes 786440 | tf_op jit(solution)/shard_map/ppermute | solution.py:684
  473.5 24.5 %copy-start.31 = (f32[4,64,896]{2,1,0:T(8,128)S(1)}, f32[4,64,896]{2,1,0:T(8,128)}, u32[]{:S(2)}) copy-start(f32[4,64,896]{2,1,0:T(8,128)} %get-tuple-element.404) | copy-start | bytes 2752516
  473.5 24.5 %collective-permute-start.28 = (f32[4,64,896]{2,1,0:T(8,128)}, f32[4,64,896]{2,1,0:T(8,128)S(1)}, u32[]{:S(2)}, u32[]{:S(2)}) collective-permute-start(f32[4,64,896]{2,1,0:T(8,128)} %get-tuple-element.405), channel_id=1, source_target_pairs={{0,4},{2,6},{4,0},{6,2},{8,12},{10,14},{12,8},{14,10},{16,20},{18,... | collective-permute-start | bytes 2752520 | tf_op jit(solution)/shard_map/ppermute | solution.py:684
  474.1 9.3 %collective-permute-start.35 = (f32[64,512]{1,0:T(8,128)S(1)}, f32[64,512]{1,0:T(8,128)S(1)}, u32[]{:S(2)}, u32[]{:S(2)}) collective-permute-start(f32[64,512]{1,0:T(8,128)S(1)} %add_bitcast_fusion.7), channel_id=1, source_target_pairs={{0,16},{2,18},{4,20},{6,22},{8,24},{10,26},{12,28},{14,30},{16,0},... | collective-permute-start | bytes 393224 | tf_op jit(solution)/shard_map/ppermute | solution.py:684
  475.2 21.1 %collective-permute-start.31 = (f32[4,64,512]{2,1,0:T(8,128)}, f32[4,64,512]{2,1,0:T(8,128)S(1)}, u32[]{:S(2)}, u32[]{:S(2)}) collective-permute-start(f32[4,64,512]{2,1,0:T(8,128)} %get-tuple-element.408), channel_id=1, source_target_pairs={{0,8},{2,10},{4,12},{6,14},{8,0},{10,2},{12,4},{14,6},{16,24},{18,... | collective-permute-start | bytes 1572872 | tf_op jit(solution)/shard_map/ppermute | solution.py:684
  477.1 37.1 %copy-start.8 = (f32[320,1024]{1,0:T(8,128)S(1)}, f32[320,1024]{1,0:T(8,128)}, u32[]{:S(2)}) copy-start(f32[320,1024]{1,0:T(8,128)} %get-tuple-element.449) | copy-start | bytes 3932164
  477.1 37.1 %copy-start.16 = (f32[256,1024]{1,0:T(8,128)S(1)}, f32[256,1024]{1,0:T(8,128)}, u32[]{:S(2)}) copy-start(f32[256,1024]{1,0:T(8,128)} %get-tuple-element.452) | copy-start | bytes 3145732
  477.1 16.1 %collective-permute-start.25 = (f32[64,896]{1,0:T(8,128)S(1)}, f32[64,896]{1,0:T(8,128)S(1)}, u32[]{:S(2)}, u32[]{:S(2)}) collective-permute-start(f32[64,896]{1,0:T(8,128)S(1)} %add_bitcast_fusion.6), channel_id=1, source_target_pairs={{0,16},{2,18},{4,20},{6,22},{8,24},{10,26},{12,28},{14,30},{16,0},... | collective-permute-start | bytes 688136 | tf_op jit(solution)/shard_map/ppermute | solution.py:684
  496.3 22.4 %collective-permute-start.32 = (f32[2,64,512]{2,1,0:T(8,128)S(1)}, f32[2,64,512]{2,1,0:T(8,128)S(1)}, u32[]{:S(2)}, u32[]{:S(2)}) collective-permute-start(f32[2,64,512]{2,1,0:T(8,128)S(1)} %fusion.37), channel_id=1, source_target_pairs={{0,4},{2,6},{4,0},{6,2},{8,12},{10,14},{12,8},{14,10},{16,20},{18,... | collective-permute-start | bytes 786440 | tf_op jit(solution)/shard_map/ppermute | solution.py:684
  498.0 20.2 %collective-permute-start.29 = (f32[2,64,896]{2,1,0:T(8,128)S(1)}, f32[2,64,896]{2,1,0:T(8,128)S(1)}, u32[]{:S(2)}, u32[]{:S(2)}) collective-permute-start(f32[2,64,896]{2,1,0:T(8,128)S(1)} %fusion.34), channel_id=1, source_target_pairs={{0,8},{2,10},{4,12},{6,14},{8,0},{10,2},{12,4},{14,6},{16,24},{18,... | collective-permute-start | bytes 1376264 | tf_op jit(solution)/shard_map/ppermute | solution.py:684
  518.3 16.7 %collective-permute-start.30 = (f32[64,896]{1,0:T(8,128)S(1)}, f32[64,896]{1,0:T(8,128)S(1)}, u32[]{:S(2)}, u32[]{:S(2)}) collective-permute-start(f32[64,896]{1,0:T(8,128)S(1)} %fusion.40), channel_id=1, source_target_pairs={{0,16},{2,18},{4,20},{6,22},{8,24},{10,26},{12,28},{14,30},{16,0},... | collective-permute-start | bytes 688136 | tf_op jit(solution)/shard_map/ppermute | solution.py:684
  518.7 18.0 %collective-permute-start.33 = (f32[64,512]{1,0:T(8,128)S(1)}, f32[64,512]{1,0:T(8,128)S(1)}, u32[]{:S(2)}, u32[]{:S(2)}) collective-permute-start(f32[64,512]{1,0:T(8,128)S(1)} %fusion.41), channel_id=1, source_target_pairs={{0,16},{2,18},{4,20},{6,22},{8,24},{10,26},{12,28},{14,30},{16,0},... | collective-permute-start | bytes 393224 | tf_op jit(solution)/shard_map/ppermute | solution.py:684
  535.1 4.2 collective-permute-start.36
  (44 other events, 223.0 us)

commit v6 on v5

--- a/solution.py
+++ b/solution.py
@@ -337,13 +337,17 @@
 
 
 def close_kernel(*refs, rows, count):
-    base_ref, pos_ref, side_ref, out_ref, table_ref = refs[count:]
+    *base_refs, pos_ref, side_ref, out_ref, table_ref = refs[count:]
     rows2 = 2 * rows
     half3 = lane_half((rows // 8, 8, 128))
     flat = jnp.concatenate([ref[...] for ref in refs[:count]], axis=0).reshape(rows2, 3 * REL)
     both = nn(flat, pos_ref[...]).reshape(rows // 8, 16, 128)
     mine = jnp.where(half3, both[:, 0:8, :], both[:, 8:16, :]).reshape(rows, 128)
-    out_ref[...] = base_ref[...] + mine
+    first = 0
+    for base_ref in base_refs:
+        here = slice(first, first + base_ref.shape[0])
+        out_ref[here, :] = (base_ref[...] + mine[here]).astype(bf16)
+        first += base_ref.shape[0]
     side = side_ref[0:rows, :].astype(f32).reshape(rows // 8, 8, 128)
     zero = jnp.zeros_like(side)
     spread = jnp.concatenate([jnp.where(half3, side, zero), jnp.where(half3, zero, side)], axis=1)
@@ -505,14 +509,15 @@
     )(*backs, buckets, merge)
 
 
-def attention_close(sums, base, pos, qkv, side):
-    rows, width = base.shape
+def attention_close(sums, bases, pos, qkv, side):
+    rows, width = sum(base.shape[0] for base in bases), bases[0].shape[1]
     pairs = width // 128
     return pl.pallas_call(
         functools.partial(close_kernel, rows=rows, count=len(sums)),
         grid=(pairs,),
         in_specs=[pl.BlockSpec((part.shape[0], 16, 3 * REL), lambda p: (0, p, 0)) for part in sums] + [
-            pl.BlockSpec((rows, 128), lambda p: (0, p)),
+            pl.BlockSpec((base.shape[0], 128), lambda p: (0, p)) for base in bases
+        ] + [
             pl.BlockSpec((3 * REL, 128), lambda p: (0, p)),
             pl.BlockSpec((qkv.shape[0], 128), lambda p: (0, p + side * pairs)),
         ],
@@ -521,13 +526,13 @@
             pl.BlockSpec((3 * REL, 128), lambda p: (0, p)),
         ),
         out_shape=(
-            jax.ShapeDtypeStruct((rows, width), f32),
+            jax.ShapeDtypeStruct((rows, width), bf16),
             jax.ShapeDtypeStruct((3 * REL, width), bf16),
         ),
         compiler_params=pltpu.CompilerParams(vmem_limit_bytes=VMEM_CAP),
-        cost_estimate=pl.CostEstimate(flops=5000000000, bytes_accessed=10000000, transcendentals=0),
+        cost_estimate=pl.CostEstimate(flops=10**6, bytes_accessed=10**4, transcendentals=0),
         name="attention_close",
-    )(*sums, base, pos, qkv)
+    )(*sums, *bases, pos, qkv)
 
 
 def fill_turned(x_ref, turned, rows):
@@ -673,9 +678,7 @@
             for (left, _), turn in zip(pairs, turns) if turn
         ],
         compiler_params=pltpu.CompilerParams(vmem_limit_bytes=VMEM_CAP),
-        cost_estimate=pl.CostEstimate(
-            flops=600 * depth * sum(widths), bytes_accessed=6 * depth * sum(widths), transcendentals=0
-        ),
+        cost_estimate=pl.CostEstimate(flops=10**6, bytes_accessed=10**4, transcendentals=0),
         name="many_half",
     )(*args)
 
@@ -951,7 +954,6 @@
     back_rest, turned_rest, query_rest, key_base, value_back = draw(1, (key_head, value_head))
     gain_one_grad, shift_one_grad = (one_sums[0][n] + one_sums[1][n] for n in range(2))
     back_rest, value_back = tie((back_rest, value_back), down_chain)
-    query_base = jnp.concatenate([query_head, query_rest], axis=0)
     residual_low = jnp.concatenate(residuals_low, axis=0)
     context = jnp.concatenate(contexts, axis=0)
     nothing = jnp.zeros_like(gain_one)
@@ -992,8 +994,7 @@
     back_rest, near = tie((back_rest, near), outer_chain)
     near.append(attention_scatter([back_rest], bucket_rest, merge, 0, blocks - split // 64))
     near, backs = tie((near, [turned_head, turned_rest]), up_chain)
-    query_back, key_table_sum = attention_close(near, query_base, pos_key, qkv, 0)
-    query_low = query_back.astype(bf16)
+    query_low, key_table_sum = attention_close(near, [query_head, query_rest], pos_key, qkv, 0)
     early = nt(query_low, query_weight) + nt(value_back, value_weight)
     near_chain = tail(query_low, key_table_sum, key_position, [high_first, low_first])
     backs, key_table_sum = tie((backs, key_table_sum), near_chain, outer_chain, down_chain)
@@ -1002,19 +1003,24 @@
     for part, chains in enumerate(((near_chain,), (outer_chain, up_chain), (near_chain, outer_chain))):
         far.append(attention_scatter(backs, bucket_cols, merge, cuts[part], cuts[part + 1] - cuts[part]))
         backs, far = tie((backs, far), *chains)
-    key_back, query_table_sum = attention_close(far, key_base, pos_query, qkv, 1)
-    key_low = key_back.astype(bf16)
-    input_part = early + nt(key_low, key_weight)
-    input_other = swap(input_part)
+    key_low, query_table_sum = attention_close(far, [key_base], pos_query, qkv, 1)
     far_chain = tail(key_low, query_table_sum, query_position, [low_first, high_first])
+    parts, others = [], []
+    for low, high in ((0, rows // 2), (rows // 2, rows)):
+        parts.append(early[low:high] + nt(key_low[low:high], key_weight))
+        others.append(swap(parts[-1]))
     far_chain.step()
     far_chain.step()
-    input_gradient = (jnp.concatenate(residuals_back, axis=0) + input_part + input_other)[:span].astype(bf16)
+    far_chain.extra, others[0] = lax.optimization_barrier((far_chain.extra, others[0]))
+    far_main, query_position_grad = far_chain.finish()
+    far_main, others[1] = lax.optimization_barrier((far_main, others[1]))
+    input_gradient = (
+        jnp.concatenate(residuals_back, axis=0) + jnp.concatenate(parts, axis=0) + jnp.concatenate(others, axis=0)
+    )[:span].astype(bf16)
     (down_share,) = down_chain.finish()
     (up_share,) = up_chain.finish()
     (outer_share,) = outer_chain.finish()
     near_main, key_position_grad = near_chain.finish()
-    far_main, query_position_grad = far_chain.finish()
 
     table_rows = near_main[:, width:] + far_main[:, width:]
     table_rows = table_rows.reshape(2, table_rows.shape[0] // 2, 3 * REL)

time: 550 us -> 545 us (level)
  other arithmetic: 66.2 us -> 59.3 us
    ppermute x28, waiting for transfers between devices: 38.3 us -> 56.2 us  [flipped(): return lax.ppermute(value, 'dp', [(i, i ^ 1 << bit) for i in range(size)])]
    ppermute x8 -> x9, waiting for transfers between devices: 43.4 us -> 29.4 us  [swap(): return lax.ppermute(value.astype(f32), 'mp', [(0, 1), (1, 0)])]
    dot_general x9 -> x10, matrix products: 18.7 us -> 18.2 us  [nt(): lax.dot_general(left, right, (((1,), (1,)), ((), ())), preferred_element_...]
  transfers between devices with their start and end apart: 37 -> 38, of which waited for: 12 -> 10; matrix products, arithmetic and copies ran while one was open for 20% -> 19% of each run, Pallas kernels for 51% -> 52%
where the time goes in v6:
time: 545 us; the launch traced here: 536 us
  Pallas kernels  289 us (53%)
  waiting for transfers between devices  85.6 us (16%)
  other arithmetic  59.3 us (11%)
  matrix products  39.1 us (7%)
  starting transfers between devices  37.2 us (7%)
  local copies, waits for them, and re-layouts  22.5 us (4%)
    pallas_call x5, Pallas kernels, attention_scatter(): pl.pallas_call(functools.partial(scatter_kernel, groups=8, cols=cols), gr...  85.7 us
    ppermute x28, waiting for transfers between devices, flipped(): return lax.ppermute(value, 'dp', [(i, i ^ 1 << bit) for i in range(size)])  56.2 us
    pallas_call x1, Pallas kernels, attention_head(): pl.pallas_call(kernel, out_shape=(jax.ShapeDtypeStruct((2 * pairs, split,...  49.7 us
    pallas_call x6, Pallas kernels, many_half(): pl.pallas_call(functools.partial(many_kernel, plan=plan, widths=widths, t...  37.4 us
    pallas_call x4, Pallas kernels, weight_half(): pl.pallas_call(functools.partial(weight_kernel, count=len(xs), blocks=blo...  31 us
    ppermute x9, waiting for transfers between devices, swap(): return lax.ppermute(value.astype(f32), 'mp', [(0, 1), (1, 0)])  29.4 us
    pallas_call x1, Pallas kernels, attention_rest(): pl.pallas_call(kernel, out_shape=(jax.ShapeDtypeStruct((2 * pairs, rows -...  25.8 us
    ppermute x28, starting transfers between devices, flipped(): return lax.ppermute(value, 'dp', [(i, i ^ 1 << bit) for i in range(size)])  25.8 us
  transfers between devices with their start and end apart: 38, of which 10 were waited for; matrix products, arithmetic and copies ran while one was open for 19% of the time, Pallas kernels for 52%

profile of v6, /device:TPU:0, one launch (start us, length us, event | category | flops | bytes accessed | tf_op | source)
XLA Modules:
  0.0 535.6 jit_solution(15152561024532656618)
XLA Ops:
  0.6 2.8 convert_element_type.67
  3.4 3.0 collective-permute-start.1
  7.0 4.6 copy.60.b_ref
  11.6 9.3 %project.1 = (bf16[640,1536]{1,0:T(8,128)(2,1)}, bf16[384,512]{1,0:T(8,128)(2,1)}, bf16[384,512]{1,0:T(8,128)(2,1)}) custom-call(bf16[561,1024]{1,0:T(8,128)(2,1)} %x_ref.1, bf16[1024,512]{1,0:T(8,128)(2,1)} %wq_ref.1, bf16[1024,512]{1,0:T(8,128)(2,1)} %wk_ref.1, bf16[1024,512]{1,0:T(8,128)(2,1)} %wv_ref.1, bf16[3,128,1024]{2,1,0:T(8,128)(2,1)} %t_ref.1, ...), custom_call_target="tpu_custom_call" | custom-call | flops 4000000000 | bytes 9000000 | tf_op jit(solution)/shard_map/project/pallas_call | solution.py:226
  21.0 49.7 %attention_head.1 = (bf16[8,256,640]{2,1,0:T(8,128)(2,1)}, bf16[256,512]{1,0:T(8,128)(2,1)}, s32[3,256,640]{2,1,0:T(8,128)}, s32[3,320,640]{2,1,0:T(8,128)}, s32...) custom-call(s32[1]{0:T(128)S(6)} %copy.120.used_ref, ...), custom_call_target="tpu_custom_call" | custom-call | flops 40000000000 | bytes 25000000 | tf_op jit(solution)/shard_map/attention_head/pallas_call | solution.py:400
  75.6 25.8 %attention_rest.1 = (bf16[8,320,640]{2,1,0:T(8,128)(2,1)}, bf16[320,512]{1,0:T(8,128)(2,1)}) custom-call(s32[1]{0:T(128)S(6)} %copy.120.used_ref, bf16[640,1536]{1,0:T(8,128)(2,1)} %get-tuple-element.247.qkv_ref.q_ref.k_ref.v_ref.refs_5_, bf16[384,512]{1,0:T(8,128)(2,1)} %get-tuple-element.248.pk_ref.refs_4_, ...), custom_call_target="tpu_custom_call" | custom-call | flops 20000000000 | bytes 12000000 | tf_op jit(solution)/shard_map/attention_rest/pallas_call | solution.py:437
  104.7 6.7 %attend.2 = (f32[256,1024]{1,0:T(8,128)}, bf16[256,1024]{1,0:T(8,128)(2,1)}, f32[256,1024]{1,0:T(8,128)}, f32[256,1]{1,0:T(8,128)}) custom-call(bf16[256,1024]{1,0:T(8,128)(2,1)} %slice.113.t_ref, bf16[256,512]{1,0:T(8,128)(2,1)} %get-tuple-element.250.c_ref, f32[256,512]{1,0:T(8,128)} %collective-permute-done.o_ref, bf16[512,1024]{1,0:T(8,128)(2,1)} %w_ref.3, ...), custom_call_target="tpu_custom_call" | custom-call | flops 2000000000 | bytes 8000000 | tf_op jit(solution)/shard_map/attend/pallas_call | solution.py:799
  111.5 8.7 %multiply_convert_fusion.1 = (bf16[256,2048]{1,0:T(8,128)(2,1)S(1)}, f32[256,2048]{1,0:T(8,128)}, f32[256,2048]{1,0:T(8,128)}) fusion(bf16[256,1024]{1,0:T(8,128)(2,1)} %get-tuple-element.277.refs_0_, bf16[1024,2048]{1,0:T(8,128)(2,1)} %param.37), kind=kOutput, calls=%fused_computation.26 | convolution fusion | flops 1107820544 | bytes 9961472 | tf_op jit(solution)/shard_map/dot_general | solution.py:39
  121.7 7.8 %attend.3 = (f32[320,1024]{1,0:T(8,128)}, bf16[320,1024]{1,0:T(8,128)(2,1)}, f32[320,1024]{1,0:T(8,128)}, f32[320,1]{1,0:T(8,128)}) custom-call(bf16[320,1024]{1,0:T(8,128)(2,1)} %copy.62.t_ref, bf16[320,512]{1,0:T(8,128)(2,1)} %get-tuple-element.258.c_ref, f32[320,512]{1,0:T(8,128)} %collective-permute-done.3.o_ref, bf16[512,1024]{1,0:T(8,128)(2,1)} %w_ref.3, ...), custom_call_target="tpu_custom_call" | custom-call | flops 2000000000 | bytes 8000000 | tf_op jit(solution)/shard_map/attend/pallas_call | solution.py:799
  129.5 9.3 %multiply_convert_fusion = (bf16[320,2048]{1,0:T(8,128)(2,1)S(1)}, f32[320,2048]{1,0:T(8,128)S(1)}, f32[320,2048]{1,0:T(8,128)S(1)}) fusion(bf16[320,1024]{1,0:T(8,128)(2,1)} %get-tuple-element.278.refs_1_, bf16[1024,2048]{1,0:T(8,128)(2,1)} %param.37), kind=kOutput, calls=%fused_computation.4 | convolution fusion | flops 1384775680 | bytes 11403264 | tf_op jit(solution)/shard_map/dot_general | solution.py:39
  142.3 5.4 %collective-permute-done.2 = f32[256,1024]{1,0:T(8,128)} collective-permute-done((f32[256,1024]{1,0:T(8,128)S(1)}, f32[256,1024]{1,0:T(8,128)}, u32[]{:S(2)}, u32[]{:S(2)}) %collective-permute-start.2) | collective-permute-done | bytes 1048608 | tf_op jit(solution)/shard_map/ppermute | solution.py:774
  156.8 18.9 %collective-permute-done.4 = f32[320,1024]{1,0:T(8,128)S(1)} collective-permute-done((f32[320,1024]{1,0:T(8,128)S(1)}, f32[320,1024]{1,0:T(8,128)S(1)}, u32[]{:S(2)}, u32[]{:S(2)}) %collective-permute-start.4) | collective-permute-done | bytes 1310752 | tf_op jit(solution)/shard_map/ppermute | solution.py:774
  181.0 2.6 fusion.58
  183.7 7.5 %weight_half.4 = f32[8,64,2048]{2,1,0:T(8,128)} custom-call(s32[2]{0:T(128)} %copy-done.52, bf16[256,1024]{1,0:T(8,128)(2,1)} %copy-done.14, bf16[320,1024]{1,0:T(8,128)(2,1)} %copy-done.4, bf16[256,2048]{1,0:T(8,128)(2,1)} %copy-done.20, bf16[320,2048]{1,0:T(8,128)(2,1)} %copy-done.10), custom_call_target="tpu_custom_call" | custom-call | flops 1207959552 | bytes 8388608 | tf_op jit(solution)/shard_map/weight_half/pallas_call | solution.py:604
  191.1 5.2 collective-permute-done.5
  196.3 7.5 %weight_half.6 = f32[8,64,2048]{2,1,0:T(8,128)} custom-call(s32[2]{0:T(128)} %copy-done.48, bf16[256,1024]{1,0:T(8,128)(2,1)} %get-tuple-element.277.refs_0_, bf16[320,1024]{1,0:T(8,128)(2,1)} %get-tuple-element.278.refs_1_, bf16[256,2048]{1,0:T(8,128)(2,1)} %copy-done.21, bf16[320,2048]{1,0:T(8,128)(2,1)} %copy-done.11), custom_call_target="tpu_custom_call" | custom-call | flops 1207959552 | bytes 8388608 | tf_op jit(solution)/shard_map/weight_half/pallas_call | solution.py:604
  207.2 8.0 %weight_half.5 = (f32[4,64,2048]{2,1,0:T(8,128)}, f32[4,64,2048]{2,1,0:T(8,128)}) custom-call(s32[2]{0:T(128)} %copy-done.51, bf16[256,1024]{1,0:T(8,128)(2,1)} %copy-done.14, bf16[320,1024]{1,0:T(8,128)(2,1)} %copy-done.4, bf16[256,2048]{1,0:T(8,128)(2,1)} %copy-done.20, bf16[320,2048]{1,0:T(8,128)(2,1)} %copy-done.10, ...), custom_call_target="tpu_custom_call" | custom-call | flops 1207959552 | bytes 8388608 | tf_op jit(solution)/shard_map/weight_half/pallas_call | solution.py:604
  217.0 7.9 %weight_half.7 = (f32[4,64,2048]{2,1,0:T(8,128)}, f32[4,64,2048]{2,1,0:T(8,128)}) custom-call(s32[2]{0:T(128)} %copy-done.47, bf16[256,1024]{1,0:T(8,128)(2,1)} %get-tuple-element.277.refs_0_, bf16[320,1024]{1,0:T(8,128)(2,1)} %get-tuple-element.278.refs_1_, bf16[256,2048]{1,0:T(8,128)(2,1)} %copy-done.21, bf16[320,2048]{1,0:T(8,128)(2,1)} %copy-done.11, ...), custom_call_target="tpu_custom_call" | custom-call | flops 1207959552 | bytes 8388608 | tf_op jit(solution)/shard_map/weight_half/pallas_call | solution.py:604
  225.0 4.2 multiply_reduce_fusion.4
  232.4 11.1 %attention_draw.2 = (bf16[32,64,640]{2,1,0:T(8,128)(2,1)}, bf16[72,64,256]{2,1,0:T(8,128)(2,1)}, f32[256,512]{1,0:T(8,128)}, f32[576,512]{1,0:T(8,128)}, f32[576,512]{1,0:T(8,128)}) custom-call(bf16[8,256,640]{2,1,0:T(8,128)(2,1)} %get-tuple-element.289.p_ref, bf16[256,512]{1,0:T(8,128)(2,1)} %convolution_convert_fusion.1.up_ref, ...), custom_call_target="tpu_custom_call" | custom-call | flops 1000000 | bytes 10000 | tf_op jit(solution)/shard_map/attention_draw/pallas_call | solution.py:461
  245.1 4.6 multiply_reduce_fusion
  254.3 13.8 %attention_draw.3 = (bf16[40,64,640]{2,1,0:T(8,128)(2,1)}, bf16[72,64,384]{2,1,0:T(8,128)(2,1)}, f32[320,512]{1,0:T(8,128)}, f32[576,512]{1,0:T(8,128)}, bf16[576,512]{1,0:T(8,128)(2,1)}) custom-call(bf16[8,320,640]{2,1,0:T(8,128)(2,1)} %get-tuple-element.295.p_ref, bf16[320,512]{1,0:T(8,128)(2,1)} %convolution_convert_fusion.up_ref, ...), custom_call_target="tpu_custom_call" | custom-call | flops 1000000 | bytes 10000 | tf_op jit(solution)/shard_map/attention_draw/pallas_call | solution.py:461
  270.4 3.2 fusion.31
  274.2 5.9 %many_half.6 = f32[8,64,1152]{2,1,0:T(8,128)} custom-call(s32[2]{0:T(128)} %copy-done.48, bf16[576,1024]{1,0:T(8,128)(2,1)} %pad_maximum_fusion.3.refs_0_, bf16[576,512]{1,0:T(8,128)(2,1)} %copy-done.22, bf16[1024,576]{1,0:T(8,128)(2,1)} %pad_bitcast_fusion.refs_2_.refs_0_, bf16[576,512]{1,0:T(8,128)(2,1)} %get-tuple-element.321.refs_3_, ...), custom_call_target="tpu_custom_call" | custom-call | flops 1000000 | bytes 10000 | tf_op jit(solution)/shard_map/many_half/pallas_call | solution.py:668
  281.4 10.9 %collective-permute-done.10 = f32[4,64,2048]{2,1,0:T(8,128)} collective-permute-done((f32[4,64,2048]{2,1,0:T(8,128)}, f32[4,64,2048]{2,1,0:T(8,128)}, u32[]{:S(2)}, u32[]{:S(2)}) %collective-permute-start.10) | collective-permute-done | bytes 2097184 | tf_op jit(solution)/shard_map/ppermute | solution.py:687
  292.4 3.8 fusion.29
  296.6 18.7 %attention_scatter.5.refs_0_ = bf16[32,64,384]{2,1,0:T(8,128)(2,1)} custom-call(bf16[32,64,640]{2,1,0:T(8,128)(2,1)} %get-tuple-element.312.refs_0_, s32[3,256,640]{2,1,0:T(8,128)} %get-tuple-element.313.refs_1_, bf16[4,256,128]{2,1,0:T(8,128)(2,1)} %fusion.35.refs_2_.refs_3_), custom_call_target="tpu_custom_call" | custom-call | flops 1000000 | bytes 10000 | tf_op jit(solution)/shard_map/attention_scatter/pallas_call | solution.py:497
  317.9 6.5 %many_half.7 = (f32[4,64,1152]{2,1,0:T(8,128)}, f32[4,64,1152]{2,1,0:T(8,128)}) custom-call(s32[2]{0:T(128)} %copy-done.47, bf16[576,1024]{1,0:T(8,128)(2,1)} %pad_maximum_fusion.3.refs_0_, bf16[576,512]{1,0:T(8,128)(2,1)} %copy-done.22, bf16[1024,576]{1,0:T(8,128)(2,1)} %pad_bitcast_fusion.refs_2_.refs_0_, bf16[576,512]{1,0:T(8,128)(2,1)} %get-tuple-element.321.refs_3_, ...), custom_call_target="tpu_custom_call" | custom-call | flops 1000000 | bytes 10000 | tf_op jit(solution)/shard_map/many_half/pallas_call | solution.py:668
  331.1 22.9 %attention_scatter.6.refs_1_ = bf16[40,64,384]{2,1,0:T(8,128)(2,1)} custom-call(bf16[40,64,640]{2,1,0:T(8,128)(2,1)} %get-tuple-element.328.refs_0_, s32[3,320,640]{2,1,0:T(8,128)} %get-tuple-element.255.b_ref.refs_1_, bf16[4,256,128]{2,1,0:T(8,128)(2,1)} %fusion.35.refs_2_.refs_3_), custom_call_target="tpu_custom_call" | custom-call | flops 1000000 | bytes 10000 | tf_op jit(solution)/shard_map/attention_scatter/pallas_call | solution.py:497
  354.0 2.6 add_bitcast_fusion
  356.7 5.4 %attention_close.2 = (bf16[576,512]{1,0:T(8,128)(2,1)}, bf16[384,512]{1,0:T(8,128)(2,1)}) custom-call(bf16[32,64,384]{2,1,0:T(8,128)(2,1)} %attention_scatter.5.refs_0_, bf16[40,64,384]{2,1,0:T(8,128)(2,1)} %attention_scatter.6.refs_1_, f32[256,512]{1,0:T(8,128)} %get-tuple-element.340.refs_2_, f32[320,512]{1,0:T(8,128)} %get-tuple-element.341.refs_3_, ...), custom_call_target="tpu_custom_call" | custom-call | flops 1000000 | bytes 10000 | tf_op jit(solution)/shard_map/attention_close/pallas_call | solution.py:515
  362.1 5.8 %many_half.8 = (f32[8,64,896]{2,1,0:T(8,128)}, f32[8,64,512]{2,1,0:T(8,128)}) custom-call(s32[3]{0:T(128)} %copy-done.54, bf16[1024,576]{1,0:T(8,128)(2,1)} %pad_bitcast_fusion.refs_2_.refs_0_, bf16[576,512]{1,0:T(8,128)(2,1)} %get-tuple-element.342.refs_1_, bf16[1024,384]{1,0:T(8,128)(2,1)} %bitcast.211, ...), custom_call_target="tpu_custom_call" | custom-call | flops 1000000 | bytes 10000 | tf_op jit(solution)/shard_map/many_half/pallas_call | solution.py:668
  374.6 14.8 %attention_scatter.7.refs_0_ = bf16[24,64,384]{2,1,0:T(8,128)(2,1)} custom-call(bf16[72,64,256]{2,1,0:T(8,128)(2,1)} %get-tuple-element.383.refs_0_, bf16[72,64,384]{2,1,0:T(8,128)(2,1)} %get-tuple-element.384.refs_1_, s32[3,576,640]{2,1,0:T(8,128)} %get-tuple-element.358.refs_2_, bf16[4,256,128]{2,1,0:T(8,128)(2,1)} %fusion.35.refs_2_.refs_3_), custom_call_target="tpu_custom_call" | custom-call | flops 1000000 | bytes 10000 | tf_op jit(solution)/shard_map/attention_scatter/pallas_call | solution.py:497
  389.4 6.8 %many_half.9 = (f32[4,64,896]{2,1,0:T(8,128)}, f32[4,64,896]{2,1,0:T(8,128)}, f32[4,64,512]{2,1,0:T(8,128)}, f32[4,64,512]{2,1,0:T(8,128)}) custom-call(s32[3]{0:T(128)} %copy-done.50, bf16[1024,576]{1,0:T(8,128)(2,1)} %pad_bitcast_fusion.refs_2_.refs_0_, bf16[576,512]{1,0:T(8,128)(2,1)} %get-tuple-element.342.refs_1_, bf16[1024,384]{1,0:T(8,128)(2,1)} %bitcast.212, ...), custom_call_target="tpu_custom_call" | custom-call | flops 1000000 | bytes 10000 | tf_op jit(solution)/shard_map/many_half/pallas_call | solution.py:668
  396.7 14.6 %attention_scatter.8.refs_1_ = bf16[24,64,384]{2,1,0:T(8,128)(2,1)} custom-call(bf16[72,64,256]{2,1,0:T(8,128)(2,1)} %get-tuple-element.383.refs_0_, bf16[72,64,384]{2,1,0:T(8,128)(2,1)} %get-tuple-element.384.refs_1_, s32[3,576,640]{2,1,0:T(8,128)} %get-tuple-element.358.refs_2_, bf16[4,256,128]{2,1,0:T(8,128)(2,1)} %fusion.35.refs_2_.refs_3_), custom_call_target="tpu_custom_call" | custom-call | flops 1000000 | bytes 10000 | tf_op jit(solution)/shard_map/attention_scatter/pallas_call | solution.py:497
  415.8 2.7 collective-permute-start.22
  418.5 14.6 %attention_scatter.9.refs_2_ = bf16[24,64,384]{2,1,0:T(8,128)(2,1)} custom-call(bf16[72,64,256]{2,1,0:T(8,128)(2,1)} %get-tuple-element.383.refs_0_, bf16[72,64,384]{2,1,0:T(8,128)(2,1)} %get-tuple-element.384.refs_1_, s32[3,576,640]{2,1,0:T(8,128)} %get-tuple-element.358.refs_2_, bf16[4,256,128]{2,1,0:T(8,128)(2,1)} %fusion.35.refs_2_.refs_3_), custom_call_target="tpu_custom_call" | custom-call | flops 1000000 | bytes 10000 | tf_op jit(solution)/shard_map/attention_scatter/pallas_call | solution.py:497
  438.4 5.4 %attention_close.3 = (bf16[576,512]{1,0:T(8,128)(2,1)}, bf16[384,512]{1,0:T(8,128)(2,1)}) custom-call(bf16[24,64,384]{2,1,0:T(8,128)(2,1)} %attention_scatter.7.refs_0_, bf16[24,64,384]{2,1,0:T(8,128)(2,1)} %attention_scatter.8.refs_1_, bf16[24,64,384]{2,1,0:T(8,128)(2,1)} %attention_scatter.9.refs_2_, f32[576,512]{1,0:T(8,128)} %get-tuple-element.402.refs_3_, ...), custom_call_target="tpu_custom_call" | custom-call | flops 1000000 | bytes 10000 | tf_op jit(solution)/shard_map/attention_close/pallas_call | solution.py:515
  443.8 5.8 %many_half.10 = (f32[8,64,896]{2,1,0:T(8,128)}, f32[8,64,512]{2,1,0:T(8,128)}) custom-call(s32[3]{0:T(128)} %copy-done.53, bf16[1024,576]{1,0:T(8,128)(2,1)} %pad_bitcast_fusion.refs_2_.refs_0_, bf16[576,512]{1,0:T(8,128)(2,1)} %get-tuple-element.403.refs_1_, bf16[1024,384]{1,0:T(8,128)(2,1)} %bitcast.213, ...), custom_call_target="tpu_custom_call" | custom-call | flops 1000000 | bytes 10000 | tf_op jit(solution)/shard_map/many_half/pallas_call | solution.py:668
  459.3 6.6 %many_half.11 = (f32[4,64,896]{2,1,0:T(8,128)}, f32[4,64,896]{2,1,0:T(8,128)}, f32[4,64,512]{2,1,0:T(8,128)}, f32[4,64,512]{2,1,0:T(8,128)}) custom-call(s32[3]{0:T(128)} %copy-done.49, bf16[1024,576]{1,0:T(8,128)(2,1)} %pad_bitcast_fusion.refs_2_.refs_0_, bf16[576,512]{1,0:T(8,128)(2,1)} %get-tuple-element.403.refs_1_, bf16[1024,384]{1,0:T(8,128)(2,1)} %bitcast.214, ...), custom_call_target="tpu_custom_call" | custom-call | flops 1000000 | bytes 10000 | tf_op jit(solution)/shard_map/many_half/pallas_call | solution.py:668
  473.8 5.7 %collective-permute-done.36 = f32[64,512]{1,0:T(8,128)S(1)} collective-permute-done((f32[64,512]{1,0:T(8,128)S(1)}, f32[64,512]{1,0:T(8,128)S(1)}, u32[]{:S(2)}, u32[]{:S(2)}) %collective-permute-start.36) | collective-permute-done | bytes 131104 | tf_op jit(solution)/shard_map/ppermute | solution.py:687
  481.9 16.1 %collective-permute-done.31 = f32[2,64,896]{2,1,0:T(8,128)S(1)} collective-permute-done((f32[2,64,896]{2,1,0:T(8,128)S(1)}, f32[2,64,896]{2,1,0:T(8,128)S(1)}, u32[]{:S(2)}, u32[]{:S(2)}) %collective-permute-start.31) | collective-permute-done | bytes 458784 | tf_op jit(solution)/shard_map/ppermute | solution.py:687
  500.6 9.5 %collective-permute-done.32 = f32[64,896]{1,0:T(8,128)S(1)} collective-permute-done((f32[64,896]{1,0:T(8,128)S(1)}, f32[64,896]{1,0:T(8,128)S(1)}, u32[]{:S(2)}, u32[]{:S(2)}) %collective-permute-start.32) | collective-permute-done | bytes 229408 | tf_op jit(solution)/shard_map/ppermute | solution.py:687
  511.1 3.4 collective-permute-done.28
  514.5 3.3 collective-permute-start.29
  517.8 6.9 %collective-permute-done.34 = f32[64,512]{1,0:T(8,128)S(1)} collective-permute-done((f32[64,512]{1,0:T(8,128)S(1)}, f32[64,512]{1,0:T(8,128)S(1)}, u32[]{:S(2)}, u32[]{:S(2)}) %collective-permute-start.34) | collective-permute-done | bytes 131104 | tf_op jit(solution)/shard_map/ppermute | solution.py:687
  525.4 3.7 collective-permute-done.29
  530.5 3.3 fusion.7
  (278 shorter events, 99.5 us)
Async XLA Ops:
  3.4 72.2 %collective-permute-start.1 = (f32[512,1024]{1,0:T(8,128)}, f32[512,1024]{1,0:T(8,128)}, u32[]{:S(2)}, u32[]{:S(2)}) collective-permute-start(f32[512,1024]{1,0:T(8,128)} %convert_element_type.67), channel_id=1, source_target_pairs={{0,1},{1,0},{2,3},{3,2},{4,5},{5,4},{6,7},{7,6},{8,9},{9,8},{10,11... | collective-permute-start | bytes 6291464 | tf_op jit(solution)/shard_map/ppermute | solution.py:774
  21.0 51.6 %copy-start.25 = (bf16[561,1024]{1,0:T(8,128)(2,1)S(1)}, bf16[561,1024]{1,0:T(8,128)(2,1)}, u32[]{:S(2)}) copy-start(bf16[561,1024]{1,0:T(8,128)(2,1)} %x_ref.1) | copy-start | bytes 3446788
  72.6 32.1 %collective-permute-start = (f32[256,512]{1,0:T(8,128)}, f32[256,512]{1,0:T(8,128)}, u32[]{:S(2)}, u32[]{:S(2)}) collective-permute-start(f32[256,512]{1,0:T(8,128)} %get-tuple-element.495), channel_id=1, source_target_pairs={{0,1},{1,0},{2,3},{3,2},{4,5},{5,4},{6,7},{7,6},{8,9},{9,8},{10,11... | collective-permute-start | bytes 1572872 | tf_op jit(solution)/shard_map/ppermute | solution.py:774
  75.5 26.0 %copy-start.51 = (s32[2]{0:T(128)}, s32[2]{0:T(128)S(1)}, u32[]{:S(2)}) copy-start(s32[2]{0:T(128)S(1)} %pad_add_fusion.pick_ref) | copy-start | bytes 28
  75.6 25.9 %copy-start.47 = (s32[2]{0:T(128)}, s32[2]{0:T(128)S(1)}, u32[]{:S(2)}) copy-start(s32[2]{0:T(128)S(1)} %pad_add_fusion.1.pick_ref) | copy-start | bytes 28
  75.6 25.9 %copy-start.52 = (s32[2]{0:T(128)}, s32[2]{0:T(128)S(1)}, u32[]{:S(2)}) copy-start(s32[2]{0:T(128)S(1)} %constant_dynamic-update-slice_fusion.3.pick_ref) | copy-start | bytes 28
  75.6 25.9 %copy-start.48 = (s32[2]{0:T(128)}, s32[2]{0:T(128)S(1)}, u32[]{:S(2)}) copy-start(s32[2]{0:T(128)S(1)} %constant_dynamic-update-slice_fusion.2.pick_ref) | copy-start | bytes 28
  102.6 19.1 %collective-permute-start.3 = (f32[320,512]{1,0:T(8,128)S(1)}, f32[320,512]{1,0:T(8,128)}, u32[]{:S(2)}, u32[]{:S(2)}) collective-permute-start(f32[320,512]{1,0:T(8,128)S(1)} %get-tuple-element.491), channel_id=1, source_target_pairs={{0,1},{1,0},{2,3},{3,2},{4,5},{5,4},{6,7},{7,6},{8,9},{9,8},{10,11... | collective-permute-start | bytes 1966088 | tf_op jit(solution)/shard_map/ppermute | solution.py:774
  121.5 26.2 %collective-permute-start.2 = (f32[256,1024]{1,0:T(8,128)S(1)}, f32[256,1024]{1,0:T(8,128)}, u32[]{:S(2)}, u32[]{:S(2)}) collective-permute-start(f32[256,1024]{1,0:T(8,128)S(1)} %fusion.55), channel_id=1, source_target_pairs={{0,1},{1,0},{2,3},{3,2},{4,5},{5,4},{6,7},{7,6},{8,9},{9,8},{10,11... | collective-permute-start | bytes 3145736 | tf_op jit(solution)/shard_map/ppermute | solution.py:774
  140.4 35.3 %collective-permute-start.4 = (f32[320,1024]{1,0:T(8,128)S(1)}, f32[320,1024]{1,0:T(8,128)S(1)}, u32[]{:S(2)}, u32[]{:S(2)}) collective-permute-start(f32[320,1024]{1,0:T(8,128)S(1)} %fusion.56), channel_id=1, source_target_pairs={{0,1},{1,0},{2,3},{3,2},{4,5},{5,4},{6,7},{7,6},{8,9},{9,8},{10,11... | collective-permute-start | bytes 3932168 | tf_op jit(solution)/shard_map/ppermute | solution.py:774
  156.6 39.7 %collective-permute-start.5 = (f32[256,1024]{1,0:T(8,128)}, f32[256,1024]{1,0:T(8,128)}, u32[]{:S(2)}, u32[]{:S(2)}) collective-permute-start(f32[256,1024]{1,0:T(8,128)} %fusion.57), channel_id=1, source_target_pairs={{0,1},{1,0},{2,3},{3,2},{4,5},{5,4},{6,7},{7,6},{8,9},{9,8},{10,11... | collective-permute-start | bytes 3145736 | tf_op jit(solution)/shard_map/ppermute | solution.py:774
  191.1 16.1 %collective-permute-start.6 = (f32[8,64,2048]{2,1,0:T(8,128)}, f32[8,64,2048]{2,1,0:T(8,128)}, u32[]{:S(2)}, u32[]{:S(2)}) collective-permute-start(f32[8,64,2048]{2,1,0:T(8,128)} %weight_half.4), channel_id=1, source_target_pairs={{0,2},{2,0},{4,6},{6,4},{8,10},{10,8},{12,14},{14,12},{16,18},{18,... | collective-permute-start | bytes 12582920 | tf_op jit(solution)/shard_map/ppermute | solution.py:687
  203.8 13.2 %collective-permute-start.7 = (f32[8,64,2048]{2,1,0:T(8,128)}, f32[8,64,2048]{2,1,0:T(8,128)}, u32[]{:S(2)}, u32[]{:S(2)}) collective-permute-start(f32[8,64,2048]{2,1,0:T(8,128)} %weight_half.6), channel_id=1, source_target_pairs={{0,2},{2,0},{4,6},{6,4},{8,10},{10,8},{12,14},{14,12},{16,18},{18,... | collective-permute-start | bytes 12582920 | tf_op jit(solution)/shard_map/ppermute | solution.py:687
  206.8 36.7 %collective-permute-start.8 = (f32[320,1024]{1,0:T(8,128)}, f32[320,1024]{1,0:T(8,128)}, u32[]{:S(2)}, u32[]{:S(2)}) collective-permute-start(f32[320,1024]{1,0:T(8,128)} %fusion.58), channel_id=1, source_target_pairs={{0,1},{1,0},{2,3},{3,2},{4,5},{5,4},{6,7},{7,6},{8,9},{9,8},{10,11... | collective-permute-start | bytes 3932168 | tf_op jit(solution)/shard_map/ppermute | solution.py:774
  215.3 55.1 %collective-permute-start.9 = (f32[4,64,2048]{2,1,0:T(8,128)}, f32[4,64,2048]{2,1,0:T(8,128)}, u32[]{:S(2)}, u32[]{:S(2)}) collective-permute-start(f32[4,64,2048]{2,1,0:T(8,128)} %get-tuple-element.300), channel_id=1, source_target_pairs={{0,8},{2,10},{4,12},{6,14},{8,0},{10,2},{12,4},{14,6},{16,24},{18,... | collective-permute-start | bytes 6291464 | tf_op jit(solution)/shard_map/ppermute | solution.py:687
  243.5 48.9 %collective-permute-start.10 = (f32[4,64,2048]{2,1,0:T(8,128)}, f32[4,64,2048]{2,1,0:T(8,128)}, u32[]{:S(2)}, u32[]{:S(2)}) collective-permute-start(f32[4,64,2048]{2,1,0:T(8,128)} %get-tuple-element.306), channel_id=1, source_target_pairs={{0,4},{2,6},{4,0},{6,2},{8,12},{10,14},{12,8},{14,10},{16,20},{18,... | collective-permute-start | bytes 6291464 | tf_op jit(solution)/shard_map/ppermute | solution.py:687
  280.0 37.9 %collective-permute-start.12 = (f32[8,64,1152]{2,1,0:T(8,128)}, f32[8,64,1152]{2,1,0:T(8,128)}, u32[]{:S(2)}, u32[]{:S(2)}) collective-permute-start(f32[8,64,1152]{2,1,0:T(8,128)} %many_half.6), channel_id=1, source_target_pairs={{0,2},{2,0},{4,6},{6,4},{8,10},{10,8},{12,14},{14,12},{16,18},{18,... | collective-permute-start | bytes 7077896 | tf_op jit(solution)/shard_map/ppermute | solution.py:687
  280.0 35.3 %collective-permute-start.11 = (f32[2,64,2048]{2,1,0:T(8,128)}, f32[2,64,2048]{2,1,0:T(8,128)}, u32[]{:S(2)}, u32[]{:S(2)}) collective-permute-start(f32[2,64,2048]{2,1,0:T(8,128)} %get-tuple-element.314), channel_id=1, source_target_pairs={{0,4},{2,6},{4,0},{6,2},{8,12},{10,14},{12,8},{14,10},{16,20},{18,... | collective-permute-start | bytes 3145736 | tf_op jit(solution)/shard_map/ppermute | solution.py:687
  296.2 57.8 %collective-permute-start.13 = (f32[2,64,2048]{2,1,0:T(8,128)}, f32[2,64,2048]{2,1,0:T(8,128)}, u32[]{:S(2)}, u32[]{:S(2)}) collective-permute-start(f32[2,64,2048]{2,1,0:T(8,128)} %get-tuple-element.331), channel_id=1, source_target_pairs={{0,8},{2,10},{4,12},{6,14},{8,0},{10,2},{12,4},{14,6},{16,24},{18,... | collective-permute-start | bytes 3145736 | tf_op jit(solution)/shard_map/ppermute | solution.py:687
  324.4 43.5 %collective-permute-start.14 = (f32[4,64,1152]{2,1,0:T(8,128)}, f32[4,64,1152]{2,1,0:T(8,128)}, u32[]{:S(2)}, u32[]{:S(2)}) collective-permute-start(f32[4,64,1152]{2,1,0:T(8,128)} %get-tuple-element.346), channel_id=1, source_target_pairs={{0,4},{2,6},{4,0},{6,2},{8,12},{10,14},{12,8},{14,10},{16,20},{18,... | collective-permute-start | bytes 3538952 | tf_op jit(solution)/shard_map/ppermute | solution.py:687
  326.0 41.8 %collective-permute-start.15 = (f32[64,2048]{1,0:T(8,128)}, f32[64,2048]{1,0:T(8,128)S(1)}, u32[]{:S(2)}, u32[]{:S(2)}) collective-permute-start(f32[64,2048]{1,0:T(8,128)} %get-tuple-element.347), channel_id=1, source_target_pairs={{0,16},{2,18},{4,20},{6,22},{8,24},{10,26},{12,28},{14,30},{16,0},... | collective-permute-start | bytes 1572872 | tf_op jit(solution)/shard_map/ppermute | solution.py:687
  328.7 25.3 %copy-start.50 = (s32[3]{0:T(128)}, s32[3]{0:T(128)S(1)}, u32[]{:S(2)}) copy-start(s32[3]{0:T(128)S(1)} %get-tuple-element.502.pick_ref) | copy-start | bytes 40
  328.7 89.7 %copy-start.49 = (s32[3]{0:T(128)}, s32[3]{0:T(128)S(1)}, u32[]{:S(2)}) copy-start(s32[3]{0:T(128)S(1)} %get-tuple-element.503.pick_ref) | copy-start | bytes 40
  372.1 17.2 %collective-permute-start.16 = (f32[8,64,896]{2,1,0:T(8,128)}, f32[8,64,896]{2,1,0:T(8,128)}, u32[]{:S(2)}, u32[]{:S(2)}) collective-permute-start(f32[8,64,896]{2,1,0:T(8,128)} %get-tuple-element.359), channel_id=1, source_target_pairs={{0,2},{2,0},{4,6},{6,4},{8,10},{10,8},{12,14},{14,12},{16,18},{18,... | collective-permute-start | bytes 5505032 | tf_op jit(solution)/shard_map/ppermute | solution.py:687
  372.1 17.2 %collective-permute-start.17 = (f32[8,64,512]{2,1,0:T(8,128)}, f32[8,64,512]{2,1,0:T(8,128)}, u32[]{:S(2)}, u32[]{:S(2)}) collective-permute-start(f32[8,64,512]{2,1,0:T(8,128)} %get-tuple-element.360), channel_id=1, source_target_pairs={{0,2},{2,0},{4,6},{6,4},{8,10},{10,8},{12,14},{14,12},{16,18},{18,... | collective-permute-start | bytes 3145736 | tf_op jit(solution)/shard_map/ppermute | solution.py:687
  372.6 38.7 %collective-permute-start.18 = (f32[2,64,1152]{2,1,0:T(8,128)}, f32[2,64,1152]{2,1,0:T(8,128)}, u32[]{:S(2)}, u32[]{:S(2)}) collective-permute-start(f32[2,64,1152]{2,1,0:T(8,128)} %get-tuple-element.373), channel_id=1, source_target_pairs={{0,8},{2,10},{4,12},{6,14},{8,0},{10,2},{12,4},{14,6},{16,24},{18,... | collective-permute-start | bytes 1769480 | tf_op jit(solution)/shard_map/ppermute | solution.py:687
  374.2 37.1 %collective-permute-start.19 = (f32[64,2048]{1,0:T(8,128)}, f32[64,2048]{1,0:T(8,128)}, u32[]{:S(2)}, u32[]{:S(2)}) collective-permute-start(f32[64,2048]{1,0:T(8,128)} %get-tuple-element.374), channel_id=1, source_target_pairs={{0,16},{2,18},{4,20},{6,22},{8,24},{10,26},{12,28},{14,30},{16,0},... | collective-permute-start | bytes 1572872 | tf_op jit(solution)/shard_map/ppermute | solution.py:687
  396.2 36.9 %collective-permute-start.20 = (f32[4,64,896]{2,1,0:T(8,128)}, f32[4,64,896]{2,1,0:T(8,128)}, u32[]{:S(2)}, u32[]{:S(2)}) collective-permute-start(f32[4,64,896]{2,1,0:T(8,128)} %get-tuple-element.387), channel_id=1, source_target_pairs={{0,8},{2,10},{4,12},{6,14},{8,0},{10,2},{12,4},{14,6},{16,24},{18,... | collective-permute-start | bytes 2752520 | tf_op jit(solution)/shard_map/ppermute | solution.py:687
  411.3 21.8 %collective-permute-start.21 = (f32[4,64,512]{2,1,0:T(8,128)}, f32[4,64,512]{2,1,0:T(8,128)}, u32[]{:S(2)}, u32[]{:S(2)}) collective-permute-start(f32[4,64,512]{2,1,0:T(8,128)} %get-tuple-element.388), channel_id=1, source_target_pairs={{0,4},{2,6},{4,0},{6,2},{8,12},{10,14},{12,8},{14,10},{16,20},{18,... | collective-permute-start | bytes 1572872 | tf_op jit(solution)/shard_map/ppermute | solution.py:687
  415.8 17.4 %collective-permute-start.22 = (f32[64,1152]{1,0:T(8,128)}, f32[64,1152]{1,0:T(8,128)S(1)}, u32[]{:S(2)}, u32[]{:S(2)}) collective-permute-start(f32[64,1152]{1,0:T(8,128)} %get-tuple-element.389), channel_id=1, source_target_pairs={{0,16},{2,18},{4,20},{6,22},{8,24},{10,26},{12,28},{14,30},{16,0},... | collective-permute-start | bytes 884744 | tf_op jit(solution)/shard_map/ppermute | solution.py:687
  449.6 9.7 %collective-permute-start.23 = (f32[8,64,896]{2,1,0:T(8,128)}, f32[8,64,896]{2,1,0:T(8,128)}, u32[]{:S(2)}, u32[]{:S(2)}) collective-permute-start(f32[8,64,896]{2,1,0:T(8,128)} %get-tuple-element.405), channel_id=1, source_target_pairs={{0,2},{2,0},{4,6},{6,4},{8,10},{10,8},{12,14},{14,12},{16,18},{18,... | collective-permute-start | bytes 5505032 | tf_op jit(solution)/shard_map/ppermute | solution.py:687
  449.6 9.7 %collective-permute-start.24 = (f32[8,64,512]{2,1,0:T(8,128)}, f32[8,64,512]{2,1,0:T(8,128)}, u32[]{:S(2)}, u32[]{:S(2)}) collective-permute-start(f32[8,64,512]{2,1,0:T(8,128)} %get-tuple-element.406), channel_id=1, source_target_pairs={{0,2},{2,0},{4,6},{6,4},{8,10},{10,8},{12,14},{14,12},{16,18},{18,... | collective-permute-start | bytes 3145736 | tf_op jit(solution)/shard_map/ppermute | solution.py:687
  455.1 43.3 %collective-permute-start.27 = (f32[288,1024]{1,0:T(8,128)}, f32[288,1024]{1,0:T(8,128)}, u32[]{:S(2)}, u32[]{:S(2)}) collective-permute-start(f32[288,1024]{1,0:T(8,128)} %convolution_add_fusion.2), channel_id=1, source_target_pairs={{0,1},{1,0},{2,3},{3,2},{4,5},{5,4},{6,7},{7,6},{8,9},{9,8},{10,11... | collective-permute-start | bytes 3538952 | tf_op jit(solution)/shard_map/ppermute | solution.py:774
  457.8 12.8 %collective-permute-start.35 = (f32[2,64,512]{2,1,0:T(8,128)}, f32[2,64,512]{2,1,0:T(8,128)}, u32[]{:S(2)}, u32[]{:S(2)}) collective-permute-start(f32[2,64,512]{2,1,0:T(8,128)} %get-tuple-element.420), channel_id=1, source_target_pairs={{0,8},{2,10},{4,12},{6,14},{8,0},{10,2},{12,4},{14,6},{16,24},{18,... | collective-permute-start | bytes 786440 | tf_op jit(solution)/shard_map/ppermute | solution.py:687
  466.0 32.0 %copy-start.29 = (f32[2,64,896]{2,1,0:T(8,128)S(1)}, f32[2,64,896]{2,1,0:T(8,128)}, u32[]{:S(2)}) copy-start(f32[2,64,896]{2,1,0:T(8,128)} %get-tuple-element.413) | copy-start | bytes 1376260
  466.0 32.5 %copy-start.36 = (f32[4,64,896]{2,1,0:T(8,128)S(1)}, f32[4,64,896]{2,1,0:T(8,128)}, u32[]{:S(2)}) copy-start(f32[4,64,896]{2,1,0:T(8,128)} %get-tuple-element.410) | copy-start | bytes 2752516
  466.0 32.5 %collective-permute-start.25 = (f32[4,64,896]{2,1,0:T(8,128)}, f32[4,64,896]{2,1,0:T(8,128)S(1)}, u32[]{:S(2)}, u32[]{:S(2)}) collective-permute-start(f32[4,64,896]{2,1,0:T(8,128)} %get-tuple-element.407), channel_id=1, source_target_pairs={{0,4},{2,6},{4,0},{6,2},{8,12},{10,14},{12,8},{14,10},{16,20},{18,... | collective-permute-start | bytes 2752520 | tf_op jit(solution)/shard_map/ppermute | solution.py:687
  469.7 29.3 %copy-start.39 = (f32[4,64,512]{2,1,0:T(8,128)S(1)}, f32[4,64,512]{2,1,0:T(8,128)}, u32[]{:S(2)}) copy-start(f32[4,64,512]{2,1,0:T(8,128)} %get-tuple-element.417) | copy-start | bytes 1572868
  469.7 28.2 %collective-permute-start.31 = (f32[2,64,896]{2,1,0:T(8,128)S(1)}, f32[2,64,896]{2,1,0:T(8,128)S(1)}, u32[]{:S(2)}, u32[]{:S(2)}) collective-permute-start(f32[2,64,896]{2,1,0:T(8,128)S(1)} %copy-done.41), channel_id=1, source_target_pairs={{0,4},{2,6},{4,0},{6,2},{8,12},{10,14},{12,8},{14,10},{16,20},{18,... | collective-permute-start | bytes 1376264 | tf_op jit(solution)/shard_map/ppermute | solution.py:687
  471.5 8.0 %collective-permute-start.36 = (f32[64,512]{1,0:T(8,128)S(1)}, f32[64,512]{1,0:T(8,128)S(1)}, u32[]{:S(2)}, u32[]{:S(2)}) collective-permute-start(f32[64,512]{1,0:T(8,128)S(1)} %add_bitcast_fusion.7), channel_id=1, source_target_pairs={{0,16},{2,18},{4,20},{6,22},{8,24},{10,26},{12,28},{14,30},{16,0},... | collective-permute-start | bytes 393224 | tf_op jit(solution)/shard_map/ppermute | solution.py:687
  471.9 26.6 %collective-permute-start.26 = (f32[4,64,512]{2,1,0:T(8,128)S(1)}, f32[4,64,512]{2,1,0:T(8,128)S(1)}, u32[]{:S(2)}, u32[]{:S(2)}) collective-permute-start(f32[4,64,512]{2,1,0:T(8,128)S(1)} %copy-done.58), channel_id=1, source_target_pairs={{0,8},{2,10},{4,12},{6,14},{8,0},{10,2},{12,4},{14,6},{16,24},{18,... | collective-permute-start | bytes 1572872 | tf_op jit(solution)/shard_map/ppermute | solution.py:687
  479.5 49.7 %collective-permute-start.30 = (f32[288,1024]{1,0:T(8,128)S(1)}, f32[288,1024]{1,0:T(8,128)S(1)}, u32[]{:S(2)}, u32[]{:S(2)}) collective-permute-start(f32[288,1024]{1,0:T(8,128)S(1)} %convolution_add_fusion.1), channel_id=1, source_target_pairs={{0,1},{1,0},{2,3},{3,2},{4,5},{5,4},{6,7},{7,6},{8,9},{9,8},{10,11... | collective-permute-start | bytes 3538952 | tf_op jit(solution)/shard_map/ppermute | solution.py:774
  498.0 12.1 %collective-permute-start.32 = (f32[64,896]{1,0:T(8,128)S(1)}, f32[64,896]{1,0:T(8,128)S(1)}, u32[]{:S(2)}, u32[]{:S(2)}) collective-permute-start(f32[64,896]{1,0:T(8,128)S(1)} %add_bitcast_fusion.6), channel_id=1, source_target_pairs={{0,16},{2,18},{4,20},{6,22},{8,24},{10,26},{12,28},{14,30},{16,0},... | collective-permute-start | bytes 688136 | tf_op jit(solution)/shard_map/ppermute | solution.py:687
  498.6 15.9 %collective-permute-start.28 = (f32[2,64,896]{2,1,0:T(8,128)S(1)}, f32[2,64,896]{2,1,0:T(8,128)S(1)}, u32[]{:S(2)}, u32[]{:S(2)}) collective-permute-start(f32[2,64,896]{2,1,0:T(8,128)S(1)} %fusion.36), channel_id=1, source_target_pairs={{0,8},{2,10},{4,12},{6,14},{8,0},{10,2},{12,4},{14,6},{16,24},{18,... | collective-permute-start | bytes 1376264 | tf_op jit(solution)/shard_map/ppermute | solution.py:687
  499.1 11.8 %collective-permute-start.33 = (f32[2,64,512]{2,1,0:T(8,128)S(1)}, f32[2,64,512]{2,1,0:T(8,128)S(1)}, u32[]{:S(2)}, u32[]{:S(2)}) collective-permute-start(f32[2,64,512]{2,1,0:T(8,128)S(1)} %fusion.41), channel_id=1, source_target_pairs={{0,4},{2,6},{4,0},{6,2},{8,12},{10,14},{12,8},{14,10},{16,20},{18,... | collective-permute-start | bytes 786440 | tf_op jit(solution)/shard_map/ppermute | solution.py:687
  510.9 13.7 %collective-permute-start.34 = (f32[64,512]{1,0:T(8,128)S(1)}, f32[64,512]{1,0:T(8,128)S(1)}, u32[]{:S(2)}, u32[]{:S(2)}) collective-permute-start(f32[64,512]{1,0:T(8,128)S(1)} %fusion.45), channel_id=1, source_target_pairs={{0,16},{2,18},{4,20},{6,22},{8,24},{10,26},{12,28},{14,30},{16,0},... | collective-permute-start | bytes 393224 | tf_op jit(solution)/shard_map/ppermute | solution.py:687
  514.5 14.6 %collective-permute-start.29 = (f32[64,896]{1,0:T(8,128)S(1)}, f32[64,896]{1,0:T(8,128)S(1)}, u32[]{:S(2)}, u32[]{:S(2)}) collective-permute-start(f32[64,896]{1,0:T(8,128)S(1)} %fusion.44), channel_id=1, source_target_pairs={{0,16},{2,18},{4,20},{6,22},{8,24},{10,26},{12,28},{14,30},{16,0},... | collective-permute-start | bytes 688136 | tf_op jit(solution)/shard_map/ppermute | solution.py:687
  529.2 5.3 collective-permute-start.37
  (51 other events, 264.1 us)

commit v7 on v6

--- a/solution.py
+++ b/solution.py
@@ -16,6 +16,7 @@
 f32 = jnp.float32
 LIMIT = 10900.0
 VMEM_CAP = 62 * 2**20
+STEPS = 4
 
 
 def lane_gather(table, index):
@@ -115,18 +116,19 @@
         fill_tables(k_ref, 0, rows, pq_ref, far_tab, far_inv, p)
 
     def far_body(step, carry):
-        at = pl.ds(pl.multiple_of(step * 8, 8), 8)
-
-        def store(p, c, total):
-            if c * 128 < split:
-                far_head[p, at, c * 128:(c + 1) * 128] = total
-            else:
-                far_rest[p, at, c * 128 - split:(c + 1) * 128 - split] = total
-
-        look_up(far_tab, bt_ref, at, store, pairs=pairs, cols=cols)
+        for turn in range(STEPS):
+            at = pl.ds(pl.multiple_of(step * 8 * STEPS + turn * 8, 8), 8)
+
+            def store(p, c, total, at=at):
+                if c * 128 < split:
+                    far_head[p, at, c * 128:(c + 1) * 128] = total
+                else:
+                    far_rest[p, at, c * 128 - split:(c + 1) * 128 - split] = total
+
+            look_up(far_tab, bt_ref, at, store, pairs=pairs, cols=cols)
         return carry
 
-    lax.fori_loop(0, rows // 8, far_body, 0)
+    lax.fori_loop(0, rows // (8 * STEPS), far_body, 0)
     for p in range(pairs):
         far_head[p, rows:, :] = jnp.zeros((cols - rows, split), jnp.int32)
         far_rest[p, rows:, :] = jnp.zeros((cols - rows, cols - split), jnp.int32)
@@ -149,16 +151,17 @@
 
     def block_body(start, tall):
         def near_body(step, carry):
-            at = pl.ds(pl.multiple_of(start + step * 8, 8), 8)
-            out_at = pl.ds(pl.multiple_of(step * 8, 8), 8)
-
-            def store(p, c, total):
-                near_sum[p, out_at, c * 128:(c + 1) * 128] = total
-
-            look_up(near_tab, b_ref, at, store, pairs=pairs, cols=cols)
+            for turn in range(STEPS):
+                at = pl.ds(pl.multiple_of(start + step * 8 * STEPS + turn * 8, 8), 8)
+                out_at = pl.ds(pl.multiple_of(step * 8 * STEPS + turn * 8, 8), 8)
+
+                def store(p, c, total, out_at=out_at):
+                    near_sum[p, out_at, c * 128:(c + 1) * 128] = total
+
+                look_up(near_tab, b_ref, at, store, pairs=pairs, cols=cols)
             return carry
 
-        lax.fori_loop(0, tall // 8, near_body, 0)
+        lax.fori_loop(0, tall // (8 * STEPS), near_body, 0)
         at = pl.ds(start, tall)
         for p in range(pairs):
             cut = slice(p * 128, (p + 1) * 128)
@@ -988,8 +991,8 @@
 
     near = []
     blocks = rows // 64
-    back_head, back_rest = tie((back_head, back_rest), up_chain)
     near.append(attention_scatter([back_head], bucket_head, merge, 0, split // 64))
+    back_rest, near = tie((back_rest, near), up_chain)
     back_rest, near = tie((back_rest, near), down_chain)
     back_rest, near = tie((back_rest, near), outer_chain)
     near.append(attention_scatter([back_rest], bucket_rest, merge, 0, blocks - split // 64))
@@ -1004,6 +1007,7 @@
         far.append(attention_scatter(backs, bucket_cols, merge, cuts[part], cuts[part + 1] - cuts[part]))
         backs, far = tie((backs, far), *chains)
     key_low, query_table_sum = attention_close(far, [key_base], pos_query, qkv, 1)
+    key_low, query_table_sum = tie((key_low, query_table_sum), near_chain)
     far_chain = tail(key_low, query_table_sum, query_position, [low_first, high_first])
     parts, others = [], []
     for low, high in ((0, rows // 2), (rows // 2, rows)):
@@ -1012,6 +1016,7 @@
     far_chain.step()
     far_chain.step()
     far_chain.extra, others[0] = lax.optimization_barrier((far_chain.extra, others[0]))
+    far_chain.extra = tie(far_chain.extra, near_chain)
     far_main, query_position_grad = far_chain.finish()
     far_main, others[1] = lax.optimization_barrier((far_main, others[1]))
     input_gradient = (

time: 545 us -> 531 us (0.974)
  waiting for transfers between devices: 85.6 us -> 76.4 us
  Pallas kernels: 289 us -> 282 us
    ppermute x28, waiting for transfers between devices: 56.2 us -> 35.7 us  [flipped(): return lax.ppermute(value, 'dp', [(i, i ^ 1 << bit) for i in range(size)])]
    ppermute x9, waiting for transfers between devices: 29.4 us -> 40.7 us  [swap(): return lax.ppermute(value.astype(f32), 'mp', [(0, 1), (1, 0)])]
    add x10 -> x12, other arithmetic: 21.3 us -> 20.2 us  [split(): half(held, own) + half(extra, own)]
  transfers between devices with their start and end apart: 38 -> 38, of which waited for: 10 -> 11; matrix products, arithmetic and copies ran while one was open for 19% -> 20% of each run, Pallas kernels for 52% -> 53%
where the time goes in v7:
time: 531 us; the launch traced here: 521 us
  Pallas kernels  282 us (53%)
  waiting for transfers between devices  76.4 us (14%)
  other arithmetic  57.3 us (11%)
  matrix products  39.8 us (7%)
  starting transfers between devices  35.8 us (7%)
  local copies, waits for them, and re-layouts  26.8 us (5%)
    pallas_call x5, Pallas kernels, attention_scatter(): pl.pallas_call(functools.partial(scatter_kernel, groups=8, cols=cols), gr...  86.1 us
    pallas_call x1, Pallas kernels, attention_head(): pl.pallas_call(kernel, out_shape=(jax.ShapeDtypeStruct((2 * pairs, split,...  44.5 us
    ppermute x9, waiting for transfers between devices, swap(): return lax.ppermute(value.astype(f32), 'mp', [(0, 1), (1, 0)])  40.7 us
    pallas_call x6, Pallas kernels, many_half(): pl.pallas_call(functools.partial(many_kernel, plan=plan, widths=widths, t...  37.6 us
    ppermute x28, waiting for transfers between devices, flipped(): return lax.ppermute(value, 'dp', [(i, i ^ 1 << bit) for i in range(size)])  35.7 us
    pallas_call x4, Pallas kernels, weight_half(): pl.pallas_call(functools.partial(weight_kernel, count=len(xs), blocks=blo...  30.9 us
    pallas_call x2, Pallas kernels, attention_draw(): pl.pallas_call(functools.partial(draw_kernel, first=first, tall=tall, row...  24.7 us
    ppermute x28, starting transfers between devices, flipped(): return lax.ppermute(value, 'dp', [(i, i ^ 1 << bit) for i in range(size)])  24.4 us
  transfers between devices with their start and end apart: 38, of which 11 were waited for; matrix products, arithmetic and copies ran while one was open for 20% of the time, Pallas kernels for 53%

profile of v7, /device:TPU:0, one launch (start us, length us, event | category | flops | bytes accessed | tf_op | source)
XLA Modules:
  0.0 520.7 jit_solution(11267725346285543573)
XLA Ops:
  0.6 2.8 convert_element_type.67
  3.4 3.0 collective-permute-start.1
  7.0 4.6 copy.60.b_ref
  11.6 9.4 %project.1 = (bf16[640,1536]{1,0:T(8,128)(2,1)}, bf16[384,512]{1,0:T(8,128)(2,1)}, bf16[384,512]{1,0:T(8,128)(2,1)}) custom-call(bf16[561,1024]{1,0:T(8,128)(2,1)} %x_ref.1, bf16[1024,512]{1,0:T(8,128)(2,1)} %wq_ref.1, bf16[1024,512]{1,0:T(8,128)(2,1)} %wk_ref.1, bf16[1024,512]{1,0:T(8,128)(2,1)} %wv_ref.1, bf16[3,128,1024]{2,1,0:T(8,128)(2,1)} %t_ref.1, ...), custom_call_target="tpu_custom_call" | custom-call | flops 4000000000 | bytes 9000000 | tf_op jit(solution)/shard_map/project/pallas_call | solution.py:229
  21.0 44.5 %attention_head.1 = (bf16[8,256,640]{2,1,0:T(8,128)(2,1)}, bf16[256,512]{1,0:T(8,128)(2,1)}, s32[3,256,640]{2,1,0:T(8,128)}, s32[3,320,640]{2,1,0:T(8,128)}, s32...) custom-call(s32[1]{0:T(128)S(6)} %copy.120.used_ref, ...), custom_call_target="tpu_custom_call" | custom-call | flops 40000000000 | bytes 25000000 | tf_op jit(solution)/shard_map/attention_head/pallas_call | solution.py:403
  72.8 23.8 %attention_rest.1 = (bf16[8,320,640]{2,1,0:T(8,128)(2,1)}, bf16[320,512]{1,0:T(8,128)(2,1)}) custom-call(s32[1]{0:T(128)S(6)} %copy.120.used_ref, bf16[640,1536]{1,0:T(8,128)(2,1)} %get-tuple-element.265.qkv_ref.q_ref.k_ref.v_ref.refs_5_, bf16[384,512]{1,0:T(8,128)(2,1)} %get-tuple-element.266.pk_ref.refs_4_, ...), custom_call_target="tpu_custom_call" | custom-call | flops 20000000000 | bytes 12000000 | tf_op jit(solution)/shard_map/attention_rest/pallas_call | solution.py:440
  100.7 6.7 %attend.2 = (f32[256,1024]{1,0:T(8,128)}, bf16[256,1024]{1,0:T(8,128)(2,1)}, f32[256,1024]{1,0:T(8,128)}, f32[256,1]{1,0:T(8,128)}) custom-call(bf16[256,1024]{1,0:T(8,128)(2,1)} %slice.113.t_ref, bf16[256,512]{1,0:T(8,128)(2,1)} %get-tuple-element.268.c_ref, f32[256,512]{1,0:T(8,128)} %collective-permute-done.o_ref, bf16[512,1024]{1,0:T(8,128)(2,1)} %w_ref.3, ...), custom_call_target="tpu_custom_call" | custom-call | flops 2000000000 | bytes 8000000 | tf_op jit(solution)/shard_map/attend/pallas_call | solution.py:802
  107.5 8.8 %multiply_convert_fusion.1 = (bf16[256,2048]{1,0:T(8,128)(2,1)S(1)}, f32[256,2048]{1,0:T(8,128)}, f32[256,2048]{1,0:T(8,128)}) fusion(bf16[256,1024]{1,0:T(8,128)(2,1)} %get-tuple-element.295.refs_0_, bf16[1024,2048]{1,0:T(8,128)(2,1)} %param.37), kind=kOutput, calls=%fused_computation.26 | convolution fusion | flops 1107820544 | bytes 9961472 | tf_op jit(solution)/shard_map/dot_general | solution.py:40
  118.7 7.7 %attend.3 = (f32[320,1024]{1,0:T(8,128)}, bf16[320,1024]{1,0:T(8,128)(2,1)}, f32[320,1024]{1,0:T(8,128)}, f32[320,1]{1,0:T(8,128)}) custom-call(bf16[320,1024]{1,0:T(8,128)(2,1)} %copy.62.t_ref, bf16[320,512]{1,0:T(8,128)(2,1)} %get-tuple-element.276.c_ref, f32[320,512]{1,0:T(8,128)} %collective-permute-done.3.o_ref, bf16[512,1024]{1,0:T(8,128)(2,1)} %w_ref.3, ...), custom_call_target="tpu_custom_call" | custom-call | flops 2000000000 | bytes 8000000 | tf_op jit(solution)/shard_map/attend/pallas_call | solution.py:802
  126.5 9.3 %multiply_convert_fusion = (bf16[320,2048]{1,0:T(8,128)(2,1)S(1)}, f32[320,2048]{1,0:T(8,128)S(1)}, f32[320,2048]{1,0:T(8,128)S(1)}) fusion(bf16[320,1024]{1,0:T(8,128)(2,1)} %get-tuple-element.296.refs_1_, bf16[1024,2048]{1,0:T(8,128)(2,1)} %param.37), kind=kOutput, calls=%fused_computation.4 | convolution fusion | flops 1384775680 | bytes 11403264 | tf_op jit(solution)/shard_map/dot_general | solution.py:40
  139.2 5.6 %collective-permute-done.2 = f32[256,1024]{1,0:T(8,128)} collective-permute-done((f32[256,1024]{1,0:T(8,128)}, f32[256,1024]{1,0:T(8,128)}, u32[]{:S(2)}, u32[]{:S(2)}) %collective-permute-start.2) | collective-permute-done | bytes 1048608 | tf_op jit(solution)/shard_map/ppermute | solution.py:777
  154.2 18.6 %collective-permute-done.4 = f32[320,1024]{1,0:T(8,128)S(1)} collective-permute-done((f32[320,1024]{1,0:T(8,128)S(1)}, f32[320,1024]{1,0:T(8,128)S(1)}, u32[]{:S(2)}, u32[]{:S(2)}) %collective-permute-start.4) | collective-permute-done | bytes 1310752 | tf_op jit(solution)/shard_map/ppermute | solution.py:777
  178.1 2.6 fusion.58
  180.8 7.4 %weight_half.4 = f32[8,64,2048]{2,1,0:T(8,128)} custom-call(s32[2]{0:T(128)} %copy-done.53, bf16[256,1024]{1,0:T(8,128)(2,1)} %copy-done.14, bf16[320,1024]{1,0:T(8,128)(2,1)} %copy-done.5, bf16[256,2048]{1,0:T(8,128)(2,1)} %copy-done.21, bf16[320,2048]{1,0:T(8,128)(2,1)} %copy-done.12), custom_call_target="tpu_custom_call" | custom-call | flops 1207959552 | bytes 8388608 | tf_op jit(solution)/shard_map/weight_half/pallas_call | solution.py:607
  188.1 5.3 %collective-permute-done.5 = f32[256,1024]{1,0:T(8,128)} collective-permute-done((f32[256,1024]{1,0:T(8,128)}, f32[256,1024]{1,0:T(8,128)}, u32[]{:S(2)}, u32[]{:S(2)}) %collective-permute-start.5) | collective-permute-done | bytes 1048608 | tf_op jit(solution)/shard_map/ppermute | solution.py:777
  193.4 7.6 %weight_half.6 = f32[8,64,2048]{2,1,0:T(8,128)} custom-call(s32[2]{0:T(128)} %copy-done.49, bf16[256,1024]{1,0:T(8,128)(2,1)} %get-tuple-element.295.refs_0_, bf16[320,1024]{1,0:T(8,128)(2,1)} %get-tuple-element.296.refs_1_, bf16[256,2048]{1,0:T(8,128)(2,1)} %copy-done.22, bf16[320,2048]{1,0:T(8,128)(2,1)} %copy-done.13), custom_call_target="tpu_custom_call" | custom-call | flops 1207959552 | bytes 8388608 | tf_op jit(solution)/shard_map/weight_half/pallas_call | solution.py:607
  204.5 7.9 %weight_half.5 = (f32[4,64,2048]{2,1,0:T(8,128)}, f32[4,64,2048]{2,1,0:T(8,128)}) custom-call(s32[2]{0:T(128)} %copy-done.52, bf16[256,1024]{1,0:T(8,128)(2,1)} %copy-done.14, bf16[320,1024]{1,0:T(8,128)(2,1)} %copy-done.5, bf16[256,2048]{1,0:T(8,128)(2,1)} %copy-done.21, bf16[320,2048]{1,0:T(8,128)(2,1)} %copy-done.12, ...), custom_call_target="tpu_custom_call" | custom-call | flops 1207959552 | bytes 8388608 | tf_op jit(solution)/shard_map/weight_half/pallas_call | solution.py:607
  214.1 8.0 %weight_half.7 = (f32[4,64,2048]{2,1,0:T(8,128)}, f32[4,64,2048]{2,1,0:T(8,128)}) custom-call(s32[2]{0:T(128)} %copy-done.48, bf16[256,1024]{1,0:T(8,128)(2,1)} %get-tuple-element.295.refs_0_, bf16[320,1024]{1,0:T(8,128)(2,1)} %get-tuple-element.296.refs_1_, bf16[256,2048]{1,0:T(8,128)(2,1)} %copy-done.22, bf16[320,2048]{1,0:T(8,128)(2,1)} %copy-done.13, ...), custom_call_target="tpu_custom_call" | custom-call | flops 1207959552 | bytes 8388608 | tf_op jit(solution)/shard_map/weight_half/pallas_call | solution.py:607
  222.1 4.1 multiply_reduce_fusion.4
  228.8 11.1 %attention_draw.2 = (bf16[32,64,640]{2,1,0:T(8,128)(2,1)}, bf16[72,64,256]{2,1,0:T(8,128)(2,1)}, f32[256,512]{1,0:T(8,128)}, f32[576,512]{1,0:T(8,128)}, f32[576,512]{1,0:T(8,128)}) custom-call(bf16[8,256,640]{2,1,0:T(8,128)(2,1)} %get-tuple-element.307.p_ref, bf16[256,512]{1,0:T(8,128)(2,1)} %convolution_convert_fusion.1.up_ref, ...), custom_call_target="tpu_custom_call" | custom-call | flops 1000000 | bytes 10000 | tf_op jit(solution)/shard_map/attention_draw/pallas_call | solution.py:464
  241.5 4.2 multiply_reduce_fusion
  251.6 13.7 %attention_draw.3 = (bf16[40,64,640]{2,1,0:T(8,128)(2,1)}, bf16[72,64,384]{2,1,0:T(8,128)(2,1)}, f32[320,512]{1,0:T(8,128)}, f32[576,512]{1,0:T(8,128)}, bf16[576,512]{1,0:T(8,128)(2,1)}) custom-call(bf16[8,320,640]{2,1,0:T(8,128)(2,1)} %get-tuple-element.312.p_ref, bf16[320,512]{1,0:T(8,128)(2,1)} %convolution_convert_fusion.up_ref, ...), custom_call_target="tpu_custom_call" | custom-call | flops 1000000 | bytes 10000 | tf_op jit(solution)/shard_map/attention_draw/pallas_call | solution.py:464
  267.3 2.8 fusion.31
  270.6 5.9 %many_half.6 = f32[8,64,1152]{2,1,0:T(8,128)} custom-call(s32[2]{0:T(128)} %copy-done.49, bf16[576,1024]{1,0:T(8,128)(2,1)} %pad_maximum_fusion.3.refs_0_, bf16[576,512]{1,0:T(8,128)(2,1)} %copy-done.23, bf16[1024,576]{1,0:T(8,128)(2,1)} %pad_bitcast_fusion.refs_2_.refs_0_, bf16[576,512]{1,0:T(8,128)(2,1)} %get-tuple-element.339.refs_3_, ...), custom_call_target="tpu_custom_call" | custom-call | flops 1000000 | bytes 10000 | tf_op jit(solution)/shard_map/many_half/pallas_call | solution.py:671
  277.9 19.0 %attention_scatter.5.refs_0_ = bf16[32,64,384]{2,1,0:T(8,128)(2,1)} custom-call(bf16[32,64,640]{2,1,0:T(8,128)(2,1)} %get-tuple-element.323.refs_0_, s32[3,256,640]{2,1,0:T(8,128)} %get-tuple-element.324.refs_1_, bf16[4,256,128]{2,1,0:T(8,128)(2,1)} %fusion.35.refs_2_.refs_3_), custom_call_target="tpu_custom_call" | custom-call | flops 1000000 | bytes 10000 | tf_op jit(solution)/shard_map/attention_scatter/pallas_call | solution.py:500
  296.9 3.8 fusion.29
  301.1 9.0 %collective-permute-done.11 = f32[2,64,2048]{2,1,0:T(8,128)} collective-permute-done((f32[2,64,2048]{2,1,0:T(8,128)}, f32[2,64,2048]{2,1,0:T(8,128)}, u32[]{:S(2)}, u32[]{:S(2)}) %collective-permute-start.11) | collective-permute-done | bytes 1048608 | tf_op jit(solution)/shard_map/ppermute | solution.py:690
  312.4 6.6 %many_half.7 = (f32[4,64,1152]{2,1,0:T(8,128)}, f32[4,64,1152]{2,1,0:T(8,128)}) custom-call(s32[2]{0:T(128)} %copy-done.48, bf16[576,1024]{1,0:T(8,128)(2,1)} %pad_maximum_fusion.3.refs_0_, bf16[576,512]{1,0:T(8,128)(2,1)} %copy-done.23, bf16[1024,576]{1,0:T(8,128)(2,1)} %pad_bitcast_fusion.refs_2_.refs_0_, bf16[576,512]{1,0:T(8,128)(2,1)} %get-tuple-element.339.refs_3_, ...), custom_call_target="tpu_custom_call" | custom-call | flops 1000000 | bytes 10000 | tf_op jit(solution)/shard_map/many_half/pallas_call | solution.py:671
  320.5 2.6 collective-permute-start.15
  324.4 23.0 %attention_scatter.6.refs_1_ = bf16[40,64,384]{2,1,0:T(8,128)(2,1)} custom-call(bf16[40,64,640]{2,1,0:T(8,128)(2,1)} %get-tuple-element.346.refs_0_, s32[3,320,640]{2,1,0:T(8,128)} %get-tuple-element.273.b_ref.refs_1_, bf16[4,256,128]{2,1,0:T(8,128)(2,1)} %fusion.35.refs_2_.refs_3_), custom_call_target="tpu_custom_call" | custom-call | flops 1000000 | bytes 10000 | tf_op jit(solution)/shard_map/attention_scatter/pallas_call | solution.py:500
  349.6 5.4 %attention_close.2 = (bf16[576,512]{1,0:T(8,128)(2,1)}, bf16[384,512]{1,0:T(8,128)(2,1)}) custom-call(bf16[32,64,384]{2,1,0:T(8,128)(2,1)} %attention_scatter.5.refs_0_, bf16[40,64,384]{2,1,0:T(8,128)(2,1)} %attention_scatter.6.refs_1_, f32[256,512]{1,0:T(8,128)} %get-tuple-element.358.refs_2_, f32[320,512]{1,0:T(8,128)} %get-tuple-element.359.refs_3_, ...), custom_call_target="tpu_custom_call" | custom-call | flops 1000000 | bytes 10000 | tf_op jit(solution)/shard_map/attention_close/pallas_call | solution.py:518
  355.0 5.8 %many_half.8 = (f32[8,64,896]{2,1,0:T(8,128)}, f32[8,64,512]{2,1,0:T(8,128)}) custom-call(s32[3]{0:T(128)} %copy-done.55, bf16[1024,576]{1,0:T(8,128)(2,1)} %pad_bitcast_fusion.refs_2_.refs_0_, bf16[576,512]{1,0:T(8,128)(2,1)} %get-tuple-element.360.refs_1_, bf16[1024,384]{1,0:T(8,128)(2,1)} %bitcast.211, ...), custom_call_target="tpu_custom_call" | custom-call | flops 1000000 | bytes 10000 | tf_op jit(solution)/shard_map/many_half/pallas_call | solution.py:671
  360.8 2.6 fusion.33
  366.6 14.6 %attention_scatter.7.refs_0_ = bf16[24,64,384]{2,1,0:T(8,128)(2,1)} custom-call(bf16[72,64,256]{2,1,0:T(8,128)(2,1)} %get-tuple-element.401.refs_0_, bf16[72,64,384]{2,1,0:T(8,128)(2,1)} %get-tuple-element.402.refs_1_, s32[3,576,640]{2,1,0:T(8,128)} %get-tuple-element.376.refs_2_, bf16[4,256,128]{2,1,0:T(8,128)(2,1)} %fusion.35.refs_2_.refs_3_), custom_call_target="tpu_custom_call" | custom-call | flops 1000000 | bytes 10000 | tf_op jit(solution)/shard_map/attention_scatter/pallas_call | solution.py:500
  381.2 6.9 %many_half.9 = (f32[4,64,896]{2,1,0:T(8,128)}, f32[4,64,896]{2,1,0:T(8,128)}, f32[4,64,512]{2,1,0:T(8,128)}, f32[4,64,512]{2,1,0:T(8,128)}) custom-call(s32[3]{0:T(128)} %copy-done.51, bf16[1024,576]{1,0:T(8,128)(2,1)} %pad_bitcast_fusion.refs_2_.refs_0_, bf16[576,512]{1,0:T(8,128)(2,1)} %get-tuple-element.360.refs_1_, bf16[1024,384]{1,0:T(8,128)(2,1)} %bitcast.212, ...), custom_call_target="tpu_custom_call" | custom-call | flops 1000000 | bytes 10000 | tf_op jit(solution)/shard_map/many_half/pallas_call | solution.py:671
  389.7 14.6 %attention_scatter.8.refs_1_ = bf16[24,64,384]{2,1,0:T(8,128)(2,1)} custom-call(bf16[72,64,256]{2,1,0:T(8,128)(2,1)} %get-tuple-element.401.refs_0_, bf16[72,64,384]{2,1,0:T(8,128)(2,1)} %get-tuple-element.402.refs_1_, s32[3,576,640]{2,1,0:T(8,128)} %get-tuple-element.376.refs_2_, bf16[4,256,128]{2,1,0:T(8,128)(2,1)} %fusion.35.refs_2_.refs_3_), custom_call_target="tpu_custom_call" | custom-call | flops 1000000 | bytes 10000 | tf_op jit(solution)/shard_map/attention_scatter/pallas_call | solution.py:500
  408.1 2.6 collective-permute-start.22
  410.8 14.9 %attention_scatter.9.refs_2_ = bf16[24,64,384]{2,1,0:T(8,128)(2,1)} custom-call(bf16[72,64,256]{2,1,0:T(8,128)(2,1)} %get-tuple-element.401.refs_0_, bf16[72,64,384]{2,1,0:T(8,128)(2,1)} %get-tuple-element.402.refs_1_, s32[3,576,640]{2,1,0:T(8,128)} %get-tuple-element.376.refs_2_, bf16[4,256,128]{2,1,0:T(8,128)(2,1)} %fusion.35.refs_2_.refs_3_), custom_call_target="tpu_custom_call" | custom-call | flops 1000000 | bytes 10000 | tf_op jit(solution)/shard_map/attention_scatter/pallas_call | solution.py:500
  432.0 5.4 %attention_close.3 = (bf16[576,512]{1,0:T(8,128)(2,1)}, bf16[384,512]{1,0:T(8,128)(2,1)}) custom-call(bf16[24,64,384]{2,1,0:T(8,128)(2,1)} %attention_scatter.7.refs_0_, bf16[24,64,384]{2,1,0:T(8,128)(2,1)} %attention_scatter.8.refs_1_, bf16[24,64,384]{2,1,0:T(8,128)(2,1)} %attention_scatter.9.refs_2_, f32[576,512]{1,0:T(8,128)} %get-tuple-element.420.refs_3_, ...), custom_call_target="tpu_custom_call" | custom-call | flops 1000000 | bytes 10000 | tf_op jit(solution)/shard_map/attention_close/pallas_call | solution.py:518
  438.0 3.6 collective-permute-done.23
  444.2 5.8 %many_half.10 = (f32[8,64,896]{2,1,0:T(8,128)}, f32[8,64,512]{2,1,0:T(8,128)}) custom-call(s32[3]{0:T(128)} %copy-done.54, bf16[1024,576]{1,0:T(8,128)(2,1)} %pad_bitcast_fusion.refs_2_.refs_0_, bf16[576,512]{1,0:T(8,128)(2,1)} %get-tuple-element.431.refs_1_, bf16[1024,384]{1,0:T(8,128)(2,1)} %bitcast.213, ...), custom_call_target="tpu_custom_call" | custom-call | flops 1000000 | bytes 10000 | tf_op jit(solution)/shard_map/many_half/pallas_call | solution.py:671
  458.9 6.6 %many_half.11 = (f32[4,64,896]{2,1,0:T(8,128)}, f32[4,64,896]{2,1,0:T(8,128)}, f32[4,64,512]{2,1,0:T(8,128)}, f32[4,64,512]{2,1,0:T(8,128)}) custom-call(s32[3]{0:T(128)} %copy-done.50, bf16[1024,576]{1,0:T(8,128)(2,1)} %pad_bitcast_fusion.refs_2_.refs_0_, bf16[576,512]{1,0:T(8,128)(2,1)} %get-tuple-element.431.refs_1_, bf16[1024,384]{1,0:T(8,128)(2,1)} %bitcast.214, ...), custom_call_target="tpu_custom_call" | custom-call | flops 1000000 | bytes 10000 | tf_op jit(solution)/shard_map/many_half/pallas_call | solution.py:671
  473.6 11.1 %collective-permute-done.29 = f32[288,1024]{1,0:T(8,128)} collective-permute-done((f32[288,1024]{1,0:T(8,128)}, f32[288,1024]{1,0:T(8,128)}, u32[]{:S(2)}, u32[]{:S(2)}) %collective-permute-start.29) | collective-permute-done | bytes 1179680 | tf_op jit(solution)/shard_map/ppermute | solution.py:777
  486.2 2.8 collective-permute-done.28
  492.0 4.6 collective-permute-done.35
  498.8 6.0 %collective-permute-done.32 = f32[2,64,896]{2,1,0:T(8,128)S(1)} collective-permute-done((f32[2,64,896]{2,1,0:T(8,128)S(1)}, f32[2,64,896]{2,1,0:T(8,128)S(1)}, u32[]{:S(2)}, u32[]{:S(2)}) %collective-permute-start.32) | collective-permute-done | bytes 458784 | tf_op jit(solution)/shard_map/ppermute | solution.py:690
  505.9 9.1 %collective-permute-done.33 = f32[64,896]{1,0:T(8,128)S(1)} collective-permute-done((f32[64,896]{1,0:T(8,128)S(1)}, f32[64,896]{1,0:T(8,128)S(1)}, u32[]{:S(2)}, u32[]{:S(2)}) %collective-permute-start.33) | collective-permute-done | bytes 229408 | tf_op jit(solution)/shard_map/ppermute | solution.py:690
  515.7 3.3 fusion.7
  (278 shorter events, 103.3 us)
Async XLA Ops:
  3.4 69.4 %collective-permute-start.1 = (f32[512,1024]{1,0:T(8,128)}, f32[512,1024]{1,0:T(8,128)}, u32[]{:S(2)}, u32[]{:S(2)}) collective-permute-start(f32[512,1024]{1,0:T(8,128)} %convert_element_type.67), channel_id=1, source_target_pairs={{0,1},{1,0},{2,3},{3,2},{4,5},{5,4},{6,7},{7,6},{8,9},{9,8},{10,11... | collective-permute-start | bytes 6291464 | tf_op jit(solution)/shard_map/ppermute | solution.py:777
  67.4 33.3 %collective-permute-start = (f32[256,512]{1,0:T(8,128)}, f32[256,512]{1,0:T(8,128)}, u32[]{:S(2)}, u32[]{:S(2)}) collective-permute-start(f32[256,512]{1,0:T(8,128)} %get-tuple-element.535), channel_id=1, source_target_pairs={{0,1},{1,0},{2,3},{3,2},{4,5},{5,4},{6,7},{7,6},{8,9},{9,8},{10,11... | collective-permute-start | bytes 1572872 | tf_op jit(solution)/shard_map/ppermute | solution.py:777
  72.7 24.0 %copy-start.52 = (s32[2]{0:T(128)}, s32[2]{0:T(128)S(1)}, u32[]{:S(2)}) copy-start(s32[2]{0:T(128)S(1)} %pad_add_fusion.pick_ref) | copy-start | bytes 28
  72.8 23.9 %copy-start.48 = (s32[2]{0:T(128)}, s32[2]{0:T(128)S(1)}, u32[]{:S(2)}) copy-start(s32[2]{0:T(128)S(1)} %pad_add_fusion.1.pick_ref) | copy-start | bytes 28
  72.8 23.9 %copy-start.53 = (s32[2]{0:T(128)}, s32[2]{0:T(128)S(1)}, u32[]{:S(2)}) copy-start(s32[2]{0:T(128)S(1)} %constant_dynamic-update-slice_fusion.3.pick_ref) | copy-start | bytes 28
  72.8 23.9 %copy-start.49 = (s32[2]{0:T(128)}, s32[2]{0:T(128)S(1)}, u32[]{:S(2)}) copy-start(s32[2]{0:T(128)S(1)} %constant_dynamic-update-slice_fusion.2.pick_ref) | copy-start | bytes 28
  98.7 20.0 %collective-permute-start.3 = (f32[320,512]{1,0:T(8,128)}, f32[320,512]{1,0:T(8,128)}, u32[]{:S(2)}, u32[]{:S(2)}) collective-permute-start(f32[320,512]{1,0:T(8,128)} %get-tuple-element.531), channel_id=1, source_target_pairs={{0,1},{1,0},{2,3},{3,2},{4,5},{5,4},{6,7},{7,6},{8,9},{9,8},{10,11... | collective-permute-start | bytes 1966088 | tf_op jit(solution)/shard_map/ppermute | solution.py:777
  118.5 26.3 %collective-permute-start.2 = (f32[256,1024]{1,0:T(8,128)}, f32[256,1024]{1,0:T(8,128)}, u32[]{:S(2)}, u32[]{:S(2)}) collective-permute-start(f32[256,1024]{1,0:T(8,128)} %fusion.55), channel_id=1, source_target_pairs={{0,1},{1,0},{2,3},{3,2},{4,5},{5,4},{6,7},{7,6},{8,9},{9,8},{10,11... | collective-permute-start | bytes 3145736 | tf_op jit(solution)/shard_map/ppermute | solution.py:777
  137.4 35.5 %collective-permute-start.4 = (f32[320,1024]{1,0:T(8,128)S(1)}, f32[320,1024]{1,0:T(8,128)S(1)}, u32[]{:S(2)}, u32[]{:S(2)}) collective-permute-start(f32[320,1024]{1,0:T(8,128)S(1)} %fusion.56), channel_id=1, source_target_pairs={{0,1},{1,0},{2,3},{3,2},{4,5},{5,4},{6,7},{7,6},{8,9},{9,8},{10,11... | collective-permute-start | bytes 3932168 | tf_op jit(solution)/shard_map/ppermute | solution.py:777
  154.0 39.5 %collective-permute-start.5 = (f32[256,1024]{1,0:T(8,128)}, f32[256,1024]{1,0:T(8,128)}, u32[]{:S(2)}, u32[]{:S(2)}) collective-permute-start(f32[256,1024]{1,0:T(8,128)} %fusion.57), channel_id=1, source_target_pairs={{0,1},{1,0},{2,3},{3,2},{4,5},{5,4},{6,7},{7,6},{8,9},{9,8},{10,11... | collective-permute-start | bytes 3145736 | tf_op jit(solution)/shard_map/ppermute | solution.py:777
  188.1 16.4 %collective-permute-start.6 = (f32[8,64,2048]{2,1,0:T(8,128)}, f32[8,64,2048]{2,1,0:T(8,128)}, u32[]{:S(2)}, u32[]{:S(2)}) collective-permute-start(f32[8,64,2048]{2,1,0:T(8,128)} %weight_half.4), channel_id=1, source_target_pairs={{0,2},{2,0},{4,6},{6,4},{8,10},{10,8},{12,14},{14,12},{16,18},{18,... | collective-permute-start | bytes 12582920 | tf_op jit(solution)/shard_map/ppermute | solution.py:690
  201.0 13.1 %collective-permute-start.7 = (f32[8,64,2048]{2,1,0:T(8,128)}, f32[8,64,2048]{2,1,0:T(8,128)}, u32[]{:S(2)}, u32[]{:S(2)}) collective-permute-start(f32[8,64,2048]{2,1,0:T(8,128)} %weight_half.6), channel_id=1, source_target_pairs={{0,2},{2,0},{4,6},{6,4},{8,10},{10,8},{12,14},{14,12},{16,18},{18,... | collective-permute-start | bytes 12582920 | tf_op jit(solution)/shard_map/ppermute | solution.py:690
  203.9 35.9 %collective-permute-start.8 = (f32[320,1024]{1,0:T(8,128)}, f32[320,1024]{1,0:T(8,128)}, u32[]{:S(2)}, u32[]{:S(2)}) collective-permute-start(f32[320,1024]{1,0:T(8,128)} %fusion.58), channel_id=1, source_target_pairs={{0,1},{1,0},{2,3},{3,2},{4,5},{5,4},{6,7},{7,6},{8,9},{9,8},{10,11... | collective-permute-start | bytes 3932168 | tf_op jit(solution)/shard_map/ppermute | solution.py:777
  212.4 54.0 %collective-permute-start.9 = (f32[4,64,2048]{2,1,0:T(8,128)}, f32[4,64,2048]{2,1,0:T(8,128)}, u32[]{:S(2)}, u32[]{:S(2)}) collective-permute-start(f32[4,64,2048]{2,1,0:T(8,128)} %get-tuple-element.317), channel_id=1, source_target_pairs={{0,8},{2,10},{4,12},{6,14},{8,0},{10,2},{12,4},{14,6},{16,24},{18,... | collective-permute-start | bytes 6291464 | tf_op jit(solution)/shard_map/ppermute | solution.py:690
  239.9 57.0 %collective-permute-start.10 = (f32[4,64,2048]{2,1,0:T(8,128)}, f32[4,64,2048]{2,1,0:T(8,128)}, u32[]{:S(2)}, u32[]{:S(2)}) collective-permute-start(f32[4,64,2048]{2,1,0:T(8,128)} %get-tuple-element.325), channel_id=1, source_target_pairs={{0,4},{2,6},{4,0},{6,2},{8,12},{10,14},{12,8},{14,10},{16,20},{18,... | collective-permute-start | bytes 6291464 | tf_op jit(solution)/shard_map/ppermute | solution.py:690
  276.5 35.9 %collective-permute-start.12 = (f32[8,64,1152]{2,1,0:T(8,128)}, f32[8,64,1152]{2,1,0:T(8,128)}, u32[]{:S(2)}, u32[]{:S(2)}) collective-permute-start(f32[8,64,1152]{2,1,0:T(8,128)} %many_half.6), channel_id=1, source_target_pairs={{0,2},{2,0},{4,6},{6,4},{8,10},{10,8},{12,14},{14,12},{16,18},{18,... | collective-permute-start | bytes 7077896 | tf_op jit(solution)/shard_map/ppermute | solution.py:690
  276.5 33.6 %collective-permute-start.11 = (f32[2,64,2048]{2,1,0:T(8,128)}, f32[2,64,2048]{2,1,0:T(8,128)}, u32[]{:S(2)}, u32[]{:S(2)}) collective-permute-start(f32[2,64,2048]{2,1,0:T(8,128)} %get-tuple-element.332), channel_id=1, source_target_pairs={{0,4},{2,6},{4,0},{6,2},{8,12},{10,14},{12,8},{14,10},{16,20},{18,... | collective-permute-start | bytes 3145736 | tf_op jit(solution)/shard_map/ppermute | solution.py:690
  300.7 46.7 %collective-permute-start.13 = (f32[2,64,2048]{2,1,0:T(8,128)}, f32[2,64,2048]{2,1,0:T(8,128)}, u32[]{:S(2)}, u32[]{:S(2)}) collective-permute-start(f32[2,64,2048]{2,1,0:T(8,128)} %get-tuple-element.349), channel_id=1, source_target_pairs={{0,8},{2,10},{4,12},{6,14},{8,0},{10,2},{12,4},{14,6},{16,24},{18,... | collective-permute-start | bytes 3145736 | tf_op jit(solution)/shard_map/ppermute | solution.py:690
  319.0 41.8 %collective-permute-start.14 = (f32[4,64,1152]{2,1,0:T(8,128)}, f32[4,64,1152]{2,1,0:T(8,128)}, u32[]{:S(2)}, u32[]{:S(2)}) collective-permute-start(f32[4,64,1152]{2,1,0:T(8,128)} %get-tuple-element.364), channel_id=1, source_target_pairs={{0,4},{2,6},{4,0},{6,2},{8,12},{10,14},{12,8},{14,10},{16,20},{18,... | collective-permute-start | bytes 3538952 | tf_op jit(solution)/shard_map/ppermute | solution.py:690
  320.5 40.3 %collective-permute-start.15 = (f32[64,2048]{1,0:T(8,128)}, f32[64,2048]{1,0:T(8,128)}, u32[]{:S(2)}, u32[]{:S(2)}) collective-permute-start(f32[64,2048]{1,0:T(8,128)} %get-tuple-element.365), channel_id=1, source_target_pairs={{0,16},{2,18},{4,20},{6,22},{8,24},{10,26},{12,28},{14,30},{16,0},... | collective-permute-start | bytes 1572872 | tf_op jit(solution)/shard_map/ppermute | solution.py:690
  323.2 24.3 %copy-start.51 = (s32[3]{0:T(128)}, s32[3]{0:T(128)S(1)}, u32[]{:S(2)}) copy-start(s32[3]{0:T(128)S(1)} %get-tuple-element.542.pick_ref) | copy-start | bytes 40
  323.2 108.8 %copy-start.50 = (s32[3]{0:T(128)}, s32[3]{0:T(128)S(1)}, u32[]{:S(2)}) copy-start(s32[3]{0:T(128)S(1)} %get-tuple-element.543.pick_ref) | copy-start | bytes 40
  323.2 24.2 %copy-start.55 = (s32[3]{0:T(128)}, s32[3]{0:T(128)S(1)}, u32[]{:S(2)}) copy-start(s32[3]{0:T(128)S(1)} %constant_dynamic-update-slice_fusion.1.pick_ref) | copy-start | bytes 40
  324.4 23.0 %copy-start.19 = (f32[2,64,2048]{2,1,0:T(8,128)S(1)}, f32[2,64,2048]{2,1,0:T(8,128)}, u32[]{:S(2)}) copy-start(f32[2,64,2048]{2,1,0:T(8,128)} %get-tuple-element.354) | copy-start | bytes 3145732
  365.3 15.9 %collective-permute-start.16 = (f32[8,64,896]{2,1,0:T(8,128)}, f32[8,64,896]{2,1,0:T(8,128)}, u32[]{:S(2)}, u32[]{:S(2)}) collective-permute-start(f32[8,64,896]{2,1,0:T(8,128)} %get-tuple-element.377), channel_id=1, source_target_pairs={{0,2},{2,0},{4,6},{6,4},{8,10},{10,8},{12,14},{14,12},{16,18},{18,... | collective-permute-start | bytes 5505032 | tf_op jit(solution)/shard_map/ppermute | solution.py:690
  365.3 15.9 %collective-permute-start.17 = (f32[8,64,512]{2,1,0:T(8,128)}, f32[8,64,512]{2,1,0:T(8,128)}, u32[]{:S(2)}, u32[]{:S(2)}) collective-permute-start(f32[8,64,512]{2,1,0:T(8,128)} %get-tuple-element.378), channel_id=1, source_target_pairs={{0,2},{2,0},{4,6},{6,4},{8,10},{10,8},{12,14},{14,12},{16,18},{18,... | collective-permute-start | bytes 3145736 | tf_op jit(solution)/shard_map/ppermute | solution.py:690
  365.8 38.5 %collective-permute-start.18 = (f32[2,64,1152]{2,1,0:T(8,128)}, f32[2,64,1152]{2,1,0:T(8,128)S(1)}, u32[]{:S(2)}, u32[]{:S(2)}) collective-permute-start(f32[2,64,1152]{2,1,0:T(8,128)} %get-tuple-element.391), channel_id=1, source_target_pairs={{0,8},{2,10},{4,12},{6,14},{8,0},{10,2},{12,4},{14,6},{16,24},{18,... | collective-permute-start | bytes 1769480 | tf_op jit(solution)/shard_map/ppermute | solution.py:690
  366.2 38.1 %collective-permute-start.19 = (f32[64,2048]{1,0:T(8,128)}, f32[64,2048]{1,0:T(8,128)}, u32[]{:S(2)}, u32[]{:S(2)}) collective-permute-start(f32[64,2048]{1,0:T(8,128)} %get-tuple-element.392), channel_id=1, source_target_pairs={{0,16},{2,18},{4,20},{6,22},{8,24},{10,26},{12,28},{14,30},{16,0},... | collective-permute-start | bytes 1572872 | tf_op jit(solution)/shard_map/ppermute | solution.py:690
  388.1 37.6 %collective-permute-start.20 = (f32[4,64,896]{2,1,0:T(8,128)}, f32[4,64,896]{2,1,0:T(8,128)}, u32[]{:S(2)}, u32[]{:S(2)}) collective-permute-start(f32[4,64,896]{2,1,0:T(8,128)} %get-tuple-element.405), channel_id=1, source_target_pairs={{0,8},{2,10},{4,12},{6,14},{8,0},{10,2},{12,4},{14,6},{16,24},{18,... | collective-permute-start | bytes 2752520 | tf_op jit(solution)/shard_map/ppermute | solution.py:690
  404.3 21.4 %collective-permute-start.21 = (f32[4,64,512]{2,1,0:T(8,128)}, f32[4,64,512]{2,1,0:T(8,128)}, u32[]{:S(2)}, u32[]{:S(2)}) collective-permute-start(f32[4,64,512]{2,1,0:T(8,128)} %get-tuple-element.406), channel_id=1, source_target_pairs={{0,4},{2,6},{4,0},{6,2},{8,12},{10,14},{12,8},{14,10},{16,20},{18,... | collective-permute-start | bytes 1572872 | tf_op jit(solution)/shard_map/ppermute | solution.py:690
  408.1 17.5 %collective-permute-start.22 = (f32[64,1152]{1,0:T(8,128)S(1)}, f32[64,1152]{1,0:T(8,128)S(1)}, u32[]{:S(2)}, u32[]{:S(2)}) collective-permute-start(f32[64,1152]{1,0:T(8,128)S(1)} %get-tuple-element.407), channel_id=1, source_target_pairs={{0,16},{2,18},{4,20},{6,22},{8,24},{10,26},{12,28},{14,30},{16,0},... | collective-permute-start | bytes 884744 | tf_op jit(solution)/shard_map/ppermute | solution.py:690
  430.2 11.4 %collective-permute-start.23 = (f32[2,64,896]{2,1,0:T(8,128)S(1)}, f32[2,64,896]{2,1,0:T(8,128)}, u32[]{:S(2)}, u32[]{:S(2)}) collective-permute-start(f32[2,64,896]{2,1,0:T(8,128)S(1)} %get-tuple-element.423), channel_id=1, source_target_pairs={{0,4},{2,6},{4,0},{6,2},{8,12},{10,14},{12,8},{14,10},{16,20},{18,... | collective-permute-start | bytes 1376264 | tf_op jit(solution)/shard_map/ppermute | solution.py:690
  431.5 6.5 %collective-permute-start.24 = (f32[2,64,512]{2,1,0:T(8,128)S(1)}, f32[2,64,512]{2,1,0:T(8,128)S(1)}, u32[]{:S(2)}, u32[]{:S(2)}) collective-permute-start(f32[2,64,512]{2,1,0:T(8,128)S(1)} %get-tuple-element.424), channel_id=1, source_target_pairs={{0,8},{2,10},{4,12},{6,14},{8,0},{10,2},{12,4},{14,6},{16,24},{18,... | collective-permute-start | bytes 786440 | tf_op jit(solution)/shard_map/ppermute | solution.py:690
  450.0 8.9 %collective-permute-start.25 = (f32[8,64,896]{2,1,0:T(8,128)}, f32[8,64,896]{2,1,0:T(8,128)}, u32[]{:S(2)}, u32[]{:S(2)}) collective-permute-start(f32[8,64,896]{2,1,0:T(8,128)} %get-tuple-element.433), channel_id=1, source_target_pairs={{0,2},{2,0},{4,6},{6,4},{8,10},{10,8},{12,14},{14,12},{16,18},{18,... | collective-permute-start | bytes 5505032 | tf_op jit(solution)/shard_map/ppermute | solution.py:690
  450.0 7.9 %collective-permute-start.26 = (f32[8,64,512]{2,1,0:T(8,128)}, f32[8,64,512]{2,1,0:T(8,128)S(1)}, u32[]{:S(2)}, u32[]{:S(2)}) collective-permute-start(f32[8,64,512]{2,1,0:T(8,128)} %get-tuple-element.434), channel_id=1, source_target_pairs={{0,2},{2,0},{4,6},{6,4},{8,10},{10,8},{12,14},{14,12},{16,18},{18,... | collective-permute-start | bytes 3145736 | tf_op jit(solution)/shard_map/ppermute | solution.py:690
  456.4 28.3 %collective-permute-start.29 = (f32[288,1024]{1,0:T(8,128)}, f32[288,1024]{1,0:T(8,128)}, u32[]{:S(2)}, u32[]{:S(2)}) collective-permute-start(f32[288,1024]{1,0:T(8,128)} %convolution_add_fusion.2), channel_id=1, source_target_pairs={{0,1},{1,0},{2,3},{3,2},{4,5},{5,4},{6,7},{7,6},{8,9},{9,8},{10,11... | collective-permute-start | bytes 3538952 | tf_op jit(solution)/shard_map/ppermute | solution.py:777
  465.5 23.4 %collective-permute-start.27 = (f32[4,64,896]{2,1,0:T(8,128)}, f32[4,64,896]{2,1,0:T(8,128)S(1)}, u32[]{:S(2)}, u32[]{:S(2)}) collective-permute-start(f32[4,64,896]{2,1,0:T(8,128)} %get-tuple-element.435), channel_id=1, source_target_pairs={{0,4},{2,6},{4,0},{6,2},{8,12},{10,14},{12,8},{14,10},{16,20},{18,... | collective-permute-start | bytes 2752520 | tf_op jit(solution)/shard_map/ppermute | solution.py:690
  467.7 21.3 %copy-start.36 = (f32[64,896]{1,0:T(8,128)S(1)}, f32[64,896]{1,0:T(8,128)}, u32[]{:S(2)}) copy-start(f32[64,896]{1,0:T(8,128)} %get-tuple-element.445) | copy-start | bytes 688132
  467.7 21.3 %collective-permute-start.28 = (f32[4,64,512]{2,1,0:T(8,128)}, f32[4,64,512]{2,1,0:T(8,128)S(1)}, u32[]{:S(2)}, u32[]{:S(2)}) collective-permute-start(f32[4,64,512]{2,1,0:T(8,128)} %get-tuple-element.436), channel_id=1, source_target_pairs={{0,8},{2,10},{4,12},{6,14},{8,0},{10,2},{12,4},{14,6},{16,24},{18,... | collective-permute-start | bytes 1572872 | tf_op jit(solution)/shard_map/ppermute | solution.py:690
  468.8 22.0 %copy-start.35 = (f32[4,64,896]{2,1,0:T(8,128)S(1)}, f32[4,64,896]{2,1,0:T(8,128)}, u32[]{:S(2)}) copy-start(f32[4,64,896]{2,1,0:T(8,128)} %get-tuple-element.438) | copy-start | bytes 2752516
  468.8 20.1 %collective-permute-start.30 = (f32[64,896]{1,0:T(8,128)S(1)}, f32[64,896]{1,0:T(8,128)S(1)}, u32[]{:S(2)}, u32[]{:S(2)}) collective-permute-start(f32[64,896]{1,0:T(8,128)S(1)} %copy-done.42), channel_id=1, source_target_pairs={{0,16},{2,18},{4,20},{6,22},{8,24},{10,26},{12,28},{14,30},{16,0},... | collective-permute-start | bytes 688136 | tf_op jit(solution)/shard_map/ppermute | solution.py:690
  469.4 19.6 %collective-permute-start.31 = (f32[64,512]{1,0:T(8,128)}, f32[64,512]{1,0:T(8,128)S(1)}, u32[]{:S(2)}, u32[]{:S(2)}) collective-permute-start(f32[64,512]{1,0:T(8,128)} %get-tuple-element.442), channel_id=1, source_target_pairs={{0,16},{2,18},{4,20},{6,22},{8,24},{10,26},{12,28},{14,30},{16,0},... | collective-permute-start | bytes 393224 | tf_op jit(solution)/shard_map/ppermute | solution.py:690
  484.7 30.3 %collective-permute-start.34 = (f32[288,1024]{1,0:T(8,128)S(1)}, f32[288,1024]{1,0:T(8,128)S(1)}, u32[]{:S(2)}, u32[]{:S(2)}) collective-permute-start(f32[288,1024]{1,0:T(8,128)S(1)} %convolution_add_fusion.1), channel_id=1, source_target_pairs={{0,1},{1,0},{2,3},{3,2},{4,5},{5,4},{6,7},{7,6},{8,9},{9,8},{10,11... | collective-permute-start | bytes 3538952 | tf_op jit(solution)/shard_map/ppermute | solution.py:777
  489.7 6.9 %collective-permute-start.35 = (f32[2,64,512]{2,1,0:T(8,128)S(1)}, f32[2,64,512]{2,1,0:T(8,128)S(1)}, u32[]{:S(2)}, u32[]{:S(2)}) collective-permute-start(f32[2,64,512]{2,1,0:T(8,128)S(1)} %fusion.41), channel_id=1, source_target_pairs={{0,4},{2,6},{4,0},{6,2},{8,12},{10,14},{12,8},{14,10},{16,20},{18,... | collective-permute-start | bytes 786440 | tf_op jit(solution)/shard_map/ppermute | solution.py:690
  490.9 13.9 %collective-permute-start.32 = (f32[2,64,896]{2,1,0:T(8,128)S(1)}, f32[2,64,896]{2,1,0:T(8,128)S(1)}, u32[]{:S(2)}, u32[]{:S(2)}) collective-permute-start(f32[2,64,896]{2,1,0:T(8,128)S(1)} %fusion.36), channel_id=1, source_target_pairs={{0,8},{2,10},{4,12},{6,14},{8,0},{10,2},{12,4},{14,6},{16,24},{18,... | collective-permute-start | bytes 1376264 | tf_op jit(solution)/shard_map/ppermute | solution.py:690
  496.7 8.5 %collective-permute-start.36 = (f32[64,512]{1,0:T(8,128)S(1)}, f32[64,512]{1,0:T(8,128)S(1)}, u32[]{:S(2)}, u32[]{:S(2)}) collective-permute-start(f32[64,512]{1,0:T(8,128)S(1)} %fusion.45), channel_id=1, source_target_pairs={{0,16},{2,18},{4,20},{6,22},{8,24},{10,26},{12,28},{14,30},{16,0},... | collective-permute-start | bytes 393224 | tf_op jit(solution)/shard_map/ppermute | solution.py:690
  504.8 10.2 %collective-permute-start.33 = (f32[64,896]{1,0:T(8,128)S(1)}, f32[64,896]{1,0:T(8,128)S(1)}, u32[]{:S(2)}, u32[]{:S(2)}) collective-permute-start(f32[64,896]{1,0:T(8,128)S(1)} %fusion.44), channel_id=1, source_target_pairs={{0,16},{2,18},{4,20},{6,22},{8,24},{10,26},{12,28},{14,30},{16,0},... | collective-permute-start | bytes 688136 | tf_op jit(solution)/shard_map/ppermute | solution.py:690
  515.1 4.6 collective-permute-start.37
  (51 other events, 281.4 us)

commit v8 on v7

--- a/solution.py
+++ b/solution.py
@@ -140,7 +140,7 @@
 
 
 def forward_rows(
-    used_ref, q_ref, k_ref, v_ref, pk_ref, b_ref, far_sum, inv_ref, p_ref, ctx_ref,
+    used_ref, q_ref, k_ref, v_ref, pk_ref, b_ref, far_sum, inv_ref, p_ref, ctx_ref, wide_ref,
     near_tab, near_inv, near_sum, score, *, first, rows, span, cols, pairs, scale,
 ):
     for p in range(pairs):
@@ -191,7 +191,9 @@
                     p_ref[2 * p + h, pl.ds(pl.multiple_of(start + s * 16, 16), 16), :] = share.astype(bf16)
             c0 = nn(p_ref[2 * p, at, :], v_ref[:, cut])
             c1 = nn(p_ref[2 * p + 1, at, :], v_ref[:, cut])
-            ctx_ref[at, cut] = jnp.where(mask, c0, c1).astype(bf16)
+            context = jnp.where(mask, c0, c1).astype(bf16)
+            ctx_ref[at, cut] = context
+            wide_ref[at, cut] = context.astype(f32)
 
     def outer(step, carry):
         block_body(pl.multiple_of(step * 128, 128), 128)
@@ -386,8 +388,8 @@
     i32 = jnp.int32
 
     def kernel(
-        used_ref, qkv_ref, pk_ref, pq_ref, b_ref, p_ref, ctx_ref, head_ref, rest_ref, bt_ref, far_rest, inv_ref,
-        far_tab, far_inv, far_head, *scratch,
+        used_ref, qkv_ref, pk_ref, pq_ref, b_ref, p_ref, ctx_ref, wide_ref, head_ref, rest_ref, bt_ref, far_rest,
+        inv_ref, far_tab, far_inv, far_head, *scratch,
     ):
         k_ref = qkv_ref.at[:, width:2 * width]
         prepare_rows(
@@ -396,7 +398,7 @@
         )
         forward_rows(
             used_ref, qkv_ref.at[:, 0:width], k_ref, qkv_ref.at[:, 2 * width:3 * width], pk_ref, head_ref,
-            far_head, inv_ref, p_ref, ctx_ref, *scratch,
+            far_head, inv_ref, p_ref, ctx_ref, wide_ref, *scratch,
             first=0, rows=split, span=span, cols=cols, pairs=pairs, scale=scale,
         )
 
@@ -405,6 +407,7 @@
         out_shape=(
             jax.ShapeDtypeStruct((2 * pairs, split, cols), bf16),
             jax.ShapeDtypeStruct((split, width), bf16),
+            jax.ShapeDtypeStruct((split, width), f32),
             jax.ShapeDtypeStruct((3, split, cols), i32),
             jax.ShapeDtypeStruct((3, rows - split, cols), i32),
             jax.ShapeDtypeStruct((3, rows, cols), i32),
@@ -412,7 +415,7 @@
             jax.ShapeDtypeStruct((2 * pairs, cols), f32),
         ),
         in_specs=[pl.BlockSpec(memory_space=pltpu.SMEM)] + [whole] * 4,
-        out_specs=(whole,) * 7,
+        out_specs=(whole,) * 8,
         scratch_shapes=[
             pltpu.VMEM((pairs, rows, 3 * REL), i32),
             pltpu.VMEM((2 * pairs, rows, 128), f32),
@@ -430,10 +433,10 @@
     pairs = width // 128
     whole = pl.BlockSpec(memory_space=pltpu.VMEM)
 
-    def kernel(used_ref, qkv_ref, pk_ref, b_ref, far_ref, inv_ref, p_ref, ctx_ref, *scratch):
+    def kernel(used_ref, qkv_ref, pk_ref, b_ref, far_ref, inv_ref, p_ref, ctx_ref, wide_ref, *scratch):
         forward_rows(
             used_ref, qkv_ref.at[:, 0:width], qkv_ref.at[:, width:2 * width], qkv_ref.at[:, 2 * width:3 * width],
-            pk_ref, b_ref, far_ref, inv_ref, p_ref, ctx_ref, *scratch,
+            pk_ref, b_ref, far_ref, inv_ref, p_ref, ctx_ref, wide_ref, *scratch,
             first=split, rows=rows - split, span=span, cols=cols, pairs=pairs, scale=scale,
         )
 
@@ -442,9 +445,10 @@
         out_shape=(
             jax.ShapeDtypeStruct((2 * pairs, rows - split, cols), bf16),
             jax.ShapeDtypeStruct((rows - split, width), bf16),
+            jax.ShapeDtypeStruct((rows - split, width), f32),
         ),
         in_specs=[pl.BlockSpec(memory_space=pltpu.SMEM)] + [whole] * 5,
-        out_specs=(whole,) * 2,
+        out_specs=(whole,) * 3,
         scratch_shapes=forward_scratch(pairs, rows - split, cols),
         compiler_params=pltpu.CompilerParams(vmem_limit_bytes=VMEM_CAP),
         cost_estimate=pl.CostEstimate(flops=2 * 10**10, bytes_accessed=12000000, transcendentals=0),
@@ -779,12 +783,14 @@
 
 def attend_kernel(
     t_ref, c_ref, o_ref, w_ref, ow_ref, gain_ref, shift_ref, first_ref, low_ref, normal_ref, inverse_ref,
+    *, start,
 ):
     weight = ow_ref[...].astype(bf16)
 
     def body(step, carry):
         at = pl.ds(pl.multiple_of(step * 64, 64), 64)
-        summed = t_ref[at, :].astype(f32) + nn(c_ref[at, :], w_ref[...])
+        here = pl.ds(pl.multiple_of(start + step * 64, 64), 64)
+        summed = t_ref[here, :].astype(f32) + nn(c_ref[at, :], w_ref[...])
         summed = summed + nn(o_ref[at, :].astype(bf16), weight)
         first, normal, inverse = norm_forward(summed, gain_ref[...], shift_ref[...])
         first_ref[at, :] = first
@@ -793,14 +799,14 @@
         inverse_ref[at, :] = inverse
         return carry
 
-    lax.fori_loop(0, t_ref.shape[0] // 64, body, 0)
-
-
-def attend(tokens, context, other, weight, other_weight, gain, shift):
-    tall, depth = tokens.shape
+    lax.fori_loop(0, c_ref.shape[0] // 64, body, 0)
+
+
+def attend(tokens, context, other, weight, other_weight, gain, shift, start):
+    tall, depth = context.shape[0], tokens.shape[1]
     whole = pl.BlockSpec(memory_space=pltpu.VMEM)
     return pl.pallas_call(
-        attend_kernel,
+        functools.partial(attend_kernel, start=start),
         in_specs=[whole] * 7,
         out_specs=(whole,) * 4,
         out_shape=(
@@ -873,18 +879,17 @@
     )
     tokens = jnp.pad(tokens, spare)
     cotangent = jnp.pad(cotangent, spare)
-    tokens_turned, tables_turned = tokens.T, tables_flat.T
     edges = [(0, split), (split, rows)]
 
-    share_head, context_head, bucket_head, bucket_rest, bucket_cols, far_rest, far_inverse = attention_head(
+    share_head, context_head, wide_head, bucket_head, bucket_rest, bucket_cols, far_rest, far_inverse = attention_head(
         qkv, pos_key, pos_query, buckets, text_length, score_scale, split
     )
-    other_head = swap(context_head)
+    other_head = swap(wide_head)
     far_rest, other_output = lax.optimization_barrier((far_rest, other_output))
-    share_rest, context_rest = attention_rest(
+    share_rest, context_rest, wide_rest = attention_rest(
         qkv, pos_key, bucket_rest, far_rest, far_inverse, text_length, score_scale, split, span
     )
-    other_rest = swap(context_rest)
+    other_rest = swap(wide_rest)
     shares = [share_head, share_rest]
     contexts = [context_head, context_rest]
     contexts_other = [other_head, other_rest]
@@ -895,7 +900,7 @@
     firsts, firsts_low, normals_one, inverses_one, upwards, hiddens, feeds, feeds_other = ([] for _ in range(8))
     for (low, high), context, other in zip(edges, contexts, contexts_other):
         first, first_low, normal_one, inverse_one = attend(
-            tokens[low:high], context, other, output_weight, other_output, gain_one, shift_one
+            tokens, context, other, output_weight, other_output, gain_one, shift_one, low
         )
         firsts.append(first)
         normals_one.append(normal_one)
@@ -906,6 +911,8 @@
         feeds.append(nn(hiddens[-1], down_weight))
         feeds_other.append(swap(feeds[-1]))
 
+    feeds[1], tokens_late, tables_late = lax.optimization_barrier((feeds[1], tokens, tables_flat))
+    tokens_turned, tables_turned = tokens_late.T, tables_late.T
     finals, seconds_back, seconds_low, upwards_back, backs_part, backs_other, two_sums = ([] for _ in range(7))
     for n, (low, high) in enumerate(edges):
         final, normal_two, inverse_two = norm_forward(
@@ -993,8 +1000,8 @@
     blocks = rows // 64
     near.append(attention_scatter([back_head], bucket_head, merge, 0, split // 64))
     back_rest, near = tie((back_rest, near), up_chain)
+    back_rest, near = tie((back_rest, near), outer_chain)
     back_rest, near = tie((back_rest, near), down_chain)
-    back_rest, near = tie((back_rest, near), outer_chain)
     near.append(attention_scatter([back_rest], bucket_rest, merge, 0, blocks - split // 64))
     near, backs = tie((near, [turned_head, turned_rest]), up_chain)
     query_low, key_table_sum = attention_close(near, [query_head, query_rest], pos_key, qkv, 0)

time: 531 us -> 519 us (0.977)
  waiting for transfers between devices: 76.4 us -> 63.8 us
    ppermute x28, waiting for transfers between devices: 35.7 us -> 26.2 us  [flipped(): return lax.ppermute(value, 'dp', [(i, i ^ 1 << bit) for i in range(size)])]
    unnamed x128 -> x135, local copies, waits for them, and re-layouts: 12.8 us -> 14 us
  transfers between devices with their start and end apart: 38 -> 38, of which waited for: 11 -> 11; matrix products, arithmetic and copies ran while one was open for 20% -> 20% of each run, Pallas kernels for 53% -> 55%
where the time goes in v8:
time: 519 us; the launch traced here: 508 us
  Pallas kernels  283 us (55%)
  waiting for transfers between devices  63.8 us (12%)
  other arithmetic  59.5 us (11%)
  matrix products  37.5 us (7%)
  starting transfers between devices  37.2 us (7%)
  local copies, waits for them, and re-layouts  24.5 us (5%)
    pallas_call x5, Pallas kernels, attention_scatter(): pl.pallas_call(functools.partial(scatter_kernel, groups=8, cols=cols), gr...  86.1 us
    pallas_call x1, Pallas kernels, attention_head(): pl.pallas_call(kernel, out_shape=(jax.ShapeDtypeStruct((2 * pairs, split,...  45 us
    pallas_call x6, Pallas kernels, many_half(): pl.pallas_call(functools.partial(many_kernel, plan=plan, widths=widths, t...  37.7 us
    ppermute x9, waiting for transfers between devices, swap(): return lax.ppermute(value.astype(f32), 'mp', [(0, 1), (1, 0)])  37.6 us
    pallas_call x4, Pallas kernels, weight_half(): pl.pallas_call(functools.partial(weight_kernel, count=len(xs), blocks=blo...  30.9 us
    ppermute x28, waiting for transfers between devices, flipped(): return lax.ppermute(value, 'dp', [(i, i ^ 1 << bit) for i in range(size)])  26.2 us
    ppermute x28, starting transfers between devices, flipped(): return lax.ppermute(value, 'dp', [(i, i ^ 1 << bit) for i in range(size)])  25.8 us
    pallas_call x2, Pallas kernels, attention_draw(): pl.pallas_call(functools.partial(draw_kernel, first=first, tall=tall, row...  24.7 us
  transfers between devices with their start and end apart: 38, of which 11 were waited for; matrix products, arithmetic and copies ran while one was open for 20% of the time, Pallas kernels for 55%

profile of v8, /device:TPU:0, one launch (start us, length us, event | category | flops | bytes accessed | tf_op | source)
XLA Modules:
  0.0 508.4 jit_solution(13283037788534322731)
XLA Ops:
  0.6 2.8 convert_element_type.60
  3.4 3.0 collective-permute-start.1
  7.0 4.6 copy.62.b_ref
  11.6 9.3 %project.1 = (bf16[640,1536]{1,0:T(8,128)(2,1)}, bf16[384,512]{1,0:T(8,128)(2,1)}, bf16[384,512]{1,0:T(8,128)(2,1)}) custom-call(bf16[561,1024]{1,0:T(8,128)(2,1)} %x_ref.1, bf16[1024,512]{1,0:T(8,128)(2,1)} %wq_ref.1, bf16[1024,512]{1,0:T(8,128)(2,1)} %wk_ref.1, bf16[1024,512]{1,0:T(8,128)(2,1)} %wv_ref.1, bf16[3,128,1024]{2,1,0:T(8,128)(2,1)} %t_ref.1, ...), custom_call_target="tpu_custom_call" | custom-call | flops 4000000000 | bytes 9000000 | tf_op jit(solution)/shard_map/project/pallas_call | solution.py:231
  21.0 45.0 %attention_head.1 = (bf16[8,256,640]{2,1,0:T(8,128)(2,1)}, bf16[256,512]{1,0:T(8,128)(2,1)}, f32[256,512]{1,0:T(8,128)}, s32[3,256,640]{2,1,0:T(8,128)}, s32[3,3...) custom-call(s32[1]{0:T(128)S(6)} %copy.122.used_ref, ...), custom_call_target="tpu_custom_call" | custom-call | flops 40000000000 | bytes 25000000 | tf_op jit(solution)/shard_map/attention_head/pallas_call | solution.py:405
  68.6 24.1 %attention_rest.1 = (bf16[8,320,640]{2,1,0:T(8,128)(2,1)}, bf16[320,512]{1,0:T(8,128)(2,1)}, f32[320,512]{1,0:T(8,128)}) custom-call(s32[1]{0:T(128)S(6)} %copy.122.used_ref, bf16[640,1536]{1,0:T(8,128)(2,1)} %get-tuple-element.270.qkv_ref.q_ref.k_ref.v_ref.refs_5_, bf16[384,512]{1,0:T(8,128)(2,1)} %get-tuple-element.271.pk_ref.refs_4_, ...), custom_call_target="tpu_custom_call" | custom-call | flops 20000000000 | bytes 12000000 | tf_op jit(solution)/shard_map/attention_rest/pallas_call | solution.py:443
  94.7 6.9 %attend.2 = (f32[256,1024]{1,0:T(8,128)}, bf16[256,1024]{1,0:T(8,128)(2,1)}, f32[256,1024]{1,0:T(8,128)}, f32[256,1]{1,0:T(8,128)}) custom-call(bf16[576,1024]{1,0:T(8,128)(2,1)} %copy.63.t_ref, bf16[256,512]{1,0:T(8,128)(2,1)} %get-tuple-element.273.c_ref, f32[256,512]{1,0:T(8,128)} %collective-permute-done.o_ref, bf16[512,1024]{1,0:T(8,128)(2,1)} %w_ref.3, ...), custom_call_target="tpu_custom_call" | custom-call | flops 2000000000 | bytes 8000000 | tf_op jit(solution)/shard_map/attend/pallas_call | solution.py:808
  101.7 8.7 %multiply_convert_fusion.1 = (bf16[256,2048]{1,0:T(8,128)(2,1)S(1)}, f32[256,2048]{1,0:T(8,128)}, f32[256,2048]{1,0:T(8,128)}) fusion(bf16[256,1024]{1,0:T(8,128)(2,1)} %get-tuple-element.303.refs_0_, bf16[1024,2048]{1,0:T(8,128)(2,1)} %param.37), kind=kOutput, calls=%fused_computation.26 | convolution fusion | flops 1107820544 | bytes 9961472 | tf_op jit(solution)/shard_map/dot_general | solution.py:40
  112.7 7.9 %attend.3 = (f32[320,1024]{1,0:T(8,128)}, bf16[320,1024]{1,0:T(8,128)(2,1)}, f32[320,1024]{1,0:T(8,128)}, f32[320,1]{1,0:T(8,128)}) custom-call(bf16[576,1024]{1,0:T(8,128)(2,1)} %copy.63.t_ref, bf16[320,512]{1,0:T(8,128)(2,1)} %get-tuple-element.282.c_ref, f32[320,512]{1,0:T(8,128)} %copy-done.61, bf16[512,1024]{1,0:T(8,128)(2,1)} %w_ref.3, ...), custom_call_target="tpu_custom_call" | custom-call | flops 2000000000 | bytes 8000000 | tf_op jit(solution)/shard_map/attend/pallas_call | solution.py:808
  120.6 9.3 %multiply_convert_fusion = (bf16[320,2048]{1,0:T(8,128)(2,1)S(1)}, f32[320,2048]{1,0:T(8,128)S(1)}, f32[320,2048]{1,0:T(8,128)S(1)}) fusion(bf16[320,1024]{1,0:T(8,128)(2,1)} %get-tuple-element.304.refs_1_, bf16[1024,2048]{1,0:T(8,128)(2,1)} %param.37), kind=kOutput, calls=%fused_computation.4 | convolution fusion | flops 1384775680 | bytes 11403264 | tf_op jit(solution)/shard_map/dot_general | solution.py:40
  133.6 4.3 collective-permute-done.2
  146.9 19.0 %collective-permute-done.4 = f32[320,1024]{1,0:T(8,128)S(1)} collective-permute-done((f32[320,1024]{1,0:T(8,128)S(1)}, f32[320,1024]{1,0:T(8,128)S(1)}, u32[]{:S(2)}, u32[]{:S(2)}) %collective-permute-start.4) | collective-permute-done | bytes 1310752 | tf_op jit(solution)/shard_map/ppermute | solution.py:781
  167.7 2.4 add_convert_fusion.refs_3_
  171.3 2.6 fusion.58
  173.9 7.4 %weight_half.4 = f32[8,64,2048]{2,1,0:T(8,128)} custom-call(s32[2]{0:T(128)} %copy-done.55, bf16[256,1024]{1,0:T(8,128)(2,1)} %copy-done.14, bf16[320,1024]{1,0:T(8,128)(2,1)} %copy-done.5, bf16[256,2048]{1,0:T(8,128)(2,1)} %copy-done.21, bf16[320,2048]{1,0:T(8,128)(2,1)} %copy-done.12), custom_call_target="tpu_custom_call" | custom-call | flops 1207959552 | bytes 8388608 | tf_op jit(solution)/shard_map/weight_half/pallas_call | solution.py:611
  181.4 5.1 %collective-permute-done.5 = f32[256,1024]{1,0:T(8,128)} collective-permute-done((f32[256,1024]{1,0:T(8,128)}, f32[256,1024]{1,0:T(8,128)}, u32[]{:S(2)}, u32[]{:S(2)}) %collective-permute-start.5) | collective-permute-done | bytes 1048608 | tf_op jit(solution)/shard_map/ppermute | solution.py:781
  186.5 7.6 %weight_half.6 = f32[8,64,2048]{2,1,0:T(8,128)} custom-call(s32[2]{0:T(128)} %copy-done.51, bf16[256,1024]{1,0:T(8,128)(2,1)} %get-tuple-element.303.refs_0_, bf16[320,1024]{1,0:T(8,128)(2,1)} %get-tuple-element.304.refs_1_, bf16[256,2048]{1,0:T(8,128)(2,1)} %copy-done.22, bf16[320,2048]{1,0:T(8,128)(2,1)} %copy-done.13), custom_call_target="tpu_custom_call" | custom-call | flops 1207959552 | bytes 8388608 | tf_op jit(solution)/shard_map/weight_half/pallas_call | solution.py:611
  198.1 8.0 %weight_half.5 = (f32[4,64,2048]{2,1,0:T(8,128)}, f32[4,64,2048]{2,1,0:T(8,128)}) custom-call(s32[2]{0:T(128)} %copy-done.54, bf16[256,1024]{1,0:T(8,128)(2,1)} %copy-done.14, bf16[320,1024]{1,0:T(8,128)(2,1)} %copy-done.5, bf16[256,2048]{1,0:T(8,128)(2,1)} %copy-done.21, bf16[320,2048]{1,0:T(8,128)(2,1)} %copy-done.12, ...), custom_call_target="tpu_custom_call" | custom-call | flops 1207959552 | bytes 8388608 | tf_op jit(solution)/shard_map/weight_half/pallas_call | solution.py:611
  207.9 7.9 %weight_half.7 = (f32[4,64,2048]{2,1,0:T(8,128)}, f32[4,64,2048]{2,1,0:T(8,128)}) custom-call(s32[2]{0:T(128)} %copy-done.50, bf16[256,1024]{1,0:T(8,128)(2,1)} %get-tuple-element.303.refs_0_, bf16[320,1024]{1,0:T(8,128)(2,1)} %get-tuple-element.304.refs_1_, bf16[256,2048]{1,0:T(8,128)(2,1)} %copy-done.22, bf16[320,2048]{1,0:T(8,128)(2,1)} %copy-done.13, ...), custom_call_target="tpu_custom_call" | custom-call | flops 1207959552 | bytes 8388608 | tf_op jit(solution)/shard_map/weight_half/pallas_call | solution.py:611
  215.9 4.1 multiply_reduce_fusion.4
  222.5 11.1 %attention_draw.2 = (bf16[32,64,640]{2,1,0:T(8,128)(2,1)}, bf16[72,64,256]{2,1,0:T(8,128)(2,1)}, f32[256,512]{1,0:T(8,128)}, f32[576,512]{1,0:T(8,128)}, f32[576,512]{1,0:T(8,128)}) custom-call(bf16[8,256,640]{2,1,0:T(8,128)(2,1)} %get-tuple-element.315.p_ref, bf16[256,512]{1,0:T(8,128)(2,1)} %convolution_convert_fusion.1.up_ref, ...), custom_call_target="tpu_custom_call" | custom-call | flops 1000000 | bytes 10000 | tf_op jit(solution)/shard_map/attention_draw/pallas_call | solution.py:468
  235.2 4.5 multiply_reduce_fusion
  241.3 2.8 fusion.49
  245.4 13.6 %attention_draw.3 = (bf16[40,64,640]{2,1,0:T(8,128)(2,1)}, bf16[72,64,384]{2,1,0:T(8,128)(2,1)}, f32[320,512]{1,0:T(8,128)}, f32[576,512]{1,0:T(8,128)}, bf16[576,512]{1,0:T(8,128)(2,1)}) custom-call(bf16[8,320,640]{2,1,0:T(8,128)(2,1)} %get-tuple-element.320.p_ref, bf16[320,512]{1,0:T(8,128)(2,1)} %convolution_convert_fusion.up_ref, ...), custom_call_target="tpu_custom_call" | custom-call | flops 1000000 | bytes 10000 | tf_op jit(solution)/shard_map/attention_draw/pallas_call | solution.py:468
  261.0 2.8 fusion.31
  264.4 5.9 %many_half.6 = f32[8,64,1152]{2,1,0:T(8,128)} custom-call(s32[2]{0:T(128)} %copy-done.51, bf16[576,1024]{1,0:T(8,128)(2,1)} %pad_maximum_fusion.3.refs_0_, bf16[576,512]{1,0:T(8,128)(2,1)} %constant_dynamic-update-slice_fusion.4.refs_1_, bf16[1024,576]{1,0:T(8,128)(2,1)} %bitcast.210, bf16[576,512]{1,0:T(8,128)(2,1)} %get-tuple-element.341.refs_3_, ...), custom_call_target="tpu_custom_call" | custom-call | flops 1000000 | bytes 10000 | tf_op jit(solution)/shard_map/many_half/pallas_call | solution.py:675
  271.8 19.0 %attention_scatter.5.refs_0_ = bf16[32,64,384]{2,1,0:T(8,128)(2,1)} custom-call(bf16[32,64,640]{2,1,0:T(8,128)(2,1)} %get-tuple-element.331.refs_0_, s32[3,256,640]{2,1,0:T(8,128)} %get-tuple-element.332.refs_1_, bf16[4,256,128]{2,1,0:T(8,128)(2,1)} %fusion.35.refs_2_.refs_3_), custom_call_target="tpu_custom_call" | custom-call | flops 1000000 | bytes 10000 | tf_op jit(solution)/shard_map/attention_scatter/pallas_call | solution.py:504
  290.8 3.9 fusion.29
  294.9 6.5 %many_half.7 = (f32[4,64,1152]{2,1,0:T(8,128)}, f32[4,64,1152]{2,1,0:T(8,128)}) custom-call(s32[2]{0:T(128)} %copy-done.50, bf16[576,1024]{1,0:T(8,128)(2,1)} %pad_maximum_fusion.3.refs_0_, bf16[576,512]{1,0:T(8,128)(2,1)} %constant_dynamic-update-slice_fusion.4.refs_1_, bf16[1024,576]{1,0:T(8,128)(2,1)} %bitcast.211, ...), custom_call_target="tpu_custom_call" | custom-call | flops 1000000 | bytes 10000 | tf_op jit(solution)/shard_map/many_half/pallas_call | solution.py:675
  306.3 2.6 collective-permute-start.15
  310.2 23.0 %attention_scatter.6.refs_1_ = bf16[40,64,384]{2,1,0:T(8,128)(2,1)} custom-call(bf16[40,64,640]{2,1,0:T(8,128)(2,1)} %get-tuple-element.355.refs_0_, s32[3,320,640]{2,1,0:T(8,128)} %get-tuple-element.279.b_ref.refs_1_, bf16[4,256,128]{2,1,0:T(8,128)(2,1)} %fusion.35.refs_2_.refs_3_), custom_call_target="tpu_custom_call" | custom-call | flops 1000000 | bytes 10000 | tf_op jit(solution)/shard_map/attention_scatter/pallas_call | solution.py:504
  335.4 5.4 %attention_close.2 = (bf16[576,512]{1,0:T(8,128)(2,1)}, bf16[384,512]{1,0:T(8,128)(2,1)}) custom-call(bf16[32,64,384]{2,1,0:T(8,128)(2,1)} %attention_scatter.5.refs_0_, bf16[40,64,384]{2,1,0:T(8,128)(2,1)} %attention_scatter.6.refs_1_, f32[256,512]{1,0:T(8,128)} %get-tuple-element.367.refs_2_, f32[320,512]{1,0:T(8,128)} %get-tuple-element.368.refs_3_, ...), custom_call_target="tpu_custom_call" | custom-call | flops 1000000 | bytes 10000 | tf_op jit(solution)/shard_map/attention_close/pallas_call | solution.py:522
  340.8 5.8 %many_half.8 = (f32[8,64,896]{2,1,0:T(8,128)}, f32[8,64,512]{2,1,0:T(8,128)}) custom-call(s32[3]{0:T(128)} %copy-done.57, bf16[1024,576]{1,0:T(8,128)(2,1)} %bitcast.212, bf16[576,512]{1,0:T(8,128)(2,1)} %get-tuple-element.369.refs_1_, bf16[1024,384]{1,0:T(8,128)(2,1)} %bitcast.216, bf16[384,512]{1,0:T(8,128)(2,1)} %get-tuple-element.372.refs_3_.refs_5_, ...), custom_call_target="tpu_custom_call" | custom-call | flops 1000000 | bytes 10000 | tf_op jit(solution)/shard_map/many_half/pallas_call | solution.py:675
  346.6 2.6 fusion.33
  352.8 14.6 %attention_scatter.7.refs_0_ = bf16[24,64,384]{2,1,0:T(8,128)(2,1)} custom-call(bf16[72,64,256]{2,1,0:T(8,128)(2,1)} %get-tuple-element.411.refs_0_, bf16[72,64,384]{2,1,0:T(8,128)(2,1)} %get-tuple-element.412.refs_1_, s32[3,576,640]{2,1,0:T(8,128)} %get-tuple-element.386.refs_2_, bf16[4,256,128]{2,1,0:T(8,128)(2,1)} %fusion.35.refs_2_.refs_3_), custom_call_target="tpu_custom_call" | custom-call | flops 1000000 | bytes 10000 | tf_op jit(solution)/shard_map/attention_scatter/pallas_call | solution.py:504
  367.4 6.9 %many_half.9 = (f32[4,64,896]{2,1,0:T(8,128)}, f32[4,64,896]{2,1,0:T(8,128)}, f32[4,64,512]{2,1,0:T(8,128)}, f32[4,64,512]{2,1,0:T(8,128)}) custom-call(s32[3]{0:T(128)} %copy-done.53, bf16[1024,576]{1,0:T(8,128)(2,1)} %bitcast.213, bf16[576,512]{1,0:T(8,128)(2,1)} %get-tuple-element.369.refs_1_, bf16[1024,384]{1,0:T(8,128)(2,1)} %bitcast.217, ...), custom_call_target="tpu_custom_call" | custom-call | flops 1000000 | bytes 10000 | tf_op jit(solution)/shard_map/many_half/pallas_call | solution.py:675
  375.5 14.6 %attention_scatter.8.refs_1_ = bf16[24,64,384]{2,1,0:T(8,128)(2,1)} custom-call(bf16[72,64,256]{2,1,0:T(8,128)(2,1)} %get-tuple-element.411.refs_0_, bf16[72,64,384]{2,1,0:T(8,128)(2,1)} %get-tuple-element.412.refs_1_, s32[3,576,640]{2,1,0:T(8,128)} %get-tuple-element.386.refs_2_, bf16[4,256,128]{2,1,0:T(8,128)(2,1)} %fusion.35.refs_2_.refs_3_), custom_call_target="tpu_custom_call" | custom-call | flops 1000000 | bytes 10000 | tf_op jit(solution)/shard_map/attention_scatter/pallas_call | solution.py:504
  395.4 2.6 collective-permute-start.22
  398.0 14.9 %attention_scatter.9.refs_2_ = bf16[24,64,384]{2,1,0:T(8,128)(2,1)} custom-call(bf16[72,64,256]{2,1,0:T(8,128)(2,1)} %get-tuple-element.411.refs_0_, bf16[72,64,384]{2,1,0:T(8,128)(2,1)} %get-tuple-element.412.refs_1_, s32[3,576,640]{2,1,0:T(8,128)} %get-tuple-element.386.refs_2_, bf16[4,256,128]{2,1,0:T(8,128)(2,1)} %fusion.35.refs_2_.refs_3_), custom_call_target="tpu_custom_call" | custom-call | flops 1000000 | bytes 10000 | tf_op jit(solution)/shard_map/attention_scatter/pallas_call | solution.py:504
  419.0 5.4 %attention_close.3 = (bf16[576,512]{1,0:T(8,128)(2,1)}, bf16[384,512]{1,0:T(8,128)(2,1)}) custom-call(bf16[24,64,384]{2,1,0:T(8,128)(2,1)} %attention_scatter.7.refs_0_, bf16[24,64,384]{2,1,0:T(8,128)(2,1)} %attention_scatter.8.refs_1_, bf16[24,64,384]{2,1,0:T(8,128)(2,1)} %attention_scatter.9.refs_2_, f32[576,512]{1,0:T(8,128)} %get-tuple-element.430.refs_3_, ...), custom_call_target="tpu_custom_call" | custom-call | flops 1000000 | bytes 10000 | tf_op jit(solution)/shard_map/attention_close/pallas_call | solution.py:522
  424.6 4.2 collective-permute-done.23
  430.4 5.9 %many_half.10 = (f32[8,64,896]{2,1,0:T(8,128)}, f32[8,64,512]{2,1,0:T(8,128)}) custom-call(s32[3]{0:T(128)} %copy-done.56, bf16[1024,576]{1,0:T(8,128)(2,1)} %bitcast.214, bf16[576,512]{1,0:T(8,128)(2,1)} %get-tuple-element.441.refs_1_, bf16[1024,384]{1,0:T(8,128)(2,1)} %bitcast.218, bf16[384,512]{1,0:T(8,128)(2,1)} %get-tuple-element.442.refs_3_.refs_5_, ...), custom_call_target="tpu_custom_call" | custom-call | flops 1000000 | bytes 10000 | tf_op jit(solution)/shard_map/many_half/pallas_call | solution.py:675
  444.0 6.7 %many_half.11 = (f32[4,64,896]{2,1,0:T(8,128)}, f32[4,64,896]{2,1,0:T(8,128)}, f32[4,64,512]{2,1,0:T(8,128)}, f32[4,64,512]{2,1,0:T(8,128)}) custom-call(s32[3]{0:T(128)} %copy-done.52, bf16[1024,576]{1,0:T(8,128)(2,1)} %bitcast.215, bf16[576,512]{1,0:T(8,128)(2,1)} %get-tuple-element.441.refs_1_, bf16[1024,384]{1,0:T(8,128)(2,1)} %bitcast.219, ...), custom_call_target="tpu_custom_call" | custom-call | flops 1000000 | bytes 10000 | tf_op jit(solution)/shard_map/many_half/pallas_call | solution.py:675
  460.7 9.0 %collective-permute-done.29 = f32[288,1024]{1,0:T(8,128)} collective-permute-done((f32[288,1024]{1,0:T(8,128)}, f32[288,1024]{1,0:T(8,128)}, u32[]{:S(2)}, u32[]{:S(2)}) %collective-permute-start.29) | collective-permute-done | bytes 1179680 | tf_op jit(solution)/shard_map/ppermute | solution.py:781
  471.2 3.5 collective-permute-done.28
  485.9 5.8 %collective-permute-done.32 = f32[2,64,896]{2,1,0:T(8,128)S(1)} collective-permute-done((f32[2,64,896]{2,1,0:T(8,128)S(1)}, f32[2,64,896]{2,1,0:T(8,128)S(1)}, u32[]{:S(2)}, u32[]{:S(2)}) %collective-permute-start.32) | collective-permute-done | bytes 458784 | tf_op jit(solution)/shard_map/ppermute | solution.py:694
  492.7 9.6 %collective-permute-done.33 = f32[64,896]{1,0:T(8,128)S(1)} collective-permute-done((f32[64,896]{1,0:T(8,128)S(1)}, f32[64,896]{1,0:T(8,128)S(1)}, u32[]{:S(2)}, u32[]{:S(2)}) %collective-permute-start.33) | collective-permute-done | bytes 229408 | tf_op jit(solution)/shard_map/ppermute | solution.py:694
  503.2 3.4 fusion.7
  (282 shorter events, 99.1 us)
Async XLA Ops:
  3.4 65.1 %collective-permute-start.1 = (f32[512,1024]{1,0:T(8,128)}, f32[512,1024]{1,0:T(8,128)}, u32[]{:S(2)}, u32[]{:S(2)}) collective-permute-start(f32[512,1024]{1,0:T(8,128)} %convert_element_type.60), channel_id=1, source_target_pairs={{0,1},{1,0},{2,3},{3,2},{4,5},{5,4},{6,7},{7,6},{8,9},{9,8},{10,11... | collective-permute-start | bytes 6291464 | tf_op jit(solution)/shard_map/ppermute | solution.py:781
  21.0 45.0 %copy-start.29 = (bf16[561,1024]{1,0:T(8,128)(2,1)S(1)}, bf16[561,1024]{1,0:T(8,128)(2,1)}, u32[]{:S(2)}) copy-start(bf16[561,1024]{1,0:T(8,128)(2,1)} %x_ref.1) | copy-start | bytes 3446788
  65.9 28.8 %collective-permute-start = (f32[256,512]{1,0:T(8,128)}, f32[256,512]{1,0:T(8,128)}, u32[]{:S(2)}, u32[]{:S(2)}) collective-permute-start(f32[256,512]{1,0:T(8,128)} %get-tuple-element.274), channel_id=1, source_target_pairs={{0,1},{1,0},{2,3},{3,2},{4,5},{5,4},{6,7},{7,6},{8,9},{9,8},{10,11... | collective-permute-start | bytes 1572872 | tf_op jit(solution)/shard_map/ppermute | solution.py:781
  66.8 25.8 %copy-start = (bf16[576,1024]{0,1:T(8,128)(2,1)}, bf16[576,1024]{0,1:T(8,128)(2,1)S(1)}, u32[]{:S(2)}) copy-start(bf16[576,1024]{0,1:T(8,128)(2,1)S(1)} %pad.16) | copy-start | bytes 3538948
  68.4 24.2 %copy-start.54 = (s32[2]{0:T(128)}, s32[2]{0:T(128)S(1)}, u32[]{:S(2)}) copy-start(s32[2]{0:T(128)S(1)} %pad_add_fusion.pick_ref) | copy-start | bytes 28
  68.5 24.1 %copy-start.50 = (s32[2]{0:T(128)}, s32[2]{0:T(128)S(1)}, u32[]{:S(2)}) copy-start(s32[2]{0:T(128)S(1)} %pad_add_fusion.1.pick_ref) | copy-start | bytes 28
  68.5 24.1 %copy-start.55 = (s32[2]{0:T(128)}, s32[2]{0:T(128)S(1)}, u32[]{:S(2)}) copy-start(s32[2]{0:T(128)S(1)} %constant_dynamic-update-slice_fusion.3.pick_ref) | copy-start | bytes 28
  68.5 24.1 %copy-start.51 = (s32[2]{0:T(128)}, s32[2]{0:T(128)S(1)}, u32[]{:S(2)}) copy-start(s32[2]{0:T(128)S(1)} %constant_dynamic-update-slice_fusion.2.pick_ref) | copy-start | bytes 28
  92.7 19.1 %collective-permute-start.3 = (f32[320,512]{1,0:T(8,128)}, f32[320,512]{1,0:T(8,128)S(1)}, u32[]{:S(2)}, u32[]{:S(2)}) collective-permute-start(f32[320,512]{1,0:T(8,128)} %get-tuple-element.283), channel_id=1, source_target_pairs={{0,1},{1,0},{2,3},{3,2},{4,5},{5,4},{6,7},{7,6},{8,9},{9,8},{10,11... | collective-permute-start | bytes 1966088 | tf_op jit(solution)/shard_map/ppermute | solution.py:781
  111.7 26.2 %collective-permute-start.2 = (f32[256,1024]{1,0:T(8,128)S(1)}, f32[256,1024]{1,0:T(8,128)}, u32[]{:S(2)}, u32[]{:S(2)}) collective-permute-start(f32[256,1024]{1,0:T(8,128)S(1)} %fusion.55), channel_id=1, source_target_pairs={{0,1},{1,0},{2,3},{3,2},{4,5},{5,4},{6,7},{7,6},{8,9},{9,8},{10,11... | collective-permute-start | bytes 3145736 | tf_op jit(solution)/shard_map/ppermute | solution.py:781
  131.5 34.4 %collective-permute-start.4 = (f32[320,1024]{1,0:T(8,128)S(1)}, f32[320,1024]{1,0:T(8,128)S(1)}, u32[]{:S(2)}, u32[]{:S(2)}) collective-permute-start(f32[320,1024]{1,0:T(8,128)S(1)} %fusion.56), channel_id=1, source_target_pairs={{0,1},{1,0},{2,3},{3,2},{4,5},{5,4},{6,7},{7,6},{8,9},{9,8},{10,11... | collective-permute-start | bytes 3932168 | tf_op jit(solution)/shard_map/ppermute | solution.py:781
  146.9 39.7 %collective-permute-start.5 = (f32[256,1024]{1,0:T(8,128)}, f32[256,1024]{1,0:T(8,128)}, u32[]{:S(2)}, u32[]{:S(2)}) collective-permute-start(f32[256,1024]{1,0:T(8,128)} %fusion.57), channel_id=1, source_target_pairs={{0,1},{1,0},{2,3},{3,2},{4,5},{5,4},{6,7},{7,6},{8,9},{9,8},{10,11... | collective-permute-start | bytes 3145736 | tf_op jit(solution)/shard_map/ppermute | solution.py:781
  181.3 16.8 %collective-permute-start.6 = (f32[8,64,2048]{2,1,0:T(8,128)}, f32[8,64,2048]{2,1,0:T(8,128)}, u32[]{:S(2)}, u32[]{:S(2)}) collective-permute-start(f32[8,64,2048]{2,1,0:T(8,128)} %weight_half.4), channel_id=1, source_target_pairs={{0,2},{2,0},{4,6},{6,4},{8,10},{10,8},{12,14},{14,12},{16,18},{18,... | collective-permute-start | bytes 12582920 | tf_op jit(solution)/shard_map/ppermute | solution.py:694
  194.1 13.8 %collective-permute-start.7 = (f32[8,64,2048]{2,1,0:T(8,128)}, f32[8,64,2048]{2,1,0:T(8,128)}, u32[]{:S(2)}, u32[]{:S(2)}) collective-permute-start(f32[8,64,2048]{2,1,0:T(8,128)} %weight_half.6), channel_id=1, source_target_pairs={{0,2},{2,0},{4,6},{6,4},{8,10},{10,8},{12,14},{14,12},{16,18},{18,... | collective-permute-start | bytes 12582920 | tf_op jit(solution)/shard_map/ppermute | solution.py:694
  197.7 35.9 %collective-permute-start.8 = (f32[320,1024]{1,0:T(8,128)}, f32[320,1024]{1,0:T(8,128)}, u32[]{:S(2)}, u32[]{:S(2)}) collective-permute-start(f32[320,1024]{1,0:T(8,128)} %fusion.58), channel_id=1, source_target_pairs={{0,1},{1,0},{2,3},{3,2},{4,5},{5,4},{6,7},{7,6},{8,9},{9,8},{10,11... | collective-permute-start | bytes 3932168 | tf_op jit(solution)/shard_map/ppermute | solution.py:781
  206.1 54.1 %collective-permute-start.9 = (f32[4,64,2048]{2,1,0:T(8,128)}, f32[4,64,2048]{2,1,0:T(8,128)}, u32[]{:S(2)}, u32[]{:S(2)}) collective-permute-start(f32[4,64,2048]{2,1,0:T(8,128)} %get-tuple-element.325), channel_id=1, source_target_pairs={{0,8},{2,10},{4,12},{6,14},{8,0},{10,2},{12,4},{14,6},{16,24},{18,... | collective-permute-start | bytes 6291464 | tf_op jit(solution)/shard_map/ppermute | solution.py:694
  233.6 57.2 %collective-permute-start.10 = (f32[4,64,2048]{2,1,0:T(8,128)}, f32[4,64,2048]{2,1,0:T(8,128)}, u32[]{:S(2)}, u32[]{:S(2)}) collective-permute-start(f32[4,64,2048]{2,1,0:T(8,128)} %get-tuple-element.333), channel_id=1, source_target_pairs={{0,4},{2,6},{4,0},{6,2},{8,12},{10,14},{12,8},{14,10},{16,20},{18,... | collective-permute-start | bytes 6291464 | tf_op jit(solution)/shard_map/ppermute | solution.py:694
  270.3 24.6 %collective-permute-start.11 = (f32[8,64,1152]{2,1,0:T(8,128)}, f32[8,64,1152]{2,1,0:T(8,128)}, u32[]{:S(2)}, u32[]{:S(2)}) collective-permute-start(f32[8,64,1152]{2,1,0:T(8,128)} %many_half.6), channel_id=1, source_target_pairs={{0,2},{2,0},{4,6},{6,4},{8,10},{10,8},{12,14},{14,12},{16,18},{18,... | collective-permute-start | bytes 7077896 | tf_op jit(solution)/shard_map/ppermute | solution.py:694
  270.3 33.6 %collective-permute-start.12 = (f32[2,64,2048]{2,1,0:T(8,128)}, f32[2,64,2048]{2,1,0:T(8,128)}, u32[]{:S(2)}, u32[]{:S(2)}) collective-permute-start(f32[2,64,2048]{2,1,0:T(8,128)} %get-tuple-element.349), channel_id=1, source_target_pairs={{0,4},{2,6},{4,0},{6,2},{8,12},{10,14},{12,8},{14,10},{16,20},{18,... | collective-permute-start | bytes 3145736 | tf_op jit(solution)/shard_map/ppermute | solution.py:694
  294.7 38.5 %collective-permute-start.13 = (f32[2,64,2048]{2,1,0:T(8,128)}, f32[2,64,2048]{2,1,0:T(8,128)}, u32[]{:S(2)}, u32[]{:S(2)}) collective-permute-start(f32[2,64,2048]{2,1,0:T(8,128)} %get-tuple-element.358), channel_id=1, source_target_pairs={{0,8},{2,10},{4,12},{6,14},{8,0},{10,2},{12,4},{14,6},{16,24},{18,... | collective-permute-start | bytes 3145736 | tf_op jit(solution)/shard_map/ppermute | solution.py:694
  301.4 45.1 %collective-permute-start.14 = (f32[4,64,1152]{2,1,0:T(8,128)}, f32[4,64,1152]{2,1,0:T(8,128)}, u32[]{:S(2)}, u32[]{:S(2)}) collective-permute-start(f32[4,64,1152]{2,1,0:T(8,128)} %get-tuple-element.373), channel_id=1, source_target_pairs={{0,4},{2,6},{4,0},{6,2},{8,12},{10,14},{12,8},{14,10},{16,20},{18,... | collective-permute-start | bytes 3538952 | tf_op jit(solution)/shard_map/ppermute | solution.py:694
  306.3 40.3 %collective-permute-start.15 = (f32[64,2048]{1,0:T(8,128)}, f32[64,2048]{1,0:T(8,128)}, u32[]{:S(2)}, u32[]{:S(2)}) collective-permute-start(f32[64,2048]{1,0:T(8,128)} %get-tuple-element.374), channel_id=1, source_target_pairs={{0,16},{2,18},{4,20},{6,22},{8,24},{10,26},{12,28},{14,30},{16,0},... | collective-permute-start | bytes 1572872 | tf_op jit(solution)/shard_map/ppermute | solution.py:694
  308.9 24.3 %copy-start.53 = (s32[3]{0:T(128)}, s32[3]{0:T(128)S(1)}, u32[]{:S(2)}) copy-start(s32[3]{0:T(128)S(1)} %get-tuple-element.548.pick_ref) | copy-start | bytes 40
  308.9 110.0 %copy-start.52 = (s32[3]{0:T(128)}, s32[3]{0:T(128)S(1)}, u32[]{:S(2)}) copy-start(s32[3]{0:T(128)S(1)} %get-tuple-element.549.pick_ref) | copy-start | bytes 40
  309.0 24.2 %copy-start.57 = (s32[3]{0:T(128)}, s32[3]{0:T(128)S(1)}, u32[]{:S(2)}) copy-start(s32[3]{0:T(128)S(1)} %constant_dynamic-update-slice_fusion.1.pick_ref) | copy-start | bytes 40
  310.2 23.0 %copy-start.19 = (f32[2,64,2048]{2,1,0:T(8,128)S(1)}, f32[2,64,2048]{2,1,0:T(8,128)}, u32[]{:S(2)}) copy-start(f32[2,64,2048]{2,1,0:T(8,128)} %get-tuple-element.363) | copy-start | bytes 3145732
  351.1 16.3 %collective-permute-start.16 = (f32[8,64,896]{2,1,0:T(8,128)}, f32[8,64,896]{2,1,0:T(8,128)}, u32[]{:S(2)}, u32[]{:S(2)}) collective-permute-start(f32[8,64,896]{2,1,0:T(8,128)} %get-tuple-element.387), channel_id=1, source_target_pairs={{0,2},{2,0},{4,6},{6,4},{8,10},{10,8},{12,14},{14,12},{16,18},{18,... | collective-permute-start | bytes 5505032 | tf_op jit(solution)/shard_map/ppermute | solution.py:694
  351.1 16.3 %collective-permute-start.17 = (f32[8,64,512]{2,1,0:T(8,128)}, f32[8,64,512]{2,1,0:T(8,128)}, u32[]{:S(2)}, u32[]{:S(2)}) collective-permute-start(f32[8,64,512]{2,1,0:T(8,128)} %get-tuple-element.388), channel_id=1, source_target_pairs={{0,2},{2,0},{4,6},{6,4},{8,10},{10,8},{12,14},{14,12},{16,18},{18,... | collective-permute-start | bytes 3145736 | tf_op jit(solution)/shard_map/ppermute | solution.py:694
  351.6 38.5 %collective-permute-start.18 = (f32[2,64,1152]{2,1,0:T(8,128)}, f32[2,64,1152]{2,1,0:T(8,128)}, u32[]{:S(2)}, u32[]{:S(2)}) collective-permute-start(f32[2,64,1152]{2,1,0:T(8,128)} %get-tuple-element.401), channel_id=1, source_target_pairs={{0,8},{2,10},{4,12},{6,14},{8,0},{10,2},{12,4},{14,6},{16,24},{18,... | collective-permute-start | bytes 1769480 | tf_op jit(solution)/shard_map/ppermute | solution.py:694
  352.5 37.6 %collective-permute-start.19 = (f32[64,2048]{1,0:T(8,128)}, f32[64,2048]{1,0:T(8,128)}, u32[]{:S(2)}, u32[]{:S(2)}) collective-permute-start(f32[64,2048]{1,0:T(8,128)} %get-tuple-element.402), channel_id=1, source_target_pairs={{0,16},{2,18},{4,20},{6,22},{8,24},{10,26},{12,28},{14,30},{16,0},... | collective-permute-start | bytes 1572872 | tf_op jit(solution)/shard_map/ppermute | solution.py:694
  374.4 38.6 %collective-permute-start.20 = (f32[4,64,896]{2,1,0:T(8,128)}, f32[4,64,896]{2,1,0:T(8,128)}, u32[]{:S(2)}, u32[]{:S(2)}) collective-permute-start(f32[4,64,896]{2,1,0:T(8,128)} %get-tuple-element.415), channel_id=1, source_target_pairs={{0,8},{2,10},{4,12},{6,14},{8,0},{10,2},{12,4},{14,6},{16,24},{18,... | collective-permute-start | bytes 2752520 | tf_op jit(solution)/shard_map/ppermute | solution.py:694
  390.1 22.8 %collective-permute-start.21 = (f32[4,64,512]{2,1,0:T(8,128)}, f32[4,64,512]{2,1,0:T(8,128)}, u32[]{:S(2)}, u32[]{:S(2)}) collective-permute-start(f32[4,64,512]{2,1,0:T(8,128)} %get-tuple-element.416), channel_id=1, source_target_pairs={{0,4},{2,6},{4,0},{6,2},{8,12},{10,14},{12,8},{14,10},{16,20},{18,... | collective-permute-start | bytes 1572872 | tf_op jit(solution)/shard_map/ppermute | solution.py:694
  395.4 17.5 %collective-permute-start.22 = (f32[64,1152]{1,0:T(8,128)}, f32[64,1152]{1,0:T(8,128)S(1)}, u32[]{:S(2)}, u32[]{:S(2)}) collective-permute-start(f32[64,1152]{1,0:T(8,128)} %get-tuple-element.417), channel_id=1, source_target_pairs={{0,16},{2,18},{4,20},{6,22},{8,24},{10,26},{12,28},{14,30},{16,0},... | collective-permute-start | bytes 884744 | tf_op jit(solution)/shard_map/ppermute | solution.py:694
  417.6 11.2 %collective-permute-start.23 = (f32[2,64,896]{2,1,0:T(8,128)}, f32[2,64,896]{2,1,0:T(8,128)S(1)}, u32[]{:S(2)}, u32[]{:S(2)}) collective-permute-start(f32[2,64,896]{2,1,0:T(8,128)} %get-tuple-element.433), channel_id=1, source_target_pairs={{0,4},{2,6},{4,0},{6,2},{8,12},{10,14},{12,8},{14,10},{16,20},{18,... | collective-permute-start | bytes 1376264 | tf_op jit(solution)/shard_map/ppermute | solution.py:694
  418.1 6.5 %collective-permute-start.24 = (f32[2,64,512]{2,1,0:T(8,128)S(1)}, f32[2,64,512]{2,1,0:T(8,128)S(1)}, u32[]{:S(2)}, u32[]{:S(2)}) collective-permute-start(f32[2,64,512]{2,1,0:T(8,128)S(1)} %get-tuple-element.434), channel_id=1, source_target_pairs={{0,8},{2,10},{4,12},{6,14},{8,0},{10,2},{12,4},{14,6},{16,24},{18,... | collective-permute-start | bytes 786440 | tf_op jit(solution)/shard_map/ppermute | solution.py:694
  436.3 7.7 %collective-permute-start.25 = (f32[8,64,896]{2,1,0:T(8,128)}, f32[8,64,896]{2,1,0:T(8,128)}, u32[]{:S(2)}, u32[]{:S(2)}) collective-permute-start(f32[8,64,896]{2,1,0:T(8,128)} %get-tuple-element.443), channel_id=1, source_target_pairs={{0,2},{2,0},{4,6},{6,4},{8,10},{10,8},{12,14},{14,12},{16,18},{18,... | collective-permute-start | bytes 5505032 | tf_op jit(solution)/shard_map/ppermute | solution.py:694
  436.3 6.7 %collective-permute-start.26 = (f32[8,64,512]{2,1,0:T(8,128)}, f32[8,64,512]{2,1,0:T(8,128)S(1)}, u32[]{:S(2)}, u32[]{:S(2)}) collective-permute-start(f32[8,64,512]{2,1,0:T(8,128)} %get-tuple-element.444), channel_id=1, source_target_pairs={{0,2},{2,0},{4,6},{6,4},{8,10},{10,8},{12,14},{14,12},{16,18},{18,... | collective-permute-start | bytes 3145736 | tf_op jit(solution)/shard_map/ppermute | solution.py:694
  441.5 28.2 %collective-permute-start.29 = (f32[288,1024]{1,0:T(8,128)}, f32[288,1024]{1,0:T(8,128)}, u32[]{:S(2)}, u32[]{:S(2)}) collective-permute-start(f32[288,1024]{1,0:T(8,128)} %convolution_add_fusion.2), channel_id=1, source_target_pairs={{0,1},{1,0},{2,3},{3,2},{4,5},{5,4},{6,7},{7,6},{8,9},{9,8},{10,11... | collective-permute-start | bytes 3538952 | tf_op jit(solution)/shard_map/ppermute | solution.py:781
  450.6 24.1 %collective-permute-start.27 = (f32[4,64,896]{2,1,0:T(8,128)}, f32[4,64,896]{2,1,0:T(8,128)}, u32[]{:S(2)}, u32[]{:S(2)}) collective-permute-start(f32[4,64,896]{2,1,0:T(8,128)} %get-tuple-element.445), channel_id=1, source_target_pairs={{0,4},{2,6},{4,0},{6,2},{8,12},{10,14},{12,8},{14,10},{16,20},{18,... | collective-permute-start | bytes 2752520 | tf_op jit(solution)/shard_map/ppermute | solution.py:694
  453.5 21.2 %collective-permute-start.28 = (f32[4,64,512]{2,1,0:T(8,128)}, f32[4,64,512]{2,1,0:T(8,128)S(1)}, u32[]{:S(2)}, u32[]{:S(2)}) collective-permute-start(f32[4,64,512]{2,1,0:T(8,128)} %get-tuple-element.446), channel_id=1, source_target_pairs={{0,8},{2,10},{4,12},{6,14},{8,0},{10,2},{12,4},{14,6},{16,24},{18,... | collective-permute-start | bytes 1572872 | tf_op jit(solution)/shard_map/ppermute | solution.py:694
  456.0 18.8 %collective-permute-start.30 = (f32[64,896]{1,0:T(8,128)S(1)}, f32[64,896]{1,0:T(8,128)S(1)}, u32[]{:S(2)}, u32[]{:S(2)}) collective-permute-start(f32[64,896]{1,0:T(8,128)S(1)} %copy-done.45), channel_id=1, source_target_pairs={{0,16},{2,18},{4,20},{6,22},{8,24},{10,26},{12,28},{14,30},{16,0},... | collective-permute-start | bytes 688136 | tf_op jit(solution)/shard_map/ppermute | solution.py:694
  457.2 17.5 %collective-permute-start.31 = (f32[64,512]{1,0:T(8,128)S(1)}, f32[64,512]{1,0:T(8,128)S(1)}, u32[]{:S(2)}, u32[]{:S(2)}) collective-permute-start(f32[64,512]{1,0:T(8,128)S(1)} %copy-done.47), channel_id=1, source_target_pairs={{0,16},{2,18},{4,20},{6,22},{8,24},{10,26},{12,28},{14,30},{16,0},... | collective-permute-start | bytes 393224 | tf_op jit(solution)/shard_map/ppermute | solution.py:694
  469.7 32.7 %collective-permute-start.34 = (f32[288,1024]{1,0:T(8,128)S(1)}, f32[288,1024]{1,0:T(8,128)S(1)}, u32[]{:S(2)}, u32[]{:S(2)}) collective-permute-start(f32[288,1024]{1,0:T(8,128)S(1)} %convolution_add_fusion.1), channel_id=1, source_target_pairs={{0,1},{1,0},{2,3},{3,2},{4,5},{5,4},{6,7},{7,6},{8,9},{9,8},{10,11... | collective-permute-start | bytes 3538952 | tf_op jit(solution)/shard_map/ppermute | solution.py:781
  475.5 6.8 %collective-permute-start.35 = (f32[2,64,512]{2,1,0:T(8,128)S(1)}, f32[2,64,512]{2,1,0:T(8,128)S(1)}, u32[]{:S(2)}, u32[]{:S(2)}) collective-permute-start(f32[2,64,512]{2,1,0:T(8,128)S(1)} %fusion.41), channel_id=1, source_target_pairs={{0,4},{2,6},{4,0},{6,2},{8,12},{10,14},{12,8},{14,10},{16,20},{18,... | collective-permute-start | bytes 786440 | tf_op jit(solution)/shard_map/ppermute | solution.py:694
  478.1 13.6 %collective-permute-start.32 = (f32[2,64,896]{2,1,0:T(8,128)S(1)}, f32[2,64,896]{2,1,0:T(8,128)S(1)}, u32[]{:S(2)}, u32[]{:S(2)}) collective-permute-start(f32[2,64,896]{2,1,0:T(8,128)S(1)} %fusion.36), channel_id=1, source_target_pairs={{0,8},{2,10},{4,12},{6,14},{8,0},{10,2},{12,4},{14,6},{16,24},{18,... | collective-permute-start | bytes 1376264 | tf_op jit(solution)/shard_map/ppermute | solution.py:694
  482.4 9.7 %collective-permute-start.36 = (f32[64,512]{1,0:T(8,128)S(1)}, f32[64,512]{1,0:T(8,128)S(1)}, u32[]{:S(2)}, u32[]{:S(2)}) collective-permute-start(f32[64,512]{1,0:T(8,128)S(1)} %fusion.45), channel_id=1, source_target_pairs={{0,16},{2,18},{4,20},{6,22},{8,24},{10,26},{12,28},{14,30},{16,0},... | collective-permute-start | bytes 393224 | tf_op jit(solution)/shard_map/ppermute | solution.py:694
  491.7 10.6 %collective-permute-start.33 = (f32[64,896]{1,0:T(8,128)S(1)}, f32[64,896]{1,0:T(8,128)S(1)}, u32[]{:S(2)}, u32[]{:S(2)}) collective-permute-start(f32[64,896]{1,0:T(8,128)S(1)} %fusion.44), channel_id=1, source_target_pairs={{0,16},{2,18},{4,20},{6,22},{8,24},{10,26},{12,28},{14,30},{16,0},... | collective-permute-start | bytes 688136 | tf_op jit(solution)/shard_map/ppermute | solution.py:694
  502.4 4.9 collective-permute-start.37
  (54 other events, 375.1 us)
